TPU v7x, 32 devices: a whole 2x2x4 slice. The times are simulated.
32 devices in a mesh: dp: 8 (over z, x), expert: 4 (over y, core).
Axes of the slice: x: 2, y: 2, z: 4, core: 2. Of those that a mesh axis runs over, the one named last changes fastest.
Arguments:
- tokens: bfloat16 [2, 8, 256, 2048], P(None, 'dp', 'expert'), may hold values from -6 to 6
- w_query: bfloat16 [4, 2048, 2048], P('expert', 'dp'), may hold values from -0.125 to 0.125
- w_out: bfloat16 [4, 2048, 2048], P('expert', 'dp'), may hold values from -1.5 to 1.5
- w_key: bfloat16 [2048, 2048], P(('dp', 'expert')), may hold values from -0.125 to 0.125
- w_value: bfloat16 [2048, 2048], P(('dp', 'expert')), may hold values from -0.125 to 0.125
- gain_attn: bfloat16 [2048], P(('dp', 'expert')), may hold values from 0.5 to 1.5
- router_attn: bfloat16 [2048, 4], P(('dp', 'expert')), may hold values from -0.09375 to 0.09375
- gain_mlp: bfloat16 [2048], P(('dp', 'expert')), may hold values from 0.5 to 1.5
- router_mlp: bfloat16 [2048, 4], P(('dp', 'expert')), may hold values from -0.09375 to 0.09375
- w_gate: bfloat16 [4, 5632, 2048], P('expert', 'dp'), may hold values from -0.125 to 0.125
- w_up: bfloat16 [4, 5632, 2048], P('expert', 'dp'), may hold values from -0.125 to 0.125
- w_down: bfloat16 [4, 5632, 2048], P('expert', 'dp'), may hold values from -0.109375 to 0.109375
- attn_route: int32 [2, 8, 256, 2], P(None, 'dp'), may hold values from 0 to 3, all different within a row
- mlp_route: int32 [2, 8, 256, 2], P(None, 'dp', 'expert'), may hold values from 0 to 3, all different within a row
- fill_order: int32 [2, 8, 256], P(None, 'dp', 'expert'), may hold values from 0 to 255, each once within a row
- parents: int32 [2, 8, 13], P(None, 'dp'), may hold values from 0 to 4, as said below
- cotangent: bfloat16 [2, 8, 256, 2048], P(None, 'dp', 'expert'), may hold values from -6 to 6
Outputs:
- layer_out: bfloat16 [2, 8, 256, 2048], P(None, 'dp', 'expert')
- tokens_grad: float32 [2, 8, 256, 2048], P(None, 'dp', 'expert')
- w_query_grad: float32 [4, 2048, 2048], P('expert', 'dp')
- w_out_grad: float32 [4, 2048, 2048], P('expert', 'dp')
- w_key_grad: float32 [2048, 2048], P(('dp', 'expert'))
- w_value_grad: float32 [2048, 2048], P(('dp', 'expert'))
- gain_attn_grad: float32 [2048], P(('dp', 'expert'))
- router_attn_grad: float32 [2048, 4], P(('dp', 'expert'))
- gain_mlp_grad: float32 [2048], P(('dp', 'expert'))
- router_mlp_grad: float32 [2048, 4], P(('dp', 'expert'))
- w_gate_grad: float32 [4, 5632, 2048], P('expert', 'dp')
- w_up_grad: float32 [4, 5632, 2048], P('expert', 'dp')
- w_down_grad: float32 [4, 5632, 2048], P('expert', 'dp')
Inputs may be any that keep to these rules, and one draw needn't show every extreme that they name: `parents`: in every tree segment 0 is the trunk, 1 to 4 the branches and 5 to 12 the leaves; the trunk's and each branch's parent is 0, and each branch is the parent of exactly two leaves. `attn_route`: each token names 2 different experts. `mlp_route`: each token names 2 different experts. `fill_order`: a permutation of the positions of each tree.
All inputs are finite; a program needn't handle non-finite values.
Results may differ from a plain program's by a relative error of at most 0.03.
Values may be sent and summed in bfloat16 or wider, within the bound.
A program may use at most 304 MiB of HBM per device.

v0:
```python
from functools import partial
import math

import jax
import jax.numpy as jnp
from jax import lax
from jax.sharding import PartitionSpec as P

HEADS = 16
HDIM = 128


EPSILON = 1e-06
HIGHEST = lax.Precision.HIGHEST


def exact_product(left, right):
    return jnp.dot(left, right, precision=HIGHEST, preferred_element_type=jnp.float32)


def product(left, right):
    return jnp.dot(left, right, preferred_element_type=jnp.float32)


def product_tn(left, right):
    return lax.dot_general(
        left, right, (((0,), (0,)), ((), ())), preferred_element_type=jnp.float32
    )


def product_nt(left, right):
    return lax.dot_general(
        left, right, (((1,), (1,)), ((), ())), preferred_element_type=jnp.float32
    )


def rms_scaled(values, gain):
    return values * lax.rsqrt(jnp.mean(values * values, axis=-1, keepdims=True) + EPSILON) * gain


def mixture_gates(picked, logits):
    labels = jnp.arange(logits.shape[1], dtype=jnp.int32)
    onehot = (picked[:, :, None] == labels[None, None, :]).astype(jnp.float32)
    chosen = jnp.sum(onehot * logits[:, None, :], axis=-1)
    weights = jax.nn.softmax(chosen, axis=-1)
    return jnp.sum(weights[:, :, None] * onehot, axis=1)


def tree_layout(segment_len, tree_len):
    places = jnp.arange(tree_len, dtype=jnp.int32)
    trunk_len = 4 * segment_len
    segment = jnp.where(
        places < trunk_len,
        0,
        jnp.where(
            places < 2 * trunk_len,
            1 + (places - trunk_len) // segment_len,
            5 + (places - 2 * trunk_len) // segment_len,
        ),
    )
    depth = jnp.where(
        places < trunk_len,
        places,
        jnp.where(
            places < 2 * trunk_len,
            trunk_len + (places - trunk_len) % segment_len,
            trunk_len + segment_len + (places - 2 * trunk_len) % segment_len,
        ),
    )
    return (places, segment, depth)


def ancestors(parent, segment):
    labels = jnp.arange(parent.shape[0], dtype=jnp.int32)
    first = jnp.where(labels > 0, parent, -1)
    lookup = jnp.maximum(first, 0)[:, None] == labels[None, :]
    second = jnp.where(first > 0, jnp.sum(jnp.where(lookup, parent[None, :], 0), axis=1), -1)
    member = segment[:, None] == labels[None, :]
    up_one = jnp.sum(jnp.where(member, first[None, :], 0), axis=1)
    up_two = jnp.sum(jnp.where(member, second[None, :], 0), axis=1)
    return (up_one, up_two)


def visible(query_seg, query_place, query_up, query_top, key_seg, key_place):
    same = (key_seg[None, :] == query_seg[:, None]) & (key_place[None, :] <= query_place[:, None])
    return same | (key_seg[None, :] == query_up[:, None]) | (key_seg[None, :] == query_top[:, None])


def rotate(values, depth, sign):
    half = values.shape[-1] // 2
    rates = 10000.0 ** (-jnp.arange(half, dtype=jnp.float32) / half)
    angle = depth.astype(jnp.float32)[:, None] * rates[None, :]
    cosine = jnp.cos(angle)[:, None, :]
    sine = sign * jnp.sin(angle)[:, None, :]
    first = values[..., :half]
    second = values[..., half:]
    return jnp.concatenate(
        [first * cosine - second * sine, second * cosine + first * sine], axis=-1
    )


def slot_table(picked, order, experts, capacity):
    labels = jnp.arange(experts, dtype=jnp.int32)
    chosen = jnp.sum((picked[:, :, None] == labels[None, None, :]).astype(jnp.float32), axis=1)
    earlier = (order[None, :] < order[:, None]).astype(jnp.float32)
    ranks = jnp.dot(earlier, chosen, precision=HIGHEST, preferred_element_type=jnp.float32)
    slots = jnp.arange(capacity, dtype=jnp.float32)
    return jnp.transpose(chosen)[:, None, :] * (
        jnp.transpose(ranks)[:, None, :] == slots[None, :, None]
    ).astype(jnp.float32)


def score_block(queries, keys, layout, scale):
    segment, places, up_one, up_two = layout
    allowed = visible(segment, places, up_one, up_two, segment, places)
    scores = jnp.einsum("qhd,khd->hqk", queries, keys, preferred_element_type=jnp.float32) * scale
    return (queries, jnp.where(allowed[None], scores, -1e30))


def attend(queries, keys, values, layout, scale):
    total_rows = queries.shape[0]
    block = min(512, total_rows)

    def one_block(block_index):
        _, scores = score_block(queries, keys, layout, scale)
        highest = jnp.max(scores, axis=-1, keepdims=True)
        weights = jnp.exp(scores - highest)
        mass = jnp.sum(weights, axis=-1, keepdims=True)
        probs = (weights / mass).astype(jnp.bfloat16)
        result = jnp.einsum(
            "hqk,khd->qhd", probs, values, preferred_element_type=jnp.float32
        ).astype(jnp.bfloat16)
        return (result, (highest + jnp.log(mass))[..., 0])

    results, logsum = lax.map(one_block, jnp.arange(total_rows // block, dtype=jnp.int32))
    return (results.reshape(queries.shape), logsum)


def attend_back(queries, keys, values, heads_grad, logsum, layout, scale):
    total_rows = queries.shape[0]
    block = min(512, total_rows)

    def one_block(carry, item):
        key_grad, value_grad = carry
        block_index, block_logsum = item
        query_block, scores = score_block(queries, keys, layout, scale)
        probs = jnp.exp(scores - block_logsum[..., None])
        rounded = probs.astype(jnp.bfloat16)
        prob_grad = jnp.einsum(
            "qhd,khd->hqk", heads_grad, values, preferred_element_type=jnp.float32
        )
        centre = jnp.sum(prob_grad * probs, axis=-1, keepdims=True)
        score_grad = (probs * (prob_grad - centre) * scale).astype(jnp.bfloat16)
        query_grad = jnp.einsum(
            "hqk,khd->qhd", score_grad, keys, preferred_element_type=jnp.float32
        )
        key_grad = key_grad + jnp.einsum(
            "hqk,qhd->khd", score_grad, query_block, preferred_element_type=jnp.float32
        )
        value_grad = value_grad + jnp.einsum(
            "hqk,qhd->khd", rounded, heads_grad, preferred_element_type=jnp.float32
        )
        return ((key_grad, value_grad), query_grad)

    zeros = jnp.zeros(keys.shape, jnp.float32)
    steps_index = jnp.arange(total_rows // block, dtype=jnp.int32)
    (key_grad, value_grad), query_grads = lax.scan(one_block, (zeros, zeros), (steps_index, logsum))
    return (query_grads.reshape(queries.shape), key_grad, value_grad)


def to_experts(buffer):
    return lax.all_to_all(buffer, "expert", split_axis=0, concat_axis=0, tiled=True)


def from_experts(buffer):
    return lax.all_to_all(buffer, "expert", split_axis=0, concat_axis=0, tiled=True)


def body(
    tokens,
    w_query,
    w_out,
    w_key,
    w_value,
    gain_attn,
    router_attn,
    gain_mlp,
    router_mlp,
    w_gate,
    w_up,
    w_down,
    attn_route,
    mlp_route,
    fill_order,
    parents,
    cotangent,
):
    experts = lax.axis_size("expert")
    position = lax.axis_index("expert")
    key_full, value_full, gain_first, router_first, gain_second, router_second = (
        lax.all_gather(w_key, ("dp", "expert"), axis=0, tiled=True),
        lax.all_gather(w_value, ("dp", "expert"), axis=0, tiled=True),
        lax.all_gather(gain_attn, ("dp", "expert"), axis=0, tiled=True),
        lax.all_gather(router_attn, ("dp", "expert"), axis=0, tiled=True),
        lax.all_gather(gain_mlp, ("dp", "expert"), axis=0, tiled=True),
        lax.all_gather(router_mlp, ("dp", "expert"), axis=0, tiled=True),
    )
    micro_count = tokens.shape[0]
    tok_rows = tokens.shape[2]
    width = tokens.shape[3]
    tree_rows = experts * tok_rows
    segment_len = tree_rows // 16
    heads_total = HEADS * HDIM
    capacity = tok_rows * mlp_route.shape[3] // experts
    scale = 1.0 / math.sqrt(HDIM)
    places, segment, depth = tree_layout(segment_len, tree_rows)
    own_depth = lax.dynamic_slice_in_dim(depth, position * tok_rows, tok_rows, 0)
    column = (jnp.arange(experts, dtype=jnp.int32) == position).astype(jnp.float32)
    first_gain = gain_first.astype(jnp.float32)
    second_gain = gain_second.astype(jnp.float32)
    first_router = router_first.astype(jnp.float32)
    second_router = router_second.astype(jnp.float32)
    grad_query = jnp.zeros((width, heads_total), jnp.float32)
    grad_output = jnp.zeros((heads_total, width), jnp.float32)
    grad_key = jnp.zeros(key_full.shape, jnp.float32)
    grad_value = jnp.zeros(value_full.shape, jnp.float32)
    grad_gain_first = jnp.zeros((width,), jnp.float32)
    grad_gain_second = jnp.zeros((width,), jnp.float32)
    grad_router_first = jnp.zeros((width, experts), jnp.float32)
    grad_router_second = jnp.zeros((width, experts), jnp.float32)
    grad_gate = jnp.zeros(w_gate.shape, jnp.float32)
    grad_upward = jnp.zeros(w_up.shape, jnp.float32)
    grad_downward = jnp.zeros(w_down.shape, jnp.float32)
    results = []
    input_grads = []
    for micro_index in range(micro_count):
        query_weight, out_weight = (
            lax.all_gather(w_query, "dp", axis=1, tiled=True),
            lax.all_gather(w_out, "dp", axis=1, tiled=True),
        )
        query_weight = query_weight[0]
        out_weight = out_weight[0]
        up_one, up_two = ancestors(parents[micro_index, 0], segment)
        layout = (segment, places, up_one, up_two)
        residual_in = tokens[micro_index, 0].astype(jnp.float32)
        normed, first_pull = jax.vjp(rms_scaled, residual_in, first_gain)
        normed = normed.astype(jnp.bfloat16)
        own_keys = rotate(product(normed, key_full).reshape(tok_rows, HEADS, HDIM), own_depth, 1.0)
        own_keys = own_keys.astype(jnp.bfloat16).reshape(tok_rows, heads_total)
        own_values = product(normed, value_full).astype(jnp.bfloat16)
        tree_input, tree_keys, tree_values = (
            lax.all_gather(normed, "expert", axis=0, tiled=True),
            lax.all_gather(own_keys, "expert", axis=0, tiled=True),
            lax.all_gather(own_values, "expert", axis=0, tiled=True),
        )
        tree_keys = tree_keys.reshape(tree_rows, HEADS, HDIM)
        tree_values = tree_values.reshape(tree_rows, HEADS, HDIM)
        queries = rotate(
            product(tree_input, query_weight).reshape(tree_rows, HEADS, HDIM), depth, 1.0
        ).astype(jnp.bfloat16)
        first_gates, first_gate_pull = jax.vjp(
            partial(mixture_gates, attn_route[micro_index, 0]), product(tree_input, router_first)
        )
        own_gate = jnp.sum(first_gates * column[None, :], axis=1)
        heads_out, logsum = attend(queries, tree_keys, tree_values, layout, scale)
        heads_flat = heads_out.reshape(tree_rows, heads_total)
        projected = product(heads_flat, out_weight)
        attention = lax.psum_scatter(
            (own_gate[:, None] * projected).astype(jnp.bfloat16),
            "expert",
            scatter_dimension=0,
            tiled=True,
        ).astype(jnp.float32)
        middle = residual_in + attention
        second_normed, second_pull = jax.vjp(rms_scaled, middle, second_gain)
        second_normed = second_normed.astype(jnp.bfloat16)
        picked_second = mlp_route[micro_index, 0]
        second_gates, second_gate_pull = jax.vjp(
            partial(mixture_gates, picked_second), product(second_normed, router_second)
        )
        table = slot_table(picked_second, fill_order[micro_index, 0], experts, capacity)
        outgoing = jnp.einsum(
            "ect,td->ecd",
            table.astype(jnp.bfloat16),
            second_normed,
            preferred_element_type=jnp.float32,
        ).astype(jnp.bfloat16)
        arrived = to_experts(outgoing).reshape(experts * capacity, width)
        gate_all, up_all, down_all = (
            lax.all_gather(w_gate, "dp", axis=1, tiled=True),
            lax.all_gather(w_up, "dp", axis=1, tiled=True),
            lax.all_gather(w_down, "dp", axis=1, tiled=True),
        )
        gate_weight = gate_all[0]
        up_weight = up_all[0]
        down_weight = down_all[0]
        gate_pre = product_nt(arrived, gate_weight)
        up_pre = product_nt(arrived, up_weight)
        sigma = jax.nn.sigmoid(gate_pre)
        inner = (gate_pre * sigma * up_pre).astype(jnp.bfloat16)
        expert_sum = product(inner, down_weight)
        returned = from_experts(
            expert_sum.astype(jnp.bfloat16).reshape(experts, capacity, width)
        ).astype(jnp.float32)
        weighted = table * jnp.transpose(second_gates)[:, None, :]
        mixed = jnp.einsum("ect,ecd->td", weighted, returned, precision=HIGHEST)
        results.append((middle + mixed).astype(jnp.bfloat16))
        top_grad = cotangent[micro_index, 0].astype(jnp.float32)
        slot_values = jnp.einsum("ect,td->ecd", table, top_grad, precision=HIGHEST)
        gate_slot_grad = jnp.sum(slot_values * returned, axis=-1)
        second_gate_grad = jnp.einsum("ect,ec->te", table, gate_slot_grad, precision=HIGHEST)
        slot_gates = jnp.einsum("ect,te->ec", table, second_gates, precision=HIGHEST)
        slot_grad = (slot_gates[:, :, None] * slot_values).astype(jnp.bfloat16)
        result_grad = to_experts(slot_grad).reshape(experts * capacity, width)
        inner_grad = product_nt(result_grad, down_weight)
        gate_grad = (inner_grad * up_pre * sigma * (1.0 + gate_pre * (1.0 - sigma))).astype(
            jnp.bfloat16
        )
        up_grad = (inner_grad * gate_pre * sigma).astype(jnp.bfloat16)
        rows_grad = product(gate_grad, gate_weight) + product(up_grad, up_weight)
        gate_share, up_share, down_share = (
            lax.psum_scatter(
                product_tn(gate_grad, arrived)[None].astype(jnp.bfloat16),
                "dp",
                scatter_dimension=1,
                tiled=True,
            ).astype(jnp.float32),
            lax.psum_scatter(
                product_tn(up_grad, arrived)[None].astype(jnp.bfloat16),
                "dp",
                scatter_dimension=1,
                tiled=True,
            ).astype(jnp.float32),
            lax.psum_scatter(
                product_tn(inner, result_grad)[None].astype(jnp.bfloat16),
                "dp",
                scatter_dimension=1,
                tiled=True,
            ).astype(jnp.float32),
        )
        grad_gate = grad_gate + gate_share
        grad_upward = grad_upward + up_share
        grad_downward = grad_downward + down_share
        came_back = from_experts(rows_grad.astype(jnp.bfloat16).reshape(experts, capacity, width))
        second_input_grad = jnp.einsum(
            "ect,ecd->td", table, came_back.astype(jnp.float32), precision=HIGHEST
        )
        (second_logit_grad,) = second_gate_pull(second_gate_grad)
        second_input_grad = second_input_grad + exact_product(
            second_logit_grad, jnp.transpose(second_router)
        )
        grad_router_second = grad_router_second + exact_product(
            jnp.transpose(second_normed.astype(jnp.float32)), second_logit_grad
        )
        middle_grad, gain_part = second_pull(second_input_grad)
        middle_grad = middle_grad + top_grad
        grad_gain_second = grad_gain_second + gain_part
        mix_grad = lax.all_gather(
            middle_grad.astype(jnp.bfloat16), "expert", axis=0, tiled=True
        ).astype(jnp.float32)
        own_gate_grad = jnp.sum(mix_grad * projected, axis=-1)
        projected_grad = (own_gate[:, None] * mix_grad).astype(jnp.bfloat16)
        grad_output = grad_output + product_tn(heads_flat, projected_grad)
        heads_grad = (
            product_nt(projected_grad, out_weight)
            .astype(jnp.bfloat16)
            .reshape(tree_rows, HEADS, HDIM)
        )
        query_grad, key_grad, value_grad = attend_back(
            queries, tree_keys, tree_values, heads_grad, logsum, layout, scale
        )
        query_pre = (
            rotate(query_grad, depth, -1.0).reshape(tree_rows, heads_total).astype(jnp.bfloat16)
        )
        key_pre = rotate(key_grad, depth, -1.0).reshape(tree_rows, heads_total).astype(jnp.bfloat16)
        value_pre = value_grad.reshape(tree_rows, heads_total).astype(jnp.bfloat16)
        (first_logit_grad,) = first_gate_pull(own_gate_grad[:, None] * column[None, :])
        grad_query = grad_query + product_tn(tree_input, query_pre)
        grad_key = grad_key + product_tn(tree_input, key_pre)
        grad_value = grad_value + product_tn(tree_input, value_pre)
        grad_router_first = grad_router_first + exact_product(
            jnp.transpose(tree_input.astype(jnp.float32)), first_logit_grad
        )
        input_term = (
            product_nt(query_pre, query_weight)
            + product_nt(key_pre, key_full)
            + product_nt(value_pre, value_full)
            + exact_product(first_logit_grad, jnp.transpose(first_router))
        )
        normed_grad = lax.psum_scatter(
            input_term.astype(jnp.bfloat16), "expert", scatter_dimension=0, tiled=True
        ).astype(jnp.float32)
        token_grad, gain_part = first_pull(normed_grad)
        grad_gain_first = grad_gain_first + gain_part
        input_grads.append(token_grad + middle_grad)
    shared_out = (
        lax.psum_scatter(grad_key, ("dp", "expert"), scatter_dimension=0, tiled=True),
        lax.psum_scatter(grad_value, ("dp", "expert"), scatter_dimension=0, tiled=True),
        lax.psum_scatter(grad_gain_first, ("dp", "expert"), scatter_dimension=0, tiled=True),
        lax.psum_scatter(grad_router_first, ("dp", "expert"), scatter_dimension=0, tiled=True),
        lax.psum_scatter(grad_gain_second, ("dp", "expert"), scatter_dimension=0, tiled=True),
        lax.psum_scatter(grad_router_second, ("dp", "expert"), scatter_dimension=0, tiled=True),
    )
    attention_out = (
        lax.psum_scatter(
            grad_query[None].astype(jnp.bfloat16), "dp", scatter_dimension=1, tiled=True
        ).astype(jnp.float32),
        lax.psum_scatter(
            grad_output[None].astype(jnp.bfloat16), "dp", scatter_dimension=1, tiled=True
        ).astype(jnp.float32),
    )
    layer_out = jnp.stack(results)[:, None]
    tokens_grad = jnp.stack(input_grads)[:, None]
    return (
        layer_out,
        tokens_grad,
        attention_out[0],
        attention_out[1],
        shared_out[0],
        shared_out[1],
        shared_out[2],
        shared_out[3],
        shared_out[4],
        shared_out[5],
        grad_gate,
        grad_upward,
        grad_downward,
    )


def solution(mesh):
    in_specs = (
        P(None, "dp", "expert", None),
        P("expert", "dp", None),
        P("expert", "dp", None),
        P(("dp", "expert"), None),
        P(("dp", "expert"), None),
        P(("dp", "expert")),
        P(("dp", "expert"), None),
        P(("dp", "expert")),
        P(("dp", "expert"), None),
        P("expert", "dp", None),
        P("expert", "dp", None),
        P("expert", "dp", None),
        P(None, "dp", None, None),
        P(None, "dp", "expert", None),
        P(None, "dp", "expert"),
        P(None, "dp", None),
        P(None, "dp", "expert", None),
    )
    out_specs = (
        P(None, "dp", "expert", None),
        P(None, "dp", "expert", None),
        P("expert", "dp", None),
        P("expert", "dp", None),
        P(("dp", "expert"), None),
        P(("dp", "expert"), None),
        P(("dp", "expert")),
        P(("dp", "expert"), None),
        P(("dp", "expert")),
        P(("dp", "expert"), None),
        P("expert", "dp", None),
        P("expert", "dp", None),
        P("expert", "dp", None),
    )
    return jax.shard_map(body, mesh=mesh, in_specs=in_specs, out_specs=out_specs, check_vma=False)
```

profile of v0, /device:TPU:0, one launch (start us, length us, event | category | flops | bytes accessed | tf_op | source)
XLA Modules:
  0.0 5397.6 jit_solution(16676344584761479839)
XLA Ops:
  10.4 43.1 all-reduce.5
  58.4 33.0 all-gather.26.cloned.1.call-done
  91.4 12.4 copy.140
  114.2 56.2 %all-gather.20.cloned.1.call-done = bf16[2048,2048]{1,0:T(8,128)(2,1)} async-done(((bf16[64,2048]{1,0:T(8,128)(2,1)}), bf16[2048,2048]{1,0:T(8,128)(2,1)}) %all-gather.20.cloned.1.call-update) | async-done | bytes 8388624 | tf_op jit(solution)/shard_map/all_gather | solution.py:202
  176.9 39.3 all-gather
  223.0 110.7 %all-gather.24.cloned.1.call-done = bf16[1,2048,2048]{2,1,0:T(8,128)(2,1)} async-done(((bf16[1,256,2048]{2,1,0:T(8,128)(2,1)}), bf16[1,2048,2048]{2,1,0:T(8,128)(2,1)}) %all-gather.24.cloned.1.call-update) | async-done | bytes 8388624 | tf_op jit(solution)/shard_map/all_gather | solution.py:238
  333.8 12.5 copy.139
  378.5 118.2 %all-gather.30.cloned.1.call-done = bf16[1,2048,2048]{2,1,0:T(8,128)(2,1)} async-done(((bf16[1,256,2048]{2,1,0:T(8,128)(2,1)}), bf16[1,2048,2048]{2,1,0:T(8,128)(2,1)}) %all-gather.30.cloned.1.call-update) | async-done | bytes 8388624 | tf_op jit(solution)/shard_map/all_gather | solution.py:239
  518.8 13.7 all-gather.40.cloned.1.call-done
  545.8 40.6 all-gather.1
  609.1 422.2 %all-gather.32.cloned.1.call-done = bf16[1,5632,2048]{2,1,0:T(8,128)(2,1)} async-done(((bf16[1,704,2048]{2,1,0:T(8,128)(2,1)}), bf16[1,5632,2048]{2,1,0:T(8,128)(2,1)}) %all-gather.32.cloned.1.call-update) | async-done | bytes 23068688 | tf_op jit(solution)/shard_map/all_gather | solution.py:290
  1031.3 13.7 fusion.24
  1045.0 428.8 %all-gather.34.cloned.1.call-done = bf16[1,5632,2048]{2,1,0:T(8,128)(2,1)} async-done(((bf16[1,704,2048]{2,1,0:T(8,128)(2,1)}), bf16[1,5632,2048]{2,1,0:T(8,128)(2,1)}) %all-gather.34.cloned.1.call-update) | async-done | bytes 23068688 | tf_op jit(solution)/shard_map/all_gather | solution.py:291
  1473.8 13.8 multiply_convert_fusion.7
  1487.6 428.7 %all-gather.36.cloned.1.call-done = bf16[1,5632,2048]{2,1,0:T(8,128)(2,1)} async-done(((bf16[1,704,2048]{2,1,0:T(8,128)(2,1)}), bf16[1,5632,2048]{2,1,0:T(8,128)(2,1)}) %all-gather.36.cloned.1.call-update) | async-done | bytes 23068688 | tf_op jit(solution)/shard_map/all_gather | solution.py:292
  1916.3 10.2 fusion.94
  1930.2 13.7 fusion.22
  1943.9 13.7 multiply_convert_fusion.6
  1957.6 10.7 fusion.97
  2004.5 14.8 multiply_convert_fusion.3
  2029.1 11.7 fusion.88
  2044.7 14.3 multiply_convert_fusion.5
  2058.9 9.8 fusion.12
  2068.8 11.7 fusion.91
  2101.9 11.5 all-gather.44.cloned.1.call-done
  2218.9 10.0 fusion.198
  2228.9 11.7 fusion.39
  2250.2 11.6 fusion.38
  2262.0 12.1 convert_bitcast_fusion
  2275.2 12.3 convert_bitcast_fusion.1
  2288.5 12.3 convert_bitcast_fusion.4
  2301.9 12.3 convert_bitcast_fusion.5
  2314.7 12.2 convert_bitcast_fusion.2
  2327.0 12.3 convert_bitcast_fusion.3
  2370.5 31.0 reduce-scatter.49.cloned.1.call-done
  2403.0 22.4 reduce-scatter.27.cloned.1.call-done
  2425.4 28.2 reduce-scatter.25.cloned.1.call-done
  2455.2 43.3 all-reduce.4
  2502.1 105.2 %reduce-scatter.31.cloned.1.call-done = bf16[1,256,2048]{2,1,0:T(8,128)(2,1)} async-done(((bf16[1,2048,2048]{2,1,0:T(8,128)(2,1)}), bf16[1,256,2048]{2,1,0:T(8,128)(2,1)}) %reduce-scatter.31.cloned.1.call-update) | async-done | bytes 1048592 | tf_op jit(solution)/shard_map/reduce_scatter | solution.py:408
  2610.1 149.3 %reduce-scatter.29.cloned.1.call-done = bf16[1,256,2048]{2,1,0:T(8,128)(2,1)} async-done(((bf16[1,2048,2048]{2,1,0:T(8,128)(2,1)}), bf16[1,256,2048]{2,1,0:T(8,128)(2,1)}) %reduce-scatter.29.cloned.1.call-update) | async-done | bytes 1048592 | tf_op jit(solution)/shard_map/reduce_scatter | solution.py:405
  2762.2 373.4 %reduce-scatter.47.cloned.1.call-done = bf16[1,704,2048]{2,1,0:T(8,128)(2,1)} async-done(((bf16[1,5632,2048]{2,1,0:T(8,128)(2,1)}), bf16[1,704,2048]{2,1,0:T(8,128)(2,1)}) %reduce-scatter.47.cloned.1.call-update) | async-done | bytes 2883600 | tf_op jit(solution)/shard_map/reduce_scatter | solution.py:334
  3135.6 376.6 %reduce-scatter.45.cloned.1.call-done = bf16[1,704,2048]{2,1,0:T(8,128)(2,1)} async-done(((bf16[1,5632,2048]{2,1,0:T(8,128)(2,1)}), bf16[1,704,2048]{2,1,0:T(8,128)(2,1)}) %reduce-scatter.45.cloned.1.call-update) | async-done | bytes 2883600 | tf_op jit(solution)/shard_map/reduce_scatter | solution.py:334
  3518.6 370.1 %reduce-scatter.39.cloned.1.call-done = bf16[1,704,2048]{2,1,0:T(8,128)(2,1)} async-done(((bf16[1,5632,2048]{2,1,0:T(8,128)(2,1)}), bf16[1,704,2048]{2,1,0:T(8,128)(2,1)}) %reduce-scatter.39.cloned.1.call-update) | async-done | bytes 2883600 | tf_op jit(solution)/shard_map/reduce_scatter | solution.py:322
  3888.7 376.4 %reduce-scatter.37.cloned.1.call-done = bf16[1,704,2048]{2,1,0:T(8,128)(2,1)} async-done(((bf16[1,5632,2048]{2,1,0:T(8,128)(2,1)}), bf16[1,704,2048]{2,1,0:T(8,128)(2,1)}) %reduce-scatter.37.cloned.1.call-update) | async-done | bytes 2883600 | tf_op jit(solution)/shard_map/reduce_scatter | solution.py:322
  4271.6 370.1 %reduce-scatter.43.cloned.1.call-done = bf16[1,704,2048]{2,1,0:T(8,128)(2,1)} async-done(((bf16[1,5632,2048]{2,1,0:T(8,128)(2,1)}), bf16[1,704,2048]{2,1,0:T(8,128)(2,1)}) %reduce-scatter.43.cloned.1.call-update) | async-done | bytes 2883600 | tf_op jit(solution)/shard_map/reduce_scatter | solution.py:328
  4641.7 376.5 %reduce-scatter.41.cloned.1.call-done = bf16[1,704,2048]{2,1,0:T(8,128)(2,1)} async-done(((bf16[1,5632,2048]{2,1,0:T(8,128)(2,1)}), bf16[1,704,2048]{2,1,0:T(8,128)(2,1)}) %reduce-scatter.41.cloned.1.call-update) | async-done | bytes 2883600 | tf_op jit(solution)/shard_map/reduce_scatter | solution.py:328
  5024.6 178.5 %reduce-scatter.35.cloned.1.call-done = f32[64,2048]{1,0:T(8,128)} async-done(((f32[2048,2048]{1,0:T(8,128)}), f32[64,2048]{1,0:T(8,128)}) %reduce-scatter.35.cloned.1.call-update) | async-done | bytes 524304 | tf_op jit(solution)/shard_map/reduce_scatter | solution.py:398
  5203.1 187.5 %reduce-scatter.33.cloned.1.call-done = f32[64,2048]{1,0:T(8,128)} async-done(((f32[2048,2048]{1,0:T(8,128)}), f32[64,2048]{1,0:T(8,128)}) %reduce-scatter.33.cloned.1.call-update) | async-done | bytes 524304 | tf_op jit(solution)/shard_map/reduce_scatter | solution.py:397
  (610 shorter events, 376.2 us)
Async XLA Ops:
  7.2 84.2 %all-gather.26.cloned.1.call-start = ((), (), s32[]{:S(2)}) async-start(), calls=%async_computation.28 | async-start | bytes 8650752 | tf_op jit(solution)/shard_map/all_gather | solution.py:201
  7.9 162.5 %all-gather.20.cloned.1.call-start = ((), (), s32[]{:S(2)}) async-start(), calls=%async_computation.25 | async-start | bytes 8650752 | tf_op jit(solution)/shard_map/all_gather | solution.py:202
  8.7 209.5 %all-gather.38.cloned.1.call-start = ((), (), s32[]{:S(2)}) async-start(), calls=%async_computation.35 | async-start | bytes 1310720 | tf_op jit(solution)/shard_map/all_gather | solution.py:252
  56.9 163.2 %all-gather.18.cloned.1.call-start = ((), (), s32[]{:S(2)}) async-start(), calls=%async_computation.24 | async-start | bytes 1310720 | tf_op jit(solution)/shard_map/all_gather | solution.py:252
  57.4 276.3 %all-gather.24.cloned.1.call-start = ((), (), s32[]{:S(2)}) async-start(), calls=%async_computation.27 | async-start | bytes 9437184 | tf_op jit(solution)/shard_map/all_gather | solution.py:238
  58.0 310.4 %all-gather.28.cloned.1.call-start = ((), (), s32[]{:S(2)}) async-start(), calls=%async_computation.29 | async-start | bytes 1310720 | tf_op jit(solution)/shard_map/all_gather | solution.py:253
  114.1 260.8 %all-gather.22.cloned.1.call-start = ((), (), s32[]{:S(2)}) async-start(), calls=%async_computation.26 | async-start | bytes 1310720 | tf_op jit(solution)/shard_map/all_gather | solution.py:254
  176.1 320.5 %all-gather.30.cloned.1.call-start = ((), (), s32[]{:S(2)}) async-start(), calls=%async_computation.30 | async-start | bytes 9437184 | tf_op jit(solution)/shard_map/all_gather | solution.py:239
  176.9 336.9 %all-gather.42.cloned.1.call-start = ((), (), s32[]{:S(2)}) async-start(), calls=%async_computation.37 | async-start | bytes 1310720 | tf_op jit(solution)/shard_map/all_gather | solution.py:253
  218.1 142.2 %copy-start.54 = (f32[256,64]{0,1:T(8,128)}, f32[256,64]{0,1:T(8,128)S(1)}, u32[]{:S(2)}) copy-start(f32[256,64]{0,1:T(8,128)S(1)} %get-tuple-element.287) | copy-start | bytes 196612
  223.0 273.6 %copy-start.124 = (f32[256]{0:T(256)}, f32[256]{0:T(256)S(1)}, u32[]{:S(2)}) copy-start(f32[256]{0:T(256)S(1)} %get-tuple-element.231) | copy-start | bytes 3076
  223.0 313.0 %copy-start.121 = (f32[256]{0:T(256)}, f32[256]{0:T(256)S(1)}, u32[]{:S(2)}) copy-start(f32[256]{0:T(256)S(1)} %get-tuple-element.232) | copy-start | bytes 3076
  354.4 178.1 %all-gather.40.cloned.1.call-start = ((), (), s32[]{:S(2)}) async-start(), calls=%async_computation.36 | async-start | bytes 1310720 | tf_op jit(solution)/shard_map/all_gather | solution.py:254
  361.9 153.4 %copy-start.62 = (bf16[256,16,64]{0,2,1:T(8,128)(2,1)}, bf16[256,16,64]{0,2,1:T(8,128)(2,1)S(1)}, u32[]{:S(2)}) copy-start(bf16[256,16,64]{0,2,1:T(8,128)(2,1)S(1)} %get-tuple-element.273) | copy-start | bytes 1572868
  361.9 153.4 %copy-start.63 = (bf16[256,16,64]{0,2,1:T(8,128)(2,1)}, bf16[256,16,64]{0,2,1:T(8,128)(2,1)S(1)}, u32[]{:S(2)}) copy-start(bf16[256,16,64]{0,2,1:T(8,128)(2,1)S(1)} %get-tuple-element.274) | copy-start | bytes 1572868
  368.1 219.3 %reduce-scatter.21.cloned.1.call-start = ((), (), s32[]{:S(2)}) async-start(), calls=%async_computation.31 | async-start | bytes 1310720 | tf_op jit(solution)/shard_map/reduce_scatter | solution.py:268
  504.1 84.6 %reduce-scatter.23.cloned.1.call-start = ((), (), s32[]{:S(2)}) async-start(), calls=%async_computation.38 | async-start | bytes 1310720 | tf_op jit(solution)/shard_map/reduce_scatter | solution.py:268
  543.8 487.5 %all-gather.32.cloned.1.call-start = ((), (), s32[]{:S(2)}) async-start(), calls=%async_computation.32 | async-start | bytes 25952256 | tf_op jit(solution)/shard_map/all_gather | solution.py:290
  544.6 929.2 %all-gather.34.cloned.1.call-start = ((), (), s32[]{:S(2)}) async-start(), calls=%async_computation.33 | async-start | bytes 25952256 | tf_op jit(solution)/shard_map/all_gather | solution.py:291
  545.2 1371.2 %all-gather.36.cloned.1.call-start = ((), (), s32[]{:S(2)}) async-start(), calls=%async_computation.34 | async-start | bytes 25952256 | tf_op jit(solution)/shard_map/all_gather | solution.py:292
  592.9 12.3 all-to-all-start
  605.2 868.6 %copy-start.10 = (bf16[4,32,2048]{2,1,0:T(8,128)(2,1)}, bf16[4,32,2048]{2,1,0:T(8,128)(2,1)S(1)}, u32[]{:S(2)}) copy-start(bf16[4,32,2048]{2,1,0:T(8,128)(2,1)S(1)} %all-to-all-done) | copy-start | bytes 1572868
  605.2 1321.3 %all-to-all-start.2 = ((bf16[4,32,2048]{2,1,0:T(8,128)(2,1)}), bf16[4,32,2048]{2,1,0:T(8,128)(2,1)S(1)}, u32[]{:S(2)}, u32[]{:S(2)}) async-start(bf16[4,32,2048]{2,1,0:T(8,128)(2,1)} %convolution_convert_fusion), calls=%async_computation.4 | async-start | bytes 1048576 | tf_op jit(solution)/shard_map/all_to_all | solution.py:172
  1487.6 438.9 %copy-start.14 = (bf16[128,5632]{1,0:T(8,128)(2,1)}, bf16[128,5632]{1,0:T(8,128)(2,1)S(1)}, u32[]{:S(2)}) copy-start(bf16[128,5632]{1,0:T(8,128)(2,1)S(1)} %get-tuple-element.316) | copy-start | bytes 4325380
  1926.5 41.8 all-to-all-start.1
  1968.4 12.4 all-to-all-start.3
  1987.7 13.1 all-to-all-start.6
  2000.8 40.0 all-to-all-start.4
  2040.8 39.8 all-to-all-start.7
  2080.6 12.4 all-to-all-start.5
  2084.2 29.2 all-gather.44.cloned.1.call-start
  2097.4 45.2 all-gather.46.cloned.1.call-start
  2098.0 271.1 %reduce-scatter.51.cloned.1.call-start = ((), (), s32[]{:S(2)}) async-start(), calls=%async_computation.54 | async-start | bytes 1081344
  2101.7 299.9 %reduce-scatter.49.cloned.1.call-start = ((), (), s32[]{:S(2)}) async-start(), calls=%async_computation.53 | async-start | bytes 1081344
  2197.5 227.9 %reduce-scatter.27.cloned.1.call-start = ((), (), s32[]{:S(2)}) async-start(), calls=%async_computation.42 | async-start | bytes 1310720 | tf_op jit(solution)/shard_map/reduce_scatter | solution.py:390
  2199.6 254.0 %reduce-scatter.25.cloned.1.call-start = ((), (), s32[]{:S(2)}) async-start(), calls=%async_computation.40 | async-start | bytes 1310720 | tf_op jit(solution)/shard_map/reduce_scatter | solution.py:390
  2218.6 388.7 %reduce-scatter.31.cloned.1.call-start = ((), (), s32[]{:S(2)}) async-start(), calls=%async_computation.44 | async-start | bytes 9437184 | tf_op jit(solution)/shard_map/reduce_scatter | solution.py:408
  2240.5 518.9 %reduce-scatter.29.cloned.1.call-start = ((), (), s32[]{:S(2)}) async-start(), calls=%async_computation.43 | async-start | bytes 9437184 | tf_op jit(solution)/shard_map/reduce_scatter | solution.py:405
  2261.8 873.8 %reduce-scatter.47.cloned.1.call-start = ((), (), s32[]{:S(2)}) async-start(), calls=%async_computation.52 | async-start | bytes 25952256 | tf_op jit(solution)/shard_map/reduce_scatter | solution.py:334
  2274.2 1238.0 %reduce-scatter.45.cloned.1.call-start = ((), (), s32[]{:S(2)}) async-start(), calls=%async_computation.51 | async-start | bytes 25952256 | tf_op jit(solution)/shard_map/reduce_scatter | solution.py:334
  2287.5 1601.2 %reduce-scatter.39.cloned.1.call-start = ((), (), s32[]{:S(2)}) async-start(), calls=%async_computation.48 | async-start | bytes 25952256 | tf_op jit(solution)/shard_map/reduce_scatter | solution.py:322
  2300.9 1964.3 %reduce-scatter.37.cloned.1.call-start = ((), (), s32[]{:S(2)}) async-start(), calls=%async_computation.47 | async-start | bytes 25952256 | tf_op jit(solution)/shard_map/reduce_scatter | solution.py:322
  2314.2 2327.5 %reduce-scatter.43.cloned.1.call-start = ((), (), s32[]{:S(2)}) async-start(), calls=%async_computation.50 | async-start | bytes 25952256 | tf_op jit(solution)/shard_map/reduce_scatter | solution.py:328
  2327.0 2691.2 %reduce-scatter.41.cloned.1.call-start = ((), (), s32[]{:S(2)}) async-start(), calls=%async_computation.49 | async-start | bytes 25952256 | tf_op jit(solution)/shard_map/reduce_scatter | solution.py:328
  2339.3 2863.8 %reduce-scatter.35.cloned.1.call-start = ((), (), s32[]{:S(2)}) async-start(), calls=%async_computation.46 | async-start | bytes 17301504 | tf_op jit(solution)/shard_map/reduce_scatter | solution.py:398
  2352.6 3038.0 %reduce-scatter.33.cloned.1.call-start = ((), (), s32[]{:S(2)}) async-start(), calls=%async_computation.45 | async-start | bytes 17301504 | tf_op jit(solution)/shard_map/reduce_scatter | solution.py:397
  2366.2 133.4 %copy-start.52 = (f32[64,2048]{1,0:T(8,128)S(1)}, f32[64,2048]{1,0:T(8,128)}, u32[]{:S(2)}) copy-start(f32[64,2048]{1,0:T(8,128)} %get-tuple-element.238) | copy-start | bytes 1572868
  2366.2 133.4 %copy-start.53 = (f32[64,2048]{1,0:T(8,128)S(1)}, f32[64,2048]{1,0:T(8,128)}, u32[]{:S(2)}) copy-start(f32[64,2048]{1,0:T(8,128)} %get-tuple-element.258) | copy-start | bytes 1572868
  (160 other events, 3414.1 us)
Sparse Core Ops, SparseCore 0:
  10.9 80.4 all-gather.25
  94.2 76.1 all-gather.19
  172.6 15.3 all-gather.37
  190.0 16.7 all-gather.17
  208.7 124.9 all-gather.23
  335.7 14.9 all-gather.27
  352.8 16.7 all-gather.21
  371.7 124.9 all-gather.29
  498.8 14.9 all-gather.41
  515.7 16.7 all-gather.39
  535.6 24.9 reduce-scatter.20
  563.7 24.8 reduce-scatter.22
  590.2 441.0 all-gather.31
  1032.7 441.0 all-gather.33
  1475.2 441.0 all-gather.35
  2097.6 15.7 all-gather.43
  2114.8 16.7 all-gather.45
  2133.7 134.7 reduce-scatter.50
  2270.8 130.7 reduce-scatter.48
  2404.5 20.8 reduce-scatter.26
  2428.7 24.8 reduce-scatter.24
  2457.2 150.0 reduce-scatter.30
  2611.4 147.9 reduce-scatter.28
  2763.1 372.4 reduce-scatter.46
  3139.5 372.6 reduce-scatter.44
  3515.9 372.7 reduce-scatter.38
  3892.5 372.6 reduce-scatter.36
  4269.0 372.6 reduce-scatter.42
  4645.6 372.5 reduce-scatter.40
  5020.9 182.1 reduce-scatter.34
  5205.9 184.5 reduce-scatter.32
where the time goes:
time: 5410 us; the launch traced here: 5400 us
  waiting for transfers between devices  4610 us (85%)
  matrix products  456 us (8%)
  blocking collectives  166 us (3%)
  other arithmetic  63.2 us (1%)
    reduce_scatter x2, waiting for transfers between devices, body(): lax.psum_scatter(product_tn(inner, result_grad)[None].astype(jnp.bfloat16...  750 us
    reduce_scatter x2, waiting for transfers between devices, body(): lax.psum_scatter(product_tn(up_grad, arrived)[None].astype(jnp.bfloat16),...  747 us
    reduce_scatter x2, waiting for transfers between devices, body(): lax.psum_scatter(product_tn(gate_grad, arrived)[None].astype(jnp.bfloat16...  747 us
    all_gather x1, waiting for transfers between devices, body(): lax.all_gather(w_up, 'dp', axis=1, tiled=True)  429 us
    all_gather x1, waiting for transfers between devices, body(): lax.all_gather(w_down, 'dp', axis=1, tiled=True)  429 us
    all_gather x1, waiting for transfers between devices, body(): lax.all_gather(w_gate, 'dp', axis=1, tiled=True)  422 us
    reduce_scatter x1, waiting for transfers between devices, body(): lax.psum_scatter(grad_key, ('dp', 'expert'), scatter_dimension=0, tiled=T...  187 us
    reduce_scatter x1, waiting for transfers between devices, body(): lax.psum_scatter(grad_value, ('dp', 'expert'), scatter_dimension=0, tiled...  178 us
  transfers between devices with their start and end apart: 39, of which 28 were waited for; matrix products, arithmetic and copies ran while one was open for 10% of the time, Pallas kernels for 0%

commit v1 on v0

v1 whole, which is shorter than its diff:
```python
from functools import partial
import math

import jax
import jax.numpy as jnp
from jax import lax
from jax.experimental import pallas as pl
from jax.experimental.pallas import tpu as pltpu
from jax.sharding import Mesh, PartitionSpec as P

HEADS = 16
HDIM = 128
EPSILON = 1e-06
HIGHEST = lax.Precision.HIGHEST
BF16 = jnp.bfloat16
F32 = jnp.float32


def product(left, right):
    return jnp.dot(left, right, preferred_element_type=F32)


def product_tn(left, right):
    return lax.dot_general(left, right, (((0,), (0,)), ((), ())), preferred_element_type=F32)


def product_nt(left, right):
    return lax.dot_general(left, right, (((1,), (1,)), ((), ())), preferred_element_type=F32)


def rms_scaled(values, gain):
    return values * lax.rsqrt(jnp.mean(values * values, axis=-1, keepdims=True) + EPSILON) * gain


def mixture_gates(picked, logits):
    labels = jnp.arange(logits.shape[1], dtype=jnp.int32)
    onehot = (picked[:, :, None] == labels[None, None, :]).astype(F32)
    chosen = jnp.sum(onehot * logits[:, None, :], axis=-1)
    weights = jax.nn.softmax(chosen, axis=-1)
    return jnp.sum(weights[:, :, None] * onehot, axis=1)


def tree_layout(segment_len, tree_len):
    places = jnp.arange(tree_len, dtype=jnp.int32)
    trunk_len = 4 * segment_len
    segment = jnp.where(
        places < trunk_len,
        0,
        jnp.where(
            places < 2 * trunk_len,
            1 + (places - trunk_len) // segment_len,
            5 + (places - 2 * trunk_len) // segment_len,
        ),
    )
    depth = jnp.where(
        places < trunk_len,
        places,
        jnp.where(
            places < 2 * trunk_len,
            trunk_len + (places - trunk_len) % segment_len,
            trunk_len + segment_len + (places - 2 * trunk_len) % segment_len,
        ),
    )
    return (places, segment, depth)


def ancestors(parent, segment):
    labels = jnp.arange(parent.shape[0], dtype=jnp.int32)
    first = jnp.where(labels > 0, parent, -1)
    lookup = jnp.maximum(first, 0)[:, None] == labels[None, :]
    second = jnp.where(first > 0, jnp.sum(jnp.where(lookup, parent[None, :], 0), axis=1), -1)
    member = segment[:, None] == labels[None, :]
    up_one = jnp.sum(jnp.where(member, first[None, :], 0), axis=1)
    up_two = jnp.sum(jnp.where(member, second[None, :], 0), axis=1)
    return (up_one, up_two)


def score_bias(parent, segment, places):
    up_one, up_two = ancestors(parent, segment)
    same = (segment[None, :] == segment[:, None]) & (places[None, :] <= places[:, None])
    seen = same | (segment[None, :] == up_one[:, None]) | (segment[None, :] == up_two[:, None])
    return jnp.where(seen, 0.0, -1e30).astype(F32)


def slot_table(picked, order, experts, capacity):
    labels = jnp.arange(experts, dtype=jnp.int32)
    chosen = jnp.sum((picked[:, :, None] == labels[None, None, :]).astype(F32), axis=1)
    earlier = (order[None, :] < order[:, None]).astype(F32)
    ranks = jnp.dot(earlier, chosen, precision=HIGHEST, preferred_element_type=F32)
    slots = jnp.arange(capacity, dtype=F32)
    return jnp.transpose(chosen)[:, None, :] * (
        jnp.transpose(ranks)[:, None, :] == slots[None, :, None]
    ).astype(F32)


def turn(values, cosine, sine):
    half = values.shape[-1] // 2
    first = values[:, :half]
    second = values[:, half:]
    return jnp.concatenate(
        [first * cosine - second * sine, second * cosine + first * sine], axis=-1
    )


def softmax_rows(queries, keys, bias, scale):
    scores = product_nt(queries, keys) * scale + bias
    highest = jnp.max(scores, axis=-1, keepdims=True)
    weights = jnp.exp(scores - highest)
    return weights / jnp.sum(weights, axis=-1, keepdims=True)


def attend_kernel(heads, scale, raw_ref, kv_ref, cos_ref, sin_ref, bias_ref, query_ref, out_ref):
    quarter, tok = raw_ref.shape[1], raw_ref.shape[3]
    rows = quarter * tok
    cosine, sine, bias = cos_ref[...], sin_ref[...], bias_ref[0, 0]
    for head in range(heads):
        cols = slice(head * HDIM, (head + 1) * HDIM)
        raw = raw_ref[0, :, 0, :, cols].reshape(rows, HDIM)
        keys = kv_ref[0, 0, 0, :, 0, :, cols].reshape(rows, HDIM)
        values = kv_ref[0, 1, 0, :, 0, :, cols].reshape(rows, HDIM)
        queries = turn(raw, cosine, sine).astype(BF16)
        probs = softmax_rows(queries, keys, bias, scale).astype(BF16)
        query_ref[0, :, 0, :, cols] = queries.reshape(quarter, tok, HDIM)
        out_ref[0, :, 0, :, cols] = product(probs, values).astype(BF16).reshape(quarter, tok, HDIM)


def attend_back_kernel(
    heads, scale, query_ref, kv_ref, grad_ref, cos_ref, sin_ref, bias_ref, dq_ref, dkv_ref
):
    quarter, tok = query_ref.shape[1], query_ref.shape[3]
    rows = quarter * tok
    cosine, sine, bias = cos_ref[...], sin_ref[...], bias_ref[0, 0]
    for head in range(heads):
        cols = slice(head * HDIM, (head + 1) * HDIM)
        queries = query_ref[0, :, 0, :, cols].reshape(rows, HDIM)
        keys = kv_ref[0, 0, 0, :, 0, :, cols].reshape(rows, HDIM)
        values = kv_ref[0, 1, 0, :, 0, :, cols].reshape(rows, HDIM)
        grad = grad_ref[0, :, 0, :, cols].reshape(rows, HDIM)
        probs = softmax_rows(queries, keys, bias, scale)
        prob_grad = product_nt(grad, values)
        centre = jnp.sum(prob_grad * probs, axis=-1, keepdims=True)
        score_grad = (probs * (prob_grad - centre) * scale).astype(BF16)
        query_grad = turn(product(score_grad, keys), cosine, -sine).astype(BF16)
        key_grad = turn(product_tn(score_grad, queries), cosine, -sine).astype(BF16)
        value_grad = product_tn(probs.astype(BF16), grad).astype(BF16)
        dq_ref[0, :, 0, :, cols] = query_grad.reshape(quarter, tok, HDIM)
        dkv_ref[0, 0, 0, :, 0, :, cols] = key_grad.reshape(quarter, tok, HDIM)
        dkv_ref[0, 1, 0, :, 0, :, cols] = value_grad.reshape(quarter, tok, HDIM)


def attention_specs(shape, slices):
    pair, quarter, micro, tok, feats = shape
    part = feats // slices
    rows = quarter * tok
    grid = (pair, micro, slices)
    flat = pl.BlockSpec((1, quarter, 1, tok, part), lambda i, m, s: (i, 0, m, 0, s))
    both = pl.BlockSpec(
        (1, 2, 1, quarter, 1, tok, part), lambda i, m, s: (s, 0, i, 0, m, 0, 0)
    )
    angle = pl.BlockSpec((rows, HDIM // 2), lambda i, m, s: (0, 0))
    bias = pl.BlockSpec((1, 1, rows, rows), lambda i, m, s: (i, m, 0, 0))
    return grid, part, flat, both, angle, bias


def attend(raw, kv, cosine, sine, bias, scale):
    slices = kv.shape[0]
    grid, part, flat, both, angle, bias_spec = attention_specs(raw.shape, slices)
    out = jax.ShapeDtypeStruct(raw.shape, BF16)
    return pl.pallas_call(
        partial(attend_kernel, part // HDIM, scale),
        grid=grid,
        in_specs=[flat, both, angle, angle, bias_spec],
        out_specs=[flat, flat],
        out_shape=[out, out],
        cost_estimate=pl.CostEstimate(
            flops=4 * raw.size * cosine.shape[0],
            bytes_accessed=12 * raw.size,
            transcendentals=raw.size * 2,
        ),
        name="attend",
    )(raw, kv, cosine, sine, bias)


def attend_back(queries, kv, grad, cosine, sine, bias, scale):
    slices = kv.shape[0]
    grid, part, flat, both, angle, bias_spec = attention_specs(queries.shape, slices)
    return pl.pallas_call(
        partial(attend_back_kernel, part // HDIM, scale),
        grid=grid,
        in_specs=[flat, both, flat, angle, angle, bias_spec],
        out_specs=[flat, both],
        out_shape=[
            jax.ShapeDtypeStruct(queries.shape, BF16),
            jax.ShapeDtypeStruct(kv.shape, BF16),
        ],
        cost_estimate=pl.CostEstimate(
            flops=10 * queries.size * cosine.shape[0],
            bytes_accessed=14 * queries.size,
            transcendentals=queries.size * 2,
        ),
        name="attend_back",
    )(queries, kv, grad, cosine, sine, bias)


def gather(value, axes, axis=0):
    return lax.all_gather(value, axes, axis=axis, tiled=True)


def scatter(value, axes, axis=0):
    return lax.psum_scatter(value, axes, scatter_dimension=axis, tiled=True)


def swap(value, axes, split=0, concat=0):
    return lax.all_to_all(value, axes, split_axis=split, concat_axis=concat, tiled=True)


DP = ("line", "pair")
ALL = ("line", "pair", "expert")
TREES = ("pair", "expert")


def body(
    tokens,
    w_query,
    w_out,
    w_key,
    w_value,
    gain_attn,
    router_attn,
    gain_mlp,
    router_mlp,
    w_gate,
    w_up,
    w_down,
    attn_route,
    mlp_route,
    fill_order,
    parents,
    cotangent,
):
    experts = lax.axis_size("expert")
    pair = lax.axis_size("pair")
    line = lax.axis_size("line")
    position = lax.axis_index("expert")
    micro, _, tok, width = tokens.shape
    tree = experts * tok
    rows = pair * experts * micro * tok
    heads_total = w_query.shape[2]
    part = heads_total // (line * pair)
    feats = heads_total // pair
    piece = feats // experts
    own_in = w_query.shape[1]
    own_kv = w_key.shape[0]
    capacity = tok * mlp_route.shape[3] // experts
    scale = 1.0 / math.sqrt(HDIM)

    places, segment, depth = tree_layout(tree // 16, tree)
    half = HDIM // 2
    rates = 10000.0 ** (-jnp.arange(half, dtype=F32) / half)
    angle = depth.astype(F32)[:, None] * rates[None, :]
    cosine, sine = jnp.cos(angle), jnp.sin(angle)

    small = jnp.concatenate(
        [gain_attn[None], gain_mlp[None], router_attn.T, router_mlp.T], axis=0
    )
    small = jnp.transpose(lax.all_gather(small, ALL, axis=0), (1, 0, 2)).reshape(-1, width)
    first_gain = small[0].astype(F32)
    second_gain = small[1].astype(F32)
    first_router = small[2 : 2 + experts]
    second_router = small[2 + experts : 2 + 2 * experts]

    residual = tokens.reshape(micro * tok, width).astype(F32)
    normed, first_pull = jax.vjp(rms_scaled, residual, first_gain)
    normed = normed.astype(BF16)
    tree_input = gather(normed, TREES)

    integers = jnp.concatenate(
        [attn_route[:, 0].reshape(micro, -1), parents[:, 0]], axis=1
    )
    integers = lax.all_gather(integers, "pair", axis=0)
    routes = integers[..., : tree * 2].reshape(pair, micro, experts, tok, 2)
    routes = jnp.transpose(routes, (0, 2, 1, 3, 4)).reshape(rows, 2)
    family = integers[..., tree * 2 :]
    bias = jax.vmap(jax.vmap(lambda parent: score_bias(parent, segment, places)))(family)

    kv_mine = jnp.stack([w_key, w_value], axis=1).reshape(own_kv, 2, line, pair, part)
    kv_mine = jnp.transpose(kv_mine, (3, 2, 0, 1, 4)).reshape(
        pair, experts, line // experts, own_kv, 2, part
    )
    kv_mine = jnp.transpose(kv_mine, (0, 1, 3, 4, 2, 5)).reshape(
        pair * experts, own_kv, 2, piece
    )
    kv_mine = swap(kv_mine, TREES).reshape(pair * experts * own_kv, 2 * piece)
    kv_weight = gather(kv_mine, "line")
    query_weight = w_query[0].reshape(own_in, line, pair, part)
    query_weight = jnp.transpose(query_weight, (2, 0, 1, 3)).reshape(pair, own_in, feats)
    query_weight = swap(query_weight, "pair").reshape(pair * own_in, feats)
    query_weight = gather(query_weight, "line")
    out_weight = gather(w_out[0], "line")

    kv_raw = product(tree_input, kv_weight)
    spread_cos = jnp.broadcast_to(
        cosine.reshape(1, experts, 1, tok, 1, half), (pair, experts, micro, tok, 1, half)
    ).reshape(rows, 1, half)
    spread_sin = jnp.broadcast_to(
        sine.reshape(1, experts, 1, tok, 1, half), (pair, experts, micro, tok, 1, half)
    ).reshape(rows, 1, half)
    key_raw = kv_raw[:, :piece].reshape(rows, piece // HDIM, HDIM)
    key_one, key_two = key_raw[..., :half], key_raw[..., half:]
    keys = jnp.concatenate(
        [
            key_one * spread_cos - key_two * spread_sin,
            key_two * spread_cos + key_one * spread_sin,
        ],
        axis=-1,
    ).reshape(rows, piece)
    kv = jnp.stack([keys.astype(BF16), kv_raw[:, piece:].astype(BF16)])
    kv = lax.all_gather(kv, "expert", axis=0)
    shape = (pair, experts, micro, tok, feats)
    kv = kv.reshape(experts, 2, pair, experts, micro, tok, piece)

    first_gates, first_gate_pull = jax.vjp(
        partial(mixture_gates, routes), product_nt(tree_input, first_router)
    )
    column = (jnp.arange(experts, dtype=jnp.int32) == position).astype(F32)
    own_gate = jnp.sum(first_gates * column[None, :], axis=1)

    raw = product(tree_input, query_weight)
    queries, heads_out = attend(raw.reshape(shape), kv, cosine, sine, bias, scale)
    heads_flat = heads_out.reshape(rows, feats)
    projected = product(heads_flat, out_weight)
    attention = scatter((own_gate[:, None] * projected).astype(BF16), TREES).astype(F32)

    middle = residual + attention
    second_normed, second_pull = jax.vjp(rms_scaled, middle, second_gain)
    second_normed = second_normed.astype(BF16)
    picked = mlp_route[:, 0].reshape(micro * tok, 2)
    second_gates, second_gate_pull = jax.vjp(
        partial(mixture_gates, picked), product_nt(second_normed, second_router)
    )
    table = jax.vmap(partial(slot_table, experts=experts, capacity=capacity))(
        mlp_route[:, 0], fill_order[:, 0]
    )
    table_low = table.astype(BF16)
    grouped = second_normed.reshape(micro, tok, width)
    outgoing = jnp.einsum("mect,mtd->emcd", table_low, grouped, preferred_element_type=F32)
    top_grad = cotangent.reshape(micro, tok, width)
    slot_values = jnp.einsum("mect,mtd->emcd", table_low, top_grad, preferred_element_type=F32)
    slot_gates = jnp.einsum(
        "mect,mte->emc", table, second_gates.reshape(micro, tok, experts), precision=HIGHEST
    )
    slot_grad = (slot_gates[..., None] * slot_values).astype(BF16)
    slots = experts * micro * capacity
    arrived = gather(swap(outgoing.astype(BF16), "expert").reshape(slots, width), DP)
    result_grad = gather(swap(slot_grad, "expert").reshape(slots, width), DP)

    gate_weight, up_weight, down_weight = w_gate[0], w_up[0], w_down[0]
    gate_pre = product_nt(arrived, gate_weight)
    up_pre = product_nt(arrived, up_weight)
    sigma = jax.nn.sigmoid(gate_pre)
    inner = (gate_pre * sigma * up_pre).astype(BF16)
    returned = scatter(product(inner, down_weight).astype(BF16), DP)
    returned = swap(returned.reshape(experts, micro, capacity, width), "expert")
    inner_grad = product_nt(result_grad, down_weight)
    gate_grad = (inner_grad * up_pre * sigma * (1.0 + gate_pre * (1.0 - sigma))).astype(BF16)
    up_grad = (inner_grad * gate_pre * sigma).astype(BF16)
    came_back = scatter(
        (product(gate_grad, gate_weight) + product(up_grad, up_weight)).astype(BF16), DP
    )
    came_back = swap(came_back.reshape(experts, micro, capacity, width), "expert")
    grad_gate = product_tn(gate_grad, arrived)[None]
    grad_upward = product_tn(up_grad, arrived)[None]
    grad_downward = product_tn(inner, result_grad)[None]

    spread = jnp.einsum("mect,emcd->emtd", table_low, returned, preferred_element_type=F32)
    spread = spread.reshape(experts, micro * tok, width)
    mixed = jnp.sum(jnp.transpose(second_gates)[:, :, None] * spread, axis=0)
    layer_out = (middle + mixed).astype(BF16)
    dz = top_grad.reshape(micro * tok, width).astype(F32)
    second_gate_grad = jnp.transpose(jnp.sum(spread * dz[None], axis=-1))
    (second_logit_grad,) = second_gate_pull(second_gate_grad)
    hn_grad = jnp.einsum("mect,emcd->mtd", table_low, came_back, preferred_element_type=F32)
    hn_grad = hn_grad.reshape(micro * tok, width)
    second_router_wide = second_router.astype(F32)
    for expert in range(experts):
        hn_grad = hn_grad + second_logit_grad[:, expert : expert + 1] * second_router_wide[expert]
    grad_router_second = jnp.dot(
        jnp.transpose(second_logit_grad),
        second_normed.astype(F32),
        precision=HIGHEST,
        preferred_element_type=F32,
    )
    middle_grad, grad_gain_second = second_pull(hn_grad)
    middle_grad = middle_grad + dz

    mix_grad = gather(middle_grad.astype(BF16), TREES).astype(F32)
    own_gate_grad = jnp.sum(mix_grad * projected, axis=-1)
    projected_grad = (own_gate[:, None] * mix_grad).astype(BF16)
    heads_grad = product_nt(projected_grad, out_weight).astype(BF16).reshape(shape)
    grad_output = scatter(product_tn(heads_flat, projected_grad).astype(BF16), "line")
    query_pre, kv_pre = attend_back(queries, kv, heads_grad, cosine, sine, bias, scale)
    query_pre = query_pre.reshape(rows, feats)
    kv_sum = scatter(kv_pre.reshape(experts * 2, rows, piece), "expert")
    grad_query = scatter(product_tn(tree_input, query_pre).astype(BF16), "line")
    grad_query = swap(grad_query.reshape(own_in * pair, line, part)[None], "pair", 1, 0)
    grad_query = jnp.transpose(grad_query, (1, 2, 0, 3)).reshape(1, own_in, heads_total)

    (first_logit_grad,) = first_gate_pull(own_gate_grad[:, None] * column[None, :])
    key_pre, value_pre = kv_sum[0], kv_sum[1]
    input_term = (
        product_nt(query_pre, query_weight)
        + product_nt(key_pre, kv_weight[:, :piece])
        + product_nt(value_pre, kv_weight[:, piece:])
    )
    first_router_wide = first_router.astype(F32)
    for expert in range(experts):
        input_term = input_term + first_logit_grad[:, expert : expert + 1] * first_router_wide[expert]
    normed_grad = scatter(input_term.astype(BF16), TREES).astype(F32)
    grad_kv = jnp.stack(
        [product_tn(tree_input, key_pre), product_tn(tree_input, value_pre)], axis=1
    )
    grad_kv = scatter(grad_kv.astype(BF16), "line")
    grad_kv = swap(grad_kv.reshape(pair * experts, own_kv, 2, piece), TREES)
    grad_kv = grad_kv.reshape(pair, experts, own_kv, 2, line // experts, part)
    grad_kv = jnp.transpose(grad_kv, (2, 3, 1, 4, 0, 5)).reshape(own_kv, 2, heads_total)
    grad_kv = grad_kv.astype(F32)
    grad_router_first = jnp.dot(
        jnp.transpose(first_logit_grad),
        tree_input.astype(F32),
        precision=HIGHEST,
        preferred_element_type=F32,
    )
    token_grad, grad_gain_first = first_pull(normed_grad)
    tokens_grad = token_grad + middle_grad

    sums = jnp.concatenate(
        [grad_gain_first[None], grad_gain_second[None], grad_router_first, grad_router_second],
        axis=0,
    )
    sums = jnp.transpose(sums.reshape(sums.shape[0], -1, own_kv), (1, 0, 2))
    sums = scatter(sums, ALL)[0]
    return (
        layer_out.reshape(micro, 1, tok, width),
        tokens_grad.reshape(micro, 1, tok, width),
        grad_query.astype(F32),
        grad_output[None].astype(F32),
        grad_kv[:, 0],
        grad_kv[:, 1],
        sums[0],
        jnp.transpose(sums[2 : 2 + experts]),
        sums[1],
        jnp.transpose(sums[2 + experts :]),
        grad_gate,
        grad_upward,
        grad_downward,
    )


def solution(mesh):
    line, experts = mesh.devices.shape
    pair = 2 if line % 2 == 0 and (HEADS % line == 0) else 1
    shaped = Mesh(mesh.devices.reshape(line // pair, pair, experts), ALL)
    in_specs = (
        P(None, DP, "expert", None),
        P("expert", DP, None),
        P("expert", DP, None),
        P(ALL, None),
        P(ALL, None),
        P(ALL),
        P(ALL, None),
        P(ALL),
        P(ALL, None),
        P("expert", DP, None),
        P("expert", DP, None),
        P("expert", DP, None),
        P(None, DP, None, None),
        P(None, DP, "expert", None),
        P(None, DP, "expert"),
        P(None, DP, None),
        P(None, DP, "expert", None),
    )
    out_specs = (
        P(None, DP, "expert", None),
        P(None, DP, "expert", None),
        P("expert", DP, None),
        P("expert", DP, None),
        P(ALL, None),
        P(ALL, None),
        P(ALL),
        P(ALL, None),
        P(ALL),
        P(ALL, None),
        P("expert", DP, None),
        P("expert", DP, None),
        P("expert", DP, None),
    )
    return jax.shard_map(body, mesh=shaped, in_specs=in_specs, out_specs=out_specs, check_vma=False)
```

time: 5410 us -> 1530 us (0.28)
  waiting for transfers between devices: 4610 us -> 1030 us
  matrix products: 456 us -> 190 us
    reduce_scatter x14 -> x9, waiting for transfers between devices: 2920 us -> 629 us  [scatter(): return lax.psum_scatter(value, axes, scatter_dimension=axis, tiled=True)]
    all_gather x15 -> x8, waiting for transfers between devices: 1630 us -> 392 us  [the longest x7 367 us: gather(): return lax.all_gather(value, axes, axis=axis, tiled=True)]
    dot_general x52 -> x14, matrix products: 194 us -> 76.9 us  [the longest x6 61.5 us: product(): return jnp.dot(left, right, preferred_element_type=F32)]
    dot_general x14 -> x7, matrix products: 143 us -> 53.5 us  [product_tn(): lax.dot_general(left, right, (((0,), (0,)), ((), ())), preferred_element_...]
    unnamed x2 -> x0, blocking collectives: 86.4 us -> none
    all_to_all x0 -> x4, blocking collectives: none -> 72.3 us  [swap(): lax.all_to_all(value, axes, split_axis=split, concat_axis=concat, tiled=T...]
    dot_general x14 -> x9, matrix products: 120 us -> 59.3 us  [product_nt(): lax.dot_general(left, right, (((1,), (1,)), ((), ())), preferred_element_...]
  transfers between devices with their start and end apart: 39 -> 21, of which waited for: 28 -> 17; matrix products, arithmetic and copies ran while one was open for 10% -> 14% of each run, Pallas kernels for 0% -> 1%
where the time goes in v1:
time: 1530 us; the launch traced here: 1520 us
  waiting for transfers between devices  1030 us (67%)
  matrix products  190 us (12%)
  blocking collectives  120 us (8%)
  local copies, waits for them, and re-layouts  65 us (4%)
  Pallas kernels  45.7 us (3%)
  other arithmetic  35.9 us (2%)
  starting transfers between devices  17.4 us (1%)
  between operations  15.5 us (1%)
    reduce_scatter x9, waiting for transfers between devices, scatter(): return lax.psum_scatter(value, axes, scatter_dimension=axis, tiled=True)  629 us
    all_gather x7, waiting for transfers between devices, gather(): return lax.all_gather(value, axes, axis=axis, tiled=True)  367 us
    all_to_all x4, blocking collectives, swap(): lax.all_to_all(value, axes, split_axis=split, concat_axis=concat, tiled=T...  72.3 us
    dot_general x6, matrix products, product(): return jnp.dot(left, right, preferred_element_type=F32)  61.5 us
    dot_general x9, matrix products, product_nt(): lax.dot_general(left, right, (((1,), (1,)), ((), ())), preferred_element_...  59.3 us
    dot_general x7, matrix products, product_tn(): lax.dot_general(left, right, (((0,), (0,)), ((), ())), preferred_element_...  53.5 us
    all_gather x1, blocking collectives, body(): lax.all_gather(small, ALL, axis=0)  42.4 us
  transfers between devices with their start and end apart: 21, of which 17 were waited for; matrix products, arithmetic and copies ran while one was open for 14% of the time, Pallas kernels for 1%

profile of v1, /device:TPU:0, one launch (start us, length us, event | category | flops | bytes accessed | tf_op | source)
XLA Modules:
  0.0 1521.7 jit_solution(11662664729170185779)
XLA Ops:
  13.1 13.9 all_to_all.44
  28.8 42.4 %all-gather.5 = bf16[32,10,64]{2,1,0:T(8,128)(2,1)S(1)} all-gather(bf16[1,10,64]{2,1,0:T(8,128)(2,1)S(1)} %maximum_bitcast_fusion.2), channel_id=3, replica_groups=mesh['line'=4,'pair'=2,'expert'=4] {'line','pair','expert'}, dimensions={0}, use_global_device_ids=true | all-gather | bytes 42240 | tf_op jit(solution)/shard_map/all_gather | solution.py:266
  77.2 23.2 %all_to_all.45 = bf16[2,256,1024]{1,2,0:T(8,128)(2,1)} all-to-all(bf16[2,256,1024]{1,2,0:T(8,128)(2,1)S(1)} %bitcast.298), channel_id=1, replica_groups=mesh['line'=4,'pair'=2,'expert'=4] {'pair'}, dimensions={0} | all-to-all | bytes 2097152 | tf_op jit(solution)/shard_map/all_to_all | solution.py:214
  110.3 4.8 all-gather.15.cloned.1.call-done
  115.0 5.3 fusion.101
  126.8 4.9 all-gather.4
  142.4 55.6 %all-gather.17.cloned.1.call-done = bf16[2048,1024]{1,0:T(8,128)(2,1)} async-done(((bf16[512,1024]{1,0:T(8,128)(2,1)}), bf16[2048,1024]{1,0:T(8,128)(2,1)}) %all-gather.17.cloned.1.call-update) | async-done | bytes 4194320 | tf_op jit(solution)/shard_map/all_gather | solution.py:206
  198.0 10.1 fusion.100
  208.1 24.9 %all-gather.27.cloned.1.call-done = bf16[8,1024,256]{2,1,0:T(8,128)(2,1)} async-done(((bf16[2,1024,256]{2,1,0:T(8,128)(2,1)}), bf16[8,1024,256]{2,1,0:T(8,128)(2,1)}) %all-gather.27.cloned.1.call-update) | async-done | bytes 4194320 | tf_op jit(solution)/shard_map/all_gather | solution.py:318
  233.0 19.9 %attend.1 = (bf16[2,4,2,64,1024]{4,3,2,1,0:T(8,128)(2,1)}, bf16[2,4,2,64,1024]{4,3,2,1,0:T(8,128)(2,1)}) custom-call(f32[2,4,2,64,1024]{4,3,2,1,0:T(8,128)} %bitcast.291, bf16[4,2,2,4,2,64,256]{6,5,4,3,2,1,0:T(8,128)(2,1)} %bitcast.289, f32[256,64]{1,0:T(8,128)} %get-tuple-element.132.cos_ref, f32[256,64]{1,0:T(8,128)} %get-tuple-element.131.sin_ref, ...), custom_call_target="tpu_custom_call" | custom-call | flops 1073741824 | bytes 12582912 | tf_op jit(solution)/shard_map/attend/pallas_call | solution.py:169
  253.0 62.3 %all-gather.29.cloned.1.call-done = bf16[1,1024,2048]{2,1,0:T(8,128)(2,1)} async-done(((bf16[1,256,2048]{2,1,0:T(8,128)(2,1)}), bf16[1,1024,2048]{2,1,0:T(8,128)(2,1)}) %all-gather.29.cloned.1.call-update) | async-done | bytes 4194320 | tf_op jit(solution)/shard_map/all_gather | solution.py:206
  315.2 12.1 multiply_convert_fusion
  328.4 49.0 %reduce-scatter.10.cloned.1.call-done = bf16[128,2048]{1,0:T(8,128)(2,1)} async-done(((bf16[1024,2048]{1,0:T(8,128)(2,1)}), bf16[128,2048]{1,0:T(8,128)(2,1)}) %reduce-scatter.10.cloned.1.call-update) | async-done | bytes 524304 | tf_op jit(solution)/shard_map/reduce_scatter | solution.py:210
  381.3 17.6 %all_to_all.46 = bf16[4,2,32,2048]{3,2,1,0:T(8,128)(2,1)} all-to-all(bf16[4,2,32,2048]{3,2,1,0:T(8,128)(2,1)S(1)} %copy.131), channel_id=1, replica_groups=mesh['line'=4,'pair'=2,'expert'=4] {'expert'}, dimensions={0} | all-to-all | bytes 2097152 | tf_op jit(solution)/shard_map/all_to_all | solution.py:214
  402.7 17.6 %all_to_all.47 = bf16[4,2,32,2048]{3,2,1,0:T(8,128)(2,1)} all-to-all(bf16[4,2,32,2048]{3,2,1,0:T(8,128)(2,1)S(1)} %copy.133), channel_id=1, replica_groups=mesh['line'=4,'pair'=2,'expert'=4] {'expert'}, dimensions={0} | all-to-all | bytes 2097152 | tf_op jit(solution)/shard_map/all_to_all | solution.py:214
  420.4 103.5 %all-gather.21.cloned.1.call-done = bf16[2048,2048]{1,0:T(8,128)(2,1)} async-done(((bf16[256,2048]{1,0:T(8,128)(2,1)}), bf16[2048,2048]{1,0:T(8,128)(2,1)}) %all-gather.21.cloned.1.call-update) | async-done | bytes 8388624 | tf_op jit(solution)/shard_map/all_gather | solution.py:206
  524.0 11.2 fusion.10
  535.1 8.0 fusion.14
  543.1 106.3 %all-gather.23.cloned.1.call-done = bf16[2048,2048]{1,0:T(8,128)(2,1)} async-done(((bf16[256,2048]{1,0:T(8,128)(2,1)}), bf16[2048,2048]{1,0:T(8,128)(2,1)}) %all-gather.23.cloned.1.call-update) | async-done | bytes 8388624 | tf_op jit(solution)/shard_map/all_gather | solution.py:206
  649.4 15.0 multiply_convert_fusion.1
  666.0 9.3 convolution_convert_fusion
  677.1 12.1 fusion.12
  689.3 12.6 add_convert_fusion
  701.9 120.8 %reduce-scatter.12.cloned.1.call-done = bf16[256,2048]{1,0:T(8,128)(2,1)} async-done(((bf16[2048,2048]{1,0:T(8,128)(2,1)}), bf16[256,2048]{1,0:T(8,128)(2,1)}) %reduce-scatter.12.cloned.1.call-update) | async-done | bytes 1048592 | tf_op jit(solution)/shard_map/reduce_scatter | solution.py:210
  822.7 4.2 all-to-all-start.3
  827.2 147.0 %reduce-scatter.14.cloned.1.call-done = bf16[256,2048]{1,0:T(8,128)(2,1)} async-done(((bf16[2048,2048]{1,0:T(8,128)(2,1)}), bf16[256,2048]{1,0:T(8,128)(2,1)}) %reduce-scatter.14.cloned.1.call-update) | async-done | bytes 1048592 | tf_op jit(solution)/shard_map/reduce_scatter | solution.py:210
  974.2 4.2 all-to-all-start.5
  982.4 10.6 all-to-all-done.5
  997.5 34.9 %all-gather.25.cloned.1.call-done = bf16[1024,2048]{1,0:T(8,128)(2,1)} async-done(((bf16[128,2048]{1,0:T(8,128)(2,1)}), bf16[1024,2048]{1,0:T(8,128)(2,1)}) %all-gather.25.cloned.1.call-update) | async-done | bytes 4194320 | tf_op jit(solution)/shard_map/all_gather | solution.py:206
  1032.4 9.3 fusion.21
  1041.7 25.7 %attend_back.1 = (bf16[2,4,2,64,1024]{4,3,2,1,0:T(8,128)(2,1)}, bf16[4,2,2,4,2,64,256]{6,5,4,3,2,1,0:T(8,128)(2,1)}) custom-call(bf16[2,4,2,64,1024]{4,3,2,1,0:T(8,128)(2,1)} %get-tuple-element.18.query_ref, bf16[4,2,2,4,2,64,256]{6,5,4,3,2,1,0:T(8,128)(2,1)} %bitcast.290, bf16[2,4,2,64,1024]{4,3,2,1,0:T(8,128)(2,1)} %bitcast.356, ...), custom_call_target="tpu_custom_call" | custom-call | flops 2684354560 | bytes 14680064 | tf_op jit(solution)/shard_map/attend_back/pallas_call | solution.py:187
  1069.1 8.5 convolution_convert_fusion.2
  1077.8 34.4 %reduce-scatter.16.cloned.1.call-done = bf16[2,1024,256]{2,1,0:T(8,128)(2,1)} async-done(((bf16[8,1024,256]{2,1,0:T(8,128)(2,1)}), bf16[2,1024,256]{2,1,0:T(8,128)(2,1)}) %reduce-scatter.16.cloned.1.call-update) | async-done | bytes 1048592 | tf_op jit(solution)/shard_map/reduce_scatter | solution.py:210
  1119.0 10.4 convolution_convert_fusion.1
  1130.1 6.5 copy.139
  1137.0 5.7 fusion.1
  1143.5 4.6 fusion.103
  1149.4 5.2 add_convert_fusion.1
  1154.7 11.1 convolution_bitcast_fusion
  1165.9 10.5 convolution_bitcast_fusion.1
  1176.4 7.9 convolution_bitcast_fusion.2
  1185.0 6.3 reduce-scatter.20.cloned.1.call-done
  1198.8 6.7 fusion.60
  1205.5 33.0 %reduce-scatter.24.cloned.1.call-done = bf16[512,2,256]{2,0,1:T(8,128)(2,1)} async-done(((bf16[2048,2,256]{2,0,1:T(8,128)(2,1)}), bf16[512,2,256]{2,0,1:T(8,128)(2,1)}) %reduce-scatter.24.cloned.1.call-update) | async-done | bytes 524304 | tf_op jit(solution)/shard_map/reduce_scatter | solution.py:210
  1244.1 72.7 %reduce-scatter.22.cloned.1.call-done = bf16[256,2048]{1,0:T(8,128)(2,1)} async-done(((bf16[1024,2048]{1,0:T(8,128)(2,1)}), bf16[256,2048]{1,0:T(8,128)(2,1)}) %reduce-scatter.22.cloned.1.call-update) | async-done | bytes 1048592 | tf_op jit(solution)/shard_map/reduce_scatter | solution.py:210
  1324.0 4.2 reshape.645
  1335.6 36.5 %reduce-scatter.18.cloned.1.call-done = bf16[128,2048]{1,0:T(8,128)(2,1)} async-done(((bf16[1024,2048]{1,0:T(8,128)(2,1)}), bf16[128,2048]{1,0:T(8,128)(2,1)}) %reduce-scatter.18.cloned.1.call-update) | async-done | bytes 524304 | tf_op jit(solution)/shard_map/reduce_scatter | solution.py:210
  1382.4 129.7 %reduce-scatter.26.cloned.1.call-done = f32[1,10,64]{2,1,0:T(8,128)} async-done(((f32[32,10,64]{2,1,0:T(8,128)}), f32[1,10,64]{2,1,0:T(8,128)}) %reduce-scatter.26.cloned.1.call-update) | async-done | bytes 2576 | tf_op jit(solution)/shard_map/reduce_scatter | solution.py:210
  (307 shorter events, 114.1 us)
Async XLA Ops:
  7.2 642.2 %copy-start = (bf16[1,704,2048]{2,1,0:T(8,128)(2,1)S(1)}, bf16[1,704,2048]{2,1,0:T(8,128)(2,1)}, u32[]{:S(2)}) copy-start(bf16[1,704,2048]{2,1,0:T(8,128)(2,1)} %param.28) | copy-start | bytes 8650756
  7.2 21.2 %copy-start.2 = (bf16[2,1,64,2048]{3,2,1,0:T(8,128)(2,1)S(1)}, bf16[2,1,64,2048]{3,2,1,0:T(8,128)(2,1)}, u32[]{:S(2)}) copy-start(bf16[2,1,64,2048]{3,2,1,0:T(8,128)(2,1)} %param.17) | copy-start | bytes 1572868
  7.2 21.5 %copy-start.47 = (bf16[64,4]{0,1:T(4,128)(2,1)S(1)}, bf16[64,4]{0,1:T(4,128)(2,1)}, u32[]{:S(2)}) copy-start(bf16[64,4]{0,1:T(4,128)(2,1)} %param.25) | copy-start | bytes 1540
  7.2 21.5 %copy-start.50 = (bf16[64]{0:T(256)(128)(2,1)S(1)}, bf16[64]{0:T(256)(128)(2,1)}, u32[]{:S(2)}) copy-start(bf16[64]{0:T(256)(128)(2,1)} %param.24) | copy-start | bytes 388
  7.2 21.5 %copy-start.48 = (bf16[64,4]{0,1:T(4,128)(2,1)S(1)}, bf16[64,4]{0,1:T(4,128)(2,1)}, u32[]{:S(2)}) copy-start(bf16[64,4]{0,1:T(4,128)(2,1)} %param.23) | copy-start | bytes 1540
  7.2 21.5 %copy-start.51 = (bf16[64]{0:T(256)(128)(2,1)S(1)}, bf16[64]{0:T(256)(128)(2,1)}, u32[]{:S(2)}) copy-start(bf16[64]{0:T(256)(128)(2,1)} %param.22) | copy-start | bytes 388
  7.2 103.0 %all-gather.19.cloned.1.call-start = ((), (), s32[]{:S(2)}) async-start(), calls=%async_computation.19 | async-start | bytes 2621440 | tf_op jit(solution)/shard_map/all_gather | solution.py:206
  28.4 86.6 %all-gather.15.cloned.1.call-start = ((), (), s32[]{:S(2)}) async-start(), calls=%async_computation.17 | async-start | bytes 4718592 | tf_op jit(solution)/shard_map/all_gather | solution.py:206
  28.7 42.5 %copy-start.60 = (f32[128]{0:T(128)}, f32[128]{0:T(128)S(1)}, u32[]{:S(2)}) copy-start(f32[128]{0:T(128)S(1)} %add.308) | copy-start | bytes 1540
  28.7 74.0 %copy-start.42 = (f32[128]{0:T(128)}, f32[128]{0:T(128)S(1)}, u32[]{:S(2)}) copy-start(f32[128]{0:T(128)S(1)} %rsqrt.20) | copy-start | bytes 1540
  72.6 30.1 %copy-start.24 = (f32[2048]{0:T(1024)}, f32[2048]{0:T(1024)S(1)}, u32[]{:S(2)}) copy-start(f32[2048]{0:T(1024)S(1)} %reshape.642) | copy-start | bytes 24580
  73.6 124.4 %all-gather.17.cloned.1.call-start = ((), (), s32[]{:S(2)}) async-start(), calls=%async_computation.18 | async-start | bytes 5242880 | tf_op jit(solution)/shard_map/all_gather | solution.py:206
  102.8 130.3 %all-gather.27.cloned.1.call-start = ((), (), s32[]{:S(2)}) async-start(), calls=%async_computation.32 | async-start | bytes 5242880 | tf_op jit(solution)/shard_map/all_gather | solution.py:318
  124.1 191.1 %all-gather.29.cloned.1.call-start = ((), (), s32[]{:S(2)}) async-start(), calls=%async_computation.33 | async-start | bytes 5242880 | tf_op jit(solution)/shard_map/all_gather | solution.py:206
  124.7 252.7 %reduce-scatter.10.cloned.1.call-start = ((), (), s32[]{:S(2)}) async-start(), calls=%async_computation.20 | async-start | bytes 4718592 | tf_op jit(solution)/shard_map/reduce_scatter | solution.py:210
  135.2 72.9 %copy-start.22 = (s32[1024,2]{0,1:T(2,128)}, s32[1024,2]{0,1:T(2,128)S(1)}, u32[]{:S(2)}) copy-start(s32[1024,2]{0,1:T(2,128)S(1)} %eq.146) | copy-start | bytes 24580
  135.2 72.9 %copy-start.45 = (f32[4]{0:T(128)}, f32[4]{0:T(128)S(1)}, u32[]{:S(2)}) copy-start(f32[4]{0:T(128)S(1)} %compare_convert_fusion) | copy-start | bytes 52
  142.2 65.9 %copy-start.18 = (f32[1024,2]{0,1:T(2,128)}, f32[1024,2]{0,1:T(2,128)S(1)}, u32[]{:S(2)}) copy-start(f32[1024,2]{0,1:T(2,128)S(1)} %select_reduce_fusion.5) | copy-start | bytes 24580
  142.2 65.9 %copy-start.31 = (f32[1024]{0:T(1024)}, f32[1024]{0:T(1024)S(1)}, u32[]{:S(2)}) copy-start(f32[1024]{0:T(1024)S(1)} %reduce_max.18) | copy-start | bytes 12292
  142.3 65.9 %copy-start.33 = (f32[1024]{0:T(1024)}, f32[1024]{0:T(1024)S(1)}, u32[]{:S(2)}) copy-start(f32[1024]{0:T(1024)S(1)} %fusion.93) | copy-start | bytes 12292
  327.4 196.6 %all-gather.21.cloned.1.call-start = ((), (), s32[]{:S(2)}) async-start(), calls=%async_computation.21 | async-start | bytes 9437184 | tf_op jit(solution)/shard_map/all_gather | solution.py:206
  378.7 616.8 %copy-start.36 = (f32[128]{0:T(128)}, f32[128]{0:T(128)S(1)}, u32[]{:S(2)}) copy-start(f32[128]{0:T(128)S(1)} %fusion.88) | copy-start | bytes 1540
  398.9 250.5 %all-gather.23.cloned.1.call-start = ((), (), s32[]{:S(2)}) async-start(), calls=%async_computation.23 | async-start | bytes 9437184 | tf_op jit(solution)/shard_map/all_gather | solution.py:206
  420.4 402.3 %reduce-scatter.12.cloned.1.call-start = ((), (), s32[]{:S(2)}) async-start(), calls=%async_computation.22 | async-start | bytes 9437184 | tf_op jit(solution)/shard_map/reduce_scatter | solution.py:210
  675.3 298.9 %reduce-scatter.14.cloned.1.call-start = ((), (), s32[]{:S(2)}) async-start(), calls=%async_computation.24 | async-start | bytes 9437184 | tf_op jit(solution)/shard_map/reduce_scatter | solution.py:210
  701.9 125.1 %copy-start.6 = (bf16[2,1,64,2048]{3,2,1,0:T(8,128)(2,1)S(1)}, bf16[2,1,64,2048]{3,2,1,0:T(8,128)(2,1)}, u32[]{:S(2)}) copy-start(bf16[2,1,64,2048]{3,2,1,0:T(8,128)(2,1)} %param.33) | copy-start | bytes 1572868
  822.7 151.5 %all-to-all-start.3 = ((bf16[4,2,32,2048]{3,2,1,0:T(8,128)(2,1)}), bf16[4,2,32,2048]{3,2,1,0:T(8,128)(2,1)}, u32[]{:S(2)}, u32[]{:S(2)}) async-start(bf16[4,2,32,2048]{3,2,1,0:T(8,128)(2,1)} %bitcast.309), calls=%async_computation.5 | async-start | bytes 2097152 | tf_op jit(solution)/shard_map/all_to_all | solution.py:214
  826.9 168.5 %copy-start.26 = (f32[1,2048]{1,0:T(1,128)}, f32[1,2048]{1,0:T(1,128)S(1)}, u32[]{:S(2)}) copy-start(f32[1,2048]{1,0:T(1,128)S(1)} %get-tuple-element.117) | copy-start | bytes 24580
  827.0 168.5 %copy-start.27 = (f32[1,2048]{1,0:T(1,128)}, f32[1,2048]{1,0:T(1,128)S(1)}, u32[]{:S(2)}) copy-start(f32[1,2048]{1,0:T(1,128)S(1)} %get-tuple-element.118) | copy-start | bytes 24580
  827.0 168.5 %copy-start.28 = (f32[1,2048]{1,0:T(1,128)}, f32[1,2048]{1,0:T(1,128)S(1)}, u32[]{:S(2)}) copy-start(f32[1,2048]{1,0:T(1,128)S(1)} %get-tuple-element.119) | copy-start | bytes 24580
  827.0 168.5 %copy-start.29 = (f32[1,2048]{1,0:T(1,128)}, f32[1,2048]{1,0:T(1,128)S(1)}, u32[]{:S(2)}) copy-start(f32[1,2048]{1,0:T(1,128)S(1)} %get-tuple-element.120) | copy-start | bytes 24580
  827.1 167.6 %copy-start.5 = (bf16[128,2048]{1,0:T(8,128)(2,1)S(1)}, bf16[128,2048]{1,0:T(8,128)(2,1)}, u32[]{:S(2)}) copy-start(bf16[128,2048]{1,0:T(8,128)(2,1)} %reduce-scatter.10.cloned.1.call-done) | copy-start | bytes 1572868
  974.2 18.8 %all-to-all-start.5 = ((bf16[4,2,32,2048]{3,2,1,0:T(8,128)(2,1)}), bf16[4,2,32,2048]{3,2,1,0:T(8,128)(2,1)}, u32[]{:S(2)}, u32[]{:S(2)}) async-start(bf16[4,2,32,2048]{3,2,1,0:T(8,128)(2,1)} %bitcast.308), calls=%async_computation.8 | async-start | bytes 2097152 | tf_op jit(solution)/shard_map/all_to_all | solution.py:214
  978.5 54.0 %all-gather.25.cloned.1.call-start = ((), (), s32[]{:S(2)}) async-start(), calls=%async_computation.25 | async-start | bytes 4718592 | tf_op jit(solution)/shard_map/all_gather | solution.py:206
  994.6 47.1 %copy-start.4 = (f32[2,64,2048,1]{2,1,3,0:T(8,128)}, f32[2,64,2048,1]{2,1,3,0:T(8,128)S(1)}, u32[]{:S(2)}) copy-start(f32[2,64,2048,1]{2,1,3,0:T(8,128)S(1)} %fusion.42) | copy-start | bytes 3145732
  995.5 46.3 %copy-start.44 = (f32[128]{0:T(128)}, f32[128]{0:T(128)S(1)}, u32[]{:S(2)}) copy-start(f32[128]{0:T(128)S(1)} %multiply_multiply_fusion.1) | copy-start | bytes 1540
  997.4 114.7 %reduce-scatter.16.cloned.1.call-start = ((), (), s32[]{:S(2)}) async-start(), calls=%async_computation.26 | async-start | bytes 5242880 | tf_op jit(solution)/shard_map/reduce_scatter | solution.py:210
  1067.5 123.7 %reduce-scatter.20.cloned.1.call-start = ((), (), s32[]{:S(2)}) async-start(), calls=%async_computation.28 | async-start | bytes 5242880 | tf_op jit(solution)/shard_map/reduce_scatter | solution.py:210
  1077.5 160.9 %reduce-scatter.24.cloned.1.call-start = ((), (), s32[]{:S(2)}) async-start(), calls=%async_computation.30 | async-start | bytes 2621440 | tf_op jit(solution)/shard_map/reduce_scatter | solution.py:210
  1119.0 197.7 %reduce-scatter.22.cloned.1.call-start = ((), (), s32[]{:S(2)}) async-start(), calls=%async_computation.29 | async-start | bytes 5242880 | tf_op jit(solution)/shard_map/reduce_scatter | solution.py:210
  1129.4 242.8 %reduce-scatter.18.cloned.1.call-start = ((), (), s32[]{:S(2)}) async-start(), calls=%async_computation.27 | async-start | bytes 4718592 | tf_op jit(solution)/shard_map/reduce_scatter | solution.py:210
  1154.7 21.7 %slice-start = ((s8[8388608]{0:T(1024)(128)(4,1)}), s8[4194304]{0:T(1024)(128)(4,1)S(1)}, s32[]{:S(2)}) async-start(s8[8388608]{0:T(1024)(128)(4,1)} %bitcast.349), calls=%async_computation.34 | async-start | bytes 8388608
  1193.9 46.5 %all-to-all-start.6 = ((bf16[1,512,4,256]{3,2,0,1:T(4,128)(2,1)}), bf16[1,512,4,256]{3,2,0,1:T(4,128)(2,1)S(1)}, u32[]{:S(2)}, u32[]{:S(2)}) async-start(bf16[1,512,4,256]{3,2,0,1:T(4,128)(2,1)} %bitcast.75), calls=%async_computation.12 | async-start | bytes 2097152 | tf_op jit(solution)/shard_map/all_to_all | solution.py:214
  1240.4 79.1 %copy-start.9 = (bf16[1,512,4,256]{3,2,0,1:T(4,128)(2,1)}, bf16[1,512,4,256]{3,2,0,1:T(4,128)(2,1)S(1)}, u32[]{:S(2)}) copy-start(bf16[1,512,4,256]{3,2,0,1:T(4,128)(2,1)S(1)} %all-to-all-done.6) | copy-start | bytes 3145732
  1240.4 87.8 %all-to-all-start.7 = ((bf16[8,64,2,256]{3,1,2,0:T(8,128)(2,1)}), bf16[8,64,2,256]{3,1,2,0:T(8,128)(2,1)S(1)}, u32[]{:S(2)}, u32[]{:S(2)}) async-start(bf16[8,64,2,256]{3,1,2,0:T(8,128)(2,1)} %copy.137), calls=%async_computation.15 | async-start | bytes 1048576 | tf_op jit(solution)/shard_map/all_to_all | solution.py:214
  1244.0 268.0 %reduce-scatter.26.cloned.1.call-start = ((), (), s32[]{:S(2)}) async-start(), calls=%async_computation.31 | async-start | bytes 270336 | tf_op jit(solution)/shard_map/reduce_scatter | solution.py:210
  1328.1 44.1 %copy-start.25 = (f32[2048]{0:T(1024)S(1)}, f32[2048]{0:T(1024)}, u32[]{:S(2)}) copy-start(f32[2048]{0:T(1024)} %copy-done.24) | copy-start | bytes 24580
  1330.0 184.6 %copy-start.1 = (bf16[1,704,2048]{2,1,0:T(8,128)(2,1)S(1)}, bf16[1,704,2048]{2,1,0:T(8,128)(2,1)}, u32[]{:S(2)}) copy-start(bf16[1,704,2048]{2,1,0:T(8,128)(2,1)} %param.28) | copy-start | bytes 8650756
  (40 other events, 275.3 us)
Sparse Core Ops, SparseCore 0:
  28.5 46.5 all-gather.18
  77.6 37.4 all-gather.14
  117.2 80.7 all-gather.16
  200.0 33.0 all-gather.26
  234.4 80.7 all-gather.28
  327.5 49.8 reduce-scatter.9
  399.0 124.8 all-gather.20
  526.3 123.0 all-gather.22
  675.4 147.1 reduce-scatter.11
  826.1 148.0 reduce-scatter.13
  997.6 34.8 all-gather.24
  1067.6 44.4 reduce-scatter.15
  1114.4 76.7 reduce-scatter.19
  1194.1 44.3 reduce-scatter.23
  1240.6 76.0 reduce-scatter.21
  1320.3 51.8 reduce-scatter.17
  1378.6 133.3 reduce-scatter.25

commit v2 on v1

--- a/solution.py
+++ b/solution.py
@@ -200,6 +200,833 @@
         ),
         name="attend_back",
     )(queries, kv, grad, cosine, sine, bias)
+
+
+MESH = pl.DeviceIdType.MESH
+ANY = pl.BlockSpec(memory_space=pl.ANY)
+VMEM = pl.BlockSpec(memory_space=pltpu.VMEM)
+DMA = pltpu.SemaphoreType.DMA
+
+
+def remote(src, dst, send, recv, target):
+    return pltpu.make_async_remote_copy(
+        src_ref=src, dst_ref=dst, send_sem=send, recv_sem=recv, device_id=target, device_id_type=MESH
+    )
+
+
+def greet(targets):
+    barrier = pltpu.get_barrier_semaphore()
+    for target in targets:
+        pl.semaphore_signal(barrier, inc=1, device_id=target, device_id_type=MESH)
+    pl.semaphore_wait(barrier, len(targets))
+
+
+def params(number, limit=None):
+    return pltpu.CompilerParams(
+        collective_id=number, has_side_effects=True, vmem_limit_bytes=limit
+    )
+
+
+def add_into(target, sources, rows):
+    step = 1
+    while step * 2 <= rows and step * 2 * target.shape[-1] <= 65536 and rows % (step * 2) == 0:
+        step *= 2
+
+    def one(index, carry):
+        where = pl.ds(pl.multiple_of(index * step, step), step)
+        total = sources[0][where].astype(F32)
+        for source in sources[1:]:
+            total = total + source[where].astype(F32)
+        target[where] = total.astype(target.dtype)
+        return carry
+
+    lax.fori_loop(0, rows // step, one, 0)
+
+
+def cube_reduce_kernel(pairs, x_ref, o_ref, half, quarter, got_core, got_side, got_pair, send, recv):
+    p = lax.axis_index("pair")
+    e = lax.axis_index("expert")
+    c, y = lax.rem(e, 2), lax.div(e, 2)
+    core = {"expert": e + 1 - 2 * c}
+    side = {"expert": e + 2 - 4 * y}
+    other = {"pair": lax.rem(p + 1, pairs)}
+    greet([core, side] + ([other] if pairs == 2 else []))
+    rows = x_ref.shape[3]
+    shifts = (1, 0) if pairs == 2 else (0,)
+    order = [(dx, dy) for dy in (1, 0) for dx in shifts]
+    first, second = [], {}
+    for slot, (dx, dy) in enumerate(order):
+        px, yy = lax.rem(p + dx, pairs), lax.rem(y + dy, 2)
+        copy = remote(
+            x_ref.at[px, yy, 1 - c], got_core.at[slot], send.at[slot], recv.at[slot], core
+        )
+        copy.start()
+        first.append(copy)
+    base = len(order)
+    for slot, (dx, dy) in enumerate(order):
+        px, yy = lax.rem(p + dx, pairs), lax.rem(y + dy, 2)
+        first[slot].wait_recv()
+        add_into(half.at[slot], [x_ref.at[px, yy, c], got_core.at[slot]], rows)
+        if dy == 1:
+            copy = remote(
+                half.at[slot], got_side.at[dx], send.at[base + dx], recv.at[base + dx], side
+            )
+            copy.start()
+            second[dx] = copy
+    last = None
+    for dx in shifts:
+        second[dx].wait_recv()
+        if dx == 1:
+            add_into(quarter, [half.at[order.index((1, 0))], got_side.at[1]], rows)
+            last = remote(quarter, got_pair, send.at[base + 2], recv.at[base + 2], other)
+            last.start()
+    if last is not None:
+        last.wait_recv()
+        add_into(o_ref, [half.at[order.index((0, 0))], got_side.at[0], got_pair], rows)
+    else:
+        add_into(o_ref, [half.at[order.index((0, 0))], got_side.at[0]], rows)
+    for copy in first + list(second.values()) + ([last] if last is not None else []):
+        copy.wait_send()
+
+
+def cube_reduce(value, pairs, number):
+    _, rows, cols = value.shape
+    value = value.reshape(pairs, 2, 2, rows, cols)
+    slots = 2 * pairs
+    block = jax.ShapeDtypeStruct((rows, cols), value.dtype)
+    return pl.pallas_call(
+        partial(cube_reduce_kernel, pairs),
+        in_specs=[VMEM],
+        out_specs=VMEM,
+        out_shape=block,
+        scratch_shapes=[
+            pltpu.VMEM((slots, rows, cols), value.dtype),
+            pltpu.VMEM((rows, cols), value.dtype),
+            pltpu.VMEM((slots, rows, cols), value.dtype),
+            pltpu.VMEM((pairs, rows, cols), value.dtype),
+            pltpu.VMEM((rows, cols), value.dtype),
+            DMA((slots + 3,)),
+            DMA((slots + 3,)),
+        ],
+        compiler_params=params(number, 48 * 2**20),
+        cost_estimate=pl.CostEstimate(
+            flops=value.size, bytes_accessed=24 * value.size, transcendentals=0
+        ),
+        name="cube_reduce",
+    )(value)
+
+
+def cube_gather_kernel(pairs, x_ref, o_ref, send, recv, local):
+    p = lax.axis_index("pair") if pairs == 2 else 0
+    e = lax.axis_index("expert")
+    c, y = lax.rem(e, 2), lax.div(e, 2)
+    core = {"expert": e + 1 - 2 * c}
+    side = {"expert": e + 2 - 4 * y}
+    other = {"pair": lax.rem(p + 1, pairs)}
+    greet([core, side] + ([other] if pairs == 2 else []))
+    q, w = lax.rem(p + 1, pairs), 1 - y
+    own = o_ref.at[p, y, c]
+    keep = pltpu.make_async_copy(x_ref, own, local)
+    keep.start()
+    copies = []
+
+    def push(slot, source, place, target):
+        copy = remote(source, place, send.at[slot], recv.at[slot], target)
+        copy.start()
+        copies.append(copy)
+        return copy
+
+    to_side = push(0, x_ref, own, side)
+    to_other = push(1, x_ref, own, other) if pairs == 2 else None
+    to_core = push(2, x_ref, own, core)
+    waits = [to_core]
+    if pairs == 2:
+        to_other.wait_recv()
+        block = o_ref.at[q, y, c]
+        far = push(3, block, block, side)
+        waits.append(push(4, block, block, core))
+    to_side.wait_recv()
+    block = o_ref.at[p, w, c]
+    waits.append(push(5, block, block, core))
+    if pairs == 2:
+        far.wait_recv()
+        block = o_ref.at[q, w, c]
+        waits.append(push(6, block, block, core))
+    for copy in waits:
+        copy.wait_recv()
+    for copy in copies:
+        copy.wait_send()
+    keep.wait()
+
+
+def cube_gather(value, pairs, number):
+    return pl.pallas_call(
+        partial(cube_gather_kernel, pairs),
+        in_specs=[VMEM],
+        out_specs=VMEM,
+        out_shape=jax.ShapeDtypeStruct((pairs, 2, 2) + value.shape, value.dtype),
+        scratch_shapes=[DMA((7,)), DMA((7,)), DMA(())],
+        compiler_params=params(number, 48 * 2**20),
+        cost_estimate=pl.CostEstimate(
+            flops=0, bytes_accessed=80 * value.size, transcendentals=0
+        ),
+        name="cube_gather",
+    )(value)
+
+
+def place_of(index, sizes):
+    line, pairs, experts = sizes
+    return {
+        "line": index // (pairs * experts),
+        "pair": (index // experts) % pairs,
+        "expert": index % experts,
+    }
+
+
+def small_kernel(sizes, reduce, x_ref, o_ref, got, send, recv):
+    line, pairs, experts = sizes
+    count = line * pairs * experts
+    me = (
+        lax.axis_index("line") * (pairs * experts)
+        + lax.axis_index("pair") * experts
+        + lax.axis_index("expert")
+    )
+    barrier = pltpu.get_barrier_semaphore()
+
+    def greet_one(offset, carry):
+        target = place_of((me + offset) % count, sizes)
+        pl.semaphore_signal(barrier, inc=1, device_id=target, device_id_type=MESH)
+        return carry
+
+    lax.fori_loop(1, count, greet_one, 0)
+    pl.semaphore_wait(barrier, count - 1)
+
+    def copy_to(offset):
+        peer = (me + offset) % count
+        source = x_ref.at[peer] if reduce else x_ref
+        return remote(source, got.at[offset], send.at[offset], recv.at[offset], place_of(peer, sizes))
+
+    def start(offset, carry):
+        copy_to(offset).start()
+        return carry
+
+    lax.fori_loop(1, count, start, 0)
+    got[0] = x_ref[me] if reduce else x_ref[...]
+
+    def finish(offset, carry):
+        copy_to(offset).wait()
+        return carry
+
+    lax.fori_loop(1, count, finish, 0)
+    if reduce:
+        o_ref[...] = jnp.sum(got[...], axis=0)
+    else:
+
+        def order(offset, carry):
+            o_ref[(me - offset + count) % count] = got[offset]
+            return carry
+
+        lax.fori_loop(0, count, order, 0)
+
+
+def small_exchange(value, sizes, reduce, number):
+    count = sizes[0] * sizes[1] * sizes[2]
+    block = value.shape[1:] if reduce else value.shape
+    return pl.pallas_call(
+        partial(small_kernel, sizes, reduce),
+        in_specs=[VMEM],
+        out_specs=VMEM,
+        out_shape=jax.ShapeDtypeStruct(block if reduce else (count,) + block, value.dtype),
+        scratch_shapes=[pltpu.VMEM((count,) + block, value.dtype), DMA((count,)), DMA((count,))],
+        compiler_params=params(number),
+        cost_estimate=pl.CostEstimate(flops=0, bytes_accessed=2**24, transcendentals=0),
+        name="small_reduce" if reduce else "small_gather",
+    )(value)
+
+
+def ff_gather_kernel(line, a_in, b_in, a_hbm, b_hbm, a_out, b_out, send, recv, local, store):
+    z, p, e = lax.axis_index("line"), lax.axis_index("pair"), lax.axis_index("expert")
+    experts = a_in.shape[0]
+    q = 1 - p
+    up, down, other = {"line": z + 1}, {"line": z - 1}, {"pair": q}
+    twin = z + 1 - 2 * lax.rem(z, 2)
+    barrier = pltpu.get_barrier_semaphore()
+    for shift in range(1, experts):
+        pl.semaphore_signal(
+            barrier, inc=1, device_id={"expert": lax.rem(e + shift, experts)}, device_id_type=MESH
+        )
+    pl.semaphore_signal(barrier, inc=1, device_id=other, device_id_type=MESH)
+
+    @pl.when(z > 0)
+    def _():
+        pl.semaphore_signal(barrier, inc=1, device_id=down, device_id_type=MESH)
+
+    @pl.when(z < line - 1)
+    def _():
+        pl.semaphore_signal(barrier, inc=1, device_id=up, device_id_type=MESH)
+
+    below, above = (z + line - 1) // line, (2 * line - 2 - z) // line
+    pl.semaphore_wait(barrier, experts + below + above)
+
+    pairs = ((a_in, a_out), (b_in, b_out))
+    UP, DOWN, SIDE = 3, 3 + line, 3 + 2 * line
+    EXTRA = SIDE + line
+    starts = []
+    for kind, (src, dst) in enumerate(pairs):
+        size = src.shape[1]
+        home = dst.at[z, p, pl.ds(pl.multiple_of(e * size, size), size)]
+        keep = pltpu.make_async_copy(src.at[e], home, local.at[kind])
+        keep.start()
+        group = []
+        for shift in range(1, experts):
+            peer = lax.rem(e + shift, experts)
+            copy = remote(
+                src.at[peer],
+                home,
+                send.at[kind, shift - 1],
+                recv.at[kind, shift - 1],
+                {"expert": peer},
+            )
+            copy.start()
+            group.append(copy)
+        starts.append((keep, group))
+
+    def to_up(kind, j, d):
+        ref = pairs[kind][1].at[j, p]
+        return remote(ref, ref, send.at[kind, UP + d], recv.at[kind, UP + d], up)
+
+    def to_down(kind, j, d):
+        ref = pairs[kind][1].at[j, p]
+        return remote(ref, ref, send.at[kind, DOWN + d], recv.at[kind, DOWN + d], down)
+
+    def to_other(kind, j):
+        ref = pairs[kind][1].at[j, p]
+        return remote(ref, ref, send.at[kind, SIDE + j], recv.at[kind, SIDE + j], other)
+
+    def to_twin(kind):
+        ref = pairs[kind][1].at[z, q]
+        return remote(ref, ref, send.at[kind, EXTRA], recv.at[kind, EXTRA], {"line": twin})
+
+    for kind in range(2):
+        keep, group = starts[kind]
+        keep.wait()
+        for copy in group:
+            copy.wait_recv()
+
+        @pl.when(z < line - 1)
+        def _():
+            to_up(kind, z, 1).start()
+
+        @pl.when(z > 0)
+        def _():
+            to_down(kind, z, 1).start()
+
+        to_other(kind, z).start()
+
+    for d in range(1, line):
+        for kind in range(2):
+
+            @pl.when(z - d >= 0)
+            def _():
+                to_up(kind, z - d, d).wait_recv()
+
+                @pl.when(z < line - 1)
+                def _():
+                    to_up(kind, z - d, d + 1).start()
+
+                if kind == 0:
+                    to_other(kind, z - d).start()
+                else:
+
+                    @pl.when(z - d != twin)
+                    def _():
+                        to_other(kind, z - d).start()
+
+            @pl.when(z + d < line)
+            def _():
+                to_down(kind, z + d, d).wait_recv()
+
+                @pl.when(z > 0)
+                def _():
+                    to_down(kind, z + d, d + 1).start()
+
+                if kind == 0:
+                    to_other(kind, z + d).start()
+                else:
+
+                    @pl.when(z + d != twin)
+                    def _():
+                        to_other(kind, z + d).start()
+
+        if d == 1:
+            to_other(1, z).wait_recv()
+            to_twin(1).start()
+
+    for j in range(line):
+        to_other(0, j).wait_recv()
+
+        @pl.when((j != twin) & (j != z))
+        def _():
+            to_other(1, j).wait_recv()
+
+        to_other(0, j).wait_send()
+
+        @pl.when(j != twin)
+        def _():
+            to_other(1, j).wait_send()
+
+    to_twin(1).wait()
+    saves = []
+    for kind, target in enumerate((a_hbm, b_hbm)):
+        save = pltpu.make_async_copy(pairs[kind][1], target, store.at[kind])
+        save.start()
+        saves.append(save)
+    for save in saves:
+        save.wait()
+    for kind in range(2):
+        for copy in starts[kind][1]:
+            copy.wait_send()
+        for d in range(1, line):
+
+            @pl.when((z - d + 1 >= 0) & (z < line - 1))
+            def _():
+                to_up(kind, z - d + 1, d).wait_send()
+
+            @pl.when((z + d - 1 < line) & (z > 0))
+            def _():
+                to_down(kind, z + d - 1, d).wait_send()
+
+
+def ff_gather(first, second, line, pairs, number):
+    uses = 3 + 3 * line + 1
+    experts, rows, cols = first.shape
+    out = jax.ShapeDtypeStruct((line, pairs, experts * rows, cols), first.dtype)
+    return pl.pallas_call(
+        partial(ff_gather_kernel, line),
+        in_specs=[VMEM, VMEM],
+        out_specs=[ANY, ANY],
+        out_shape=[out, out],
+        scratch_shapes=[
+            pltpu.VMEM(out.shape, out.dtype),
+            pltpu.VMEM(out.shape, out.dtype),
+            DMA((2, uses)),
+            DMA((2, uses)),
+            DMA((2,)),
+            DMA((2,)),
+        ],
+        compiler_params=params(number, 48 * 2**20),
+        cost_estimate=pl.CostEstimate(
+            flops=0, bytes_accessed=100 * first.size * line, transcendentals=0
+        ),
+        name="ff_gather",
+    )(first, second)
+
+
+def ff_reduce_kernel(
+    line, a_in, b_in, a_out, b_out, mine, side, far, near, done, send, recv, load, local
+):
+    z, p, e = lax.axis_index("line"), lax.axis_index("pair"), lax.axis_index("expert")
+    experts = a_out.shape[0]
+    q = 1 - p
+    up, down, other = {"line": z + 1}, {"line": z - 1}, {"pair": q}
+    barrier = pltpu.get_barrier_semaphore()
+    for shift in range(1, experts):
+        pl.semaphore_signal(
+            barrier, inc=1, device_id={"expert": lax.rem(e + shift, experts)}, device_id_type=MESH
+        )
+    pl.semaphore_signal(barrier, inc=1, device_id=other, device_id_type=MESH)
+
+    @pl.when(z > 0)
+    def _():
+        pl.semaphore_signal(barrier, inc=1, device_id=down, device_id_type=MESH)
+
+    @pl.when(z < line - 1)
+    def _():
+        pl.semaphore_signal(barrier, inc=1, device_id=up, device_id_type=MESH)
+
+    below, above = (z + line - 1) // line, (2 * line - 2 - z) // line
+    pl.semaphore_wait(barrier, experts + below + above)
+
+    kinds = (a_in, b_in)
+    outs = (a_out, b_out)
+    UP, DOWN, SIDE, BACK = 0, line, 2 * line, 3 * line
+    rows = mine.shape[2]
+
+    def to_other(kind, j):
+        return remote(
+            kinds[kind].at[j, q],
+            side.at[kind, j],
+            send.at[kind, SIDE + j],
+            recv.at[kind, SIDE + j],
+            other,
+        )
+
+    def fetch(kind, j):
+        return pltpu.make_async_copy(kinds[kind].at[j, p], mine.at[kind, j], load.at[kind, j])
+
+    def to_up(kind, j):
+        return remote(
+            mine.at[kind, j], far.at[kind, j], send.at[kind, UP + j], recv.at[kind, UP + j], up
+        )
+
+    def to_down(kind, j, dst=None):
+        return remote(
+            mine.at[kind, j], near.at[kind, j], send.at[kind, DOWN + j], recv.at[kind, DOWN + j], down
+        )
+
+    for d in range(line - 1, -1, -1):
+        for kind in range(2):
+
+            @pl.when(z + d < line)
+            def _():
+                to_other(kind, z + d).start()
+                fetch(kind, z + d).start()
+
+            if d > 0:
+
+                @pl.when(z - d >= 0)
+                def _():
+                    to_other(kind, z - d).start()
+                    fetch(kind, z - d).start()
+
+    for d in range(line - 1, 0, -1):
+        for kind in range(2):
+
+            @pl.when(z + d < line)
+            def _():
+                j = z + d
+                fetch(kind, j).wait()
+                to_other(kind, j).wait_recv()
+                add_into(mine.at[kind, j], [mine.at[kind, j], side.at[kind, j]], rows)
+
+                @pl.when(z > 0)
+                def _():
+                    to_up(kind, j).wait_recv()
+                    add_into(mine.at[kind, j], [mine.at[kind, j], far.at[kind, j]], rows)
+
+                to_up(kind, j).start()
+
+            @pl.when(z - d >= 0)
+            def _():
+                j = z - d
+                fetch(kind, j).wait()
+                to_other(kind, j).wait_recv()
+                add_into(mine.at[kind, j], [mine.at[kind, j], side.at[kind, j]], rows)
+
+                @pl.when(z < line - 1)
+                def _():
+                    to_down(kind, j).wait_recv()
+                    add_into(mine.at[kind, j], [mine.at[kind, j], near.at[kind, j]], rows)
+
+                to_down(kind, j).start()
+
+    back = []
+    for kind in range(2):
+        fetch(kind, z).wait()
+        to_other(kind, z).wait_recv()
+
+        @pl.when(z > 0)
+        def _():
+            to_up(kind, z).wait_recv()
+
+        @pl.when(z < line - 1)
+        def _():
+            to_down(kind, z).wait_recv()
+
+        total = done.at[kind]
+
+        @pl.when((z > 0) & (z < line - 1))
+        def _():
+            add_into(
+                total,
+                [mine.at[kind, z], side.at[kind, z], far.at[kind, z], near.at[kind, z]],
+                rows,
+            )
+
+        @pl.when(z == 0)
+        def _():
+            add_into(total, [mine.at[kind, z], side.at[kind, z], near.at[kind, z]], rows)
+
+        @pl.when(z == line - 1)
+        def _():
+            add_into(total, [mine.at[kind, z], side.at[kind, z], far.at[kind, z]], rows)
+
+        size = rows // experts
+        keep = pltpu.make_async_copy(
+            done.at[kind, pl.ds(pl.multiple_of(e * size, size), size)], outs[kind].at[e], local.at[kind]
+        )
+        keep.start()
+        for shift in range(1, experts):
+            peer = lax.rem(e + shift, experts)
+            copy = remote(
+                done.at[kind, pl.ds(pl.multiple_of(peer * size, size), size)],
+                outs[kind].at[e],
+                send.at[kind, BACK + shift],
+                recv.at[kind, BACK + shift],
+                {"expert": peer},
+            )
+            copy.start()
+            back.append(copy)
+        back.append(keep)
+    for copy in back:
+        copy.wait()
+    for kind in range(2):
+        for j in range(line):
+            to_other(kind, j).wait_send()
+
+            @pl.when(j > z)
+            def _():
+                to_up(kind, j).wait_send()
+
+            @pl.when(j < z)
+            def _():
+                to_down(kind, j).wait_send()
+
+
+def ff_reduce(first, second, line, pairs, experts, number):
+    cols = first.shape[1]
+    rows = first.shape[0] // (line * pairs)
+    shape = (line, pairs, rows, cols)
+    out = jax.ShapeDtypeStruct((experts, rows // experts, cols), first.dtype)
+    uses = 3 * line + experts
+    block = lambda: pltpu.VMEM((2, line, rows, cols), first.dtype)
+    return pl.pallas_call(
+        partial(ff_reduce_kernel, line),
+        in_specs=[ANY, ANY],
+        out_specs=[ANY, ANY],
+        out_shape=[out, out],
+        scratch_shapes=[
+            block(),
+            block(),
+            block(),
+            block(),
+            pltpu.VMEM((2, rows, cols), first.dtype),
+            DMA((2, uses)),
+            DMA((2, uses)),
+            DMA((2, line)),
+            DMA((2,)),
+        ],
+        compiler_params=params(number, 56 * 2**20),
+        cost_estimate=pl.CostEstimate(
+            flops=0, bytes_accessed=40 * first.size, transcendentals=0
+        ),
+        name="ff_reduce",
+    )(first.reshape(shape), second.reshape(shape))
+
+
+def pair_swap_kernel(a_ref, b_ref, a_out, b_out, send, recv, local):
+    p = lax.axis_index("pair")
+    other = {"pair": 1 - p}
+    greet([other])
+    copies = []
+    for slot, (src, dst) in enumerate(((a_ref.at[1 - p], a_out.at[p]), (b_ref, b_out.at[p]))):
+        copy = remote(src, dst, send.at[slot], recv.at[slot], other)
+        copy.start()
+        copies.append(copy)
+    for slot, (src, dst) in enumerate(((a_ref.at[p], a_out.at[p]), (b_ref, b_out.at[p]))):
+        copy = pltpu.make_async_copy(src, dst, local.at[slot])
+        copy.start()
+        copies.append(copy)
+    for copy in copies:
+        copy.wait()
+
+
+def pair_swap(value, shared, number):
+    return pl.pallas_call(
+        pair_swap_kernel,
+        in_specs=[VMEM, VMEM],
+        out_specs=[VMEM, VMEM],
+        out_shape=[
+            jax.ShapeDtypeStruct(value.shape, value.dtype),
+            jax.ShapeDtypeStruct((2,) + shared.shape, shared.dtype),
+        ],
+        scratch_shapes=[DMA((2,)), DMA((2,)), DMA((2,))],
+        compiler_params=params(number),
+        cost_estimate=pl.CostEstimate(
+            flops=0, bytes_accessed=20 * value.size, transcendentals=0
+        ),
+        name="pair_swap",
+    )(value, shared)
+
+
+def start_kernel(
+    sizes, walk, tok_ref, small_ref, kv_ref, tok_out, small_out, kv_out, send, recv, peer_send, peer_recv, local
+):
+    line, pairs, experts = sizes
+    z = lax.axis_index("line")
+    p = lax.axis_index("pair") if pairs == 2 else 0
+    e = lax.axis_index("expert")
+    c, y = lax.rem(e, 2), lax.div(e, 2)
+    core = {"expert": e + 1 - 2 * c}
+    side = {"expert": e + 2 - 4 * y}
+    other = {"pair": lax.rem(p + 1, pairs)}
+    count = line * pairs * experts
+    trees = pairs * experts
+    local_me = p * experts + e
+    me = z * trees + local_me
+    barrier = pltpu.get_barrier_semaphore()
+
+    def greet_one(offset, carry):
+        target = place_of((me + offset) % count, sizes)
+        pl.semaphore_signal(barrier, inc=1, device_id=target, device_id_type=MESH)
+        return carry
+
+    lax.fori_loop(1, count, greet_one, 0)
+    pl.semaphore_wait(barrier, count - 1)
+
+    size = kv_ref.shape[1]
+    home = kv_out.at[z if walk else 0, pl.ds(pl.multiple_of(local_me * size, size), size)]
+    keeps = [
+        pltpu.make_async_copy(kv_ref.at[local_me], home, local.at[0]),
+        pltpu.make_async_copy(tok_ref, tok_out.at[p, y, c], local.at[1]),
+        pltpu.make_async_copy(small_ref, small_out.at[me], local.at[2]),
+    ]
+    for copy in keeps:
+        copy.start()
+    KV = 7
+    pieces = []
+    for shift in range(1, trees):
+        peer = lax.rem(local_me + shift, trees)
+        copy = remote(
+            kv_ref.at[peer],
+            home,
+            send.at[KV + shift],
+            recv.at[KV + shift],
+            {"pair": peer // experts, "expert": peer % experts},
+        )
+        copy.start()
+        pieces.append(copy)
+
+    q, w = lax.rem(p + 1, pairs), 1 - y
+    own = tok_out.at[p, y, c]
+    copies = []
+
+    def push(slot, source, place, target):
+        copy = remote(source, place, send.at[slot], recv.at[slot], target)
+        copy.start()
+        copies.append(copy)
+        return copy
+
+    to_side = push(0, tok_ref, own, side)
+    to_other = push(1, tok_ref, own, other) if pairs == 2 else None
+    waits = [push(2, tok_ref, own, core)]
+
+    def small_to(offset):
+        return remote(
+            small_ref,
+            small_out.at[me],
+            peer_send.at[offset],
+            peer_recv.at[offset],
+            place_of((me + offset) % count, sizes),
+        )
+
+    def small_start(offset, carry):
+        small_to(offset).start()
+        return carry
+
+    lax.fori_loop(1, count, small_start, 0)
+
+    base = KV + trees
+    keeps[0].wait()
+    for copy in pieces:
+        copy.wait_recv()
+
+    def to_up(j, d):
+        ref = kv_out.at[j]
+        return remote(ref, ref, send.at[base + d], recv.at[base + d], {"line": z + 1})
+
+    def to_down(j, d):
+        ref = kv_out.at[j]
+        return remote(ref, ref, send.at[base + line + d], recv.at[base + line + d], {"line": z - 1})
+
+    if walk:
+
+        @pl.when(z < line - 1)
+        def _():
+            to_up(z, 1).start()
+
+        @pl.when(z > 0)
+        def _():
+            to_down(z, 1).start()
+
+    if pairs == 2:
+        to_other.wait_recv()
+        block = tok_out.at[q, y, c]
+        far = push(3, block, block, side)
+        waits.append(push(4, block, block, core))
+    to_side.wait_recv()
+    block = tok_out.at[p, w, c]
+    waits.append(push(5, block, block, core))
+    if pairs == 2:
+        far.wait_recv()
+        block = tok_out.at[q, w, c]
+        waits.append(push(6, block, block, core))
+
+    if walk:
+        for d in range(1, line):
+
+            @pl.when(z - d >= 0)
+            def _():
+                to_up(z - d, d).wait_recv()
+
+                @pl.when(z < line - 1)
+                def _():
+                    to_up(z - d, d + 1).start()
+
+            @pl.when(z + d < line)
+            def _():
+                to_down(z + d, d).wait_recv()
+
+                @pl.when(z > 0)
+                def _():
+                    to_down(z + d, d + 1).start()
+
+        for d in range(1, line):
+
+            @pl.when((z - d + 1 >= 0) & (z < line - 1))
+            def _():
+                to_up(z - d + 1, d).wait_send()
+
+            @pl.when((z + d - 1 < line) & (z > 0))
+            def _():
+                to_down(z + d - 1, d).wait_send()
+
+    for copy in waits:
+        copy.wait_recv()
+    for copy in copies + pieces:
+        copy.wait_send()
+    for copy in keeps[1:]:
+        copy.wait()
+
+    def small_finish(offset, carry):
+        small_to(offset).wait()
+        return carry
+
+    lax.fori_loop(1, count, small_finish, 0)
+
+
+def start_exchange(tokens, small, kv, sizes, number):
+    line, pairs, experts = sizes
+    trees, rows, cols = kv.shape
+    walk = line <= 4
+    count = line * trees
+    uses = 7 + trees + 2 * line + 2
+    return pl.pallas_call(
+        partial(start_kernel, sizes, walk),
+        in_specs=[VMEM, VMEM, VMEM],
+        out_specs=[VMEM, VMEM, VMEM],
+        out_shape=[
+            jax.ShapeDtypeStruct((pairs, 2, 2) + tokens.shape, tokens.dtype),
+            jax.ShapeDtypeStruct((count,) + small.shape, small.dtype),
+            jax.ShapeDtypeStruct((line if walk else 1, trees * rows, cols), kv.dtype),
+        ],
+        scratch_shapes=[DMA((uses,)), DMA((uses,)), DMA((count,)), DMA((count,)), DMA((3,))],
+        compiler_params=params(number, 32 * 2**20),
+        cost_estimate=pl.CostEstimate(
+            flops=0, bytes_accessed=100 * kv.size, transcendentals=0
+        ),
+        name="start_exchange",
+    )(tokens, small, kv)
 
 
 def gather(value, axes, axis=0):
@@ -260,43 +1087,51 @@
     angle = depth.astype(F32)[:, None] * rates[None, :]
     cosine, sine = jnp.cos(angle), jnp.sin(angle)
 
+    sizes = (line, pair, experts)
+    walk = line <= 4 and pair == 2
+    query_mine = w_query[0].reshape(own_in, line, pair, part)
+    query_mine = jnp.transpose(query_mine, (2, 0, 1, 3)).reshape(pair, own_in, feats)
+    integers = jnp.concatenate([attn_route[:, 0].reshape(micro, -1), parents[:, 0]], axis=1)
+    if pair == 2:
+        flat = integers.reshape(-1)
+        flat = jnp.pad(flat, (0, -flat.shape[0] % 1024)).reshape(-1, 128)
+        query_mine, flat = pair_swap(query_mine, flat, 1)
+        integers = flat.reshape(pair, -1)[:, : integers.size].reshape((pair,) + integers.shape)
+    else:
+        integers = integers[None]
+    query_weight = gather(query_mine.reshape(pair * own_in, feats), "line")
+
     small = jnp.concatenate(
         [gain_attn[None], gain_mlp[None], router_attn.T, router_mlp.T], axis=0
     )
-    small = jnp.transpose(lax.all_gather(small, ALL, axis=0), (1, 0, 2)).reshape(-1, width)
+    kv_mine = jnp.stack([w_key, w_value], axis=1).reshape(
+        own_kv, 2, experts, line // experts, pair, part
+    )
+    kv_mine = jnp.transpose(kv_mine, (4, 2, 0, 1, 3, 5)).reshape(
+        pair * experts, own_kv, 2 * piece
+    )
+    own_tokens = tokens.reshape(micro * tok, width)
+    tree_tokens, small, kv_weight = start_exchange(own_tokens, small, kv_mine, sizes, 2)
+    kv_weight = kv_weight.reshape(-1, 2 * piece)
+    if kv_weight.shape[0] < width:
+        kv_weight = gather(kv_weight, "line")
+    out_mine, small = lax.optimization_barrier((w_out[0], small))
+    out_weight = gather(out_mine, "line")
+
+    small = jnp.transpose(small, (1, 0, 2)).reshape(-1, width)
     first_gain = small[0].astype(F32)
     second_gain = small[1].astype(F32)
     first_router = small[2 : 2 + experts]
     second_router = small[2 + experts : 2 + 2 * experts]
 
-    residual = tokens.reshape(micro * tok, width).astype(F32)
-    normed, first_pull = jax.vjp(rms_scaled, residual, first_gain)
-    normed = normed.astype(BF16)
-    tree_input = gather(normed, TREES)
-
-    integers = jnp.concatenate(
-        [attn_route[:, 0].reshape(micro, -1), parents[:, 0]], axis=1
-    )
-    integers = lax.all_gather(integers, "pair", axis=0)
+    residual = own_tokens.astype(F32)
+    _, first_pull = jax.vjp(rms_scaled, residual, first_gain)
+    tree_input = rms_scaled(tree_tokens.reshape(rows, width).astype(F32), first_gain).astype(BF16)
+
     routes = integers[..., : tree * 2].reshape(pair, micro, experts, tok, 2)
     routes = jnp.transpose(routes, (0, 2, 1, 3, 4)).reshape(rows, 2)
     family = integers[..., tree * 2 :]
     bias = jax.vmap(jax.vmap(lambda parent: score_bias(parent, segment, places)))(family)
-
-    kv_mine = jnp.stack([w_key, w_value], axis=1).reshape(own_kv, 2, line, pair, part)
-    kv_mine = jnp.transpose(kv_mine, (3, 2, 0, 1, 4)).reshape(
-        pair, experts, line // experts, own_kv, 2, part
-    )
-    kv_mine = jnp.transpose(kv_mine, (0, 1, 3, 4, 2, 5)).reshape(
-        pair * experts, own_kv, 2, piece
-    )
-    kv_mine = swap(kv_mine, TREES).reshape(pair * experts * own_kv, 2 * piece)
-    kv_weight = gather(kv_mine, "line")
-    query_weight = w_query[0].reshape(own_in, line, pair, part)
-    query_weight = jnp.transpose(query_weight, (2, 0, 1, 3)).reshape(pair, own_in, feats)
-    query_weight = swap(query_weight, "pair").reshape(pair * own_in, feats)
-    query_weight = gather(query_weight, "line")
-    out_weight = gather(w_out[0], "line")
 
     kv_raw = product(tree_input, kv_weight)
     spread_cos = jnp.broadcast_to(
@@ -314,8 +1149,8 @@
         ],
         axis=-1,
     ).reshape(rows, piece)
-    kv = jnp.stack([keys.astype(BF16), kv_raw[:, piece:].astype(BF16)])
-    kv = lax.all_gather(kv, "expert", axis=0)
+    kv = jnp.concatenate([keys.astype(BF16), kv_raw[:, piece:].astype(BF16)], axis=0)
+    kv = cube_gather(kv, 1, 3)
     shape = (pair, experts, micro, tok, feats)
     kv = kv.reshape(experts, 2, pair, experts, micro, tok, piece)
 
@@ -329,7 +1164,8 @@
     queries, heads_out = attend(raw.reshape(shape), kv, cosine, sine, bias, scale)
     heads_flat = heads_out.reshape(rows, feats)
     projected = product(heads_flat, out_weight)
-    attention = scatter((own_gate[:, None] * projected).astype(BF16), TREES).astype(F32)
+    gated = (own_gate[:, None] * projected).astype(BF16)
+    attention = cube_reduce(gated.reshape(pair * experts, micro * tok, width), pair, 4).astype(F32)
 
     middle = residual + attention
     second_normed, second_pull = jax.vjp(rms_scaled, middle, second_gain)
@@ -351,23 +1187,37 @@
     )
     slot_grad = (slot_gates[..., None] * slot_values).astype(BF16)
     slots = experts * micro * capacity
-    arrived = gather(swap(outgoing.astype(BF16), "expert").reshape(slots, width), DP)
-    result_grad = gather(swap(slot_grad, "expert").reshape(slots, width), DP)
+    outgoing = outgoing.astype(BF16).reshape(experts, micro * capacity, width)
+    slot_grad = slot_grad.reshape(experts, micro * capacity, width)
+    if walk:
+        arrived, result_grad = ff_gather(outgoing, slot_grad, line, pair, 5)
+        arrived = arrived.reshape(-1, width)
+        result_grad = result_grad.reshape(-1, width)
+    else:
+        arrived = gather(swap(outgoing, "expert").reshape(slots, width), DP)
+        result_grad = gather(swap(slot_grad, "expert").reshape(slots, width), DP)
 
     gate_weight, up_weight, down_weight = w_gate[0], w_up[0], w_down[0]
     gate_pre = product_nt(arrived, gate_weight)
     up_pre = product_nt(arrived, up_weight)
     sigma = jax.nn.sigmoid(gate_pre)
     inner = (gate_pre * sigma * up_pre).astype(BF16)
-    returned = scatter(product(inner, down_weight).astype(BF16), DP)
-    returned = swap(returned.reshape(experts, micro, capacity, width), "expert")
+    returned = product(inner, down_weight).astype(BF16)
     inner_grad = product_nt(result_grad, down_weight)
     gate_grad = (inner_grad * up_pre * sigma * (1.0 + gate_pre * (1.0 - sigma))).astype(BF16)
     up_grad = (inner_grad * gate_pre * sigma).astype(BF16)
-    came_back = scatter(
-        (product(gate_grad, gate_weight) + product(up_grad, up_weight)).astype(BF16), DP
-    )
-    came_back = swap(came_back.reshape(experts, micro, capacity, width), "expert")
+    came_back = (product(gate_grad, gate_weight) + product(up_grad, up_weight)).astype(BF16)
+    if walk:
+        returned, came_back = ff_reduce(returned, came_back, line, pair, experts, 6)
+    else:
+        back = (experts, micro * capacity, width)
+        returned = swap(scatter(returned, DP).reshape(back), "expert")
+        came_back = swap(scatter(came_back, DP).reshape(back), "expert")
+    gate_grad, up_grad, inner, arrived, result_grad, returned, came_back = lax.optimization_barrier(
+        (gate_grad, up_grad, inner, arrived, result_grad, returned, came_back)
+    )
+    returned = returned.reshape(experts, micro, capacity, width)
+    came_back = came_back.reshape(experts, micro, capacity, width)
     grad_gate = product_tn(gate_grad, arrived)[None]
     grad_upward = product_tn(up_grad, arrived)[None]
     grad_downward = product_tn(inner, result_grad)[None]
@@ -393,20 +1243,20 @@
     middle_grad, grad_gain_second = second_pull(hn_grad)
     middle_grad = middle_grad + dz
 
-    mix_grad = gather(middle_grad.astype(BF16), TREES).astype(F32)
+    mix_grad = cube_gather(middle_grad.astype(BF16), pair, 7).reshape(rows, width).astype(F32)
     own_gate_grad = jnp.sum(mix_grad * projected, axis=-1)
     projected_grad = (own_gate[:, None] * mix_grad).astype(BF16)
     heads_grad = product_nt(projected_grad, out_weight).astype(BF16).reshape(shape)
     grad_output = scatter(product_tn(heads_flat, projected_grad).astype(BF16), "line")
     query_pre, kv_pre = attend_back(queries, kv, heads_grad, cosine, sine, bias, scale)
     query_pre = query_pre.reshape(rows, feats)
-    kv_sum = scatter(kv_pre.reshape(experts * 2, rows, piece), "expert")
+    kv_sum = cube_reduce(kv_pre.reshape(experts, 2 * rows, piece), 1, 8)
     grad_query = scatter(product_tn(tree_input, query_pre).astype(BF16), "line")
     grad_query = swap(grad_query.reshape(own_in * pair, line, part)[None], "pair", 1, 0)
     grad_query = jnp.transpose(grad_query, (1, 2, 0, 3)).reshape(1, own_in, heads_total)
 
     (first_logit_grad,) = first_gate_pull(own_gate_grad[:, None] * column[None, :])
-    key_pre, value_pre = kv_sum[0], kv_sum[1]
+    key_pre, value_pre = kv_sum[:rows], kv_sum[rows:]
     input_term = (
         product_nt(query_pre, query_weight)
         + product_nt(key_pre, kv_weight[:, :piece])
@@ -415,7 +1265,8 @@
     first_router_wide = first_router.astype(F32)
     for expert in range(experts):
         input_term = input_term + first_logit_grad[:, expert : expert + 1] * first_router_wide[expert]
-    normed_grad = scatter(input_term.astype(BF16), TREES).astype(F32)
+    input_term = input_term.astype(BF16).reshape(pair * experts, micro * tok, width)
+    normed_grad = cube_reduce(input_term, pair, 9).astype(F32)
     grad_kv = jnp.stack(
         [product_tn(tree_input, key_pre), product_tn(tree_input, value_pre)], axis=1
     )
@@ -438,7 +1289,7 @@
         axis=0,
     )
     sums = jnp.transpose(sums.reshape(sums.shape[0], -1, own_kv), (1, 0, 2))
-    sums = scatter(sums, ALL)[0]
+    sums = small_exchange(sums, sizes, True, 10)
     return (
         layer_out.reshape(micro, 1, tok, width),
         tokens_grad.reshape(micro, 1, tok, width),

time: 1530 us -> 1110 us (0.73)
  waiting for transfers between devices: 1030 us -> 57.4 us
  Pallas kernels: 45.7 us -> 716 us
  blocking collectives: 120 us -> 0 us
    pallas_call x0 -> x10, Pallas kernels: none -> 670 us  [the longest x1 200 us: ff_reduce(): pl.pallas_call(partial(ff_reduce_kernel, line), in_specs=[ANY, ANY], out_...]
    reduce_scatter x9 -> x3, waiting for transfers between devices: 629 us -> 50.3 us  [scatter(): return lax.psum_scatter(value, axes, scatter_dimension=axis, tiled=True)]
    all_gather x7 -> x2, waiting for transfers between devices: 367 us -> 0.02 us  [gather(): return lax.all_gather(value, axes, axis=axis, tiled=True)]
    all_to_all x4 -> x0, blocking collectives: 72.3 us -> none  [swap(): lax.all_to_all(value, axes, split_axis=split, concat_axis=concat, tiled=T...]
    all_gather x2 -> x0, blocking collectives: 47.3 us -> none  [the longest x1 42.4 us: body(): lax.all_gather(small, ALL, axis=0)]
    all_gather x1 -> x0, waiting for transfers between devices: 24.9 us -> none  [body(): kv = lax.all_gather(kv, 'expert', axis=0)]
  transfers between devices with their start and end apart: 21 -> 7, of which waited for: 17 -> 2; matrix products, arithmetic and copies ran while one was open for 14% -> 15% of each run, Pallas kernels for 1% -> 18%
where the time goes in v2:
time: 1110 us; the launch traced here: 1100 us
  Pallas kernels  716 us (65%)
  matrix products  179 us (16%)
  local copies, waits for them, and re-layouts  78.4 us (7%)
  waiting for transfers between devices  57.4 us (5%)
  other arithmetic  48.5 us (4%)
  between operations  15.2 us (1%)
    pallas_call x1, Pallas kernels, ff_reduce(): pl.pallas_call(partial(ff_reduce_kernel, line), in_specs=[ANY, ANY], out_...  200 us
    pallas_call x1, Pallas kernels, ff_gather(): pl.pallas_call(partial(ff_gather_kernel, line), in_specs=[VMEM, VMEM], ou...  191 us
    pallas_call x1, Pallas kernels, start_exchange(): pl.pallas_call(partial(start_kernel, sizes, walk), in_specs=[VMEM, VMEM,...  106 us
    pallas_call x3, Pallas kernels, cube_reduce(): pl.pallas_call(partial(cube_reduce_kernel, pairs), in_specs=[VMEM], out_s...  88.6 us
    pallas_call x2, Pallas kernels, cube_gather(): pl.pallas_call(partial(cube_gather_kernel, pairs), in_specs=[VMEM], out_s...  57.5 us
    dot_general x6, matrix products, product(): return jnp.dot(left, right, preferred_element_type=F32)  57.3 us
    dot_general x9, matrix products, product_nt(): lax.dot_general(left, right, (((1,), (1,)), ((), ())), preferred_element_...  56.5 us
    reduce_scatter x3, waiting for transfers between devices, scatter(): return lax.psum_scatter(value, axes, scatter_dimension=axis, tiled=True)  50.3 us
  transfers between devices with their start and end apart: 7, of which 2 were waited for; matrix products, arithmetic and copies ran while one was open for 15% of the time, Pallas kernels for 18%

profile of v2, /device:TPU:0, one launch (start us, length us, event | category | flops | bytes accessed | tf_op | source)
XLA Modules:
  0.0 1103.0 jit_solution(6204086976821149567)
XLA Ops:
  7.3 2.8 reshape_squeeze.6
  10.0 2.6 copy.179
  17.9 17.3 %pair_swap.1 = (bf16[2,256,1024]{2,1,0:T(8,128)(2,1)}, s32[2,16,128]{2,1,0:T(8,128)}) custom-call(bf16[2,256,1024]{2,1,0:T(8,128)(2,1)} %reshape.707.a_ref, s32[16,128]{1,0:T(8,128)} %pad_bitcast_fusion.b_ref), custom_call_target="tpu_custom_call" | custom-call | bytes 10485760 | tf_op jit(solution)/shard_map/pair_swap/pallas_call | solution.py:835
  42.5 3.1 maximum_bitcast_fusion
  48.9 105.8 %start_exchange.1 = (bf16[2,2,2,128,2048]{4,3,2,1,0:T(8,128)(2,1)S(1)}, bf16[32,10,64]{2,1,0:T(8,128)(2,1)S(1)}, bf16[4,512,512]{2,1,0:T(8,128)(2,1)S(1)}) custom-call(bf16[128,2048]{1,0:T(8,128)(2,1)S(1)} %bitcast.281, bf16[10,64]{1,0:T(8,128)(2,1)S(1)} %pad_maximum_fusion.3.small_ref, bf16[8,64,512]{2,1,0:T(8,128)(2,1)S(1)} %copy-done.12), custom_call_target="tpu_custom_call" | custom-call | bytes 26214400 | tf_op jit(solution)/shard_map/start_exchange/pallas_call | solution.py:1014
  160.2 3.2 multiply_reduce_fusion
  170.8 2.7 copy.161
  183.8 3.5 fusion.98
  191.1 27.6 %cube_gather.2 = bf16[1,2,2,2048,256]{4,3,2,1,0:T(8,128)(2,1)S(1)} custom-call(bf16[2048,256]{1,0:T(8,128)(2,1)S(1)} %copy-done.11), custom_call_target="tpu_custom_call" | custom-call | bytes 41943040 | tf_op jit(solution)/shard_map/cube_gather/pallas_call | solution.py:363
  234.7 5.2 fusion.1
  239.9 10.0 fusion.5.raw_ref
  249.9 20.1 %attend.1 = (bf16[2,4,2,64,1024]{4,3,2,1,0:T(8,128)(2,1)}, bf16[2,4,2,64,1024]{4,3,2,1,0:T(8,128)(2,1)}) custom-call(f32[2,4,2,64,1024]{4,3,2,1,0:T(8,128)} %fusion.5.raw_ref, bf16[4,2,2,4,2,64,256]{6,5,4,3,2,1,0:T(8,128)(2,1)} %bitcast.282, f32[256,64]{1,0:T(8,128)} %get-tuple-element.172.cos_ref, f32[256,64]{1,0:T(8,128)} %get-tuple-element.171.sin_ref, ...), custom_call_target="tpu_custom_call" | custom-call | flops 1073741824 | bytes 12582912 | tf_op jit(solution)/shard_map/attend/pallas_call | solution.py:169
  270.1 10.5 multiply_convert_fusion
  280.6 30.1 %cube_reduce.3 = bf16[128,2048]{1,0:T(8,128)(2,1)S(1)} custom-call(bf16[2,2,2,128,2048]{4,3,2,1,0:T(8,128)(2,1)S(1)} %bitcast.286), custom_call_target="tpu_custom_call" | custom-call | flops 2097152 | bytes 50331648 | tf_op jit(solution)/shard_map/cube_reduce/pallas_call | solution.py:297
  315.4 190.9 %ff_gather.1 = (bf16[4,2,256,2048]{3,2,1,0:T(8,128)(2,1)}, bf16[4,2,256,2048]{3,2,1,0:T(8,128)(2,1)}) custom-call(bf16[4,64,2048]{2,1,0:T(8,128)(2,1)S(1)} %bitcast.288, bf16[4,64,2048]{2,1,0:T(8,128)(2,1)S(1)} %bitcast.287), custom_call_target="tpu_custom_call" | custom-call | bytes 209715200 | tf_op jit(solution)/shard_map/ff_gather/pallas_call | solution.py:604
  506.3 10.3 fusion.11
  516.6 8.0 fusion.17
  524.6 13.3 %multiply_convert_fusion.3 = (bf16[2048,704]{0,1:T(8,128)(2,1)}, bf16[2048,704]{0,1:T(8,128)(2,1)}, bf16[2048,704]{0,1:T(8,128)(2,1)}) fusion(f32[2048,704]{0,1:T(8,128)} %fusion.11, f32[2048,704]{0,1:T(8,128)} %fusion.17, bf16[2048,2048]{1,0:T(8,128)(2,1)S(1)} %bitcast.367, bf16[1,704,2048]{2,1,0:T(8,128)(2,1)S(1)} %copy-done), kind=kOutput, calls=%fused_computation.16 | convolution fusion | flops 5928648704 | bytes 31457280 | tf_op jit(solution)/shard_map/dot_general | solution.py:28
  537.9 12.7 %fusion.9 = f32[2048,2048]{1,0:T(8,128)} fusion(bf16[2048,704]{0,1:T(8,128)(2,1)} %get-tuple-element.52, bf16[1,704,2048]{2,1,0:T(8,128)(2,1)S(1)} %copy-done.55), kind=kOutput, calls=%fused_computation.31 | convolution fusion | flops 5905580032 | bytes 22544384 | tf_op jit(solution)/shard_map/dot_general | solution.py:20
  550.6 9.1 convolution_convert_fusion
  559.7 12.5 %add_convert_fusion = bf16[2048,2048]{1,0:T(8,128)(2,1)} fusion(f32[2048,2048]{1,0:T(8,128)} %fusion.9, bf16[2048,704]{0,1:T(8,128)(2,1)S(1)} %copy-done.60, bf16[1,704,2048]{2,1,0:T(8,128)(2,1)S(1)} %copy-done), kind=kOutput, calls=%fused_computation | convolution fusion | flops 5913968640 | bytes 30932992 | tf_op jit(solution)/shard_map/dot_general | solution.py:20
  572.2 199.6 %ff_reduce.1 = (bf16[4,64,2048]{2,1,0:T(8,128)(2,1)}, bf16[4,64,2048]{2,1,0:T(8,128)(2,1)}) custom-call(bf16[4,2,256,2048]{3,2,1,0:T(8,128)(2,1)} %bitcast.301, bf16[4,2,256,2048]{3,2,1,0:T(8,128)(2,1)} %bitcast.302), custom_call_target="tpu_custom_call" | custom-call | bytes 167772160 | tf_op jit(solution)/shard_map/ff_reduce/pallas_call | solution.py:793
  771.9 3.4 multiply_reduce_fusion.1
  779.7 29.9 %cube_gather.3 = bf16[2,2,2,128,2048]{4,3,2,1,0:T(8,128)(2,1)S(1)} custom-call(bf16[128,2048]{1,0:T(8,128)(2,1)S(1)} %get-tuple-element.143.x_ref), custom_call_target="tpu_custom_call" | custom-call | bytes 20971520 | tf_op jit(solution)/shard_map/cube_gather/pallas_call | solution.py:363
  809.6 5.9 fusion.4
  815.8 5.8 convolution_convert_fusion.6
  821.5 25.7 %attend_back.1 = (bf16[2,4,2,64,1024]{4,3,2,1,0:T(8,128)(2,1)}, bf16[4,2,2,4,2,64,256]{6,5,4,3,2,1,0:T(8,128)(2,1)}) custom-call(bf16[2,4,2,64,1024]{4,3,2,1,0:T(8,128)(2,1)} %get-tuple-element.48.query_ref, bf16[4,2,2,4,2,64,256]{6,5,4,3,2,1,0:T(8,128)(2,1)} %bitcast.283, bf16[2,4,2,64,1024]{4,3,2,1,0:T(8,128)(2,1)} %bitcast.374, ...), custom_call_target="tpu_custom_call" | custom-call | flops 2684354560 | bytes 14680064 | tf_op jit(solution)/shard_map/attend_back/pallas_call | solution.py:187
  849.4 28.6 %cube_reduce.4 = bf16[2048,256]{1,0:T(8,128)(2,1)S(1)} custom-call(bf16[1,2,2,2048,256]{4,3,2,1,0:T(8,128)(2,1)S(1)} %bitcast.284), custom_call_target="tpu_custom_call" | custom-call | flops 2097152 | bytes 50331648 | tf_op jit(solution)/shard_map/cube_reduce/pallas_call | solution.py:297
  882.4 9.4 convolution_convert_fusion.2
  892.3 6.4 copy.150
  899.4 2.7 fusion.30
  902.6 6.8 fusion.101
  909.4 6.0 add_convert_fusion.1
  915.4 29.9 %cube_reduce.5 = bf16[128,2048]{1,0:T(8,128)(2,1)S(1)} custom-call(bf16[2,2,2,128,2048]{4,3,2,1,0:T(8,128)(2,1)S(1)} %bitcast.285), custom_call_target="tpu_custom_call" | custom-call | flops 2097152 | bytes 50331648 | tf_op jit(solution)/shard_map/cube_reduce/pallas_call | solution.py:297
  947.0 6.2 convolution_convert_fusion.1
  958.0 6.7 fusion.57
  965.5 10.6 small_reduce.1
  978.8 11.4 %convolution_bitcast_fusion.1 = f32[1,704,2048]{2,1,0:T(8,128)} fusion(bf16[2048,704]{0,1:T(8,128)(2,1)} %get-tuple-element.54, bf16[2048,2048]{1,0:T(8,128)(2,1)} %bitcast.363), kind=kOutput, calls=%fused_computation.29 | convolution fusion | flops 5905580032 | bytes 17039360 | tf_op jit(solution)/shard_map/dot_general | solution.py:24
  990.1 10.2 convolution_bitcast_fusion.2
  1000.4 7.9 convolution_bitcast_fusion
  1010.1 4.2 all-to-all-start.1
  1016.4 6.9 all-to-all-done.1
  1027.2 2.7 broadcast_in_dim_reshape.4
  1029.9 3.8 all-to-all-start
  1033.7 50.3 %reduce-scatter.6.cloned.1.call-done = bf16[256,2048]{1,0:T(8,128)(2,1)} async-done(((bf16[1024,2048]{1,0:T(8,128)(2,1)}), bf16[256,2048]{1,0:T(8,128)(2,1)}) %reduce-scatter.6.cloned.1.call-update) | async-done | bytes 1048592 | tf_op jit(solution)/shard_map/reduce_scatter | solution.py:1037
  1084.0 2.8 bitcast_convert_fusion
  1089.4 2.9 copy.147
  1092.3 3.9 reshape.741
  (284 shorter events, 96.0 us)
Async XLA Ops:
  7.2 517.4 %copy-start = (bf16[1,704,2048]{2,1,0:T(8,128)(2,1)S(1)}, bf16[1,704,2048]{2,1,0:T(8,128)(2,1)}, u32[]{:S(2)}) copy-start(bf16[1,704,2048]{2,1,0:T(8,128)(2,1)} %param.27) | copy-start | bytes 8650756
  7.2 8.0 copy-start.44
  7.2 10.0 copy-start.47
  7.2 232.7 %all-gather.3.cloned.1.call-start = ((), (), s32[]{:S(2)}) async-start(), calls=%async_computation.5 | async-start | bytes 5242880 | tf_op jit(solution)/shard_map/all_gather | solution.py:1033
  15.2 32.6 %copy-start.48 = (bf16[64,4]{0,1:T(4,128)(2,1)S(1)}, bf16[64,4]{0,1:T(4,128)(2,1)}, u32[]{:S(2)}) copy-start(bf16[64,4]{0,1:T(4,128)(2,1)} %param.25) | copy-start | bytes 1540
  15.2 32.6 %copy-start.49 = (bf16[64,4]{0,1:T(4,128)(2,1)S(1)}, bf16[64,4]{0,1:T(4,128)(2,1)}, u32[]{:S(2)}) copy-start(bf16[64,4]{0,1:T(4,128)(2,1)} %param.23) | copy-start | bytes 1540
  15.2 32.6 %copy-start.50 = (bf16[64]{0:T(256)(128)(2,1)S(1)}, bf16[64]{0:T(256)(128)(2,1)}, u32[]{:S(2)}) copy-start(bf16[64]{0:T(256)(128)(2,1)} %param.24) | copy-start | bytes 388
  15.2 32.6 %copy-start.51 = (bf16[64]{0:T(256)(128)(2,1)S(1)}, bf16[64]{0:T(256)(128)(2,1)}, u32[]{:S(2)}) copy-start(bf16[64]{0:T(256)(128)(2,1)} %param.22) | copy-start | bytes 388
  15.2 32.6 %copy-start.6 = (bf16[2,1,64,2048]{3,2,1,0:T(8,128)(2,1)S(1)}, bf16[2,1,64,2048]{3,2,1,0:T(8,128)(2,1)}, u32[]{:S(2)}) copy-start(bf16[2,1,64,2048]{3,2,1,0:T(8,128)(2,1)} %param.17) | copy-start | bytes 1572868
  35.3 234.8 %all-gather.5.cloned.1.call-start = ((), (), s32[]{:S(2)}) async-start(), calls=%async_computation.6 | async-start | bytes 5242880 | tf_op jit(solution)/shard_map/all_gather | solution.py:1033
  158.1 850.2 %reduce-scatter.8.cloned.1.call-start = ((), (), s32[]{:S(2)}) async-start(), calls=%async_computation.9 | async-start | bytes 2621440 | tf_op jit(solution)/shard_map/reduce_scatter | solution.py:1037
  160.2 79.7 %copy-start.32 = (f32[2048]{0:T(1024)}, f32[2048]{0:T(1024)S(1)}, u32[]{:S(2)}) copy-start(f32[2048]{0:T(1024)S(1)} %reshape.736) | copy-start | bytes 24580
  176.9 6.8 copy-start.37
  183.8 35.0 %copy-start.30 = (bf16[4,2048]{1,0:T(4,128)(2,1)}, bf16[4,2048]{1,0:T(4,128)(2,1)S(1)}, u32[]{:S(2)}) copy-start(bf16[4,2048]{1,0:T(4,128)(2,1)S(1)} %slice.124) | copy-start | bytes 49156
  187.3 36.8 %copy-start.42 = (f32[32,64]{1,0:T(8,128)S(1)}, f32[32,64]{1,0:T(8,128)}, u32[]{:S(2)}) copy-start(f32[32,64]{1,0:T(8,128)} %get-tuple-element.128) | copy-start | bytes 24580
  187.3 36.9 %copy-start.36 = (bf16[4,32,64]{2,0,1:T(4,128)(2,1)S(1)}, bf16[4,32,64]{2,0,1:T(4,128)(2,1)}, u32[]{:S(2)}) copy-start(bf16[4,32,64]{2,0,1:T(4,128)(2,1)} %get-tuple-element.147) | copy-start | bytes 49156
  224.1 15.8 %copy-start.34 = (s32[1024,2]{0,1:T(2,128)}, s32[1024,2]{0,1:T(2,128)S(1)}, u32[]{:S(2)}) copy-start(s32[1024,2]{0,1:T(2,128)S(1)} %eq.146) | copy-start | bytes 24580
  225.1 14.8 %copy-start.28 = (f32[1024,2]{0,1:T(2,128)}, f32[1024,2]{0,1:T(2,128)S(1)}, u32[]{:S(2)}) copy-start(f32[1024,2]{0,1:T(2,128)S(1)} %select_reduce_fusion.5) | copy-start | bytes 24580
  314.8 191.5 %copy-start.55 = (bf16[1,704,2048]{2,1,0:T(8,128)(2,1)S(1)}, bf16[1,704,2048]{2,1,0:T(8,128)(2,1)}, u32[]{:S(2)}) copy-start(bf16[1,704,2048]{2,1,0:T(8,128)(2,1)} %param.26) | copy-start | bytes 8650756
  506.2 10.3 copy-start.52
  506.3 10.3 copy-start.56
  506.3 18.3 %slice-start.2 = ((s8[8388608]{0:T(1024)(128)(4,1)}), s8[4194304]{0:T(1024)(128)(4,1)S(1)}, s32[]{:S(2)}) async-start(s8[8388608]{0:T(1024)(128)(4,1)} %bitcast.365), calls=%async_computation.12 | async-start | bytes 8388608
  516.6 8.0 slice-start.3
  537.9 12.7 %copy-start.61 = (bf16[2048,704]{0,1:T(8,128)(2,1)S(1)}, bf16[2048,704]{0,1:T(8,128)(2,1)}, u32[]{:S(2)}) copy-start(bf16[2048,704]{0,1:T(8,128)(2,1)} %get-tuple-element.55) | copy-start | bytes 8650756
  550.6 9.1 copy-start.60
  572.2 199.7 %copy-start.27 = (f32[2,64,2048]{2,1,0:T(8,128)S(1)}, f32[2,64,2048]{2,1,0:T(8,128)}, u32[]{:S(2)}) copy-start(f32[2,64,2048]{2,1,0:T(8,128)} %bitcast_convert_fusion.1) | copy-start | bytes 3145732
  771.8 6.1 copy-start.18
  809.6 5.9 copy-start.4
  809.6 6.2 copy-start.54
  849.4 28.7 %copy-start.17 = (bf16[1024,2048]{1,0:T(8,128)(2,1)S(1)}, bf16[1024,2048]{1,0:T(8,128)(2,1)}, u32[]{:S(2)}) copy-start(bf16[1024,2048]{1,0:T(8,128)(2,1)} %fusion.1) | copy-start | bytes 12582916
  882.3 144.9 %reduce-scatter.4.cloned.1.call-start = ((), (), s32[]{:S(2)}) async-start(), calls=%async_computation.7 | async-start | bytes 5242880 | tf_op jit(solution)/shard_map/reduce_scatter | solution.py:1037
  891.8 192.2 %reduce-scatter.6.cloned.1.call-start = ((), (), s32[]{:S(2)}) async-start(), calls=%async_computation.8 | async-start | bytes 5242880 | tf_op jit(solution)/shard_map/reduce_scatter | solution.py:1037
  892.3 6.8 copy-start.41
  892.3 6.8 copy-start.31
  892.3 6.8 copy-start.46
  892.3 6.9 copy-start.35
  892.3 6.9 copy-start.29
  892.3 6.9 copy-start.39
  902.6 6.8 copy-start.15
  915.4 29.9 %copy-start.5 = (bf16[2,2,2,128,2048]{4,3,2,1,0:T(8,128)(2,1)S(1)}, bf16[2,2,2,128,2048]{4,3,2,1,0:T(8,128)(2,1)}, u32[]{:S(2)}) copy-start(bf16[2,2,2,128,2048]{4,3,2,1,0:T(8,128)(2,1)} %copy-done.4) | copy-start | bytes 12582916
  978.8 11.4 %copy-start.59 = (bf16[2048,704]{0,1:T(8,128)(2,1)S(1)}, bf16[2048,704]{0,1:T(8,128)(2,1)}, u32[]{:S(2)}) copy-start(bf16[2048,704]{0,1:T(8,128)(2,1)} %get-tuple-element.52) | copy-start | bytes 8650756
  978.8 21.6 %slice-start = ((s8[8388608]{0:T(1024)(128)(4,1)}), s8[4194304]{0:T(1024)(128)(4,1)S(1)}, s32[]{:S(2)}) async-start(s8[8388608]{0:T(1024)(128)(4,1)} %bitcast.359), calls=%async_computation.10 | async-start | bytes 8388608
  990.1 10.2 slice-start.1
  990.1 10.2 copy-start.62
  1000.4 13.9 %copy-start.19 = (bf16[2,1,64,2048]{3,2,1,0:T(8,128)(2,1)S(1)}, bf16[2,1,64,2048]{3,2,1,0:T(8,128)(2,1)}, u32[]{:S(2)}) copy-start(bf16[2,1,64,2048]{3,2,1,0:T(8,128)(2,1)} %param.33) | copy-start | bytes 1572868
  1010.1 13.2 %all-to-all-start.1 = ((bf16[8,64,2,256]{3,1,2,0:T(8,128)(2,1)}), bf16[8,64,2,256]{3,1,2,0:T(8,128)(2,1)}, u32[]{:S(2)}, u32[]{:S(2)}) async-start(bf16[8,64,2,256]{3,1,2,0:T(8,128)(2,1)} %copy.148), calls=%async_computation.4 | async-start | bytes 1048576 | tf_op jit(solution)/shard_map/all_to_all | solution.py:1041
  1029.9 56.9 %all-to-all-start = ((bf16[1,512,4,256]{3,2,0,1:T(4,128)(2,1)}), bf16[1,512,4,256]{3,2,0,1:T(4,128)(2,1)S(1)}, u32[]{:S(2)}, u32[]{:S(2)}) async-start(bf16[1,512,4,256]{3,2,0,1:T(4,128)(2,1)} %bitcast.80), calls=%async_computation.1 | async-start | bytes 2097152 | tf_op jit(solution)/shard_map/all_to_all | solution.py:1041
  1087.7 8.5 copy-start.1
  (26 other events, 56.0 us)
Sparse Core Ops, SparseCore 0:
  35.4 107.1 all-gather.2
  158.2 79.1 all-gather.4
  882.4 41.0 reduce-scatter.7
  925.8 78.7 reduce-scatter.3
  1006.7 77.2 reduce-scatter.5

commit v3 on v2

--- a/solution.py
+++ b/solution.py
@@ -444,376 +444,6 @@
     )(value)
 
 
-def ff_gather_kernel(line, a_in, b_in, a_hbm, b_hbm, a_out, b_out, send, recv, local, store):
-    z, p, e = lax.axis_index("line"), lax.axis_index("pair"), lax.axis_index("expert")
-    experts = a_in.shape[0]
-    q = 1 - p
-    up, down, other = {"line": z + 1}, {"line": z - 1}, {"pair": q}
-    twin = z + 1 - 2 * lax.rem(z, 2)
-    barrier = pltpu.get_barrier_semaphore()
-    for shift in range(1, experts):
-        pl.semaphore_signal(
-            barrier, inc=1, device_id={"expert": lax.rem(e + shift, experts)}, device_id_type=MESH
-        )
-    pl.semaphore_signal(barrier, inc=1, device_id=other, device_id_type=MESH)
-
-    @pl.when(z > 0)
-    def _():
-        pl.semaphore_signal(barrier, inc=1, device_id=down, device_id_type=MESH)
-
-    @pl.when(z < line - 1)
-    def _():
-        pl.semaphore_signal(barrier, inc=1, device_id=up, device_id_type=MESH)
-
-    below, above = (z + line - 1) // line, (2 * line - 2 - z) // line
-    pl.semaphore_wait(barrier, experts + below + above)
-
-    pairs = ((a_in, a_out), (b_in, b_out))
-    UP, DOWN, SIDE = 3, 3 + line, 3 + 2 * line
-    EXTRA = SIDE + line
-    starts = []
-    for kind, (src, dst) in enumerate(pairs):
-        size = src.shape[1]
-        home = dst.at[z, p, pl.ds(pl.multiple_of(e * size, size), size)]
-        keep = pltpu.make_async_copy(src.at[e], home, local.at[kind])
-        keep.start()
-        group = []
-        for shift in range(1, experts):
-            peer = lax.rem(e + shift, experts)
-            copy = remote(
-                src.at[peer],
-                home,
-                send.at[kind, shift - 1],
-                recv.at[kind, shift - 1],
-                {"expert": peer},
-            )
-            copy.start()
-            group.append(copy)
-        starts.append((keep, group))
-
-    def to_up(kind, j, d):
-        ref = pairs[kind][1].at[j, p]
-        return remote(ref, ref, send.at[kind, UP + d], recv.at[kind, UP + d], up)
-
-    def to_down(kind, j, d):
-        ref = pairs[kind][1].at[j, p]
-        return remote(ref, ref, send.at[kind, DOWN + d], recv.at[kind, DOWN + d], down)
-
-    def to_other(kind, j):
-        ref = pairs[kind][1].at[j, p]
-        return remote(ref, ref, send.at[kind, SIDE + j], recv.at[kind, SIDE + j], other)
-
-    def to_twin(kind):
-        ref = pairs[kind][1].at[z, q]
-        return remote(ref, ref, send.at[kind, EXTRA], recv.at[kind, EXTRA], {"line": twin})
-
-    for kind in range(2):
-        keep, group = starts[kind]
-        keep.wait()
-        for copy in group:
-            copy.wait_recv()
-
-        @pl.when(z < line - 1)
-        def _():
-            to_up(kind, z, 1).start()
-
-        @pl.when(z > 0)
-        def _():
-            to_down(kind, z, 1).start()
-
-        to_other(kind, z).start()
-
-    for d in range(1, line):
-        for kind in range(2):
-
-            @pl.when(z - d >= 0)
-            def _():
-                to_up(kind, z - d, d).wait_recv()
-
-                @pl.when(z < line - 1)
-                def _():
-                    to_up(kind, z - d, d + 1).start()
-
-                if kind == 0:
-                    to_other(kind, z - d).start()
-                else:
-
-                    @pl.when(z - d != twin)
-                    def _():
-                        to_other(kind, z - d).start()
-
-            @pl.when(z + d < line)
-            def _():
-                to_down(kind, z + d, d).wait_recv()
-
-                @pl.when(z > 0)
-                def _():
-                    to_down(kind, z + d, d + 1).start()
-
-                if kind == 0:
-                    to_other(kind, z + d).start()
-                else:
-
-                    @pl.when(z + d != twin)
-                    def _():
-                        to_other(kind, z + d).start()
-
-        if d == 1:
-            to_other(1, z).wait_recv()
-            to_twin(1).start()
-
-    for j in range(line):
-        to_other(0, j).wait_recv()
-
-        @pl.when((j != twin) & (j != z))
-        def _():
-            to_other(1, j).wait_recv()
-
-        to_other(0, j).wait_send()
-
-        @pl.when(j != twin)
-        def _():
-            to_other(1, j).wait_send()
-
-    to_twin(1).wait()
-    saves = []
-    for kind, target in enumerate((a_hbm, b_hbm)):
-        save = pltpu.make_async_copy(pairs[kind][1], target, store.at[kind])
-        save.start()
-        saves.append(save)
-    for save in saves:
-        save.wait()
-    for kind in range(2):
-        for copy in starts[kind][1]:
-            copy.wait_send()
-        for d in range(1, line):
-
-            @pl.when((z - d + 1 >= 0) & (z < line - 1))
-            def _():
-                to_up(kind, z - d + 1, d).wait_send()
-
-            @pl.when((z + d - 1 < line) & (z > 0))
-            def _():
-                to_down(kind, z + d - 1, d).wait_send()
-
-
-def ff_gather(first, second, line, pairs, number):
-    uses = 3 + 3 * line + 1
-    experts, rows, cols = first.shape
-    out = jax.ShapeDtypeStruct((line, pairs, experts * rows, cols), first.dtype)
-    return pl.pallas_call(
-        partial(ff_gather_kernel, line),
-        in_specs=[VMEM, VMEM],
-        out_specs=[ANY, ANY],
-        out_shape=[out, out],
-        scratch_shapes=[
-            pltpu.VMEM(out.shape, out.dtype),
-            pltpu.VMEM(out.shape, out.dtype),
-            DMA((2, uses)),
-            DMA((2, uses)),
-            DMA((2,)),
-            DMA((2,)),
-        ],
-        compiler_params=params(number, 48 * 2**20),
-        cost_estimate=pl.CostEstimate(
-            flops=0, bytes_accessed=100 * first.size * line, transcendentals=0
-        ),
-        name="ff_gather",
-    )(first, second)
-
-
-def ff_reduce_kernel(
-    line, a_in, b_in, a_out, b_out, mine, side, far, near, done, send, recv, load, local
-):
-    z, p, e = lax.axis_index("line"), lax.axis_index("pair"), lax.axis_index("expert")
-    experts = a_out.shape[0]
-    q = 1 - p
-    up, down, other = {"line": z + 1}, {"line": z - 1}, {"pair": q}
-    barrier = pltpu.get_barrier_semaphore()
-    for shift in range(1, experts):
-        pl.semaphore_signal(
-            barrier, inc=1, device_id={"expert": lax.rem(e + shift, experts)}, device_id_type=MESH
-        )
-    pl.semaphore_signal(barrier, inc=1, device_id=other, device_id_type=MESH)
-
-    @pl.when(z > 0)
-    def _():
-        pl.semaphore_signal(barrier, inc=1, device_id=down, device_id_type=MESH)
-
-    @pl.when(z < line - 1)
-    def _():
-        pl.semaphore_signal(barrier, inc=1, device_id=up, device_id_type=MESH)
-
-    below, above = (z + line - 1) // line, (2 * line - 2 - z) // line
-    pl.semaphore_wait(barrier, experts + below + above)
-
-    kinds = (a_in, b_in)
-    outs = (a_out, b_out)
-    UP, DOWN, SIDE, BACK = 0, line, 2 * line, 3 * line
-    rows = mine.shape[2]
-
-    def to_other(kind, j):
-        return remote(
-            kinds[kind].at[j, q],
-            side.at[kind, j],
-            send.at[kind, SIDE + j],
-            recv.at[kind, SIDE + j],
-            other,
-        )
-
-    def fetch(kind, j):
-        return pltpu.make_async_copy(kinds[kind].at[j, p], mine.at[kind, j], load.at[kind, j])
-
-    def to_up(kind, j):
-        return remote(
-            mine.at[kind, j], far.at[kind, j], send.at[kind, UP + j], recv.at[kind, UP + j], up
-        )
-
-    def to_down(kind, j, dst=None):
-        return remote(
-            mine.at[kind, j], near.at[kind, j], send.at[kind, DOWN + j], recv.at[kind, DOWN + j], down
-        )
-
-    for d in range(line - 1, -1, -1):
-        for kind in range(2):
-
-            @pl.when(z + d < line)
-            def _():
-                to_other(kind, z + d).start()
-                fetch(kind, z + d).start()
-
-            if d > 0:
-
-                @pl.when(z - d >= 0)
-                def _():
-                    to_other(kind, z - d).start()
-                    fetch(kind, z - d).start()
-
-    for d in range(line - 1, 0, -1):
-        for kind in range(2):
-
-            @pl.when(z + d < line)
-            def _():
-                j = z + d
-                fetch(kind, j).wait()
-                to_other(kind, j).wait_recv()
-                add_into(mine.at[kind, j], [mine.at[kind, j], side.at[kind, j]], rows)
-
-                @pl.when(z > 0)
-                def _():
-                    to_up(kind, j).wait_recv()
-                    add_into(mine.at[kind, j], [mine.at[kind, j], far.at[kind, j]], rows)
-
-                to_up(kind, j).start()
-
-            @pl.when(z - d >= 0)
-            def _():
-                j = z - d
-                fetch(kind, j).wait()
-                to_other(kind, j).wait_recv()
-                add_into(mine.at[kind, j], [mine.at[kind, j], side.at[kind, j]], rows)
-
-                @pl.when(z < line - 1)
-                def _():
-                    to_down(kind, j).wait_recv()
-                    add_into(mine.at[kind, j], [mine.at[kind, j], near.at[kind, j]], rows)
-
-                to_down(kind, j).start()
-
-    back = []
-    for kind in range(2):
-        fetch(kind, z).wait()
-        to_other(kind, z).wait_recv()
-
-        @pl.when(z > 0)
-        def _():
-            to_up(kind, z).wait_recv()
-
-        @pl.when(z < line - 1)
-        def _():
-            to_down(kind, z).wait_recv()
-
-        total = done.at[kind]
-
-        @pl.when((z > 0) & (z < line - 1))
-        def _():
-            add_into(
-                total,
-                [mine.at[kind, z], side.at[kind, z], far.at[kind, z], near.at[kind, z]],
-                rows,
-            )
-
-        @pl.when(z == 0)
-        def _():
-            add_into(total, [mine.at[kind, z], side.at[kind, z], near.at[kind, z]], rows)
-
-        @pl.when(z == line - 1)
-        def _():
-            add_into(total, [mine.at[kind, z], side.at[kind, z], far.at[kind, z]], rows)
-
-        size = rows // experts
-        keep = pltpu.make_async_copy(
-            done.at[kind, pl.ds(pl.multiple_of(e * size, size), size)], outs[kind].at[e], local.at[kind]
-        )
-        keep.start()
-        for shift in range(1, experts):
-            peer = lax.rem(e + shift, experts)
-            copy = remote(
-                done.at[kind, pl.ds(pl.multiple_of(peer * size, size), size)],
-                outs[kind].at[e],
-                send.at[kind, BACK + shift],
-                recv.at[kind, BACK + shift],
-                {"expert": peer},
-            )
-            copy.start()
-            back.append(copy)
-        back.append(keep)
-    for copy in back:
-        copy.wait()
-    for kind in range(2):
-        for j in range(line):
-            to_other(kind, j).wait_send()
-
-            @pl.when(j > z)
-            def _():
-                to_up(kind, j).wait_send()
-
-            @pl.when(j < z)
-            def _():
-                to_down(kind, j).wait_send()
-
-
-def ff_reduce(first, second, line, pairs, experts, number):
-    cols = first.shape[1]
-    rows = first.shape[0] // (line * pairs)
-    shape = (line, pairs, rows, cols)
-    out = jax.ShapeDtypeStruct((experts, rows // experts, cols), first.dtype)
-    uses = 3 * line + experts
-    block = lambda: pltpu.VMEM((2, line, rows, cols), first.dtype)
-    return pl.pallas_call(
-        partial(ff_reduce_kernel, line),
-        in_specs=[ANY, ANY],
-        out_specs=[ANY, ANY],
-        out_shape=[out, out],
-        scratch_shapes=[
-            block(),
-            block(),
-            block(),
-            block(),
-            pltpu.VMEM((2, rows, cols), first.dtype),
-            DMA((2, uses)),
-            DMA((2, uses)),
-            DMA((2, line)),
-            DMA((2,)),
-        ],
-        compiler_params=params(number, 56 * 2**20),
-        cost_estimate=pl.CostEstimate(
-            flops=0, bytes_accessed=40 * first.size, transcendentals=0
-        ),
-        name="ff_reduce",
-    )(first.reshape(shape), second.reshape(shape))
-
-
 def pair_swap_kernel(a_ref, b_ref, a_out, b_out, send, recv, local):
     p = lax.axis_index("pair")
     other = {"pair": 1 - p}
@@ -1027,6 +657,429 @@
         ),
         name="start_exchange",
     )(tokens, small, kv)
+
+
+def ff_kernel(
+    a_in, b_in, gate_hbm, up_hbm, down_hbm,
+    a_out, b_out, a_save, b_save, inner_save, dgate_save, dup_save,
+    a_buf, b_buf, side, hop, extra, w_gate, w_up, w_down, mid, acc,
+    send, recv, load, store, local,
+):
+    z, p, e = lax.axis_index("line"), lax.axis_index("pair"), lax.axis_index("expert")
+    line, _, rows, width = a_buf.shape
+    experts, size = a_in.shape[0], a_in.shape[1]
+    q = 1 - p
+    twin = z + 1 - 2 * (z % 2)
+    up, down, other, across = {"line": z + 1}, {"line": z - 1}, {"pair": q}, {"line": twin}
+    ins, bufs, outs, saves = (a_in, b_in), (a_buf, b_buf), (a_out, b_out), (a_save, b_save)
+    high = z // 2
+    near = z + high * (line - 1 - 2 * z)
+
+    def order(t):
+        j = t + near * (1 - t // 2) * (1 - 2 * t)
+        return j + high * (line - 1 - 2 * j)
+
+    weights = [
+        pltpu.make_async_copy(src, dst, load.at[i])
+        for i, (src, dst) in enumerate(((gate_hbm, w_gate), (up_hbm, w_up), (down_hbm, w_down)))
+    ]
+    for copy in weights:
+        copy.start()
+
+    barrier = pltpu.get_barrier_semaphore()
+    for shift in range(1, experts):
+        pl.semaphore_signal(
+            barrier, inc=1, device_id={"expert": (e + shift) % experts}, device_id_type=MESH
+        )
+    pl.semaphore_signal(barrier, inc=1, device_id=other, device_id_type=MESH)
+
+    @pl.when(z > 0)
+    def _():
+        pl.semaphore_signal(barrier, inc=1, device_id=down, device_id_type=MESH)
+
+    @pl.when(z < line - 1)
+    def _():
+        pl.semaphore_signal(barrier, inc=1, device_id=up, device_id_type=MESH)
+
+    below, above = (z + line - 1) // line, (2 * line - 2 - z) // line
+    pl.semaphore_wait(barrier, experts + below + above)
+
+    UP, DOWN, SIDE, SUMUP, SUMDOWN, SUMSIDE = (i * line for i in range(6))
+    TWIN, SUMTWIN, SWAP = 6 * line, 6 * line + 1, 6 * line + 2
+    BACK = SWAP + experts
+
+    def push(src, dst, kind, use, target):
+        return remote(src, dst, send.at[kind, use], recv.at[kind, use], target)
+
+    def to_up(kind, j):
+        return push(bufs[kind].at[j, p], bufs[kind].at[j, p], kind, UP + j, up)
+
+    def to_down(kind, j):
+        return push(bufs[kind].at[j, p], bufs[kind].at[j, p], kind, DOWN + j, down)
+
+    def to_other(kind, j):
+        return push(bufs[kind].at[j, p], bufs[kind].at[j, p], kind, SIDE + j, other)
+
+    def to_twin():
+        return push(bufs[1].at[z, q], bufs[1].at[z, q], 1, TWIN, across)
+
+    def sum_up(kind, j):
+        return push(bufs[kind].at[j, p], hop.at[kind, j], kind, SUMUP + j, up)
+
+    def sum_down(kind, j, slot):
+        return push(bufs[kind].at[j, p], hop.at[kind, slot], kind, SUMDOWN + j, down)
+
+    def sum_other(kind, j):
+        return push(bufs[kind].at[j, q], side.at[kind, j], kind, SUMSIDE + j, other)
+
+    def sum_twin():
+        return push(bufs[1].at[twin, q], extra, 1, SUMTWIN, across)
+
+    def piece(index):
+        return pl.ds(pl.multiple_of(index * size, size), size)
+
+    def save(kind, j, column):
+        return pltpu.make_async_copy(
+            bufs[kind].at[j, column], saves[kind].at[j, column], store.at[kind, j, column]
+        )
+
+    swaps = []
+    for kind in range(2):
+        home = bufs[kind].at[z, p, piece(e)]
+        keep = pltpu.make_async_copy(ins[kind].at[e], home, local.at[kind])
+        keep.start()
+        group = []
+        for shift in range(1, experts):
+            peer = (e + shift) % experts
+            copy = push(ins[kind].at[peer], home, kind, SWAP + shift, {"expert": peer})
+            copy.start()
+            group.append(copy)
+        swaps.append((keep, group))
+
+    def spread(t, first=False):
+        j = order(t)
+        for kind in range(2):
+            if first:
+                swaps[kind][0].wait()
+                for copy in swaps[kind][1]:
+                    copy.wait_recv()
+            else:
+
+                @pl.when(j < z)
+                def _():
+                    to_up(kind, j).wait_recv()
+
+                @pl.when(j > z)
+                def _():
+                    to_down(kind, j).wait_recv()
+
+            @pl.when((j <= z) & (z < line - 1))
+            def _():
+                to_up(kind, j).start()
+
+            @pl.when((j >= z) & (z > 0))
+            def _():
+                to_down(kind, j).start()
+
+            if kind == 0:
+                to_other(kind, j).start()
+            else:
+
+                @pl.when(j != twin)
+                def _():
+                    to_other(kind, j).start()
+
+            save(kind, j, p).start()
+
+    chunk = 512
+    steps = width // chunk
+
+    def first_half(j, column):
+        for index in range(3):
+            acc[index] = jnp.zeros(acc.shape[1:], F32)
+
+        def one(k, carry):
+            where = pl.ds(pl.multiple_of(k * chunk, chunk), chunk)
+            left = a_buf[j, column, :, where]
+            acc[0] += product_nt(left, w_gate[:, where])
+            acc[1] += product_nt(left, w_up[:, where])
+            acc[2] += product_nt(b_buf[j, column, :, where], w_down[:, where])
+            return carry
+
+        lax.fori_loop(0, steps, one, 0)
+        part = 32
+
+        def two(i, carry):
+            where = pl.ds(pl.multiple_of(i * part, part), part)
+            gate, lift, grad = acc[0, where], acc[1, where], acc[2, where]
+            sigma = jax.nn.sigmoid(gate)
+            mid[j, column, 0, where] = (gate * sigma * lift).astype(BF16)
+            mid[j, column, 1, where] = (
+                grad * lift * sigma * (1.0 + gate * (1.0 - sigma))
+            ).astype(BF16)
+            mid[j, column, 2, where] = (grad * gate * sigma).astype(BF16)
+            return carry
+
+        lax.fori_loop(0, rows // part, two, 0)
+
+    def second_half(j, column):
+        def one(k, carry):
+            where = pl.ds(pl.multiple_of(k * chunk, chunk), chunk)
+            a_buf[j, column, :, where] = product(mid[j, column, 0], w_down[:, where]).astype(BF16)
+            b_buf[j, column, :, where] = (
+                product(mid[j, column, 1], w_gate[:, where])
+                + product(mid[j, column, 2], w_up[:, where])
+            ).astype(BF16)
+            return carry
+
+        lax.fori_loop(0, steps, one, 0)
+
+    def arrive(j):
+        for kind in range(2):
+            if kind == 0:
+                to_other(kind, j).wait_recv()
+            else:
+
+                @pl.when(j != twin)
+                def _():
+                    to_other(kind, j).wait_recv()
+
+                @pl.when(j == twin)
+                def _():
+                    to_twin().wait_recv()
+
+            save(kind, j, q).start()
+
+        @pl.when(j == z)
+        def _():
+            to_twin().start()
+
+    def step(s, carry):
+        @pl.when(s == 0)
+        def _():
+            spread(0, True)
+            for copy in weights:
+                copy.wait()
+
+        @pl.when(s == 1)
+        def _():
+            spread(1)
+            spread(2)
+
+        @pl.when(s == 3)
+        def _():
+            spread(3)
+
+        def half(c, inner_carry):
+            t = s - c
+            column = p + c * (q - p)
+
+            @pl.when((t >= 0) & (t < line))
+            def _():
+                j = order(t)
+
+                @pl.when(c == 1)
+                def _():
+                    arrive(j)
+
+                first_half(j, column)
+
+                @pl.when(c == 1)
+                def _():
+                    @pl.when(j == z)
+                    def _():
+                        to_twin().wait_send()
+
+                    for kind in range(2):
+                        save(kind, j, q).wait()
+                    second_half(j, column)
+
+            return inner_carry
+
+        return lax.fori_loop(0, 2, half, carry)
+
+    lax.fori_loop(0, line + 1, step, 0)
+
+    sum_twin().start()
+
+    def emit(t, carry):
+        j = order(line - 1 - t)
+        sum_other(0, j).start()
+
+        @pl.when((j != twin) & (j != z))
+        def _():
+            sum_other(1, j).start()
+
+        return carry
+
+    lax.fori_loop(0, line, emit, 0)
+
+    for copy in (
+        pltpu.make_async_copy(mid.at[:, :, 0], inner_save, local.at[2]),
+        pltpu.make_async_copy(mid.at[:, :, 1], dgate_save, local.at[3]),
+        pltpu.make_async_copy(mid.at[:, :, 2], dup_save, local.at[4]),
+    ):
+        copy.start()
+    sum_twin().wait_recv()
+    add_into(b_buf.at[z, q], [b_buf.at[z, q], extra], rows)
+    sum_other(1, z).start()
+
+    def fold(s, carry):
+        t = line - 1 - s
+        j = order(t)
+        for kind in range(2):
+            save(kind, j, p).wait()
+
+            @pl.when((j <= z) & (z < line - 1))
+            def _():
+                to_up(kind, j).wait_send()
+
+            @pl.when((j >= z) & (z > 0))
+            def _():
+                to_down(kind, j).wait_send()
+
+            if kind == 0:
+                to_other(kind, j).wait_send()
+            else:
+
+                @pl.when(j != twin)
+                def _():
+                    to_other(kind, j).wait_send()
+
+        second_half(j, p)
+        for kind in range(2):
+            mine = bufs[kind].at[j, p]
+            if kind == 0:
+                sum_other(kind, j).wait_recv()
+                add_into(mine, [mine, side.at[kind, j]], rows)
+            else:
+
+                @pl.when(j != twin)
+                def _():
+                    sum_other(kind, j).wait_recv()
+                    add_into(mine, [mine, side.at[kind, j]], rows)
+
+            @pl.when((j >= z) & (z > 0))
+            def _():
+                sum_up(kind, j).wait_recv()
+                add_into(mine, [mine, hop.at[kind, j]], rows)
+
+            @pl.when((j < z) & (z < line - 1))
+            def _():
+                sum_down(kind, j, j).wait_recv()
+                add_into(mine, [mine, hop.at[kind, j]], rows)
+
+            @pl.when((j == z) & (z < line - 1))
+            def _():
+                sum_down(kind, j, line).wait_recv()
+                add_into(mine, [mine, hop.at[kind, line]], rows)
+
+            @pl.when(j > z)
+            def _():
+                sum_up(kind, j).start()
+
+            @pl.when((j < z) & (j != z - 1))
+            def _():
+                sum_down(kind, j, j).start()
+
+            @pl.when((j < z) & (j == z - 1))
+            def _():
+                sum_down(kind, j, line).start()
+
+        return carry
+
+    lax.fori_loop(0, line, fold, 0)
+
+    back = []
+    for kind in range(2):
+        keep = pltpu.make_async_copy(
+            bufs[kind].at[z, p, piece(e)], outs[kind].at[e], local.at[kind]
+        )
+        keep.start()
+        back.append(keep)
+        for shift in range(1, experts):
+            peer = (e + shift) % experts
+            copy = push(
+                bufs[kind].at[z, p, piece(peer)], outs[kind].at[e], kind, BACK + shift, {"expert": peer}
+            )
+            copy.start()
+            back.append(copy)
+    for copy in back:
+        copy.wait()
+
+    def drain(j, carry):
+        for kind in range(2):
+            if kind == 0:
+                sum_other(kind, j).wait_send()
+            else:
+
+                @pl.when(j != twin)
+                def _():
+                    sum_other(kind, j).wait_send()
+
+            @pl.when(j > z)
+            def _():
+                sum_up(kind, j).wait_send()
+
+            @pl.when(j < z)
+            def _():
+                sum_down(kind, j, j).wait_send()
+
+        return carry
+
+    lax.fori_loop(0, line, drain, 0)
+    sum_twin().wait_send()
+    for copy in (
+        pltpu.make_async_copy(mid.at[:, :, 0], inner_save, local.at[2]),
+        pltpu.make_async_copy(mid.at[:, :, 1], dgate_save, local.at[3]),
+        pltpu.make_async_copy(mid.at[:, :, 2], dup_save, local.at[4]),
+    ):
+        copy.wait()
+    for keep, group in swaps:
+        for copy in group:
+            copy.wait_send()
+
+
+def feed_forward(first, second, w_gate, w_up, w_down, line, pairs, number):
+    experts, size, width = first.shape
+    hidden = w_gate.shape[0]
+    rows = experts * size
+    blocks = (line, pairs, rows)
+    back = jax.ShapeDtypeStruct(first.shape, BF16)
+    wide = jax.ShapeDtypeStruct(blocks + (width,), BF16)
+    thin = jax.ShapeDtypeStruct(blocks + (hidden,), BF16)
+    uses = 6 * line + 2 + 2 * experts
+    total = line * pairs * rows
+    return pl.pallas_call(
+        ff_kernel,
+        in_specs=[ANY] * 5,
+        out_specs=[ANY] * 7,
+        out_shape=[back, back, wide, wide, thin, thin, thin],
+        scratch_shapes=[
+            pltpu.VMEM(blocks + (width,), BF16),
+            pltpu.VMEM(blocks + (width,), BF16),
+            pltpu.VMEM((2, line, rows, width), BF16),
+            pltpu.VMEM((2, line + 1, rows, width), BF16),
+            pltpu.VMEM((rows, width), BF16),
+            pltpu.VMEM((hidden, width), BF16),
+            pltpu.VMEM((hidden, width), BF16),
+            pltpu.VMEM((hidden, width), BF16),
+            pltpu.VMEM((line, pairs, 3, rows, hidden), BF16),
+            pltpu.VMEM((3, rows, hidden), F32),
+            DMA((2, uses)),
+            DMA((2, uses)),
+            DMA((3,)),
+            DMA((2, line, pairs)),
+            DMA((5,)),
+        ],
+        compiler_params=params(number, 63 * 2**20),
+        cost_estimate=pl.CostEstimate(
+            flops=12 * total * hidden * width,
+            bytes_accessed=12 * total * width,
+            transcendentals=total * hidden,
+        ),
+        name="feed_forward",
+    )(first, second, w_gate, w_up, w_down)
 
 
 def gather(value, axes, axis=0):
@@ -1189,33 +1242,30 @@
     slots = experts * micro * capacity
     outgoing = outgoing.astype(BF16).reshape(experts, micro * capacity, width)
     slot_grad = slot_grad.reshape(experts, micro * capacity, width)
+    gate_weight, up_weight, down_weight = w_gate[0], w_up[0], w_down[0]
     if walk:
-        arrived, result_grad = ff_gather(outgoing, slot_grad, line, pair, 5)
-        arrived = arrived.reshape(-1, width)
-        result_grad = result_grad.reshape(-1, width)
+        returned, came_back, arrived, result_grad, inner, gate_grad, up_grad = feed_forward(
+            outgoing, slot_grad, gate_weight, up_weight, down_weight, line, pair, 5
+        )
+        arrived, result_grad, inner, gate_grad, up_grad = (
+            value.reshape(-1, value.shape[-1])
+            for value in (arrived, result_grad, inner, gate_grad, up_grad)
+        )
     else:
         arrived = gather(swap(outgoing, "expert").reshape(slots, width), DP)
         result_grad = gather(swap(slot_grad, "expert").reshape(slots, width), DP)
-
-    gate_weight, up_weight, down_weight = w_gate[0], w_up[0], w_down[0]
-    gate_pre = product_nt(arrived, gate_weight)
-    up_pre = product_nt(arrived, up_weight)
-    sigma = jax.nn.sigmoid(gate_pre)
-    inner = (gate_pre * sigma * up_pre).astype(BF16)
-    returned = product(inner, down_weight).astype(BF16)
-    inner_grad = product_nt(result_grad, down_weight)
-    gate_grad = (inner_grad * up_pre * sigma * (1.0 + gate_pre * (1.0 - sigma))).astype(BF16)
-    up_grad = (inner_grad * gate_pre * sigma).astype(BF16)
-    came_back = (product(gate_grad, gate_weight) + product(up_grad, up_weight)).astype(BF16)
-    if walk:
-        returned, came_back = ff_reduce(returned, came_back, line, pair, experts, 6)
-    else:
+        gate_pre = product_nt(arrived, gate_weight)
+        up_pre = product_nt(arrived, up_weight)
+        sigma = jax.nn.sigmoid(gate_pre)
+        inner = (gate_pre * sigma * up_pre).astype(BF16)
+        returned = product(inner, down_weight).astype(BF16)
+        inner_grad = product_nt(result_grad, down_weight)
+        gate_grad = (inner_grad * up_pre * sigma * (1.0 + gate_pre * (1.0 - sigma))).astype(BF16)
+        up_grad = (inner_grad * gate_pre * sigma).astype(BF16)
+        came_back = (product(gate_grad, gate_weight) + product(up_grad, up_weight)).astype(BF16)
         back = (experts, micro * capacity, width)
         returned = swap(scatter(returned, DP).reshape(back), "expert")
         came_back = swap(scatter(came_back, DP).reshape(back), "expert")
-    gate_grad, up_grad, inner, arrived, result_grad, returned, came_back = lax.optimization_barrier(
-        (gate_grad, up_grad, inner, arrived, result_grad, returned, came_back)
-    )
     returned = returned.reshape(experts, micro, capacity, width)
     came_back = came_back.reshape(experts, micro, capacity, width)
     grad_gate = product_tn(gate_grad, arrived)[None]
@@ -1246,17 +1296,23 @@
     mix_grad = cube_gather(middle_grad.astype(BF16), pair, 7).reshape(rows, width).astype(F32)
     own_gate_grad = jnp.sum(mix_grad * projected, axis=-1)
     projected_grad = (own_gate[:, None] * mix_grad).astype(BF16)
+    grad_output = product_tn(heads_flat, projected_grad).astype(BF16)
+    grad_output, projected_grad = lax.optimization_barrier((grad_output, projected_grad))
+    grad_output = scatter(grad_output, "line")
     heads_grad = product_nt(projected_grad, out_weight).astype(BF16).reshape(shape)
-    grad_output = scatter(product_tn(heads_flat, projected_grad).astype(BF16), "line")
     query_pre, kv_pre = attend_back(queries, kv, heads_grad, cosine, sine, bias, scale)
     query_pre = query_pre.reshape(rows, feats)
+    grad_query = product_tn(tree_input, query_pre).astype(BF16)
+    grad_query, kv_pre = lax.optimization_barrier((grad_query, kv_pre))
     kv_sum = cube_reduce(kv_pre.reshape(experts, 2 * rows, piece), 1, 8)
-    grad_query = scatter(product_tn(tree_input, query_pre).astype(BF16), "line")
-    grad_query = swap(grad_query.reshape(own_in * pair, line, part)[None], "pair", 1, 0)
-    grad_query = jnp.transpose(grad_query, (1, 2, 0, 3)).reshape(1, own_in, heads_total)
-
     (first_logit_grad,) = first_gate_pull(own_gate_grad[:, None] * column[None, :])
     key_pre, value_pre = kv_sum[:rows], kv_sum[rows:]
+    grad_kv = jnp.stack(
+        [product_tn(tree_input, key_pre), product_tn(tree_input, value_pre)], axis=1
+    )
+    grad_kv, key_pre, value_pre = lax.optimization_barrier(
+        (grad_kv.astype(BF16), key_pre, value_pre)
+    )
     input_term = (
         product_nt(query_pre, query_weight)
         + product_nt(key_pre, kv_weight[:, :piece])
@@ -1266,11 +1322,15 @@
     for expert in range(experts):
         input_term = input_term + first_logit_grad[:, expert : expert + 1] * first_router_wide[expert]
     input_term = input_term.astype(BF16).reshape(pair * experts, micro * tok, width)
+    grad_query, grad_output, input_term = lax.optimization_barrier(
+        (grad_query, grad_output, input_term)
+    )
+    grad_query = scatter(grad_query, "line")
     normed_grad = cube_reduce(input_term, pair, 9).astype(F32)
-    grad_kv = jnp.stack(
-        [product_tn(tree_input, key_pre), product_tn(tree_input, value_pre)], axis=1
-    )
-    grad_kv = scatter(grad_kv.astype(BF16), "line")
+    grad_kv, grad_query = lax.optimization_barrier((grad_kv, grad_query))
+    grad_kv = scatter(grad_kv, "line")
+    grad_query = swap(grad_query.reshape(own_in * pair, line, part)[None], "pair", 1, 0)
+    grad_query = jnp.transpose(grad_query, (1, 2, 0, 3)).reshape(1, own_in, heads_total)
     grad_kv = swap(grad_kv.reshape(pair * experts, own_kv, 2, piece), TREES)
     grad_kv = grad_kv.reshape(pair, experts, own_kv, 2, line // experts, part)
     grad_kv = jnp.transpose(grad_kv, (2, 3, 1, 4, 0, 5)).reshape(own_kv, 2, heads_total)

time: 1110 us -> 1030 us (0.928)
  matrix products: 179 us -> 109 us
  local copies, waits for them, and re-layouts: 78.4 us -> 46.2 us
  Pallas kernels: 716 us -> 738 us
  waiting for transfers between devices: 57.4 us -> 70.6 us
  other arithmetic: 48.5 us -> 36.2 us
    dot_general x9 -> x6, matrix products: 56.5 us -> 21.8 us  [product_nt(): lax.dot_general(left, right, (((1,), (1,)), ((), ())), preferred_element_...]
    dot_general x6 -> x3, matrix products: 57.3 us -> 23 us  [product(): return jnp.dot(left, right, preferred_element_type=F32)]
    unnamed x142 -> x86, local copies, waits for them, and re-layouts: 27.1 us -> 12.7 us
    pallas_call x2 -> x1, Pallas kernels: 390 us -> 401 us  [feed_forward(): pl.pallas_call(ff_kernel, in_specs=[ANY] * 5, out_specs=[ANY] * 7, out_sh...]
  transfers between devices with their start and end apart: 7 -> 7, of which waited for: 2 -> 3; matrix products, arithmetic and copies ran while one was open for 15% -> 14% of each run, Pallas kernels for 18% -> 25%
where the time goes in v3:
time: 1030 us; the launch traced here: 1020 us
  Pallas kernels  738 us (72%)
  matrix products  109 us (11%)
  waiting for transfers between devices  70.6 us (7%)
  local copies, waits for them, and re-layouts  46.2 us (4%)
  other arithmetic  36.2 us (4%)
  between operations  15.1 us (1%)
    pallas_call x1, Pallas kernels, feed_forward(): pl.pallas_call(ff_kernel, in_specs=[ANY] * 5, out_specs=[ANY] * 7, out_sh...  401 us
    pallas_call x1, Pallas kernels, start_exchange(): pl.pallas_call(partial(start_kernel, sizes, walk), in_specs=[VMEM, VMEM,...  114 us
    pallas_call x3, Pallas kernels, cube_reduce(): pl.pallas_call(partial(cube_reduce_kernel, pairs), in_specs=[VMEM], out_s...  89.3 us
    pallas_call x2, Pallas kernels, cube_gather(): pl.pallas_call(partial(cube_gather_kernel, pairs), in_specs=[VMEM], out_s...  59.7 us
    reduce_scatter x3, waiting for transfers between devices, scatter(): return lax.psum_scatter(value, axes, scatter_dimension=axis, tiled=True)  56.3 us
    dot_general x7, matrix products, product_tn(): lax.dot_general(left, right, (((0,), (0,)), ((), ())), preferred_element_...  51 us
    pallas_call x1, Pallas kernels, attend_back(): pl.pallas_call(partial(attend_back_kernel, part // HDIM, scale), grid=gri...  25.7 us
    dot_general x3, matrix products, product(): return jnp.dot(left, right, preferred_element_type=F32)  23 us
  transfers between devices with their start and end apart: 7, of which 3 were waited for; matrix products, arithmetic and copies ran while one was open for 14% of the time, Pallas kernels for 25%

profile of v3, /device:TPU:0, one launch (start us, length us, event | category | flops | bytes accessed | tf_op | source)
XLA Modules:
  0.0 1022.9 jit_solution(2279940207105483364)
XLA Ops:
  7.3 1.9 reshape_squeeze.6
  9.6 1.5 reshape.706.a_ref
  12.2 17.3 %pair_swap.1 = (bf16[2,256,1024]{2,1,0:T(8,128)(2,1)}, s32[2,16,128]{2,1,0:T(8,128)}) custom-call(bf16[2,256,1024]{2,1,0:T(8,128)(2,1)} %reshape.706.a_ref, s32[16,128]{1,0:T(8,128)} %pad_bitcast_fusion.b_ref), custom_call_target="tpu_custom_call" | custom-call | bytes 10485760 | tf_op jit(solution)/shard_map/pair_swap/pallas_call | solution.py:465
  32.4 113.8 %start_exchange.1 = (bf16[2,2,2,128,2048]{4,3,2,1,0:T(8,128)(2,1)S(1)}, bf16[32,10,64]{2,1,0:T(8,128)(2,1)S(1)}, bf16[4,512,512]{2,1,0:T(8,128)(2,1)S(1)}) custom-call(bf16[128,2048]{1,0:T(8,128)(2,1)S(1)} %bitcast.272, bf16[10,64]{1,0:T(8,128)(2,1)S(1)} %pad_maximum_fusion.3.small_ref, bf16[8,64,512]{2,1,0:T(8,128)(2,1)S(1)} %reshape.712.kv_ref), custom_call_target="tpu_custom_call" | custom-call | bytes 26214400 | tf_op jit(solution)/shard_map/start_exchange/pallas_call | solution.py:644
  146.2 2.0 copy-done
  148.5 3.6 multiply_reduce_fusion
  153.4 2.4 fusion.88
  163.2 27.9 %cube_gather.2 = bf16[1,2,2,2048,256]{4,3,2,1,0:T(8,128)(2,1)S(1)} custom-call(bf16[2048,256]{1,0:T(8,128)(2,1)S(1)} %pad_maximum_fusion.1.x_ref), custom_call_target="tpu_custom_call" | custom-call | bytes 41943040 | tf_op jit(solution)/shard_map/cube_gather/pallas_call | solution.py:363
  191.0 2.1 copy-done.5
  194.4 3.4 fusion.87
  203.1 10.0 fusion.5.raw_ref
  213.1 19.9 %attend.1 = (bf16[2,4,2,64,1024]{4,3,2,1,0:T(8,128)(2,1)}, bf16[2,4,2,64,1024]{4,3,2,1,0:T(8,128)(2,1)}) custom-call(f32[2,4,2,64,1024]{4,3,2,1,0:T(8,128)} %fusion.5.raw_ref, bf16[4,2,2,4,2,64,256]{6,5,4,3,2,1,0:T(8,128)(2,1)} %bitcast.273, f32[256,64]{1,0:T(8,128)} %get-tuple-element.187.cos_ref, f32[256,64]{1,0:T(8,128)} %get-tuple-element.186.sin_ref, ...), custom_call_target="tpu_custom_call" | custom-call | flops 1073741824 | bytes 12582912 | tf_op jit(solution)/shard_map/attend/pallas_call | solution.py:169
  233.0 10.6 %multiply_convert_fusion = (bf16[1024,2048]{1,0:T(8,128)(2,1)S(1)}, f32[1024,2048]{1,0:T(8,128)}) fusion(f32[1024]{0:T(1024)S(1)} %multiply_reduce_fusion.7, bf16[1024,1024]{1,0:T(8,128)(2,1)} %bitcast.351, bf16[1024,2048]{1,0:T(8,128)(2,1)} %all-gather.5.cloned.1.call-done), kind=kOutput, calls=%fused_computation.10 | convolution fusion | flops 4299161600 | bytes 18878464 | tf_op jit(solution)/shard_map/dot_general | solution.py:20
  243.6 30.0 %cube_reduce.3 = bf16[128,2048]{1,0:T(8,128)(2,1)S(1)} custom-call(bf16[2,2,2,128,2048]{4,3,2,1,0:T(8,128)(2,1)S(1)} %bitcast.277), custom_call_target="tpu_custom_call" | custom-call | flops 2097152 | bytes 50331648 | tf_op jit(solution)/shard_map/cube_reduce/pallas_call | solution.py:297
  278.4 401.3 %feed_forward.1 = (bf16[4,64,2048]{2,1,0:T(8,128)(2,1)}, bf16[4,64,2048]{2,1,0:T(8,128)(2,1)}, bf16[4,2,256,2048]{3,2,1,0:T(8,128)(2,1)}, bf16[4,2,256,2048]{3,2...) custom-call(bf16[4,64,2048]{2,1,0:T(8,128)(2,1)} %bitcast.306, ...), custom_call_target="tpu_custom_call" | custom-call | flops 35433480192 | bytes 50331648 | tf_op jit(solution)/shard_map/feed_forward/pallas_call | solution.py:1053
  679.8 2.7 multiply_reduce_fusion.1
  682.7 1.6 fusion.26
  685.1 1.7 fusion.79
  686.8 31.9 %cube_gather.3 = bf16[2,2,2,128,2048]{4,3,2,1,0:T(8,128)(2,1)S(1)} custom-call(bf16[128,2048]{1,0:T(8,128)(2,1)S(1)} %get-tuple-element.158.x_ref), custom_call_target="tpu_custom_call" | custom-call | bytes 20971520 | tf_op jit(solution)/shard_map/cube_gather/pallas_call | solution.py:363
  718.7 5.6 fusion.4
  725.8 6.1 convolution_convert_fusion.1
  732.1 5.4 fusion.1
  738.2 5.9 convolution_convert_fusion.5
  744.2 25.7 %attend_back.1 = (bf16[2,4,2,64,1024]{4,3,2,1,0:T(8,128)(2,1)}, bf16[4,2,2,4,2,64,256]{6,5,4,3,2,1,0:T(8,128)(2,1)}) custom-call(bf16[2,4,2,64,1024]{4,3,2,1,0:T(8,128)(2,1)} %get-tuple-element.52.query_ref, bf16[4,2,2,4,2,64,256]{6,5,4,3,2,1,0:T(8,128)(2,1)} %bitcast.274, bf16[2,4,2,64,1024]{4,3,2,1,0:T(8,128)(2,1)} %bitcast.356, ...), custom_call_target="tpu_custom_call" | custom-call | flops 2684354560 | bytes 14680064 | tf_op jit(solution)/shard_map/attend_back/pallas_call | solution.py:187
  769.9 9.5 convolution_convert_fusion
  779.4 2.2 copy-done.6
  781.6 29.0 %cube_reduce.4 = bf16[2048,256]{1,0:T(8,128)(2,1)S(1)} custom-call(bf16[1,2,2,2048,256]{4,3,2,1,0:T(8,128)(2,1)S(1)} %bitcast.275), custom_call_target="tpu_custom_call" | custom-call | flops 2097152 | bytes 50331648 | tf_op jit(solution)/shard_map/cube_reduce/pallas_call | solution.py:297
  816.7 2.5 fusion.20
  819.7 4.6 fusion.90
  824.3 5.2 add_convert_fusion
  829.6 6.5 copy.162
  836.4 11.1 %convolution_bitcast_fusion.1 = f32[1,704,2048]{2,1,0:T(8,128)} fusion(bf16[4,2,256,704]{3,2,1,0:T(8,128)(2,1)} %get-tuple-element.70, bf16[4,2,256,2048]{3,2,1,0:T(8,128)(2,1)} %get-tuple-element.69), kind=kOutput, calls=%fused_computation.23 | convolution fusion | flops 5905580032 | bytes 17039360 | tf_op jit(solution)/shard_map/dot_general | solution.py:24
  847.5 56.3 %reduce-scatter.6.cloned.1.call-done = bf16[512,1024]{1,0:T(8,128)(2,1)} async-done(((bf16[2048,1024]{1,0:T(8,128)(2,1)}), bf16[512,1024]{1,0:T(8,128)(2,1)}) %reduce-scatter.6.cloned.1.call-update) | async-done | bytes 1048592 | tf_op jit(solution)/shard_map/reduce_scatter | solution.py:1090
  903.9 11.2 %convolution_bitcast_fusion.2 = f32[1,704,2048]{2,1,0:T(8,128)} fusion(bf16[4,2,256,704]{3,2,1,0:T(8,128)(2,1)} %get-tuple-element.68, bf16[4,2,256,2048]{3,2,1,0:T(8,128)(2,1)} %get-tuple-element.69), kind=kOutput, calls=%fused_computation.24 | convolution fusion | flops 5905580032 | bytes 17039360 | tf_op jit(solution)/shard_map/dot_general | solution.py:24
  916.7 6.7 fusion.43
  923.4 10.3 %convolution_bitcast_fusion = f32[1,704,2048]{2,1,0:T(8,128)} fusion(bf16[4,2,256,704]{3,2,1,0:T(8,128)(2,1)S(1)} %copy-done.38, bf16[4,2,256,2048]{3,2,1,0:T(8,128)(2,1)} %get-tuple-element.72), kind=kOutput, calls=%fused_computation.22 | convolution fusion | flops 5905580032 | bytes 17039360 | tf_op jit(solution)/shard_map/dot_general | solution.py:24
  933.8 30.3 %cube_reduce.5 = bf16[128,2048]{1,0:T(8,128)(2,1)S(1)} custom-call(bf16[2,2,2,128,2048]{4,3,2,1,0:T(8,128)(2,1)S(1)} %bitcast.276), custom_call_target="tpu_custom_call" | custom-call | flops 2097152 | bytes 50331648 | tf_op jit(solution)/shard_map/cube_reduce/pallas_call | solution.py:297
  965.5 10.7 %small_reduce.1 = f32[10,64]{1,0:T(8,128)} custom-call(f32[32,10,64]{2,1,0:T(8,128)} %maximum_bitcast_fusion.1.x_ref), custom_call_target="tpu_custom_call" | custom-call | bytes 16777216 | tf_op jit(solution)/shard_map/small_reduce/pallas_call | solution.py:435
  977.6 2.1 fusion.17
  979.6 2.7 broadcast_in_dim_reshape.4
  982.4 4.0 all-to-all-start
  986.4 1.6 bitcast_convert_fusion
  988.0 1.9 copy.160
  989.8 11.3 %all-to-all-done = bf16[1,512,4,256]{3,2,0,1:T(4,128)(2,1)S(1)} async-done(((bf16[1,512,4,256]{3,2,0,1:T(4,128)(2,1)}), bf16[1,512,4,256]{3,2,0,1:T(4,128)(2,1)S(1)}, u32[]{:S(2)}, u32[]{:S(2)}) %all-to-all-start) | async-done | bytes 1048608 | tf_op jit(solution)/shard_map/all_to_all | solution.py:1094
  1001.1 3.5 all-to-all-start.1
  1006.2 1.6 copy.159
  1007.8 2.7 reshape.739
  1010.5 2.9 all-to-all-done.1
  (221 shorter events, 43.3 us)
Async XLA Ops:
  7.2 3.9 copy-start.27
  7.2 4.3 copy-start.28
  7.2 22.4 %copy-start.22 = (bf16[64,2048]{1,0:T(8,128)(2,1)S(1)}, bf16[64,2048]{1,0:T(8,128)(2,1)}, u32[]{:S(2)}) copy-start(bf16[64,2048]{1,0:T(8,128)(2,1)} %param.20) | copy-start | bytes 786436
  7.2 195.9 %all-gather.3.cloned.1.call-start = ((), (), s32[]{:S(2)}) async-start(), calls=%async_computation.5 | async-start | bytes 5242880 | tf_op jit(solution)/shard_map/all_gather | solution.py:1086
  9.1 21.0 %copy-start.23 = (bf16[64,2048]{1,0:T(8,128)(2,1)S(1)}, bf16[64,2048]{1,0:T(8,128)(2,1)}, u32[]{:S(2)}) copy-start(bf16[64,2048]{1,0:T(8,128)(2,1)} %param.21) | copy-start | bytes 786436
  11.1 21.2 %copy-start.29 = (bf16[64,4]{0,1:T(4,128)(2,1)S(1)}, bf16[64,4]{0,1:T(4,128)(2,1)}, u32[]{:S(2)}) copy-start(bf16[64,4]{0,1:T(4,128)(2,1)} %param.25) | copy-start | bytes 1540
  11.1 21.2 %copy-start.30 = (bf16[64,4]{0,1:T(4,128)(2,1)S(1)}, bf16[64,4]{0,1:T(4,128)(2,1)}, u32[]{:S(2)}) copy-start(bf16[64,4]{0,1:T(4,128)(2,1)} %param.23) | copy-start | bytes 1540
  11.1 21.2 %copy-start.31 = (bf16[64]{0:T(256)(128)(2,1)S(1)}, bf16[64]{0:T(256)(128)(2,1)}, u32[]{:S(2)}) copy-start(bf16[64]{0:T(256)(128)(2,1)} %param.24) | copy-start | bytes 388
  11.1 21.2 %copy-start.32 = (bf16[64]{0:T(256)(128)(2,1)S(1)}, bf16[64]{0:T(256)(128)(2,1)}, u32[]{:S(2)}) copy-start(bf16[64]{0:T(256)(128)(2,1)} %param.22) | copy-start | bytes 388
  11.1 21.2 %copy-start.2 = (bf16[2,1,64,2048]{3,2,1,0:T(8,128)(2,1)S(1)}, bf16[2,1,64,2048]{3,2,1,0:T(8,128)(2,1)}, u32[]{:S(2)}) copy-start(bf16[2,1,64,2048]{3,2,1,0:T(8,128)(2,1)} %param.17) | copy-start | bytes 1572868
  29.5 203.5 %all-gather.5.cloned.1.call-start = ((), (), s32[]{:S(2)}) async-start(), calls=%async_computation.6 | async-start | bytes 5242880 | tf_op jit(solution)/shard_map/all_gather | solution.py:1086
  146.2 2.0 copy-start
  148.2 5.3 copy-start.8
  148.2 681.3 %reduce-scatter.4.cloned.1.call-start = ((), (), s32[]{:S(2)}) async-start(), calls=%async_computation.7 | async-start | bytes 5242880 | tf_op jit(solution)/shard_map/reduce_scatter | solution.py:1090
  148.5 3.9 copy-start.1
  153.4 2.5 copy-start.10
  153.4 2.7 copy-start.25
  156.3 5.0 copy-start.24
  162.8 30.5 %slice-start = ((s32[2,2,525]{2,1,0:T(2,128)}), s32[2,2,512]{2,1,0:T(2,128)S(1)}, s32[]{:S(2)}) async-start(s32[2,2,525]{2,1,0:T(2,128)} %copy-done.24), calls=%async_computation.10 | async-start | bytes 16384 | tf_op jit(solution)/shard_map/slice | solution.py:1184
  163.1 31.3 %copy-start.26 = (s32[2,1,64,2]{2,3,1,0:T(2,128)S(1)}, s32[2,1,64,2]{2,3,1,0:T(2,128)}, u32[]{:S(2)}) copy-start(s32[2,1,64,2]{2,3,1,0:T(2,128)} %param.30) | copy-start | bytes 3076
  191.0 2.1 copy-start.5
  193.1 5.9 copy-start.36
  193.3 8.6 copy-start.14
  273.6 0.8 copy-start.3
  274.6 2.2 copy-start.17
  679.8 4.5 copy-start.4
  679.8 5.3 copy-start.15
  684.3 34.4 %copy-start.11 = (f32[2,64,2048,1]{2,1,3,0:T(8,128)}, f32[2,64,2048,1]{2,1,3,0:T(8,128)S(1)}, u32[]{:S(2)}) copy-start(f32[2,64,2048,1]{2,1,3,0:T(8,128)S(1)} %fusion.26) | copy-start | bytes 3145732
  724.3 1.6 copy-start.35
  732.0 171.8 %reduce-scatter.6.cloned.1.call-start = ((), (), s32[]{:S(2)}) async-start(), calls=%async_computation.8 | async-start | bytes 5242880 | tf_op jit(solution)/shard_map/reduce_scatter | solution.py:1090
  732.1 5.6 copy-start.19
  732.1 6.1 copy-start.34
  779.4 2.2 copy-start.6
  781.6 30.1 %copy-start.13 = (bf16[1024,2048]{1,0:T(8,128)(2,1)S(1)}, bf16[1024,2048]{1,0:T(8,128)(2,1)}, u32[]{:S(2)}) copy-start(bf16[1024,2048]{1,0:T(8,128)(2,1)} %fusion.1) | copy-start | bytes 12582916
  814.4 2.3 copy-start.9
  816.7 2.5 copy-start.33
  816.7 3.0 copy-start.37
  819.7 4.6 copy-start.21
  829.5 158.4 %reduce-scatter.8.cloned.1.call-start = ((), (), s32[]{:S(2)}) async-start(), calls=%async_computation.9 | async-start | bytes 2621440 | tf_op jit(solution)/shard_map/reduce_scatter | solution.py:1090
  903.9 11.2 %copy-start.18 = (bf16[128,2048]{1,0:T(8,128)(2,1)S(1)}, bf16[128,2048]{1,0:T(8,128)(2,1)}, u32[]{:S(2)}) copy-start(bf16[128,2048]{1,0:T(8,128)(2,1)} %copy-done.17) | copy-start | bytes 1572868
  915.4 8.0 copy-start.38
  923.4 10.3 %copy-start.7 = (bf16[1024,2048]{1,0:T(8,128)(2,1)S(1)}, bf16[1024,2048]{1,0:T(8,128)(2,1)}, u32[]{:S(2)}) copy-start(bf16[1024,2048]{1,0:T(8,128)(2,1)} %add_convert_fusion) | copy-start | bytes 12582916
  933.7 43.8 %copy-start.12 = (f32[2,64,2048,1]{2,1,3,0:T(8,128)S(1)}, f32[2,64,2048,1]{2,1,3,0:T(8,128)}, u32[]{:S(2)}) copy-start(f32[2,64,2048,1]{2,1,3,0:T(8,128)} %copy-done.11) | copy-start | bytes 3145732
  933.8 43.8 %copy-start.16 = (bf16[2,1,64,2048]{3,2,1,0:T(8,128)(2,1)S(1)}, bf16[2,1,64,2048]{3,2,1,0:T(8,128)(2,1)}, u32[]{:S(2)}) copy-start(bf16[2,1,64,2048]{3,2,1,0:T(8,128)(2,1)} %param.33) | copy-start | bytes 1572868
  979.6 6.8 copy-start.20
  982.4 18.7 %all-to-all-start = ((bf16[1,512,4,256]{3,2,0,1:T(4,128)(2,1)}), bf16[1,512,4,256]{3,2,0,1:T(4,128)(2,1)S(1)}, u32[]{:S(2)}, u32[]{:S(2)}) async-start(bf16[1,512,4,256]{3,2,0,1:T(4,128)(2,1)} %bitcast.83), calls=%async_computation.2 | async-start | bytes 2097152 | tf_op jit(solution)/shard_map/all_to_all | solution.py:1094
  1001.1 12.3 %all-to-all-start.1 = ((bf16[8,64,2,256]{3,1,2,0:T(8,128)(2,1)}), bf16[8,64,2,256]{3,1,2,0:T(8,128)(2,1)S(1)}, u32[]{:S(2)}, u32[]{:S(2)}) async-start(bf16[8,64,2,256]{3,1,2,0:T(8,128)(2,1)} %copy.160), calls=%async_computation.4 | async-start | bytes 1048576 | tf_op jit(solution)/shard_map/all_to_all | solution.py:1094
Sparse Core Ops, SparseCore 0:
  29.6 104.3 all-gather.2
  148.3 79.1 all-gather.4
  732.1 74.8 reduce-scatter.3
  829.6 74.1 reduce-scatter.5
  906.5 44.4 reduce-scatter.7

commit v4 on v3

--- a/solution.py
+++ b/solution.py
@@ -854,6 +854,14 @@
         def _():
             to_twin().start()
 
+    def emit(t):
+        j = order(t)
+        sum_other(0, j).start()
+
+        @pl.when((j != twin) & (j != z))
+        def _():
+            sum_other(1, j).start()
+
     def step(s, carry):
         @pl.when(s == 0)
         def _():
@@ -870,6 +878,10 @@
         def _():
             spread(3)
 
+        @pl.when(s == line)
+        def _():
+            sum_twin().start()
+
         def half(c, inner_carry):
             t = s - c
             column = p + c * (q - p)
@@ -900,19 +912,8 @@
 
     lax.fori_loop(0, line + 1, step, 0)
 
-    sum_twin().start()
-
-    def emit(t, carry):
-        j = order(line - 1 - t)
-        sum_other(0, j).start()
-
-        @pl.when((j != twin) & (j != z))
-        def _():
-            sum_other(1, j).start()
-
-        return carry
-
-    lax.fori_loop(0, line, emit, 0)
+    for t in (3, 2, 1, 0):
+        emit(t)
 
     for copy in (
         pltpu.make_async_copy(mid.at[:, :, 0], inner_save, local.at[2]),
@@ -924,6 +925,21 @@
     add_into(b_buf.at[z, q], [b_buf.at[z, q], extra], rows)
     sum_other(1, z).start()
 
+    def back(kind):
+        own = pltpu.make_async_copy(
+            bufs[kind].at[z, p, piece(e)], outs[kind].at[e], local.at[kind]
+        )
+        return [own] + [
+            push(
+                bufs[kind].at[z, p, piece((e + shift) % experts)],
+                outs[kind].at[e],
+                kind,
+                BACK + shift,
+                {"expert": (e + shift) % experts},
+            )
+            for shift in range(1, experts)
+        ]
+
     def fold(s, carry):
         t = line - 1 - s
         j = order(t)
@@ -974,6 +990,11 @@
                 sum_down(kind, j, line).wait_recv()
                 add_into(mine, [mine, hop.at[kind, line]], rows)
 
+            @pl.when(j == z)
+            def _():
+                for copy in back(kind):
+                    copy.start()
+
             @pl.when(j > z)
             def _():
                 sum_up(kind, j).start()
@@ -990,22 +1011,9 @@
 
     lax.fori_loop(0, line, fold, 0)
 
-    back = []
     for kind in range(2):
-        keep = pltpu.make_async_copy(
-            bufs[kind].at[z, p, piece(e)], outs[kind].at[e], local.at[kind]
-        )
-        keep.start()
-        back.append(keep)
-        for shift in range(1, experts):
-            peer = (e + shift) % experts
-            copy = push(
-                bufs[kind].at[z, p, piece(peer)], outs[kind].at[e], kind, BACK + shift, {"expert": peer}
-            )
-            copy.start()
-            back.append(copy)
-    for copy in back:
-        copy.wait()
+        for copy in back(kind):
+            copy.wait()
 
     def drain(j, carry):
         for kind in range(2):
@@ -1082,6 +1090,187 @@
     )(first, second, w_gate, w_up, w_down)
 
 
+def end_kernel(
+    pairs, x_ref, g_hbm, o_ref, k_ref,
+    g_ref, half, quarter, got_core, got_side, got_pair, hop, send, recv, local,
+):
+    z, p, e = lax.axis_index("line"), lax.axis_index("pair"), lax.axis_index("expert")
+    line, span, _ = g_ref.shape
+    trees, piece, _ = k_ref.shape
+    c, y = e % 2, e // 2
+    core, side = {"expert": e + 1 - 2 * c}, {"expert": e + 2 - 4 * y}
+    other, up, down = {"pair": 1 - p}, {"line": z + 1}, {"line": z - 1}
+    experts = trees // pairs
+    me = p * experts + e
+    high = z // 2
+    near = z + high * (line - 1 - 2 * z)
+
+    def order(t):
+        j = t + near * (1 - t // 2) * (1 - 2 * t)
+        return j + high * (line - 1 - 2 * j)
+
+    def place(index):
+        return {"pair": index // experts, "expert": index % experts}
+
+    fetch = pltpu.make_async_copy(g_hbm, g_ref, local)
+    fetch.start()
+    barrier = pltpu.get_barrier_semaphore()
+    for shift in range(1, trees):
+        pl.semaphore_signal(
+            barrier, inc=1, device_id=place((me + shift) % trees), device_id_type=MESH
+        )
+
+    @pl.when(z > 0)
+    def _():
+        pl.semaphore_signal(barrier, inc=1, device_id=down, device_id_type=MESH)
+
+    @pl.when(z < line - 1)
+    def _():
+        pl.semaphore_signal(barrier, inc=1, device_id=up, device_id_type=MESH)
+
+    below, above = (z + line - 1) // line, (2 * line - 2 - z) // line
+    pl.semaphore_wait(barrier, trees - 1 + below + above)
+    UP, DOWN, SWAP = 7, 7 + line, 7 + 2 * line
+    rows = x_ref.shape[3]
+
+    def sum_up(j):
+        return remote(g_ref.at[j], hop.at[j], send.at[UP + j], recv.at[UP + j], up)
+
+    def sum_down(j, slot):
+        return remote(g_ref.at[j], hop.at[slot], send.at[DOWN + j], recv.at[DOWN + j], down)
+
+    def fold(t):
+        j = order(t)
+        mine = g_ref.at[j]
+
+        @pl.when((j >= z) & (z > 0))
+        def _():
+            sum_up(j).wait_recv()
+            add_into(mine, [mine, hop.at[j]], span)
+
+        @pl.when((j < z) & (z < line - 1))
+        def _():
+            sum_down(j, j).wait_recv()
+            add_into(mine, [mine, hop.at[j]], span)
+
+        @pl.when((j == z) & (z < line - 1))
+        def _():
+            sum_down(j, line).wait_recv()
+            add_into(mine, [mine, hop.at[line]], span)
+
+        @pl.when(j > z)
+        def _():
+            sum_up(j).start()
+
+        @pl.when((j < z) & (j != z - 1))
+        def _():
+            sum_down(j, j).start()
+
+        @pl.when((j < z) & (j == z - 1))
+        def _():
+            sum_down(j, line).start()
+
+    corners = [(1, 1), (0, 1), (1, 0), (0, 0)]
+    first, second = [], {}
+    for slot, (dx, dy) in enumerate(corners):
+        copy = remote(
+            x_ref.at[(p + dx) % 2, (y + dy) % 2, 1 - c],
+            got_core.at[slot],
+            send.at[slot],
+            recv.at[slot],
+            core,
+        )
+        copy.start()
+        first.append(copy)
+    fetch.wait()
+    fold(3)
+    for slot, (dx, dy) in enumerate(corners):
+        first[slot].wait_recv()
+        add_into(
+            half.at[slot], [x_ref.at[(p + dx) % 2, (y + dy) % 2, c], got_core.at[slot]], rows
+        )
+        if dy == 1:
+            second[dx] = remote(
+                half.at[slot], got_side.at[dx], send.at[4 + dx], recv.at[4 + dx], side
+            )
+            second[dx].start()
+    fold(2)
+    second[1].wait_recv()
+    add_into(quarter, [half.at[2], got_side.at[1]], rows)
+    last = remote(quarter, got_pair, send.at[6], recv.at[6], other)
+    last.start()
+    fold(1)
+    second[0].wait_recv()
+    last.wait_recv()
+    add_into(o_ref, [half.at[3], got_side.at[0], got_pair], rows)
+    fold(0)
+
+    def part(index):
+        return g_ref.at[z, pl.ds(pl.multiple_of(index * piece, piece), piece)]
+
+    keep = pltpu.make_async_copy(part(me), k_ref.at[me], local)
+    keep.start()
+    swaps = []
+    for shift in range(1, trees):
+        peer = (me + shift) % trees
+        copy = remote(
+            part(peer), k_ref.at[me], send.at[SWAP + shift], recv.at[SWAP + shift], place(peer)
+        )
+        copy.start()
+        swaps.append(copy)
+    for copy in swaps:
+        copy.wait()
+    keep.wait()
+    for copy in first + list(second.values()) + [last]:
+        copy.wait_send()
+
+    def drain(j, carry):
+        @pl.when(j > z)
+        def _():
+            sum_up(j).wait_send()
+
+        @pl.when(j < z)
+        def _():
+            sum_down(j, j).wait_send()
+
+        return carry
+
+    lax.fori_loop(0, line, drain, 0)
+
+
+def end_exchange(value, grads, line, pairs, number):
+    trees, rows, cols = value.shape
+    span, thin = grads.shape[0] // line, grads.shape[1]
+    uses = 7 + 2 * line + trees
+    block = pltpu.VMEM((rows, cols), BF16)
+    return pl.pallas_call(
+        partial(end_kernel, pairs),
+        in_specs=[VMEM, ANY],
+        out_specs=[VMEM, VMEM],
+        out_shape=[
+            jax.ShapeDtypeStruct((rows, cols), BF16),
+            jax.ShapeDtypeStruct((trees, span // trees, thin), BF16),
+        ],
+        scratch_shapes=[
+            pltpu.VMEM((line, span, thin), BF16),
+            pltpu.VMEM((4, rows, cols), BF16),
+            block,
+            pltpu.VMEM((4, rows, cols), BF16),
+            pltpu.VMEM((2, rows, cols), BF16),
+            block,
+            pltpu.VMEM((line + 1, span, thin), BF16),
+            DMA((uses,)),
+            DMA((uses,)),
+            DMA(()),
+        ],
+        compiler_params=params(number, 48 * 2**20),
+        cost_estimate=pl.CostEstimate(
+            flops=value.size, bytes_accessed=32 * value.size, transcendentals=0
+        ),
+        name="end_exchange",
+    )(value.reshape(pairs, 2, 2, rows, cols), grads.reshape(line, span, thin))
+
+
 def gather(value, axes, axis=0):
     return lax.all_gather(value, axes, axis=axis, tiled=True)
 
@@ -1268,10 +1457,6 @@
         came_back = swap(scatter(came_back, DP).reshape(back), "expert")
     returned = returned.reshape(experts, micro, capacity, width)
     came_back = came_back.reshape(experts, micro, capacity, width)
-    grad_gate = product_tn(gate_grad, arrived)[None]
-    grad_upward = product_tn(up_grad, arrived)[None]
-    grad_downward = product_tn(inner, result_grad)[None]
-
     spread = jnp.einsum("mect,emcd->emtd", table_low, returned, preferred_element_type=F32)
     spread = spread.reshape(experts, micro * tok, width)
     mixed = jnp.sum(jnp.transpose(second_gates)[:, :, None] * spread, axis=0)
@@ -1305,9 +1490,10 @@
     grad_query = product_tn(tree_input, query_pre).astype(BF16)
     grad_query, kv_pre = lax.optimization_barrier((grad_query, kv_pre))
     kv_sum = cube_reduce(kv_pre.reshape(experts, 2 * rows, piece), 1, 8)
+    grad_query, grad_output, kv_sum = lax.optimization_barrier((grad_query, grad_output, kv_sum))
     (first_logit_grad,) = first_gate_pull(own_gate_grad[:, None] * column[None, :])
     key_pre, value_pre = kv_sum[:rows], kv_sum[rows:]
-    grad_kv = jnp.stack(
+    grad_kv = jnp.concatenate(
         [product_tn(tree_input, key_pre), product_tn(tree_input, value_pre)], axis=1
     )
     grad_kv, key_pre, value_pre = lax.optimization_barrier(
@@ -1322,16 +1508,22 @@
     for expert in range(experts):
         input_term = input_term + first_logit_grad[:, expert : expert + 1] * first_router_wide[expert]
     input_term = input_term.astype(BF16).reshape(pair * experts, micro * tok, width)
-    grad_query, grad_output, input_term = lax.optimization_barrier(
-        (grad_query, grad_output, input_term)
-    )
+    if walk:
+        normed_grad, grad_kv = end_exchange(input_term, grad_kv, line, pair, 9)
+    else:
+        normed_grad = cube_reduce(input_term, pair, 9)
+        grad_kv = scatter(grad_kv, "line")
+        grad_kv = swap(grad_kv.reshape(pair * experts, own_kv, 2 * piece), TREES)
+    gate_grad, up_grad, inner, arrived, result_grad, normed_grad = lax.optimization_barrier(
+        (gate_grad, up_grad, inner, arrived, result_grad, normed_grad)
+    )
+    grad_gate = product_tn(gate_grad, arrived)[None]
+    grad_upward = product_tn(up_grad, arrived)[None]
+    grad_downward = product_tn(inner, result_grad)[None]
+    normed_grad = normed_grad.astype(F32)
     grad_query = scatter(grad_query, "line")
-    normed_grad = cube_reduce(input_term, pair, 9).astype(F32)
-    grad_kv, grad_query = lax.optimization_barrier((grad_kv, grad_query))
-    grad_kv = scatter(grad_kv, "line")
     grad_query = swap(grad_query.reshape(own_in * pair, line, part)[None], "pair", 1, 0)
     grad_query = jnp.transpose(grad_query, (1, 2, 0, 3)).reshape(1, own_in, heads_total)
-    grad_kv = swap(grad_kv.reshape(pair * experts, own_kv, 2, piece), TREES)
     grad_kv = grad_kv.reshape(pair, experts, own_kv, 2, line // experts, part)
     grad_kv = jnp.transpose(grad_kv, (2, 3, 1, 4, 0, 5)).reshape(own_kv, 2, heads_total)
     grad_kv = grad_kv.astype(F32)

time: 1030 us -> 1010 us (0.981)
  waiting for transfers between devices: 70.6 us -> 13.2 us
  Pallas kernels: 738 us -> 767 us
    pallas_call x0 -> x1, Pallas kernels: none -> 79.1 us  [end_exchange(): pl.pallas_call(partial(end_kernel, pairs), in_specs=[VMEM, ANY], out_spec...]
    reduce_scatter x3 -> x2, waiting for transfers between devices: 56.3 us -> 0.01 us  [scatter(): return lax.psum_scatter(value, axes, scatter_dimension=axis, tiled=True)]
    pallas_call x3 -> x2, Pallas kernels: 89.3 us -> 59 us  [cube_reduce(): pl.pallas_call(partial(cube_reduce_kernel, pairs), in_specs=[VMEM], out_s...]
    pallas_call x1, Pallas kernels: 401 us -> 381 us  [feed_forward(): pl.pallas_call(ff_kernel, in_specs=[ANY] * 5, out_specs=[ANY] * 7, out_sh...]
  transfers between devices with their start and end apart: 7 -> 5, of which waited for: 3 -> 1; matrix products, arithmetic and copies ran while one was open for 14% -> 14% of each run, Pallas kernels for 25% -> 31%
where the time goes in v4:
time: 1010 us; the launch traced here: 1000 us
  Pallas kernels  767 us (76%)
  matrix products  115 us (11%)
  local copies, waits for them, and re-layouts  52.9 us (5%)
  other arithmetic  37.3 us (4%)
  between operations  15 us (1%)
  waiting for transfers between devices  13.2 us (1%)
    pallas_call x1, Pallas kernels, feed_forward(): pl.pallas_call(ff_kernel, in_specs=[ANY] * 5, out_specs=[ANY] * 7, out_sh...  381 us
    pallas_call x1, Pallas kernels, start_exchange(): pl.pallas_call(partial(start_kernel, sizes, walk), in_specs=[VMEM, VMEM,...  114 us
    pallas_call x1, Pallas kernels, end_exchange(): pl.pallas_call(partial(end_kernel, pairs), in_specs=[VMEM, ANY], out_spec...  79.1 us
    pallas_call x2, Pallas kernels, cube_reduce(): pl.pallas_call(partial(cube_reduce_kernel, pairs), in_specs=[VMEM], out_s...  59 us
    pallas_call x2, Pallas kernels, cube_gather(): pl.pallas_call(partial(cube_gather_kernel, pairs), in_specs=[VMEM], out_s...  58.7 us
    dot_general x7, matrix products, product_tn(): lax.dot_general(left, right, (((0,), (0,)), ((), ())), preferred_element_...  48.4 us
    dot_general x6, matrix products, product_nt(): lax.dot_general(left, right, (((1,), (1,)), ((), ())), preferred_element_...  31.2 us
    pallas_call x1, Pallas kernels, attend_back(): pl.pallas_call(partial(attend_back_kernel, part // HDIM, scale), grid=gri...  25.7 us
  transfers between devices with their start and end apart: 5, of which 1 were waited for; matrix products, arithmetic and copies ran while one was open for 14% of the time, Pallas kernels for 31%

profile of v4, /device:TPU:0, one launch (start us, length us, event | category | flops | bytes accessed | tf_op | source)
XLA Modules:
  0.0 1004.1 jit_solution(8814468793488334554)
XLA Ops:
  7.3 1.9 reshape_squeeze.6
  12.2 17.3 %pair_swap.1 = (bf16[2,256,1024]{2,1,0:T(8,128)(2,1)}, s32[2,16,128]{2,1,0:T(8,128)}) custom-call(bf16[2,256,1024]{2,1,0:T(8,128)(2,1)} %reshape.710.a_ref, s32[16,128]{1,0:T(8,128)} %pad_bitcast_fusion.b_ref), custom_call_target="tpu_custom_call" | custom-call | bytes 10485760 | tf_op jit(solution)/shard_map/pair_swap/pallas_call | solution.py:465
  32.4 113.8 %start_exchange.1 = (bf16[2,2,2,128,2048]{4,3,2,1,0:T(8,128)(2,1)S(1)}, bf16[32,10,64]{2,1,0:T(8,128)(2,1)S(1)}, bf16[4,512,512]{2,1,0:T(8,128)(2,1)S(1)}) custom-call(bf16[128,2048]{1,0:T(8,128)(2,1)S(1)} %bitcast.257, bf16[10,64]{1,0:T(8,128)(2,1)S(1)} %pad_maximum_fusion.3.small_ref, bf16[8,64,512]{2,1,0:T(8,128)(2,1)S(1)} %reshape.716.kv_ref), custom_call_target="tpu_custom_call" | custom-call | bytes 26214400 | tf_op jit(solution)/shard_map/start_exchange/pallas_call | solution.py:644
  146.2 2.0 copy-done
  148.4 3.6 multiply_reduce_fusion
  153.4 2.4 fusion.86
  163.3 27.8 %cube_gather.2 = bf16[1,2,2,2048,256]{4,3,2,1,0:T(8,128)(2,1)S(1)} custom-call(bf16[2048,256]{1,0:T(8,128)(2,1)S(1)} %pad_maximum_fusion.1.x_ref), custom_call_target="tpu_custom_call" | custom-call | bytes 41943040 | tf_op jit(solution)/shard_map/cube_gather/pallas_call | solution.py:363
  191.2 2.0 copy-done.5
  194.6 3.4 fusion.85
  203.1 10.0 fusion.5.raw_ref
  213.2 19.9 %attend.1 = (bf16[2,4,2,64,1024]{4,3,2,1,0:T(8,128)(2,1)}, bf16[2,4,2,64,1024]{4,3,2,1,0:T(8,128)(2,1)}) custom-call(f32[2,4,2,64,1024]{4,3,2,1,0:T(8,128)} %fusion.5.raw_ref, bf16[4,2,2,4,2,64,256]{6,5,4,3,2,1,0:T(8,128)(2,1)} %bitcast.258, f32[256,64]{1,0:T(8,128)} %get-tuple-element.199.cos_ref, f32[256,64]{1,0:T(8,128)} %get-tuple-element.198.sin_ref, ...), custom_call_target="tpu_custom_call" | custom-call | flops 1073741824 | bytes 12582912 | tf_op jit(solution)/shard_map/attend/pallas_call | solution.py:169
  233.0 10.5 %multiply_convert_fusion = (bf16[1024,2048]{1,0:T(8,128)(2,1)S(1)}, f32[1024,2048]{1,0:T(8,128)}) fusion(f32[1024]{0:T(1024)S(1)} %multiply_reduce_fusion.7, bf16[1024,1024]{1,0:T(8,128)(2,1)} %bitcast.336, bf16[1024,2048]{1,0:T(8,128)(2,1)} %all-gather.5.cloned.1.call-done), kind=kOutput, calls=%fused_computation.10 | convolution fusion | flops 4299161600 | bytes 18878464 | tf_op jit(solution)/shard_map/dot_general | solution.py:20
  243.6 30.0 %cube_reduce.2 = bf16[128,2048]{1,0:T(8,128)(2,1)S(1)} custom-call(bf16[2,2,2,128,2048]{4,3,2,1,0:T(8,128)(2,1)S(1)} %bitcast.262), custom_call_target="tpu_custom_call" | custom-call | flops 2097152 | bytes 50331648 | tf_op jit(solution)/shard_map/cube_reduce/pallas_call | solution.py:297
  278.4 381.4 %feed_forward.1 = (bf16[4,64,2048]{2,1,0:T(8,128)(2,1)}, bf16[4,64,2048]{2,1,0:T(8,128)(2,1)}, bf16[4,2,256,2048]{3,2,1,0:T(8,128)(2,1)}, bf16[4,2,256,2048]{3,2...) custom-call(bf16[4,64,2048]{2,1,0:T(8,128)(2,1)} %bitcast.292, ...), custom_call_target="tpu_custom_call" | custom-call | flops 35433480192 | bytes 50331648 | tf_op jit(solution)/shard_map/feed_forward/pallas_call | solution.py:1061
  659.9 2.7 multiply_reduce_fusion.1
  665.2 1.7 fusion.77
  666.8 30.9 %cube_gather.3 = bf16[2,2,2,128,2048]{4,3,2,1,0:T(8,128)(2,1)S(1)} custom-call(bf16[128,2048]{1,0:T(8,128)(2,1)S(1)} %get-tuple-element.170.x_ref), custom_call_target="tpu_custom_call" | custom-call | bytes 20971520 | tf_op jit(solution)/shard_map/cube_gather/pallas_call | solution.py:363
  697.7 5.6 fusion.4
  704.9 6.2 convolution_convert_fusion.1
  711.1 5.4 fusion.1
  716.5 6.6 copy.152
  723.6 9.4 convolution_convert_fusion.5
  733.0 25.7 %attend_back.1 = (bf16[2,4,2,64,1024]{4,3,2,1,0:T(8,128)(2,1)}, bf16[4,2,2,4,2,64,256]{6,5,4,3,2,1,0:T(8,128)(2,1)}) custom-call(bf16[2,4,2,64,1024]{4,3,2,1,0:T(8,128)(2,1)} %get-tuple-element.63.query_ref, bf16[4,2,2,4,2,64,256]{6,5,4,3,2,1,0:T(8,128)(2,1)} %bitcast.259, bf16[2,4,2,64,1024]{4,3,2,1,0:T(8,128)(2,1)} %bitcast.351, ...), custom_call_target="tpu_custom_call" | custom-call | flops 2684354560 | bytes 14680064 | tf_op jit(solution)/shard_map/attend_back/pallas_call | solution.py:187
  758.7 9.4 convolution_convert_fusion
  768.5 2.3 copy-done.7
  770.8 29.0 %cube_reduce.3 = bf16[2048,256]{1,0:T(8,128)(2,1)S(1)} custom-call(bf16[1,2,2,2048,256]{4,3,2,1,0:T(8,128)(2,1)S(1)} %bitcast.261), custom_call_target="tpu_custom_call" | custom-call | flops 2097152 | bytes 50331648 | tf_op jit(solution)/shard_map/cube_reduce/pallas_call | solution.py:297
  801.2 5.0 fusion.41
  806.2 8.3 fusion.88
  814.5 3.6 convolution_convert_fusion.4
  818.2 2.3 convolution_convert_fusion.3
  820.5 2.7 pad_maximum_fusion
  824.2 4.3 copy.148
  828.6 2.4 fusion.18
  831.0 7.4 add_convert_fusion
  838.4 79.1 %end_exchange.1 = (bf16[128,2048]{1,0:T(8,128)(2,1)S(1)}, bf16[8,64,512]{2,1,0:T(8,128)(2,1)S(1)}) custom-call(bf16[2,2,2,128,2048]{4,3,2,1,0:T(8,128)(2,1)} %bitcast.276, bf16[4,512,512]{2,1,0:T(8,128)(2,1)S(1)} %bitcast.260), custom_call_target="tpu_custom_call" | custom-call | flops 2097152 | bytes 67108864 | tf_op jit(solution)/shard_map/end_exchange/pallas_call | solution.py:1246
  919.0 12.6 %small_reduce.1 = f32[10,64]{1,0:T(8,128)} custom-call(f32[32,10,64]{2,1,0:T(8,128)} %maximum_bitcast_fusion.1.x_ref), custom_call_target="tpu_custom_call" | custom-call | bytes 16777216 | tf_op jit(solution)/shard_map/small_reduce/pallas_call | solution.py:435
  933.2 3.1 copy.151
  936.3 3.0 reshape.748
  940.4 2.3 slice_bitcast_fusion
  942.7 2.1 fusion.15
  944.8 10.4 %convolution_bitcast_fusion.1 = f32[1,704,2048]{2,1,0:T(8,128)} fusion(bf16[2048,704]{1,0:T(8,128)(2,1)S(1)} %bitcast.348, bf16[2048,2048]{1,0:T(8,128)(2,1)} %bitcast.342), kind=kOutput, calls=%fused_computation.23 | convolution fusion | flops 5905580032 | bytes 17039360 | tf_op jit(solution)/shard_map/dot_general | solution.py:24
  955.2 8.1 convolution_bitcast_fusion.2
  963.4 8.3 convolution_bitcast_fusion
  971.7 2.7 broadcast_in_dim_reshape.4
  974.5 3.6 all-to-all-start
  979.6 13.1 %all-to-all-done = bf16[1,512,4,256]{3,2,0,1:T(4,128)(2,1)S(1)} async-done(((bf16[1,512,4,256]{3,2,0,1:T(4,128)(2,1)}), bf16[1,512,4,256]{3,2,0,1:T(4,128)(2,1)S(1)}, u32[]{:S(2)}, u32[]{:S(2)}) %all-to-all-start) | async-done | bytes 1048608 | tf_op jit(solution)/shard_map/all_to_all | solution.py:1283
  993.0 1.6 copy.150
  994.6 2.7 reshape.746
  (228 shorter events, 39.4 us)
Async XLA Ops:
  7.2 3.9 copy-start.28
  7.2 4.3 copy-start.29
  7.2 22.3 %copy-start.22 = (bf16[64,2048]{1,0:T(8,128)(2,1)S(1)}, bf16[64,2048]{1,0:T(8,128)(2,1)}, u32[]{:S(2)}) copy-start(bf16[64,2048]{1,0:T(8,128)(2,1)} %param.20) | copy-start | bytes 786436
  7.2 195.9 %all-gather.3.cloned.1.call-start = ((), (), s32[]{:S(2)}) async-start(), calls=%async_computation.3 | async-start | bytes 5242880 | tf_op jit(solution)/shard_map/all_gather | solution.py:1275
  9.1 21.0 %copy-start.23 = (bf16[64,2048]{1,0:T(8,128)(2,1)S(1)}, bf16[64,2048]{1,0:T(8,128)(2,1)}, u32[]{:S(2)}) copy-start(bf16[64,2048]{1,0:T(8,128)(2,1)} %param.21) | copy-start | bytes 786436
  11.1 21.2 %copy-start.30 = (bf16[64,4]{0,1:T(4,128)(2,1)S(1)}, bf16[64,4]{0,1:T(4,128)(2,1)}, u32[]{:S(2)}) copy-start(bf16[64,4]{0,1:T(4,128)(2,1)} %param.25) | copy-start | bytes 1540
  11.1 21.2 %copy-start.31 = (bf16[64,4]{0,1:T(4,128)(2,1)S(1)}, bf16[64,4]{0,1:T(4,128)(2,1)}, u32[]{:S(2)}) copy-start(bf16[64,4]{0,1:T(4,128)(2,1)} %param.23) | copy-start | bytes 1540
  11.1 21.2 %copy-start.32 = (bf16[64]{0:T(256)(128)(2,1)S(1)}, bf16[64]{0:T(256)(128)(2,1)}, u32[]{:S(2)}) copy-start(bf16[64]{0:T(256)(128)(2,1)} %param.24) | copy-start | bytes 388
  11.1 21.2 %copy-start.33 = (bf16[64]{0:T(256)(128)(2,1)S(1)}, bf16[64]{0:T(256)(128)(2,1)}, u32[]{:S(2)}) copy-start(bf16[64]{0:T(256)(128)(2,1)} %param.22) | copy-start | bytes 388
  11.1 21.2 %copy-start.2 = (bf16[2,1,64,2048]{3,2,1,0:T(8,128)(2,1)S(1)}, bf16[2,1,64,2048]{3,2,1,0:T(8,128)(2,1)}, u32[]{:S(2)}) copy-start(bf16[2,1,64,2048]{3,2,1,0:T(8,128)(2,1)} %param.17) | copy-start | bytes 1572868
  29.5 203.6 %all-gather.5.cloned.1.call-start = ((), (), s32[]{:S(2)}) async-start(), calls=%async_computation.4 | async-start | bytes 5242880 | tf_op jit(solution)/shard_map/all_gather | solution.py:1275
  146.1 2.0 copy-start
  148.2 5.3 copy-start.8
  148.2 666.3 %reduce-scatter.3.cloned.1.call-start = ((), (), s32[]{:S(2)}) async-start(), calls=%async_computation.5 | async-start | bytes 5242880 | tf_op jit(solution)/shard_map/reduce_scatter | solution.py:1279
  148.4 3.9 copy-start.1
  153.4 2.5 copy-start.10
  153.4 2.7 copy-start.26
  156.2 5.2 copy-start.24
  163.0 30.5 %slice-start = ((s32[2,2,525]{2,1,0:T(2,128)}), s32[2,2,512]{2,1,0:T(2,128)S(1)}, s32[]{:S(2)}) async-start(s32[2,2,525]{2,1,0:T(2,128)} %copy-done.24), calls=%async_computation.7 | async-start | bytes 16384 | tf_op jit(solution)/shard_map/slice | solution.py:1373
  163.2 31.3 %copy-start.27 = (s32[2,1,64,2]{2,3,1,0:T(2,128)S(1)}, s32[2,1,64,2]{2,3,1,0:T(2,128)}, u32[]{:S(2)}) copy-start(s32[2,1,64,2]{2,3,1,0:T(2,128)} %param.30) | copy-start | bytes 3076
  191.1 2.0 copy-start.5
  193.2 5.9 copy-start.36
  193.5 8.6 copy-start.15
  274.6 2.3 copy-start.18
  659.8 4.5 copy-start.4
  659.8 5.3 copy-start.16
  664.3 33.4 %copy-start.11 = (f32[2,64,2048,1]{2,1,3,0:T(8,128)}, f32[2,64,2048,1]{2,1,3,0:T(8,128)S(1)}, u32[]{:S(2)}) copy-start(f32[2,64,2048,1]{2,1,3,0:T(8,128)S(1)} %fusion.24) | copy-start | bytes 3145732
  711.1 260.7 %reduce-scatter.5.cloned.1.call-start = ((), (), s32[]{:S(2)}) async-start(), calls=%async_computation.6 | async-start | bytes 5242880 | tf_op jit(solution)/shard_map/reduce_scatter | solution.py:1279
  758.7 9.4 copy-start.19
  768.5 2.3 copy-start.7
  770.8 30.4 %copy-start.14 = (bf16[2048,1024]{1,0:T(8,128)(2,1)S(1)}, bf16[2048,1024]{1,0:T(8,128)(2,1)}, u32[]{:S(2)}) copy-start(bf16[2048,1024]{1,0:T(8,128)(2,1)} %copy.152) | copy-start | bytes 12582916
  770.8 35.4 %copy-start.34 = (bf16[2048,1024]{1,0:T(8,128)(2,1)S(1)}, bf16[2048,1024]{1,0:T(8,128)(2,1)}, u32[]{:S(2)}) copy-start(bf16[2048,1024]{1,0:T(8,128)(2,1)} %all-gather.3.cloned.1.call-done) | copy-start | bytes 12582916
  814.5 3.6 copy-start.13
  824.2 4.3 copy-start.9
  828.6 2.4 copy-start.21
  831.0 7.5 copy-start.6
  918.2 24.6 %copy-start.12 = (f32[2,64,2048,1]{2,1,3,0:T(8,128)S(1)}, f32[2,64,2048,1]{2,1,3,0:T(8,128)}, u32[]{:S(2)}) copy-start(f32[2,64,2048,1]{2,1,3,0:T(8,128)} %copy-done.11) | copy-start | bytes 3145732
  931.6 7.7 copy-start.25
  933.2 9.5 copy-start.17
  939.3 5.5 copy-start.39
  942.7 12.5 %slice-start.3 = ((s8[8388608]{0:T(1024)(128)(4,1)}), s8[4194304]{0:T(1024)(128)(4,1)S(1)}, s32[]{:S(2)}) async-start(s8[8388608]{0:T(1024)(128)(4,1)} %bitcast.343), calls=%async_computation.10 | async-start | bytes 8388608
  944.8 10.4 %slice-start.4 = ((s8[8388608]{0:T(1024)(128)(4,1)}), s8[4194304]{0:T(1024)(128)(4,1)S(1)}, s32[]{:S(2)}) async-start(s8[8388608]{0:T(1024)(128)(4,1)} %bitcast.343), calls=%async_computation.11 | async-start | bytes 8388608
  944.8 10.4 %copy-start.38 = (bf16[4,2,256,704]{3,2,1,0:T(8,128)(2,1)S(1)}, bf16[4,2,256,704]{3,2,1,0:T(8,128)(2,1)}, u32[]{:S(2)}) copy-start(bf16[4,2,256,704]{3,2,1,0:T(8,128)(2,1)} %get-tuple-element.58) | copy-start | bytes 8650756
  944.8 18.6 %slice-start.1 = ((s8[8388608]{0:T(1024)(128)(4,1)}), s8[4194304]{0:T(1024)(128)(4,1)S(1)}, s32[]{:S(2)}) async-start(s8[8388608]{0:T(1024)(128)(4,1)} %bitcast.339), calls=%async_computation.8 | async-start | bytes 8388608
  955.2 8.2 slice-start.2
  955.2 8.2 copy-start.37
  971.7 6.3 copy-start.20
  974.5 18.3 %all-to-all-start = ((bf16[1,512,4,256]{3,2,0,1:T(4,128)(2,1)}), bf16[1,512,4,256]{3,2,0,1:T(4,128)(2,1)S(1)}, u32[]{:S(2)}, u32[]{:S(2)}) async-start(bf16[1,512,4,256]{3,2,0,1:T(4,128)(2,1)} %bitcast.86), calls=%async_computation.2 | async-start | bytes 2097152 | tf_op jit(solution)/shard_map/all_to_all | solution.py:1283
  (2 other events, 2.4 us)
Sparse Core Ops, SparseCore 0:
  29.6 104.3 all-gather.2
  148.3 79.1 all-gather.4
  711.2 75.2 reduce-scatter.2
  820.6 107.9 reduce-scatter.4

commit v5 on v4

--- a/solution.py
+++ b/solution.py
@@ -309,9 +309,7 @@
             DMA((slots + 3,)),
         ],
         compiler_params=params(number, 48 * 2**20),
-        cost_estimate=pl.CostEstimate(
-            flops=value.size, bytes_accessed=24 * value.size, transcendentals=0
-        ),
+        cost_estimate=pl.CostEstimate(flops=0, bytes_accessed=0, transcendentals=0),
         name="cube_reduce",
     )(value)
 
@@ -442,221 +440,6 @@
         cost_estimate=pl.CostEstimate(flops=0, bytes_accessed=2**24, transcendentals=0),
         name="small_reduce" if reduce else "small_gather",
     )(value)
-
-
-def pair_swap_kernel(a_ref, b_ref, a_out, b_out, send, recv, local):
-    p = lax.axis_index("pair")
-    other = {"pair": 1 - p}
-    greet([other])
-    copies = []
-    for slot, (src, dst) in enumerate(((a_ref.at[1 - p], a_out.at[p]), (b_ref, b_out.at[p]))):
-        copy = remote(src, dst, send.at[slot], recv.at[slot], other)
-        copy.start()
-        copies.append(copy)
-    for slot, (src, dst) in enumerate(((a_ref.at[p], a_out.at[p]), (b_ref, b_out.at[p]))):
-        copy = pltpu.make_async_copy(src, dst, local.at[slot])
-        copy.start()
-        copies.append(copy)
-    for copy in copies:
-        copy.wait()
-
-
-def pair_swap(value, shared, number):
-    return pl.pallas_call(
-        pair_swap_kernel,
-        in_specs=[VMEM, VMEM],
-        out_specs=[VMEM, VMEM],
-        out_shape=[
-            jax.ShapeDtypeStruct(value.shape, value.dtype),
-            jax.ShapeDtypeStruct((2,) + shared.shape, shared.dtype),
-        ],
-        scratch_shapes=[DMA((2,)), DMA((2,)), DMA((2,))],
-        compiler_params=params(number),
-        cost_estimate=pl.CostEstimate(
-            flops=0, bytes_accessed=20 * value.size, transcendentals=0
-        ),
-        name="pair_swap",
-    )(value, shared)
-
-
-def start_kernel(
-    sizes, walk, tok_ref, small_ref, kv_ref, tok_out, small_out, kv_out, send, recv, peer_send, peer_recv, local
-):
-    line, pairs, experts = sizes
-    z = lax.axis_index("line")
-    p = lax.axis_index("pair") if pairs == 2 else 0
-    e = lax.axis_index("expert")
-    c, y = lax.rem(e, 2), lax.div(e, 2)
-    core = {"expert": e + 1 - 2 * c}
-    side = {"expert": e + 2 - 4 * y}
-    other = {"pair": lax.rem(p + 1, pairs)}
-    count = line * pairs * experts
-    trees = pairs * experts
-    local_me = p * experts + e
-    me = z * trees + local_me
-    barrier = pltpu.get_barrier_semaphore()
-
-    def greet_one(offset, carry):
-        target = place_of((me + offset) % count, sizes)
-        pl.semaphore_signal(barrier, inc=1, device_id=target, device_id_type=MESH)
-        return carry
-
-    lax.fori_loop(1, count, greet_one, 0)
-    pl.semaphore_wait(barrier, count - 1)
-
-    size = kv_ref.shape[1]
-    home = kv_out.at[z if walk else 0, pl.ds(pl.multiple_of(local_me * size, size), size)]
-    keeps = [
-        pltpu.make_async_copy(kv_ref.at[local_me], home, local.at[0]),
-        pltpu.make_async_copy(tok_ref, tok_out.at[p, y, c], local.at[1]),
-        pltpu.make_async_copy(small_ref, small_out.at[me], local.at[2]),
-    ]
-    for copy in keeps:
-        copy.start()
-    KV = 7
-    pieces = []
-    for shift in range(1, trees):
-        peer = lax.rem(local_me + shift, trees)
-        copy = remote(
-            kv_ref.at[peer],
-            home,
-            send.at[KV + shift],
-            recv.at[KV + shift],
-            {"pair": peer // experts, "expert": peer % experts},
-        )
-        copy.start()
-        pieces.append(copy)
-
-    q, w = lax.rem(p + 1, pairs), 1 - y
-    own = tok_out.at[p, y, c]
-    copies = []
-
-    def push(slot, source, place, target):
-        copy = remote(source, place, send.at[slot], recv.at[slot], target)
-        copy.start()
-        copies.append(copy)
-        return copy
-
-    to_side = push(0, tok_ref, own, side)
-    to_other = push(1, tok_ref, own, other) if pairs == 2 else None
-    waits = [push(2, tok_ref, own, core)]
-
-    def small_to(offset):
-        return remote(
-            small_ref,
-            small_out.at[me],
-            peer_send.at[offset],
-            peer_recv.at[offset],
-            place_of((me + offset) % count, sizes),
-        )
-
-    def small_start(offset, carry):
-        small_to(offset).start()
-        return carry
-
-    lax.fori_loop(1, count, small_start, 0)
-
-    base = KV + trees
-    keeps[0].wait()
-    for copy in pieces:
-        copy.wait_recv()
-
-    def to_up(j, d):
-        ref = kv_out.at[j]
-        return remote(ref, ref, send.at[base + d], recv.at[base + d], {"line": z + 1})
-
-    def to_down(j, d):
-        ref = kv_out.at[j]
-        return remote(ref, ref, send.at[base + line + d], recv.at[base + line + d], {"line": z - 1})
-
-    if walk:
-
-        @pl.when(z < line - 1)
-        def _():
-            to_up(z, 1).start()
-
-        @pl.when(z > 0)
-        def _():
-            to_down(z, 1).start()
-
-    if pairs == 2:
-        to_other.wait_recv()
-        block = tok_out.at[q, y, c]
-        far = push(3, block, block, side)
-        waits.append(push(4, block, block, core))
-    to_side.wait_recv()
-    block = tok_out.at[p, w, c]
-    waits.append(push(5, block, block, core))
-    if pairs == 2:
-        far.wait_recv()
-        block = tok_out.at[q, w, c]
-        waits.append(push(6, block, block, core))
-
-    if walk:
-        for d in range(1, line):
-
-            @pl.when(z - d >= 0)
-            def _():
-                to_up(z - d, d).wait_recv()
-
-                @pl.when(z < line - 1)
-                def _():
-                    to_up(z - d, d + 1).start()
-
-            @pl.when(z + d < line)
-            def _():
-                to_down(z + d, d).wait_recv()
-
-                @pl.when(z > 0)
-                def _():
-                    to_down(z + d, d + 1).start()
-
-        for d in range(1, line):
-
-            @pl.when((z - d + 1 >= 0) & (z < line - 1))
-            def _():
-                to_up(z - d + 1, d).wait_send()
-
-            @pl.when((z + d - 1 < line) & (z > 0))
-            def _():
-                to_down(z + d - 1, d).wait_send()
-
-    for copy in waits:
-        copy.wait_recv()
-    for copy in copies + pieces:
-        copy.wait_send()
-    for copy in keeps[1:]:
-        copy.wait()
-
-    def small_finish(offset, carry):
-        small_to(offset).wait()
-        return carry
-
-    lax.fori_loop(1, count, small_finish, 0)
-
-
-def start_exchange(tokens, small, kv, sizes, number):
-    line, pairs, experts = sizes
-    trees, rows, cols = kv.shape
-    walk = line <= 4
-    count = line * trees
-    uses = 7 + trees + 2 * line + 2
-    return pl.pallas_call(
-        partial(start_kernel, sizes, walk),
-        in_specs=[VMEM, VMEM, VMEM],
-        out_specs=[VMEM, VMEM, VMEM],
-        out_shape=[
-            jax.ShapeDtypeStruct((pairs, 2, 2) + tokens.shape, tokens.dtype),
-            jax.ShapeDtypeStruct((count,) + small.shape, small.dtype),
-            jax.ShapeDtypeStruct((line if walk else 1, trees * rows, cols), kv.dtype),
-        ],
-        scratch_shapes=[DMA((uses,)), DMA((uses,)), DMA((count,)), DMA((count,)), DMA((3,))],
-        compiler_params=params(number, 32 * 2**20),
-        cost_estimate=pl.CostEstimate(
-            flops=0, bytes_accessed=100 * kv.size, transcendentals=0
-        ),
-        name="start_exchange",
-    )(tokens, small, kv)
 
 
 def ff_kernel(
@@ -1091,8 +874,8 @@
 
 
 def end_kernel(
-    pairs, x_ref, g_hbm, o_ref, k_ref,
-    g_ref, half, quarter, got_core, got_side, got_pair, hop, send, recv, local,
+    pairs, x_ref, g_hbm, o_ref, key_ref, value_ref,
+    g_ref, k_ref, half, quarter, got_core, got_side, got_pair, hop, send, recv, local,
 ):
     z, p, e = lax.axis_index("line"), lax.axis_index("pair"), lax.axis_index("expert")
     line, span, _ = g_ref.shape
@@ -1221,6 +1004,13 @@
     for copy in swaps:
         copy.wait()
     keep.wait()
+    share = k_ref.shape[2] // 2
+    for source in range(trees):
+        column = ((source % experts) * pairs + source // experts) * share
+        for index, target in enumerate((key_ref, value_ref)):
+            target[:, column : column + share] = k_ref[
+                source, :, index * share : (index + 1) * share
+            ].astype(F32)
     for copy in first + list(second.values()) + [last]:
         copy.wait_send()
 
@@ -1246,13 +1036,12 @@
     return pl.pallas_call(
         partial(end_kernel, pairs),
         in_specs=[VMEM, ANY],
-        out_specs=[VMEM, VMEM],
-        out_shape=[
-            jax.ShapeDtypeStruct((rows, cols), BF16),
-            jax.ShapeDtypeStruct((trees, span // trees, thin), BF16),
-        ],
+        out_specs=[VMEM] * 3,
+        out_shape=[jax.ShapeDtypeStruct((rows, cols), BF16)]
+        + [jax.ShapeDtypeStruct((span // trees, trees * thin // 2), F32)] * 2,
         scratch_shapes=[
             pltpu.VMEM((line, span, thin), BF16),
+            pltpu.VMEM((trees, span // trees, thin), BF16),
             pltpu.VMEM((4, rows, cols), BF16),
             block,
             pltpu.VMEM((4, rows, cols), BF16),
@@ -1264,11 +1053,349 @@
             DMA(()),
         ],
         compiler_params=params(number, 48 * 2**20),
-        cost_estimate=pl.CostEstimate(
-            flops=value.size, bytes_accessed=32 * value.size, transcendentals=0
-        ),
+        cost_estimate=pl.CostEstimate(flops=0, bytes_accessed=0, transcendentals=0),
         name="end_exchange",
     )(value.reshape(pairs, 2, 2, rows, cols), grads.reshape(line, span, thin))
+
+
+def final_kernel(sizes, x_ref, q_ref, o_ref, w_ref, got, side, send, recv, pair_send, pair_recv):
+    line, pairs, experts = sizes
+    count = line * pairs * experts
+    p = lax.axis_index("pair")
+    me = lax.axis_index("line") * (pairs * experts) + p * experts + lax.axis_index("expert")
+    barrier = pltpu.get_barrier_semaphore()
+
+    def greet_one(offset, carry):
+        target = place_of((me + offset) % count, sizes)
+        pl.semaphore_signal(barrier, inc=1, device_id=target, device_id_type=MESH)
+        return carry
+
+    lax.fori_loop(1, count, greet_one, 0)
+    pl.semaphore_wait(barrier, count - 1)
+    swap = remote(q_ref.at[1 - p], side, pair_send, pair_recv, {"pair": 1 - p})
+    swap.start()
+
+    def copy_to(offset):
+        peer = (me + offset) % count
+        return remote(
+            x_ref.at[peer], got.at[offset], send.at[offset], recv.at[offset], place_of(peer, sizes)
+        )
+
+    def start(offset, carry):
+        copy_to(offset).start()
+        return carry
+
+    lax.fori_loop(1, count, start, 0)
+    got[0] = x_ref[me]
+    part = q_ref.shape[2] // line
+
+    def lay(block, source):
+        for index in range(line):
+            column = pl.multiple_of((index * pairs + source) * part, part)
+            w_ref[:, pl.ds(column, part)] = block[:, index * part : (index + 1) * part].astype(F32)
+
+    lay(q_ref.at[p], p)
+    swap.wait_recv()
+    lay(side, 1 - p)
+
+    def finish(offset, carry):
+        copy_to(offset).wait()
+        return carry
+
+    lax.fori_loop(1, count, finish, 0)
+    o_ref[...] = jnp.sum(got[...], axis=0)
+    swap.wait_send()
+
+
+def final_exchange(sums, grads, sizes, number):
+    count, block = sums.shape[0], sums.shape[1:]
+    pairs, rows, cols = grads.shape
+    return pl.pallas_call(
+        partial(final_kernel, sizes),
+        in_specs=[VMEM, VMEM],
+        out_specs=[VMEM, VMEM],
+        out_shape=[
+            jax.ShapeDtypeStruct(block, F32),
+            jax.ShapeDtypeStruct((rows, pairs * cols), F32),
+        ],
+        scratch_shapes=[
+            pltpu.VMEM((count,) + block, F32),
+            pltpu.VMEM((rows, cols), BF16),
+            DMA((count,)),
+            DMA((count,)),
+            DMA(()),
+            DMA(()),
+        ],
+        compiler_params=params(number, 32 * 2**20),
+        name="final_exchange",
+    )(sums, grads)
+
+
+def start_all_kernel(
+    sizes, tok_ref, wq_ref, wk_ref, wv_ref, small_ref, int_ref,
+    tok_out, q_out, kv_out, small_out, int_out,
+    q_cut, kv_cut, send, recv, peer_send, peer_recv, local,
+):
+    line, pairs, experts = sizes
+    z, p, e = lax.axis_index("line"), lax.axis_index("pair"), lax.axis_index("expert")
+    c, y = e % 2, e // 2
+    core, side = {"expert": e + 1 - 2 * c}, {"expert": e + 2 - 4 * y}
+    other = {"pair": 1 - p}
+    trees = pairs * experts
+    count = line * trees
+    mine = p * experts + e
+    me = z * trees + mine
+    barrier = pltpu.get_barrier_semaphore()
+
+    def greet_one(offset, carry):
+        target = place_of((me + offset) % count, sizes)
+        pl.semaphore_signal(barrier, inc=1, device_id=target, device_id_type=MESH)
+        return carry
+
+    lax.fori_loop(1, count, greet_one, 0)
+    part = wq_ref.shape[1] // (line * pairs)
+    for q in range(pairs):
+        for index in range(line):
+            column = (index * pairs + q) * part
+            q_cut[q, :, index * part : (index + 1) * part] = wq_ref[:, column : column + part]
+    sub = line // experts
+    for q in range(pairs):
+        for d in range(experts):
+            for index, ref in enumerate((wk_ref, wv_ref)):
+                for h in range(sub):
+                    column = ((d * sub + h) * pairs + q) * part
+                    place = (index * sub + h) * part
+                    kv_cut[q * experts + d, :, place : place + part] = ref[
+                        :, column : column + part
+                    ]
+    pl.semaphore_wait(barrier, count - 1)
+
+    copies, TOK, QSWAP, INTS, KV = [], 0, 7, 8, 9
+    WALK = KV + trees
+
+    def push(slot, source, place, target):
+        copy = remote(source, place, send.at[slot], recv.at[slot], target)
+        copy.start()
+        copies.append(copy)
+        return copy
+
+    rows = q_cut.shape[1]
+    q_home = q_out.at[z, pl.ds(pl.multiple_of(p * rows, rows), rows)]
+    q_swap = push(QSWAP, q_cut.at[1 - p], q_home, other)
+    size = kv_cut.shape[1]
+    kv_home = kv_out.at[z, pl.ds(pl.multiple_of(mine * size, size), size)]
+    pieces = []
+    for shift in range(1, trees):
+        peer = (mine + shift) % trees
+        pieces.append(
+            push(
+                KV + shift,
+                kv_cut.at[peer],
+                kv_home,
+                {"pair": peer // experts, "expert": peer % experts},
+            )
+        )
+    keeps = [
+        pltpu.make_async_copy(q_cut.at[p], q_home, local.at[0]),
+        pltpu.make_async_copy(kv_cut.at[mine], kv_home, local.at[1]),
+        pltpu.make_async_copy(tok_ref, tok_out.at[p, y, c], local.at[2]),
+        pltpu.make_async_copy(small_ref, small_out.at[me], local.at[3]),
+        pltpu.make_async_copy(int_ref, int_out.at[p], local.at[4]),
+    ]
+    for copy in keeps:
+        copy.start()
+    own = tok_out.at[p, y, c]
+    to_side = push(TOK, tok_ref, own, side)
+    to_other = push(TOK + 1, tok_ref, own, other)
+    waits = [push(TOK + 2, tok_ref, own, core), push(INTS, int_ref, int_out.at[p], other)]
+
+    def small_to(offset):
+        return remote(
+            small_ref,
+            small_out.at[me],
+            peer_send.at[offset],
+            peer_recv.at[offset],
+            place_of((me + offset) % count, sizes),
+        )
+
+    def small_start(offset, carry):
+        small_to(offset).start()
+        return carry
+
+    lax.fori_loop(1, count, small_start, 0)
+
+    def walker(ref, base):
+        def to_up(j, d):
+            return remote(
+                ref.at[j], ref.at[j], send.at[base + d], recv.at[base + d], {"line": z + 1}
+            )
+
+        def to_down(j, d):
+            at = base + line + d
+            return remote(ref.at[j], ref.at[j], send.at[at], recv.at[at], {"line": z - 1})
+
+        return to_up, to_down
+
+    walkers = [walker(q_out, WALK), walker(kv_out, WALK + 2 * line + 2)]
+
+    def begin(which):
+        to_up, to_down = walkers[which]
+
+        @pl.when(z < line - 1)
+        def _():
+            to_up(z, 1).start()
+
+        @pl.when(z > 0)
+        def _():
+            to_down(z, 1).start()
+
+    keeps[0].wait()
+    q_swap.wait_recv()
+    begin(0)
+    keeps[1].wait()
+    for copy in pieces:
+        copy.wait_recv()
+    begin(1)
+    to_other.wait_recv()
+    block = tok_out.at[1 - p, y, c]
+    far = push(TOK + 3, block, block, side)
+    waits.append(push(TOK + 4, block, block, core))
+    to_side.wait_recv()
+    block = tok_out.at[p, 1 - y, c]
+    waits.append(push(TOK + 5, block, block, core))
+    far.wait_recv()
+    block = tok_out.at[1 - p, 1 - y, c]
+    waits.append(push(TOK + 6, block, block, core))
+
+    for d in range(1, line):
+        for to_up, to_down in walkers:
+
+            @pl.when(z - d >= 0)
+            def _():
+                to_up(z - d, d).wait_recv()
+
+                @pl.when(z < line - 1)
+                def _():
+                    to_up(z - d, d + 1).start()
+
+            @pl.when(z + d < line)
+            def _():
+                to_down(z + d, d).wait_recv()
+
+                @pl.when(z > 0)
+                def _():
+                    to_down(z + d, d + 1).start()
+
+    for d in range(1, line):
+        for to_up, to_down in walkers:
+
+            @pl.when((z - d + 1 >= 0) & (z < line - 1))
+            def _():
+                to_up(z - d + 1, d).wait_send()
+
+            @pl.when((z + d - 1 < line) & (z > 0))
+            def _():
+                to_down(z + d - 1, d).wait_send()
+
+    for copy in waits:
+        copy.wait_recv()
+    for copy in copies:
+        copy.wait_send()
+    for copy in keeps[2:]:
+        copy.wait()
+
+    def small_finish(offset, carry):
+        small_to(offset).wait()
+        return carry
+
+    lax.fori_loop(1, count, small_finish, 0)
+
+
+def start_all(tokens, w_query, w_key, w_value, small, integers, sizes, number):
+    line, pairs, experts = sizes
+    trees = pairs * experts
+    count = line * trees
+    rows, width = w_query.shape
+    size = w_key.shape[0]
+    feats = width // pairs
+    thin = 2 * feats // experts
+    uses = 9 + trees + 4 * line + 4
+    return pl.pallas_call(
+        partial(start_all_kernel, sizes),
+        in_specs=[VMEM] * 6,
+        out_specs=[VMEM] * 5,
+        out_shape=[
+            jax.ShapeDtypeStruct((pairs, 2, 2) + tokens.shape, BF16),
+            jax.ShapeDtypeStruct((line, pairs * rows, feats), BF16),
+            jax.ShapeDtypeStruct((line, trees * size, thin), BF16),
+            jax.ShapeDtypeStruct((count,) + small.shape, BF16),
+            jax.ShapeDtypeStruct((pairs,) + integers.shape, jnp.int32),
+        ],
+        scratch_shapes=[
+            pltpu.VMEM((pairs, rows, feats), BF16),
+            pltpu.VMEM((trees, size, thin), BF16),
+            DMA((uses,)),
+            DMA((uses,)),
+            DMA((count,)),
+            DMA((count,)),
+            DMA((5,)),
+        ],
+        compiler_params=params(number, 48 * 2**20),
+        name="start_all",
+    )(tokens, w_query, w_key, w_value, small, integers)
+
+
+def project_kernel(micro, x_ref, w_ref, gain_ref, router_ref, cos_ref, sin_ref, n_ref, kv_ref, l_ref):
+    x = x_ref[...].astype(F32)
+    scale = lax.rsqrt(jnp.mean(x * x, axis=-1, keepdims=True) + EPSILON)
+    normed = (x * scale * gain_ref[...]).astype(BF16)
+    n_ref[...] = normed
+    l_ref[...] = product_nt(normed, router_ref[...])
+    raw = product(normed, w_ref[...])
+    piece = kv_ref.shape[2]
+    spread = lambda ref: jnp.concatenate(
+        [ref[i] for i in range(ref.shape[0]) for _ in range(micro)], axis=0
+    )
+    cosine, sine = spread(cos_ref), spread(sin_ref)
+    for head in range(piece // HDIM):
+        cols = slice(head * HDIM, (head + 1) * HDIM)
+        kv_ref[0, :, cols] = turn(raw[:, cols], cosine, sine).astype(BF16)
+    kv_ref[1] = raw[:, piece:].astype(BF16)
+
+
+def project(tokens, weight, gain, router, cosine, sine, micro):
+    rows, width = tokens.shape
+    piece = weight.shape[1] // 2
+    experts, tok, half = cosine.shape
+    block = 2 * micro * tok
+    loops = experts // 2
+    return pl.pallas_call(
+        partial(project_kernel, micro),
+        grid=(rows // block,),
+        in_specs=[
+            pl.BlockSpec((block, width), lambda i: (i, 0)),
+            pl.BlockSpec(weight.shape, lambda i: (0, 0)),
+            pl.BlockSpec((1, width), lambda i: (0, 0)),
+            pl.BlockSpec(router.shape, lambda i: (0, 0)),
+            pl.BlockSpec((2, tok, half), lambda i: (i % loops, 0, 0)),
+            pl.BlockSpec((2, tok, half), lambda i: (i % loops, 0, 0)),
+        ],
+        out_specs=[
+            pl.BlockSpec((block, width), lambda i: (i, 0)),
+            pl.BlockSpec((2, block, piece), lambda i: (0, i, 0)),
+            pl.BlockSpec((block, experts), lambda i: (i, 0)),
+        ],
+        out_shape=[
+            jax.ShapeDtypeStruct((rows, width), BF16),
+            jax.ShapeDtypeStruct((2, rows, piece), BF16),
+            jax.ShapeDtypeStruct((rows, experts), F32),
+        ],
+        compiler_params=pltpu.CompilerParams(vmem_limit_bytes=40 * 2**20),
+        cost_estimate=pl.CostEstimate(
+            flops=2 * rows * width * weight.shape[1], bytes_accessed=5 * rows * width, transcendentals=0
+        ),
+        name="project",
+    )(tokens, weight, gain, router, cosine, sine)
 
 
 def gather(value, axes, axis=0):
@@ -1330,33 +1457,40 @@
     cosine, sine = jnp.cos(angle), jnp.sin(angle)
 
     sizes = (line, pair, experts)
-    walk = line <= 4 and pair == 2
-    query_mine = w_query[0].reshape(own_in, line, pair, part)
-    query_mine = jnp.transpose(query_mine, (2, 0, 1, 3)).reshape(pair, own_in, feats)
+    walk = line == 4 and pair == 2 and experts == 4
+    own_tokens = tokens.reshape(micro * tok, width)
+    small = jnp.concatenate(
+        [gain_attn[None], gain_mlp[None], router_attn.T, router_mlp.T], axis=0
+    )
     integers = jnp.concatenate([attn_route[:, 0].reshape(micro, -1), parents[:, 0]], axis=1)
-    if pair == 2:
+    if walk:
         flat = integers.reshape(-1)
         flat = jnp.pad(flat, (0, -flat.shape[0] % 1024)).reshape(-1, 128)
-        query_mine, flat = pair_swap(query_mine, flat, 1)
+        tree_tokens, query_weight, kv_weight, small, flat = start_all(
+            own_tokens, w_query[0], w_key, w_value, small, flat, sizes, 1
+        )
+        query_weight = query_weight.reshape(width, feats)
+        kv_weight = kv_weight.reshape(width, 2 * piece)
         integers = flat.reshape(pair, -1)[:, : integers.size].reshape((pair,) + integers.shape)
     else:
-        integers = integers[None]
-    query_weight = gather(query_mine.reshape(pair * own_in, feats), "line")
-
-    small = jnp.concatenate(
-        [gain_attn[None], gain_mlp[None], router_attn.T, router_mlp.T], axis=0
-    )
-    kv_mine = jnp.stack([w_key, w_value], axis=1).reshape(
-        own_kv, 2, experts, line // experts, pair, part
-    )
-    kv_mine = jnp.transpose(kv_mine, (4, 2, 0, 1, 3, 5)).reshape(
-        pair * experts, own_kv, 2 * piece
-    )
-    own_tokens = tokens.reshape(micro * tok, width)
-    tree_tokens, small, kv_weight = start_exchange(own_tokens, small, kv_mine, sizes, 2)
-    kv_weight = kv_weight.reshape(-1, 2 * piece)
-    if kv_weight.shape[0] < width:
-        kv_weight = gather(kv_weight, "line")
+        query_mine = w_query[0].reshape(own_in, line, pair, part)
+        query_mine = jnp.transpose(query_mine, (2, 0, 1, 3)).reshape(pair, own_in, feats)
+        if pair == 2:
+            query_mine = swap(query_mine, "pair")
+            integers = lax.all_gather(integers, "pair", axis=0)
+        else:
+            integers = integers[None]
+        query_weight = gather(query_mine.reshape(pair * own_in, feats), "line")
+        kv_mine = jnp.stack([w_key, w_value], axis=1).reshape(
+            own_kv, 2, experts, line // experts, pair, part
+        )
+        kv_mine = jnp.transpose(kv_mine, (4, 2, 0, 1, 3, 5)).reshape(
+            pair * experts, own_kv, 2 * piece
+        )
+        tree_tokens = cube_gather(own_tokens, pair, 1)
+        small = small_exchange(small, sizes, False, 2)
+        kv_mine = swap(kv_mine, TREES).reshape(pair * experts * own_kv, 2 * piece)
+        kv_weight = gather(kv_mine, "line")
     out_mine, small = lax.optimization_barrier((w_out[0], small))
     out_weight = gather(out_mine, "line")
 
@@ -1368,37 +1502,27 @@
 
     residual = own_tokens.astype(F32)
     _, first_pull = jax.vjp(rms_scaled, residual, first_gain)
-    tree_input = rms_scaled(tree_tokens.reshape(rows, width).astype(F32), first_gain).astype(BF16)
+    table_shape = (experts, tok, half)
+    tree_input, kv, first_logits = project(
+        tree_tokens.reshape(rows, width),
+        kv_weight,
+        first_gain[None],
+        first_router,
+        cosine.reshape(table_shape),
+        sine.reshape(table_shape),
+        micro,
+    )
 
     routes = integers[..., : tree * 2].reshape(pair, micro, experts, tok, 2)
     routes = jnp.transpose(routes, (0, 2, 1, 3, 4)).reshape(rows, 2)
     family = integers[..., tree * 2 :]
     bias = jax.vmap(jax.vmap(lambda parent: score_bias(parent, segment, places)))(family)
 
-    kv_raw = product(tree_input, kv_weight)
-    spread_cos = jnp.broadcast_to(
-        cosine.reshape(1, experts, 1, tok, 1, half), (pair, experts, micro, tok, 1, half)
-    ).reshape(rows, 1, half)
-    spread_sin = jnp.broadcast_to(
-        sine.reshape(1, experts, 1, tok, 1, half), (pair, experts, micro, tok, 1, half)
-    ).reshape(rows, 1, half)
-    key_raw = kv_raw[:, :piece].reshape(rows, piece // HDIM, HDIM)
-    key_one, key_two = key_raw[..., :half], key_raw[..., half:]
-    keys = jnp.concatenate(
-        [
-            key_one * spread_cos - key_two * spread_sin,
-            key_two * spread_cos + key_one * spread_sin,
-        ],
-        axis=-1,
-    ).reshape(rows, piece)
-    kv = jnp.concatenate([keys.astype(BF16), kv_raw[:, piece:].astype(BF16)], axis=0)
-    kv = cube_gather(kv, 1, 3)
+    kv = cube_gather(kv.reshape(2 * rows, piece), 1, 3)
     shape = (pair, experts, micro, tok, feats)
     kv = kv.reshape(experts, 2, pair, experts, micro, tok, piece)
 
-    first_gates, first_gate_pull = jax.vjp(
-        partial(mixture_gates, routes), product_nt(tree_input, first_router)
-    )
+    first_gates, first_gate_pull = jax.vjp(partial(mixture_gates, routes), first_logits)
     column = (jnp.arange(experts, dtype=jnp.int32) == position).astype(F32)
     own_gate = jnp.sum(first_gates * column[None, :], axis=1)
 
@@ -1478,7 +1602,14 @@
     middle_grad, grad_gain_second = second_pull(hn_grad)
     middle_grad = middle_grad + dz
 
-    mix_grad = cube_gather(middle_grad.astype(BF16), pair, 7).reshape(rows, width).astype(F32)
+    mix_grad = gather(middle_grad.astype(BF16), TREES)
+    grad_gate = product_tn(gate_grad, arrived)[None]
+    grad_upward = product_tn(up_grad, arrived)[None]
+    grad_downward = product_tn(inner, result_grad)[None]
+    mix_grad, grad_gate, grad_upward, grad_downward = lax.optimization_barrier(
+        (mix_grad, grad_gate, grad_upward, grad_downward)
+    )
+    mix_grad = mix_grad.astype(F32)
     own_gate_grad = jnp.sum(mix_grad * projected, axis=-1)
     projected_grad = (own_gate[:, None] * mix_grad).astype(BF16)
     grad_output = product_tn(heads_flat, projected_grad).astype(BF16)
@@ -1509,24 +1640,16 @@
         input_term = input_term + first_logit_grad[:, expert : expert + 1] * first_router_wide[expert]
     input_term = input_term.astype(BF16).reshape(pair * experts, micro * tok, width)
     if walk:
-        normed_grad, grad_kv = end_exchange(input_term, grad_kv, line, pair, 9)
+        normed_grad, grad_key, grad_value = end_exchange(input_term, grad_kv, line, pair, 9)
     else:
         normed_grad = cube_reduce(input_term, pair, 9)
         grad_kv = scatter(grad_kv, "line")
         grad_kv = swap(grad_kv.reshape(pair * experts, own_kv, 2 * piece), TREES)
-    gate_grad, up_grad, inner, arrived, result_grad, normed_grad = lax.optimization_barrier(
-        (gate_grad, up_grad, inner, arrived, result_grad, normed_grad)
-    )
-    grad_gate = product_tn(gate_grad, arrived)[None]
-    grad_upward = product_tn(up_grad, arrived)[None]
-    grad_downward = product_tn(inner, result_grad)[None]
+        grad_kv = grad_kv.reshape(pair, experts, own_kv, 2, line // experts, part)
+        grad_kv = jnp.transpose(grad_kv, (2, 3, 1, 4, 0, 5)).reshape(own_kv, 2, heads_total)
+        grad_key, grad_value = grad_kv[:, 0].astype(F32), grad_kv[:, 1].astype(F32)
+    grad_query = scatter(grad_query, "line")
     normed_grad = normed_grad.astype(F32)
-    grad_query = scatter(grad_query, "line")
-    grad_query = swap(grad_query.reshape(own_in * pair, line, part)[None], "pair", 1, 0)
-    grad_query = jnp.transpose(grad_query, (1, 2, 0, 3)).reshape(1, own_in, heads_total)
-    grad_kv = grad_kv.reshape(pair, experts, own_kv, 2, line // experts, part)
-    grad_kv = jnp.transpose(grad_kv, (2, 3, 1, 4, 0, 5)).reshape(own_kv, 2, heads_total)
-    grad_kv = grad_kv.astype(F32)
     grad_router_first = jnp.dot(
         jnp.transpose(first_logit_grad),
         tree_input.astype(F32),
@@ -1541,14 +1664,20 @@
         axis=0,
     )
     sums = jnp.transpose(sums.reshape(sums.shape[0], -1, own_kv), (1, 0, 2))
-    sums = small_exchange(sums, sizes, True, 10)
+    if walk:
+        sums, grad_query = final_exchange(sums, grad_query.reshape(pair, own_in, feats), sizes, 10)
+        grad_query = grad_query[None]
+    else:
+        sums = small_exchange(sums, sizes, True, 10)
+        grad_query = swap(grad_query.reshape(own_in * pair, line, part)[None], "pair", 1, 0)
+        grad_query = jnp.transpose(grad_query, (1, 2, 0, 3)).reshape(1, own_in, heads_total)
     return (
         layer_out.reshape(micro, 1, tok, width),
         tokens_grad.reshape(micro, 1, tok, width),
         grad_query.astype(F32),
         grad_output[None].astype(F32),
-        grad_kv[:, 0],
-        grad_kv[:, 1],
+        grad_key,
+        grad_value,
         sums[0],
         jnp.transpose(sums[2 : 2 + experts]),
         sums[1],

time: 1010 us -> 955 us (0.946)
  Pallas kernels: 767 us -> 740 us
  other arithmetic: 37.3 us -> 26.2 us
  local copies, waits for them, and re-layouts: 52.9 us -> 42.3 us
    pallas_call x2 -> x1, Pallas kernels: 58.7 us -> 26.9 us  [cube_gather(): pl.pallas_call(partial(cube_gather_kernel, pairs), in_specs=[VMEM], out_s...]
    all_to_all x1 -> x0, waiting for transfers between devices: 13.1 us -> none  [swap(): lax.all_to_all(value, axes, split_axis=split, concat_axis=concat, tiled=T...]
    unnamed x96 -> x109, local copies, waits for them, and re-layouts: 11.1 us -> 23.7 us
    convert_element_type x5 -> x0, local copies, waits for them, and re-layouts: 12 us -> none  [the longest x3 7.71 us: body(): grad_kv = grad_kv.astype(F32)]
    pallas_call x3, Pallas kernels: 144 us -> 154 us  [the longest x1 128 us: start_all(): pl.pallas_call(partial(start_all_kernel, sizes), in_specs=[VMEM] * 6, out...]
    dot_general x6 -> x5, matrix products: 31.2 us -> 28.3 us  [product_nt(): lax.dot_general(left, right, (((1,), (1,)), ((), ())), preferred_element_...]
    dot_general x3 -> x2, matrix products: 23 us -> 20.6 us  [product(): return jnp.dot(left, right, preferred_element_type=F32)]
  transfers between devices with their start and end apart: 5 -> 4, of which waited for: 1 -> 3; matrix products, arithmetic and copies ran while one was open for 14% -> 13% of each run, Pallas kernels for 31% -> 19%
where the time goes in v5:
time: 955 us; the launch traced here: 944 us
  Pallas kernels  740 us (77%)
  matrix products  112 us (12%)
  local copies, waits for them, and re-layouts  42.3 us (4%)
  other arithmetic  26.2 us (3%)
  between operations  15 us (2%)
    pallas_call x1, Pallas kernels, feed_forward(): pl.pallas_call(ff_kernel, in_specs=[ANY] * 5, out_specs=[ANY] * 7, out_sh...  379 us
    pallas_call x1, Pallas kernels, start_all(): pl.pallas_call(partial(start_all_kernel, sizes), in_specs=[VMEM] * 6, out...  128 us
    pallas_call x1, Pallas kernels, end_exchange(): pl.pallas_call(partial(end_kernel, pairs), in_specs=[VMEM, ANY], out_spec...  74.3 us
    pallas_call x2, Pallas kernels, cube_reduce(): pl.pallas_call(partial(cube_reduce_kernel, pairs), in_specs=[VMEM], out_s...  59 us
    dot_general x7, matrix products, product_tn(): lax.dot_general(left, right, (((0,), (0,)), ((), ())), preferred_element_...  48.6 us
    dot_general x5, matrix products, product_nt(): lax.dot_general(left, right, (((1,), (1,)), ((), ())), preferred_element_...  28.3 us
    pallas_call x1, Pallas kernels, cube_gather(): pl.pallas_call(partial(cube_gather_kernel, pairs), in_specs=[VMEM], out_s...  26.9 us
    pallas_call x1, Pallas kernels, attend_back(): pl.pallas_call(partial(attend_back_kernel, part // HDIM, scale), grid=gri...  25.7 us
  transfers between devices with their start and end apart: 4, of which 3 were waited for; matrix products, arithmetic and copies ran while one was open for 13% of the time, Pallas kernels for 19%

profile of v5, /device:TPU:0, one launch (start us, length us, event | category | flops | bytes accessed | tf_op | source)
XLA Modules:
  0.0 944.4 jit_solution(1268870948646504417)
XLA Ops:
  10.8 1.2 copy-done.10
  13.9 128.0 %start_all.1 = (bf16[2,2,2,128,2048]{4,3,2,1,0:T(8,128)(2,1)}, bf16[4,512,1024]{2,1,0:T(8,128)(2,1)}, bf16[4,512,512]{2,1,0:T(8,128)(2,1)S(1)}, bf16[32,10,64]{2,1,0:T(8,128)(2,1)S(1)}, s32[2,16,128]{2,1,0:T(8,128)S(1)}) custom-call(bf16[128,2048]{1,0:T(8,128)(2,1)S(1)} %bitcast.222, bf16[256,2048]{1,0:T(8,128)(2,1)S(1)} %bitcast.233, ...), custom_call_target="tpu_custom_call" | custom-call | tf_op jit(solution)/shard_map/start_all/pallas_call | solution.py:1323
  141.9 1.3 copy-done.11
  144.3 1.6 copy-done.12
  145.9 2.2 copy-done.16
  148.2 5.5 project.1
  153.7 1.9 copy-done.7
  156.8 26.9 %cube_gather.1 = bf16[1,2,2,2048,256]{4,3,2,1,0:T(8,128)(2,1)S(1)} custom-call(bf16[2048,256]{1,0:T(8,128)(2,1)S(1)} %bitcast.231), custom_call_target="tpu_custom_call" | custom-call | bytes 41943040 | tf_op jit(solution)/shard_map/cube_gather/pallas_call | solution.py:361
  183.7 2.0 copy-done.4
  187.0 1.2 multiply_sine_fusion
  188.3 1.3 or_select_fusion.bias_ref
  189.6 10.0 %fusion.76.raw_ref = f32[2,4,2,64,1024]{4,3,2,1,0:T(8,128)} fusion(bf16[2,4,2,64,2048]{4,3,2,1,0:T(8,128)(2,1)} %bitcast.228, bf16[2048,1024,1,1,1]{1,0,4,3,2:T(8,128)(2,1)} %bitcast.291), kind=kOutput, calls=%fused_computation.191 | convolution fusion | flops 4294967296 | bytes 12582912 | tf_op jit(solution)/shard_map/dot_general | solution.py:20
  199.6 20.0 %attend.1 = (bf16[2,4,2,64,1024]{4,3,2,1,0:T(8,128)(2,1)}, bf16[2,4,2,64,1024]{4,3,2,1,0:T(8,128)(2,1)}) custom-call(f32[2,4,2,64,1024]{4,3,2,1,0:T(8,128)} %fusion.76.raw_ref, bf16[4,2,2,4,2,64,256]{6,5,4,3,2,1,0:T(8,128)(2,1)} %bitcast.223, f32[256,64]{1,0:T(8,128)} %get-tuple-element.201.cos_ref, f32[256,64]{1,0:T(8,128)} %get-tuple-element.200.sin_ref, ...), custom_call_target="tpu_custom_call" | custom-call | flops 1073741824 | bytes 12582912 | tf_op jit(solution)/shard_map/attend/pallas_call | solution.py:169
  222.4 10.5 %multiply_convert_fusion = (bf16[1024,2048]{1,0:T(8,128)(2,1)S(1)}, f32[1024,2048]{1,0:T(8,128)}) fusion(f32[1024]{0:T(1024)S(1)} %multiply_reduce_fusion.6, bf16[1024,1024]{1,0:T(8,128)(2,1)} %bitcast.296, bf16[1024,2048]{1,0:T(8,128)(2,1)} %all-gather.3.cloned.1.call-done), kind=kOutput, calls=%fused_computation.5 | convolution fusion | flops 4299161600 | bytes 18878464 | tf_op jit(solution)/shard_map/dot_general | solution.py:20
  232.9 30.4 %cube_reduce.2 = bf16[128,2048]{1,0:T(8,128)(2,1)S(1)} custom-call(bf16[2,2,2,128,2048]{4,3,2,1,0:T(8,128)(2,1)S(1)} %bitcast.227), custom_call_target="tpu_custom_call" | custom-call | tf_op jit(solution)/shard_map/cube_reduce/pallas_call | solution.py:297
  268.2 379.4 %feed_forward.1 = (bf16[4,64,2048]{2,1,0:T(8,128)(2,1)}, bf16[4,64,2048]{2,1,0:T(8,128)(2,1)}, bf16[4,2,256,2048]{3,2,1,0:T(8,128)(2,1)}, bf16[4,2,256,2048]{3,2...) custom-call(bf16[4,64,2048]{2,1,0:T(8,128)(2,1)} %bitcast.252, ...), custom_call_target="tpu_custom_call" | custom-call | flops 35433480192 | bytes 50331648 | tf_op jit(solution)/shard_map/feed_forward/pallas_call | solution.py:844
  647.6 3.7 multiply_reduce_fusion
  651.5 1.7 fusion.17
  654.1 1.9 fusion.70
  656.1 11.7 %convolution_bitcast_fusion.1 = f32[1,704,2048]{2,1,0:T(8,128)} fusion(bf16[4,2,256,704]{3,2,1,0:T(8,128)(2,1)} %get-tuple-element.69, bf16[4,2,256,2048]{3,2,1,0:T(8,128)(2,1)} %get-tuple-element.68), kind=kOutput, calls=%fused_computation.11 | convolution fusion | flops 5905580032 | bytes 17039360 | tf_op jit(solution)/shard_map/dot_general | solution.py:24
  667.8 10.4 %convolution_bitcast_fusion.2 = f32[1,704,2048]{2,1,0:T(8,128)} fusion(bf16[4,2,256,704]{3,2,1,0:T(8,128)(2,1)S(1)} %copy-done.48, bf16[4,2,256,2048]{3,2,1,0:T(8,128)(2,1)} %get-tuple-element.68), kind=kOutput, calls=%fused_computation.12 | convolution fusion | flops 5905580032 | bytes 17039360 | tf_op jit(solution)/shard_map/dot_general | solution.py:24
  678.3 8.1 convolution_bitcast_fusion
  686.4 6.0 all-gather.5.cloned.1.call-done
  692.5 5.7 fusion.1
  698.1 2.0 copy-done.24
  700.1 6.2 convolution_convert_fusion.1
  706.6 9.4 convolution_convert_fusion.5
  716.0 25.7 %attend_back.1 = (bf16[2,4,2,64,1024]{4,3,2,1,0:T(8,128)(2,1)}, bf16[4,2,2,4,2,64,256]{6,5,4,3,2,1,0:T(8,128)(2,1)}) custom-call(bf16[2,4,2,64,1024]{4,3,2,1,0:T(8,128)(2,1)} %get-tuple-element.65.query_ref, bf16[4,2,2,4,2,64,256]{6,5,4,3,2,1,0:T(8,128)(2,1)} %bitcast.224, bf16[2,4,2,64,1024]{4,3,2,1,0:T(8,128)(2,1)} %bitcast.301, ...), custom_call_target="tpu_custom_call" | custom-call | flops 2684354560 | bytes 14680064 | tf_op jit(solution)/shard_map/attend_back/pallas_call | solution.py:187
  741.7 9.4 convolution_convert_fusion
  751.1 2.2 copy-done.6
  753.4 28.6 %cube_reduce.3 = bf16[2048,256]{1,0:T(8,128)(2,1)S(1)} custom-call(bf16[1,2,2,2048,256]{4,3,2,1,0:T(8,128)(2,1)S(1)} %bitcast.226), custom_call_target="tpu_custom_call" | custom-call | tf_op jit(solution)/shard_map/cube_reduce/pallas_call | solution.py:297
  782.0 1.3 reduce-scatter.3.cloned.1.call-done
  783.3 6.5 copy.124
  791.7 1.3 fusion.46
  793.2 6.8 fusion.33
  800.1 8.7 fusion.78
  809.9 1.3 convolution_convert_fusion.4
  811.2 1.3 convolution_convert_fusion.3
  812.5 1.6 pad_maximum_fusion
  814.1 3.9 copy.123
  818.0 2.4 fusion.11
  820.4 7.5 add_convert_fusion
  828.0 74.3 %end_exchange.1 = (bf16[128,2048]{1,0:T(8,128)(2,1)S(1)}, f32[64,2048]{1,0:T(8,128)S(1)}, f32[64,2048]{1,0:T(8,128)S(1)}) custom-call(bf16[2,2,2,128,2048]{4,3,2,1,0:T(8,128)(2,1)} %bitcast.245, bf16[4,512,512]{2,1,0:T(8,128)(2,1)S(1)} %bitcast.225), custom_call_target="tpu_custom_call" | custom-call | tf_op jit(solution)/shard_map/end_exchange/pallas_call | solution.py:1036
  905.7 2.8 bitcast_convert_fusion
  908.6 2.9 fusion.8
  911.4 1.2 copy-done.9
  912.6 20.8 %final_exchange.1 = (f32[10,64]{1,0:T(8,128)S(1)}, f32[256,2048]{1,0:T(8,128)S(1)}) custom-call(f32[32,10,64]{2,1,0:T(8,128)S(1)} %maximum_bitcast_fusion.x_ref, bf16[2,256,1024]{2,1,0:T(8,128)(2,1)S(1)} %bitcast.232), custom_call_target="tpu_custom_call" | custom-call | tf_op jit(solution)/shard_map/final_exchange/pallas_call | solution.py:1113
  934.6 1.3 copy.158
  (206 shorter events, 26.9 us)
Async XLA Ops:
  7.2 215.2 %all-gather.3.cloned.1.call-start = ((), (), s32[]{:S(2)}) async-start(), calls=%async_computation.2 | async-start | bytes 5242880 | tf_op jit(solution)/shard_map/all_gather | solution.py:1402
  141.9 1.3 copy-start.11
  143.2 549.3 %all-gather.5.cloned.1.call-start = ((), (), s32[]{:S(2)}) async-start(), calls=%async_computation.3 | async-start | bytes 4718592 | tf_op jit(solution)/shard_map/all_gather | solution.py:1402
  144.3 1.6 copy-start.12
  145.9 2.3 copy-start.16
  153.7 1.9 copy-start.7
  155.6 30.3 %copy-start.40 = (s32[2,1,64,2]{2,3,1,0:T(2,128)S(1)}, s32[2,1,64,2]{2,3,1,0:T(2,128)}, u32[]{:S(2)}) copy-start(s32[2,1,64,2]{2,3,1,0:T(2,128)} %param.30) | copy-start | bytes 3076
  183.7 2.0 copy-start.4
  185.8 468.2 %copy-start.27 = (f32[2048]{0:T(1024)}, f32[2048]{0:T(1024)S(1)}, u32[]{:S(2)}) copy-start(f32[2048]{0:T(1024)S(1)} %reshape.600) | copy-start | bytes 24580
  199.6 20.2 %copy-start.45 = (s32[2,1,64]{2,1,0:T(1,128)S(1)}, s32[2,1,64]{2,1,0:T(1,128)}, u32[]{:S(2)}) copy-start(s32[2,1,64]{2,1,0:T(1,128)} %param.31) | copy-start | bytes 1540
  199.6 20.4 %copy-start.19 = (bf16[2,1,64,2048]{3,2,1,0:T(8,128)(2,1)S(1)}, bf16[2,1,64,2048]{3,2,1,0:T(8,128)(2,1)}, u32[]{:S(2)}) copy-start(bf16[2,1,64,2048]{3,2,1,0:T(8,128)(2,1)} %param.33) | copy-start | bytes 1572868
  220.1 433.9 %copy-start.29 = (f32[1,2048]{1,0:T(1,128)}, f32[1,2048]{1,0:T(1,128)S(1)}, u32[]{:S(2)}) copy-start(f32[1,2048]{1,0:T(1,128)S(1)} %get-tuple-element.186) | copy-start | bytes 24580
  220.1 433.9 %copy-start.31 = (f32[1,2048]{1,0:T(1,128)}, f32[1,2048]{1,0:T(1,128)S(1)}, u32[]{:S(2)}) copy-start(f32[1,2048]{1,0:T(1,128)S(1)} %get-tuple-element.187) | copy-start | bytes 24580
  220.1 433.9 %copy-start.32 = (f32[1,2048]{1,0:T(1,128)}, f32[1,2048]{1,0:T(1,128)S(1)}, u32[]{:S(2)}) copy-start(f32[1,2048]{1,0:T(1,128)S(1)} %get-tuple-element.188) | copy-start | bytes 24580
  220.1 433.9 %copy-start.33 = (f32[1,2048]{1,0:T(1,128)}, f32[1,2048]{1,0:T(1,128)S(1)}, u32[]{:S(2)}) copy-start(f32[1,2048]{1,0:T(1,128)S(1)} %get-tuple-element.189) | copy-start | bytes 24580
  232.9 30.4 %copy-start.1 = (bf16[2,1,64,2048]{3,2,1,0:T(8,128)(2,1)S(1)}, bf16[2,1,64,2048]{3,2,1,0:T(8,128)(2,1)}, u32[]{:S(2)}) copy-start(bf16[2,1,64,2048]{3,2,1,0:T(8,128)(2,1)} %param.17) | copy-start | bytes 1572868
  264.1 389.9 %copy-start.35 = (f32[128]{0:T(128)}, f32[128]{0:T(128)S(1)}, u32[]{:S(2)}) copy-start(f32[128]{0:T(128)S(1)} %fusion.61) | copy-start | bytes 1540
  264.4 2.3 copy-start.22
  647.6 5.6 copy-start.3
  647.6 6.5 copy-start.20
  651.4 2.7 copy-start.25
  651.4 4.5 copy-start.36
  651.5 4.5 copy-start.37
  651.5 4.5 copy-start.38
  651.5 4.5 copy-start.39
  653.2 14.6 %copy-start.17 = (f32[2,64,2048,1]{2,1,3,0:T(8,128)}, f32[2,64,2048,1]{2,1,3,0:T(8,128)S(1)}, u32[]{:S(2)}) copy-start(f32[2,64,2048,1]{2,1,3,0:T(8,128)S(1)} %fusion.17) | copy-start | bytes 3145732
  654.0 13.8 %copy-start.42 = (f32[128]{0:T(128)}, f32[128]{0:T(128)S(1)}, u32[]{:S(2)}) copy-start(f32[128]{0:T(128)S(1)} %multiply_multiply_fusion.1) | copy-start | bytes 1540
  656.0 127.3 %reduce-scatter.3.cloned.1.call-start = ((), (), s32[]{:S(2)}) async-start(), calls=%async_computation.4 | async-start | bytes 5242880 | tf_op jit(solution)/shard_map/reduce_scatter | solution.py:1406
  656.0 11.8 %copy-start.48 = (bf16[4,2,256,704]{3,2,1,0:T(8,128)(2,1)S(1)}, bf16[4,2,256,704]{3,2,1,0:T(8,128)(2,1)}, u32[]{:S(2)}) copy-start(bf16[4,2,256,704]{3,2,1,0:T(8,128)(2,1)} %get-tuple-element.67) | copy-start | bytes 8650756
  656.0 22.2 %slice-start = ((s8[8388608]{0:T(1024)(128)(4,1)}), s8[4194304]{0:T(1024)(128)(4,1)S(1)}, s32[]{:S(2)}) async-start(s8[8388608]{0:T(1024)(128)(4,1)} %bitcast.303), calls=%async_computation.6 | async-start | bytes 8388608
  667.8 10.5 %slice-start.1 = ((s8[8388608]{0:T(1024)(128)(4,1)}), s8[4194304]{0:T(1024)(128)(4,1)S(1)}, s32[]{:S(2)}) async-start(s8[8388608]{0:T(1024)(128)(4,1)} %bitcast.303), calls=%async_computation.7 | async-start | bytes 8388608
  667.8 10.5 %copy-start.47 = (bf16[4,2,256,704]{3,2,1,0:T(8,128)(2,1)S(1)}, bf16[4,2,256,704]{3,2,1,0:T(8,128)(2,1)}, u32[]{:S(2)}) copy-start(bf16[4,2,256,704]{3,2,1,0:T(8,128)(2,1)} %get-tuple-element.70) | copy-start | bytes 8650756
  692.5 7.6 copy-start.44
  698.1 2.0 copy-start.24
  706.4 205.1 %reduce-scatter.5.cloned.1.call-start = ((), (), s32[]{:S(2)}) async-start(), calls=%async_computation.5 | async-start | bytes 5242880 | tf_op jit(solution)/shard_map/reduce_scatter | solution.py:1406
  751.1 2.2 copy-start.6
  783.3 7.4 copy-start.23
  789.9 112.5 %copy-start.34 = (f32[2048]{0:T(1024)}, f32[2048]{0:T(1024)S(1)}, u32[]{:S(2)}) copy-start(f32[2048]{0:T(1024)S(1)} %reshape.602) | copy-start | bytes 24580
  790.7 111.7 %copy-start.41 = (f32[128]{0:T(128)}, f32[128]{0:T(128)S(1)}, u32[]{:S(2)}) copy-start(f32[128]{0:T(128)S(1)} %rsqrt.21) | copy-start | bytes 1540
  791.7 8.4 copy-start.43
  800.1 9.8 %copy-start.8 = (bf16[1024,2048]{1,0:T(8,128)(2,1)S(1)}, bf16[1024,2048]{1,0:T(8,128)(2,1)}, u32[]{:S(2)}) copy-start(bf16[1024,2048]{1,0:T(8,128)(2,1)} %copy-done.7) | copy-start | bytes 12582916
  812.5 5.5 copy-start.13
  818.0 2.4 copy-start.26
  820.4 7.5 copy-start.5
  828.0 80.5 %copy-start.21 = (bf16[2,1,64,2048]{3,2,1,0:T(8,128)(2,1)S(1)}, bf16[2,1,64,2048]{3,2,1,0:T(8,128)(2,1)}, u32[]{:S(2)}) copy-start(bf16[2,1,64,2048]{3,2,1,0:T(8,128)(2,1)} %param.33) | copy-start | bytes 1572868
  828.0 80.5 %copy-start.28 = (f32[2048]{0:T(1024)S(1)}, f32[2048]{0:T(1024)}, u32[]{:S(2)}) copy-start(f32[2048]{0:T(1024)} %copy-done.27) | copy-start | bytes 24580
  828.0 80.5 %copy-start.30 = (f32[1,2048]{1,0:T(1,128)S(1)}, f32[1,2048]{1,0:T(1,128)}, u32[]{:S(2)}) copy-start(f32[1,2048]{1,0:T(1,128)} %copy-done.29) | copy-start | bytes 24580
  904.1 4.4 copy-start.18
  (7 other events, 6.7 us)
Sparse Core Ops, SparseCore 0:
  143.3 78.9 all-gather.2
  656.1 36.3 all-gather.4
  706.5 76.7 reduce-scatter.2
  785.5 101.1 reduce-scatter.4

commit v6 on v5

--- a/solution.py
+++ b/solution.py
@@ -26,6 +26,16 @@
 
 def product_nt(left, right):
     return lax.dot_general(left, right, (((1,), (1,)), ((), ())), preferred_element_type=F32)
+
+
+def split_product(values, rows):
+    parts, rest = [], values
+    for _ in range(3):
+        parts.append(lax.reduce_precision(rest, 8, 7))
+        rest = rest - parts[-1]
+    count = values.shape[1]
+    total = product_tn(jnp.concatenate(parts, axis=1).astype(BF16), rows)
+    return total[:count] + total[count : 2 * count] + total[2 * count :]
 
 
 def rms_scaled(values, gain):
@@ -873,18 +883,18 @@
     )(first, second, w_gate, w_up, w_down)
 
 
-def end_kernel(
-    pairs, x_ref, g_hbm, o_ref, key_ref, value_ref,
-    g_ref, k_ref, half, quarter, got_core, got_side, got_pair, hop, send, recv, local,
+def last_kernel(
+    sizes, x_ref, q_ref, g_hbm, o_ref, w_ref, key_ref, value_ref,
+    got, side, g_ref, k_ref, hop, send, recv, peer_send, peer_recv, local,
 ):
+    line, pairs, experts = sizes
+    trees = pairs * experts
+    count = line * trees
     z, p, e = lax.axis_index("line"), lax.axis_index("pair"), lax.axis_index("expert")
-    line, span, _ = g_ref.shape
-    trees, piece, _ = k_ref.shape
-    c, y = e % 2, e // 2
-    core, side = {"expert": e + 1 - 2 * c}, {"expert": e + 2 - 4 * y}
-    other, up, down = {"pair": 1 - p}, {"line": z + 1}, {"line": z - 1}
-    experts = trees // pairs
-    me = p * experts + e
+    mine = p * experts + e
+    me = z * trees + mine
+    span, piece = g_ref.shape[1], k_ref.shape[1]
+    up, down = {"line": z + 1}, {"line": z - 1}
     high = z // 2
     near = z + high * (line - 1 - 2 * z)
 
@@ -892,29 +902,18 @@
         j = t + near * (1 - t // 2) * (1 - 2 * t)
         return j + high * (line - 1 - 2 * j)
 
-    def place(index):
-        return {"pair": index // experts, "expert": index % experts}
-
     fetch = pltpu.make_async_copy(g_hbm, g_ref, local)
     fetch.start()
     barrier = pltpu.get_barrier_semaphore()
-    for shift in range(1, trees):
-        pl.semaphore_signal(
-            barrier, inc=1, device_id=place((me + shift) % trees), device_id_type=MESH
-        )
-
-    @pl.when(z > 0)
-    def _():
-        pl.semaphore_signal(barrier, inc=1, device_id=down, device_id_type=MESH)
-
-    @pl.when(z < line - 1)
-    def _():
-        pl.semaphore_signal(barrier, inc=1, device_id=up, device_id_type=MESH)
-
-    below, above = (z + line - 1) // line, (2 * line - 2 - z) // line
-    pl.semaphore_wait(barrier, trees - 1 + below + above)
-    UP, DOWN, SWAP = 7, 7 + line, 7 + 2 * line
-    rows = x_ref.shape[3]
+
+    def greet_one(offset, carry):
+        target = place_of((me + offset) % count, sizes)
+        pl.semaphore_signal(barrier, inc=1, device_id=target, device_id_type=MESH)
+        return carry
+
+    lax.fori_loop(1, count, greet_one, 0)
+    pl.semaphore_wait(barrier, count - 1)
+    UP, DOWN, SWAP, PAIR = 0, line, 2 * line, 2 * line + trees
 
     def sum_up(j):
         return remote(g_ref.at[j], hop.at[j], send.at[UP + j], recv.at[UP + j], up)
@@ -924,22 +923,22 @@
 
     def fold(t):
         j = order(t)
-        mine = g_ref.at[j]
+        own = g_ref.at[j]
 
         @pl.when((j >= z) & (z > 0))
         def _():
             sum_up(j).wait_recv()
-            add_into(mine, [mine, hop.at[j]], span)
+            add_into(own, [own, hop.at[j]], span)
 
         @pl.when((j < z) & (z < line - 1))
         def _():
             sum_down(j, j).wait_recv()
-            add_into(mine, [mine, hop.at[j]], span)
+            add_into(own, [own, hop.at[j]], span)
 
         @pl.when((j == z) & (z < line - 1))
         def _():
             sum_down(j, line).wait_recv()
-            add_into(mine, [mine, hop.at[line]], span)
+            add_into(own, [own, hop.at[line]], span)
 
         @pl.when(j > z)
         def _():
@@ -953,57 +952,68 @@
         def _():
             sum_down(j, line).start()
 
-    corners = [(1, 1), (0, 1), (1, 0), (0, 0)]
-    first, second = [], {}
-    for slot, (dx, dy) in enumerate(corners):
-        copy = remote(
-            x_ref.at[(p + dx) % 2, (y + dy) % 2, 1 - c],
-            got_core.at[slot],
-            send.at[slot],
-            recv.at[slot],
-            core,
-        )
-        copy.start()
-        first.append(copy)
     fetch.wait()
     fold(3)
-    for slot, (dx, dy) in enumerate(corners):
-        first[slot].wait_recv()
-        add_into(
-            half.at[slot], [x_ref.at[(p + dx) % 2, (y + dy) % 2, c], got_core.at[slot]], rows
+    swap = remote(q_ref.at[1 - p], side, send.at[PAIR], recv.at[PAIR], {"pair": 1 - p})
+    swap.start()
+
+    def copy_to(offset):
+        peer = (me + offset) % count
+        return remote(
+            x_ref.at[peer],
+            got.at[offset],
+            peer_send.at[offset],
+            peer_recv.at[offset],
+            place_of(peer, sizes),
         )
-        if dy == 1:
-            second[dx] = remote(
-                half.at[slot], got_side.at[dx], send.at[4 + dx], recv.at[4 + dx], side
-            )
-            second[dx].start()
+
+    def start(offset, carry):
+        copy_to(offset).start()
+        return carry
+
+    lax.fori_loop(1, count, start, 0)
+    got[0] = x_ref[me]
     fold(2)
-    second[1].wait_recv()
-    add_into(quarter, [half.at[2], got_side.at[1]], rows)
-    last = remote(quarter, got_pair, send.at[6], recv.at[6], other)
-    last.start()
+    part = q_ref.shape[2] // line
+
+    def lay(block, source):
+        for index in range(line):
+            column = pl.multiple_of((index * pairs + source) * part, part)
+            w_ref[:, pl.ds(column, part)] = block[:, index * part : (index + 1) * part].astype(F32)
+
+    lay(q_ref.at[p], p)
     fold(1)
-    second[0].wait_recv()
-    last.wait_recv()
-    add_into(o_ref, [half.at[3], got_side.at[0], got_pair], rows)
+    swap.wait_recv()
+    lay(side, 1 - p)
+
+    def finish(offset, carry):
+        copy_to(offset).wait()
+        return carry
+
+    lax.fori_loop(1, count, finish, 0)
+    o_ref[...] = jnp.sum(got[...], axis=0)
     fold(0)
 
-    def part(index):
+    def share_of(index):
         return g_ref.at[z, pl.ds(pl.multiple_of(index * piece, piece), piece)]
 
-    keep = pltpu.make_async_copy(part(me), k_ref.at[me], local)
+    keep = pltpu.make_async_copy(share_of(mine), k_ref.at[mine], local)
     keep.start()
     swaps = []
     for shift in range(1, trees):
-        peer = (me + shift) % trees
+        peer = (mine + shift) % trees
         copy = remote(
-            part(peer), k_ref.at[me], send.at[SWAP + shift], recv.at[SWAP + shift], place(peer)
+            share_of(peer),
+            k_ref.at[mine],
+            send.at[SWAP + shift],
+            recv.at[SWAP + shift],
+            {"pair": peer // experts, "expert": peer % experts},
         )
         copy.start()
         swaps.append(copy)
+    keep.wait()
     for copy in swaps:
         copy.wait()
-    keep.wait()
     share = k_ref.shape[2] // 2
     for source in range(trees):
         column = ((source % experts) * pairs + source // experts) * share
@@ -1011,8 +1021,7 @@
             target[:, column : column + share] = k_ref[
                 source, :, index * share : (index + 1) * share
             ].astype(F32)
-    for copy in first + list(second.values()) + [last]:
-        copy.wait_send()
+    swap.wait_send()
 
     def drain(j, carry):
         @pl.when(j > z)
@@ -1028,107 +1037,40 @@
     lax.fori_loop(0, line, drain, 0)
 
 
-def end_exchange(value, grads, line, pairs, number):
-    trees, rows, cols = value.shape
+def last_exchange(sums, query, grads, sizes, number):
+    line, pairs, experts = sizes
+    trees = pairs * experts
+    count, block = sums.shape[0], sums.shape[1:]
+    _, rows, cols = query.shape
     span, thin = grads.shape[0] // line, grads.shape[1]
-    uses = 7 + 2 * line + trees
-    block = pltpu.VMEM((rows, cols), BF16)
+    uses = 2 * line + trees + 1
+    wide = jax.ShapeDtypeStruct((span // trees, trees * thin // 2), F32)
     return pl.pallas_call(
-        partial(end_kernel, pairs),
-        in_specs=[VMEM, ANY],
-        out_specs=[VMEM] * 3,
-        out_shape=[jax.ShapeDtypeStruct((rows, cols), BF16)]
-        + [jax.ShapeDtypeStruct((span // trees, trees * thin // 2), F32)] * 2,
+        partial(last_kernel, sizes),
+        in_specs=[VMEM, VMEM, ANY],
+        out_specs=[VMEM] * 4,
+        out_shape=[
+            jax.ShapeDtypeStruct(block, F32),
+            jax.ShapeDtypeStruct((rows, pairs * cols), F32),
+            wide,
+            wide,
+        ],
         scratch_shapes=[
+            pltpu.VMEM((count,) + block, F32),
+            pltpu.VMEM((rows, cols), BF16),
             pltpu.VMEM((line, span, thin), BF16),
             pltpu.VMEM((trees, span // trees, thin), BF16),
-            pltpu.VMEM((4, rows, cols), BF16),
-            block,
-            pltpu.VMEM((4, rows, cols), BF16),
-            pltpu.VMEM((2, rows, cols), BF16),
-            block,
             pltpu.VMEM((line + 1, span, thin), BF16),
             DMA((uses,)),
             DMA((uses,)),
+            DMA((count,)),
+            DMA((count,)),
             DMA(()),
         ],
         compiler_params=params(number, 48 * 2**20),
         cost_estimate=pl.CostEstimate(flops=0, bytes_accessed=0, transcendentals=0),
-        name="end_exchange",
-    )(value.reshape(pairs, 2, 2, rows, cols), grads.reshape(line, span, thin))
-
-
-def final_kernel(sizes, x_ref, q_ref, o_ref, w_ref, got, side, send, recv, pair_send, pair_recv):
-    line, pairs, experts = sizes
-    count = line * pairs * experts
-    p = lax.axis_index("pair")
-    me = lax.axis_index("line") * (pairs * experts) + p * experts + lax.axis_index("expert")
-    barrier = pltpu.get_barrier_semaphore()
-
-    def greet_one(offset, carry):
-        target = place_of((me + offset) % count, sizes)
-        pl.semaphore_signal(barrier, inc=1, device_id=target, device_id_type=MESH)
-        return carry
-
-    lax.fori_loop(1, count, greet_one, 0)
-    pl.semaphore_wait(barrier, count - 1)
-    swap = remote(q_ref.at[1 - p], side, pair_send, pair_recv, {"pair": 1 - p})
-    swap.start()
-
-    def copy_to(offset):
-        peer = (me + offset) % count
-        return remote(
-            x_ref.at[peer], got.at[offset], send.at[offset], recv.at[offset], place_of(peer, sizes)
-        )
-
-    def start(offset, carry):
-        copy_to(offset).start()
-        return carry
-
-    lax.fori_loop(1, count, start, 0)
-    got[0] = x_ref[me]
-    part = q_ref.shape[2] // line
-
-    def lay(block, source):
-        for index in range(line):
-            column = pl.multiple_of((index * pairs + source) * part, part)
-            w_ref[:, pl.ds(column, part)] = block[:, index * part : (index + 1) * part].astype(F32)
-
-    lay(q_ref.at[p], p)
-    swap.wait_recv()
-    lay(side, 1 - p)
-
-    def finish(offset, carry):
-        copy_to(offset).wait()
-        return carry
-
-    lax.fori_loop(1, count, finish, 0)
-    o_ref[...] = jnp.sum(got[...], axis=0)
-    swap.wait_send()
-
-
-def final_exchange(sums, grads, sizes, number):
-    count, block = sums.shape[0], sums.shape[1:]
-    pairs, rows, cols = grads.shape
-    return pl.pallas_call(
-        partial(final_kernel, sizes),
-        in_specs=[VMEM, VMEM],
-        out_specs=[VMEM, VMEM],
-        out_shape=[
-            jax.ShapeDtypeStruct(block, F32),
-            jax.ShapeDtypeStruct((rows, pairs * cols), F32),
-        ],
-        scratch_shapes=[
-            pltpu.VMEM((count,) + block, F32),
-            pltpu.VMEM((rows, cols), BF16),
-            DMA((count,)),
-            DMA((count,)),
-            DMA(()),
-            DMA(()),
-        ],
-        compiler_params=params(number, 32 * 2**20),
-        name="final_exchange",
-    )(sums, grads)
+        name="last_exchange",
+    )(sums, query, grads.reshape(line, span, thin))
 
 
 def start_all_kernel(
@@ -1343,6 +1285,43 @@
         compiler_params=params(number, 48 * 2**20),
         name="start_all",
     )(tokens, w_query, w_key, w_value, small, integers)
+
+
+def input_kernel(dq_ref, wq_ref, kv_ref, wkv_ref, dl_ref, router_ref, o_ref):
+    piece = kv_ref.shape[2]
+    total = product_nt(dq_ref[...], wq_ref[...])
+    total = total + product_nt(kv_ref[0], wkv_ref[:, :piece])
+    total = total + product_nt(kv_ref[1], wkv_ref[:, piece:])
+    for expert in range(router_ref.shape[0]):
+        total = total + dl_ref[:, expert : expert + 1] * router_ref[expert : expert + 1, :]
+    o_ref[...] = total.astype(BF16)
+
+
+def input_gradient(query_pre, query_weight, kv_sum, kv_weight, logit_grad, router):
+    rows, feats = query_pre.shape
+    width = query_weight.shape[0]
+    piece = kv_sum.shape[2]
+    experts = router.shape[0]
+    block, lanes = min(512, rows), 512
+    return pl.pallas_call(
+        input_kernel,
+        grid=(width // lanes, rows // block),
+        in_specs=[
+            pl.BlockSpec((block, feats), lambda n, i: (i, 0)),
+            pl.BlockSpec((lanes, feats), lambda n, i: (n, 0)),
+            pl.BlockSpec((2, block, piece), lambda n, i: (0, i, 0)),
+            pl.BlockSpec((lanes, 2 * piece), lambda n, i: (n, 0)),
+            pl.BlockSpec((block, experts), lambda n, i: (i, 0)),
+            pl.BlockSpec((experts, lanes), lambda n, i: (0, n)),
+        ],
+        out_specs=pl.BlockSpec((block, lanes), lambda n, i: (i, n)),
+        out_shape=jax.ShapeDtypeStruct((rows, width), BF16),
+        compiler_params=pltpu.CompilerParams(vmem_limit_bytes=40 * 2**20),
+        cost_estimate=pl.CostEstimate(
+            flops=2 * rows * width * (feats + 2 * piece), bytes_accessed=6 * rows * width, transcendentals=0
+        ),
+        name="input_gradient",
+    )(query_pre, query_weight, kv_sum, kv_weight, logit_grad, router)
 
 
 def project_kernel(micro, x_ref, w_ref, gain_ref, router_ref, cos_ref, sin_ref, n_ref, kv_ref, l_ref):
@@ -1531,6 +1510,7 @@
     heads_flat = heads_out.reshape(rows, feats)
     projected = product(heads_flat, out_weight)
     gated = (own_gate[:, None] * projected).astype(BF16)
+    projected = projected.astype(BF16)
     attention = cube_reduce(gated.reshape(pair * experts, micro * tok, width), pair, 4).astype(F32)
 
     middle = residual + attention
@@ -1593,24 +1573,12 @@
     second_router_wide = second_router.astype(F32)
     for expert in range(experts):
         hn_grad = hn_grad + second_logit_grad[:, expert : expert + 1] * second_router_wide[expert]
-    grad_router_second = jnp.dot(
-        jnp.transpose(second_logit_grad),
-        second_normed.astype(F32),
-        precision=HIGHEST,
-        preferred_element_type=F32,
-    )
+    grad_router_second = split_product(second_logit_grad, second_normed)
     middle_grad, grad_gain_second = second_pull(hn_grad)
     middle_grad = middle_grad + dz
 
-    mix_grad = gather(middle_grad.astype(BF16), TREES)
-    grad_gate = product_tn(gate_grad, arrived)[None]
-    grad_upward = product_tn(up_grad, arrived)[None]
-    grad_downward = product_tn(inner, result_grad)[None]
-    mix_grad, grad_gate, grad_upward, grad_downward = lax.optimization_barrier(
-        (mix_grad, grad_gate, grad_upward, grad_downward)
-    )
-    mix_grad = mix_grad.astype(F32)
-    own_gate_grad = jnp.sum(mix_grad * projected, axis=-1)
+    mix_grad = cube_gather(middle_grad.astype(BF16), pair, 7).reshape(rows, width).astype(F32)
+    own_gate_grad = jnp.sum(mix_grad * projected.astype(F32), axis=-1)
     projected_grad = (own_gate[:, None] * mix_grad).astype(BF16)
     grad_output = product_tn(heads_flat, projected_grad).astype(BF16)
     grad_output, projected_grad = lax.optimization_barrier((grad_output, projected_grad))
@@ -1623,39 +1591,29 @@
     kv_sum = cube_reduce(kv_pre.reshape(experts, 2 * rows, piece), 1, 8)
     grad_query, grad_output, kv_sum = lax.optimization_barrier((grad_query, grad_output, kv_sum))
     (first_logit_grad,) = first_gate_pull(own_gate_grad[:, None] * column[None, :])
-    key_pre, value_pre = kv_sum[:rows], kv_sum[rows:]
+    kv_sum = kv_sum.reshape(2, rows, piece)
     grad_kv = jnp.concatenate(
-        [product_tn(tree_input, key_pre), product_tn(tree_input, value_pre)], axis=1
-    )
-    grad_kv, key_pre, value_pre = lax.optimization_barrier(
-        (grad_kv.astype(BF16), key_pre, value_pre)
-    )
-    input_term = (
-        product_nt(query_pre, query_weight)
-        + product_nt(key_pre, kv_weight[:, :piece])
-        + product_nt(value_pre, kv_weight[:, piece:])
-    )
-    first_router_wide = first_router.astype(F32)
-    for expert in range(experts):
-        input_term = input_term + first_logit_grad[:, expert : expert + 1] * first_router_wide[expert]
-    input_term = input_term.astype(BF16).reshape(pair * experts, micro * tok, width)
-    if walk:
-        normed_grad, grad_key, grad_value = end_exchange(input_term, grad_kv, line, pair, 9)
-    else:
-        normed_grad = cube_reduce(input_term, pair, 9)
+        [product_tn(tree_input, kv_sum[0]), product_tn(tree_input, kv_sum[1])], axis=1
+    ).astype(BF16)
+    input_term = input_gradient(
+        query_pre, query_weight, kv_sum, kv_weight, first_logit_grad, first_router.astype(F32)
+    ).reshape(pair * experts, micro * tok, width)
+    normed_grad = cube_reduce(input_term, pair, 9)
+    if not walk:
         grad_kv = scatter(grad_kv, "line")
         grad_kv = swap(grad_kv.reshape(pair * experts, own_kv, 2 * piece), TREES)
         grad_kv = grad_kv.reshape(pair, experts, own_kv, 2, line // experts, part)
         grad_kv = jnp.transpose(grad_kv, (2, 3, 1, 4, 0, 5)).reshape(own_kv, 2, heads_total)
         grad_key, grad_value = grad_kv[:, 0].astype(F32), grad_kv[:, 1].astype(F32)
     grad_query = scatter(grad_query, "line")
+    gate_grad, up_grad, inner, arrived, result_grad, normed_grad = lax.optimization_barrier(
+        (gate_grad, up_grad, inner, arrived, result_grad, normed_grad)
+    )
+    grad_gate = product_tn(gate_grad, arrived)[None]
+    grad_upward = product_tn(up_grad, arrived)[None]
+    grad_downward = product_tn(inner, result_grad)[None]
     normed_grad = normed_grad.astype(F32)
-    grad_router_first = jnp.dot(
-        jnp.transpose(first_logit_grad),
-        tree_input.astype(F32),
-        precision=HIGHEST,
-        preferred_element_type=F32,
-    )
+    grad_router_first = split_product(first_logit_grad, tree_input)
     token_grad, grad_gain_first = first_pull(normed_grad)
     tokens_grad = token_grad + middle_grad
 
@@ -1665,7 +1623,9 @@
     )
     sums = jnp.transpose(sums.reshape(sums.shape[0], -1, own_kv), (1, 0, 2))
     if walk:
-        sums, grad_query = final_exchange(sums, grad_query.reshape(pair, own_in, feats), sizes, 10)
+        sums, grad_query, grad_key, grad_value = last_exchange(
+            sums, grad_query.reshape(pair, own_in, feats), grad_kv, sizes, 10
+        )
         grad_query = grad_query[None]
     else:
         sums = small_exchange(sums, sizes, True, 10)

time: 955 us -> 936 us (0.980)
  Pallas kernels: 740 us -> 768 us
  matrix products: 112 us -> 85.1 us
    pallas_call x2, Pallas kernels: 95.1 us -> 59.5 us  [the longest x1 49.3 us: last_exchange(): pl.pallas_call(partial(last_kernel, sizes), in_specs=[VMEM, VMEM, ANY], o...]
    pallas_call x1 -> x2, Pallas kernels: 26.9 us -> 58.2 us  [cube_gather(): pl.pallas_call(partial(cube_gather_kernel, pairs), in_specs=[VMEM], out_s...]
    pallas_call x2 -> x3, Pallas kernels: 59 us -> 88.9 us  [cube_reduce(): pl.pallas_call(partial(cube_reduce_kernel, pairs), in_specs=[VMEM], out_s...]
    dot_general x5 -> x2, matrix products: 28.3 us -> 10.4 us  [product_nt(): lax.dot_general(left, right, (((1,), (1,)), ((), ())), preferred_element_...]
    unnamed x109 -> x81, local copies, waits for them, and re-layouts: 23.7 us -> 29.3 us
    dot_general x7 -> x9, matrix products: 48.6 us -> 48.4 us  [product_tn(): lax.dot_general(left, right, (((0,), (0,)), ((), ())), preferred_element_...]
  transfers between devices with their start and end apart: 4 -> 3, of which waited for: 3 -> 1; matrix products, arithmetic and copies ran while one was open for 13% -> 8% of each run, Pallas kernels for 19% -> 16%
where the time goes in v6:
time: 936 us; the launch traced here: 926 us
  Pallas kernels  768 us (82%)
  matrix products  85.1 us (9%)
  local copies, waits for them, and re-layouts  35.5 us (4%)
  other arithmetic  21.9 us (2%)
  between operations  14.9 us (2%)
    pallas_call x1, Pallas kernels, feed_forward(): pl.pallas_call(ff_kernel, in_specs=[ANY] * 5, out_specs=[ANY] * 7, out_sh...  382 us
    pallas_call x1, Pallas kernels, start_all(): pl.pallas_call(partial(start_all_kernel, sizes), in_specs=[VMEM] * 6, out...  128 us
    pallas_call x3, Pallas kernels, cube_reduce(): pl.pallas_call(partial(cube_reduce_kernel, pairs), in_specs=[VMEM], out_s...  88.9 us
    pallas_call x2, Pallas kernels, cube_gather(): pl.pallas_call(partial(cube_gather_kernel, pairs), in_specs=[VMEM], out_s...  58.2 us
    pallas_call x1, Pallas kernels, last_exchange(): pl.pallas_call(partial(last_kernel, sizes), in_specs=[VMEM, VMEM, ANY], o...  49.3 us
    dot_general x9, matrix products, product_tn(): lax.dot_general(left, right, (((0,), (0,)), ((), ())), preferred_element_...  48.4 us
    unnamed x81, local copies, waits for them, and re-layouts  29.3 us
    pallas_call x1, Pallas kernels, attend_back(): pl.pallas_call(partial(attend_back_kernel, part // HDIM, scale), grid=gri...  25.7 us
  transfers between devices with their start and end apart: 3, of which 1 were waited for; matrix products, arithmetic and copies ran while one was open for 8% of the time, Pallas kernels for 16%

profile of v6, /device:TPU:0, one launch (start us, length us, event | category | flops | bytes accessed | tf_op | source)
XLA Modules:
  0.0 925.8 jit_solution(7130792539081444268)
XLA Ops:
  9.7 1.0 copy-done
  10.8 1.2 copy-done.8
  13.9 127.9 %start_all.1 = (bf16[2,2,2,128,2048]{4,3,2,1,0:T(8,128)(2,1)}, bf16[4,512,1024]{2,1,0:T(8,128)(2,1)}, bf16[4,512,512]{2,1,0:T(8,128)(2,1)S(1)}, bf16[32,10,64]{2,1,0:T(8,128)(2,1)S(1)}, s32[2,16,128]{2,1,0:T(8,128)S(1)}) custom-call(bf16[128,2048]{1,0:T(8,128)(2,1)S(1)} %bitcast.204, bf16[256,2048]{1,0:T(8,128)(2,1)S(1)} %bitcast.214, ...), custom_call_target="tpu_custom_call" | custom-call | tf_op jit(solution)/shard_map/start_all/pallas_call | solution.py:1265
  141.8 1.3 copy-done.14
  146.1 2.3 copy-done.13
  148.5 1.8 copy-done.15
  150.3 5.6 project.1
  155.9 2.0 copy-done.6
  158.1 26.8 %cube_gather.2 = bf16[1,2,2,2048,256]{4,3,2,1,0:T(8,128)(2,1)S(1)} custom-call(bf16[2048,256]{1,0:T(8,128)(2,1)S(1)} %bitcast.213), custom_call_target="tpu_custom_call" | custom-call | bytes 41943040 | tf_op jit(solution)/shard_map/cube_gather/pallas_call | solution.py:371
  184.9 2.0 copy-done.4
  187.9 1.2 multiply_sine_fusion
  189.1 1.3 or_select_fusion.bias_ref
  190.5 10.0 %fusion.85.raw_ref = f32[2,4,2,64,1024]{4,3,2,1,0:T(8,128)} fusion(bf16[2,4,2,64,2048]{4,3,2,1,0:T(8,128)(2,1)} %bitcast.210, bf16[2048,1024,1,1,1]{1,0,4,3,2:T(8,128)(2,1)} %bitcast.220), kind=kOutput, calls=%fused_computation.212 | convolution fusion | flops 4294967296 | bytes 12582912 | tf_op jit(solution)/shard_map/dot_general | solution.py:20
  200.5 20.0 %attend.1 = (bf16[2,4,2,64,1024]{4,3,2,1,0:T(8,128)(2,1)}, bf16[2,4,2,64,1024]{4,3,2,1,0:T(8,128)(2,1)}) custom-call(f32[2,4,2,64,1024]{4,3,2,1,0:T(8,128)} %fusion.85.raw_ref, bf16[4,2,2,4,2,64,256]{6,5,4,3,2,1,0:T(8,128)(2,1)} %bitcast.205, f32[256,64]{1,0:T(8,128)} %get-tuple-element.193.cos_ref, f32[256,64]{1,0:T(8,128)} %get-tuple-element.192.sin_ref, ...), custom_call_target="tpu_custom_call" | custom-call | flops 1073741824 | bytes 12582912 | tf_op jit(solution)/shard_map/attend/pallas_call | solution.py:179
  220.9 1.1 bitcast_convert_fusion.1
  222.4 9.3 %multiply_convert_fusion = (bf16[1024,2048]{1,0:T(8,128)(2,1)S(1)}, bf16[1024,2048]{1,0:T(8,128)(2,1)}) fusion(f32[1024]{0:T(1024)S(1)} %multiply_reduce_fusion.6, bf16[1024,1024]{1,0:T(8,128)(2,1)} %bitcast.271, bf16[1024,2048]{1,0:T(8,128)(2,1)} %all-gather.2.cloned.1.call-done), kind=kOutput, calls=%fused_computation.6 | convolution fusion | flops 4301258752 | bytes 14684160 | tf_op jit(solution)/shard_map/dot_general | solution.py:20
  231.7 30.7 %cube_reduce.3 = bf16[128,2048]{1,0:T(8,128)(2,1)S(1)} custom-call(bf16[2,2,2,128,2048]{4,3,2,1,0:T(8,128)(2,1)S(1)} %bitcast.209), custom_call_target="tpu_custom_call" | custom-call | tf_op jit(solution)/shard_map/cube_reduce/pallas_call | solution.py:307
  264.8 1.1 copy.103
  266.2 1.0 copy.102
  267.3 381.9 %feed_forward.1 = (bf16[4,64,2048]{2,1,0:T(8,128)(2,1)}, bf16[4,64,2048]{2,1,0:T(8,128)(2,1)}, bf16[4,2,256,2048]{3,2,1,0:T(8,128)(2,1)}, bf16[4,2,256,2048]{3,2...) custom-call(bf16[4,64,2048]{2,1,0:T(8,128)(2,1)} %bitcast.233, ...), custom_call_target="tpu_custom_call" | custom-call | flops 35433480192 | bytes 50331648 | tf_op jit(solution)/shard_map/feed_forward/pallas_call | solution.py:854
  649.2 1.7 fusion.15
  650.8 3.9 multiply_reduce_fusion
  655.8 3.2 fusion.82
  659.0 31.4 %cube_gather.3 = bf16[2,2,2,128,2048]{4,3,2,1,0:T(8,128)(2,1)S(1)} custom-call(bf16[128,2048]{1,0:T(8,128)(2,1)S(1)} %get-tuple-element.168.x_ref), custom_call_target="tpu_custom_call" | custom-call | bytes 20971520 | tf_op jit(solution)/shard_map/cube_gather/pallas_call | solution.py:371
  690.4 3.3 fusion.2
  695.3 6.1 convolution_convert_fusion.1
  702.3 10.1 %convolution_convert_fusion.5 = bf16[1024,1024]{1,0:T(8,128)(2,1)} fusion(bf16[1024,2048]{1,0:T(8,128)(2,1)} %get-tuple-element.70, bf16[1024,2048]{1,0:T(8,128)(2,1)} %all-gather.2.cloned.1.call-done), kind=kOutput, calls=%fused_computation.22 | convolution fusion | flops 4296015872 | bytes 10485760 | tf_op jit(solution)/shard_map/dot_general | solution.py:28
  712.4 25.7 %attend_back.1 = (bf16[2,4,2,64,1024]{4,3,2,1,0:T(8,128)(2,1)}, bf16[4,2,2,4,2,64,256]{6,5,4,3,2,1,0:T(8,128)(2,1)}) custom-call(bf16[2,4,2,64,1024]{4,3,2,1,0:T(8,128)(2,1)} %get-tuple-element.68.query_ref, bf16[4,2,2,4,2,64,256]{6,5,4,3,2,1,0:T(8,128)(2,1)} %bitcast.206, bf16[2,4,2,64,1024]{4,3,2,1,0:T(8,128)(2,1)} %bitcast.284, ...), custom_call_target="tpu_custom_call" | custom-call | flops 2684354560 | bytes 14680064 | tf_op jit(solution)/shard_map/attend_back/pallas_call | solution.py:197
  738.1 9.5 %convolution_convert_fusion = bf16[2048,1024]{1,0:T(8,128)(2,1)} fusion(bf16[1024,2048]{1,0:T(8,128)(2,1)} %copy-done.6, bf16[1024,1024]{1,0:T(8,128)(2,1)} %bitcast.225), kind=kOutput, calls=%fused_computation.9 | convolution fusion | flops 4297064448 | bytes 10485760 | tf_op jit(solution)/shard_map/dot_general | solution.py:24
  747.6 2.2 copy-done.5
  749.8 28.6 %cube_reduce.4 = bf16[2048,256]{1,0:T(8,128)(2,1)S(1)} custom-call(bf16[1,2,2,2048,256]{4,3,2,1,0:T(8,128)(2,1)S(1)} %bitcast.207), custom_call_target="tpu_custom_call" | custom-call | tf_op jit(solution)/shard_map/cube_reduce/pallas_call | solution.py:307
  778.8 2.8 fusion.29
  782.3 2.2 copy-done.12
  784.5 1.9 copy-done.16
  786.4 1.6 copy-done.17
  788.0 10.3 %input_gradient.1 = bf16[1024,2048]{1,0:T(8,128)(2,1)S(1)} custom-call(bf16[1024,1024]{1,0:T(8,128)(2,1)S(1)} %bitcast.226, bf16[2048,1024]{1,0:T(8,128)(2,1)S(1)} %bitcast.221, bf16[2,1024,256]{2,1,0:T(8,128)(2,1)S(1)} %bitcast.212, bf16[2048,512]{1,0:T(8,128)(2,1)S(1)} %bitcast.224, f32[1024,4]{1,0:T(8,128)S(1)} %copy.106.dl_ref, ...), custom_call_target="tpu_custom_call" | custom-call | flops 6442450944 | bytes 12582912 | tf_op jit(solution)/shard_map/input_gradient/pallas_call | solution.py:1306
  798.3 29.6 %cube_reduce.5 = bf16[128,2048]{1,0:T(8,128)(2,1)S(1)} custom-call(bf16[2,2,2,128,2048]{4,3,2,1,0:T(8,128)(2,1)S(1)} %bitcast.208), custom_call_target="tpu_custom_call" | custom-call | tf_op jit(solution)/shard_map/cube_reduce/pallas_call | solution.py:307
  828.7 3.7 convolution_convert_fusion.3
  832.4 1.4 convolution_convert_fusion.4
  833.9 1.5 pad_maximum_fusion.g_hbm
  835.4 1.6 bitcast_convert_fusion
  837.0 2.1 fusion.9
  839.6 8.1 convolution_bitcast_fusion.2
  847.8 8.1 convolution_bitcast_fusion.1
  855.9 8.4 convolution_bitcast_fusion
  864.3 1.2 copy-done.9
  865.5 49.3 %last_exchange.1 = (f32[10,64]{1,0:T(8,128)S(1)}, f32[256,2048]{1,0:T(8,128)S(1)}, f32[64,2048]{1,0:T(8,128)S(1)}, f32[64,2048]{1,0:T(8,128)S(1)}) custom-call(f32[32,10,64]{2,1,0:T(8,128)S(1)} %maximum_bitcast_fusion.x_ref, bf16[2,256,1024]{2,1,0:T(8,128)(2,1)S(1)} %bitcast.215, bf16[4,512,512]{2,1,0:T(8,128)(2,1)} %pad_maximum_fusion.g_hbm), custom_call_target="tpu_custom_call" | custom-call | tf_op jit(solution)/shard_map/last_exchange/pallas_call | solution.py:1048
  915.9 1.3 copy.135
  (180 shorter events, 20.4 us)
Async XLA Ops:
  7.2 215.2 %all-gather.2.cloned.1.call-start = ((), (), s32[]{:S(2)}) async-start(), calls=%async_computation.2 | async-start | bytes 5242880 | tf_op jit(solution)/shard_map/all_gather | solution.py:1381
  9.7 1.0 copy-start
  10.8 1.2 copy-start.8
  12.0 0.9 copy-start.10
  13.0 0.9 copy-start.11
  141.8 1.3 copy-start.14
  143.2 635.6 %reduce-scatter.3.cloned.1.call-start = ((), (), s32[]{:S(2)}) async-start(), calls=%async_computation.3 | async-start | bytes 5242880 | tf_op jit(solution)/shard_map/reduce_scatter | solution.py:1385
  146.1 2.3 copy-start.13
  148.5 1.8 copy-start.15
  155.9 2.0 copy-start.6
  184.9 2.0 copy-start.4
  200.4 20.0 %copy-start.27 = (s32[2,1,64,2]{2,3,1,0:T(2,128)S(1)}, s32[2,1,64,2]{2,3,1,0:T(2,128)}, u32[]{:S(2)}) copy-start(s32[2,1,64,2]{2,3,1,0:T(2,128)} %param.30) | copy-start | bytes 3076
  200.4 20.2 %copy-start.29 = (s32[2,1,64]{2,1,0:T(1,128)S(1)}, s32[2,1,64]{2,1,0:T(1,128)}, u32[]{:S(2)}) copy-start(s32[2,1,64]{2,1,0:T(1,128)} %param.31) | copy-start | bytes 1540
  200.5 20.5 %copy-start.20 = (bf16[2,1,64,2048]{3,2,1,0:T(8,128)(2,1)S(1)}, bf16[2,1,64,2048]{3,2,1,0:T(8,128)(2,1)}, u32[]{:S(2)}) copy-start(bf16[2,1,64,2048]{3,2,1,0:T(8,128)(2,1)} %param.33) | copy-start | bytes 1572868
  231.7 30.7 %copy-start.1 = (bf16[2,1,64,2048]{3,2,1,0:T(8,128)(2,1)S(1)}, bf16[2,1,64,2048]{3,2,1,0:T(8,128)(2,1)}, u32[]{:S(2)}) copy-start(bf16[2,1,64,2048]{3,2,1,0:T(8,128)(2,1)} %param.17) | copy-start | bytes 1572868
  262.4 0.8 copy-start.2
  263.4 2.4 copy-start.23
  649.1 5.8 copy-start.3
  649.1 6.6 copy-start.21
  650.8 8.2 copy-start.18
  655.8 34.7 %copy-start.25 = (bf16[1024,2048]{1,0:T(8,128)(2,1)S(1)}, bf16[1024,2048]{1,0:T(8,128)(2,1)}, u32[]{:S(2)}) copy-start(bf16[1024,2048]{1,0:T(8,128)(2,1)} %get-tuple-element.195) | copy-start | bytes 12582916
  693.7 1.6 copy-start.28
  701.5 162.8 %reduce-scatter.5.cloned.1.call-start = ((), (), s32[]{:S(2)}) async-start(), calls=%async_computation.4 | async-start | bytes 5242880 | tf_op jit(solution)/shard_map/reduce_scatter | solution.py:1385
  738.1 40.5 %copy-start.24 = (bf16[128,2048]{1,0:T(8,128)(2,1)S(1)}, bf16[128,2048]{1,0:T(8,128)(2,1)}, u32[]{:S(2)}) copy-start(bf16[128,2048]{1,0:T(8,128)(2,1)} %copy-done.23) | copy-start | bytes 1572868
  747.6 2.2 copy-start.5
  782.3 2.2 copy-start.12
  784.5 1.9 copy-start.16
  786.4 1.6 copy-start.17
  828.7 3.7 copy-start.7
  832.4 6.6 slice-start.2
  833.8 1.6 copy-start.26
  833.8 3.1 copy-start.19
  833.8 3.1 copy-start.22
  833.8 5.2 slice-start.3
  835.4 4.3 copy-start.32
  839.6 8.1 copy-start.31
  839.6 16.3 %slice-start = ((s8[8388608]{0:T(1024)(128)(4,1)}), s8[4194304]{0:T(1024)(128)(4,1)S(1)}, s32[]{:S(2)}) async-start(s8[8388608]{0:T(1024)(128)(4,1)} %bitcast.274), calls=%async_computation.5 | async-start | bytes 8388608
  847.8 8.1 slice-start.1
  847.8 8.1 copy-start.30
  864.3 1.2 copy-start.9
Sparse Core Ops, SparseCore 0:
  143.3 79.0 all-gather.1
  701.6 73.9 reduce-scatter.2
  778.9 76.3 reduce-scatter.4

commit v7 on v6

--- a/solution.py
+++ b/solution.py
@@ -498,7 +498,7 @@
     pl.semaphore_wait(barrier, experts + below + above)
 
     UP, DOWN, SIDE, SUMUP, SUMDOWN, SUMSIDE = (i * line for i in range(6))
-    TWIN, SUMTWIN, SWAP = 6 * line, 6 * line + 1, 6 * line + 2
+    SUMTWIN, SWAP = 6 * line, 6 * line + 1
     BACK = SWAP + experts
 
     def push(src, dst, kind, use, target):
@@ -512,9 +512,6 @@
 
     def to_other(kind, j):
         return push(bufs[kind].at[j, p], bufs[kind].at[j, p], kind, SIDE + j, other)
-
-    def to_twin():
-        return push(bufs[1].at[z, q], bufs[1].at[z, q], 1, TWIN, across)
 
     def sum_up(kind, j):
         return push(bufs[kind].at[j, p], hop.at[kind, j], kind, SUMUP + j, up)
@@ -574,14 +571,7 @@
             def _():
                 to_down(kind, j).start()
 
-            if kind == 0:
-                to_other(kind, j).start()
-            else:
-
-                @pl.when(j != twin)
-                def _():
-                    to_other(kind, j).start()
-
+            to_other(kind, j).start()
             save(kind, j, p).start()
 
     chunk = 512
@@ -629,23 +619,8 @@
 
     def arrive(j):
         for kind in range(2):
-            if kind == 0:
-                to_other(kind, j).wait_recv()
-            else:
-
-                @pl.when(j != twin)
-                def _():
-                    to_other(kind, j).wait_recv()
-
-                @pl.when(j == twin)
-                def _():
-                    to_twin().wait_recv()
-
+            to_other(kind, j).wait_recv()
             save(kind, j, q).start()
-
-        @pl.when(j == z)
-        def _():
-            to_twin().start()
 
     def emit(t):
         j = order(t)
@@ -691,10 +666,6 @@
 
                 @pl.when(c == 1)
                 def _():
-                    @pl.when(j == z)
-                    def _():
-                        to_twin().wait_send()
-
                     for kind in range(2):
                         save(kind, j, q).wait()
                     second_half(j, column)
@@ -747,13 +718,7 @@
             def _():
                 to_down(kind, j).wait_send()
 
-            if kind == 0:
-                to_other(kind, j).wait_send()
-            else:
-
-                @pl.when(j != twin)
-                def _():
-                    to_other(kind, j).wait_send()
+            to_other(kind, j).wait_send()
 
         second_half(j, p)
         for kind in range(2):
@@ -1096,10 +1061,6 @@
 
     lax.fori_loop(1, count, greet_one, 0)
     part = wq_ref.shape[1] // (line * pairs)
-    for q in range(pairs):
-        for index in range(line):
-            column = (index * pairs + q) * part
-            q_cut[q, :, index * part : (index + 1) * part] = wq_ref[:, column : column + part]
     sub = line // experts
     for q in range(pairs):
         for d in range(experts):
@@ -1110,6 +1071,10 @@
                     kv_cut[q * experts + d, :, place : place + part] = ref[
                         :, column : column + part
                     ]
+    for q in range(pairs):
+        for index in range(line):
+            column = (index * pairs + q) * part
+            q_cut[q, :, index * part : (index + 1) * part] = wq_ref[:, column : column + part]
     pl.semaphore_wait(barrier, count - 1)
 
     copies, TOK, QSWAP, INTS, KV = [], 0, 7, 8, 9
@@ -1121,9 +1086,6 @@
         copies.append(copy)
         return copy
 
-    rows = q_cut.shape[1]
-    q_home = q_out.at[z, pl.ds(pl.multiple_of(p * rows, rows), rows)]
-    q_swap = push(QSWAP, q_cut.at[1 - p], q_home, other)
     size = kv_cut.shape[1]
     kv_home = kv_out.at[z, pl.ds(pl.multiple_of(mine * size, size), size)]
     pieces = []
@@ -1137,6 +1099,9 @@
                 {"pair": peer // experts, "expert": peer % experts},
             )
         )
+    rows = q_cut.shape[1]
+    q_home = q_out.at[z, pl.ds(pl.multiple_of(p * rows, rows), rows)]
+    q_swap = push(QSWAP, q_cut.at[1 - p], q_home, other)
     keeps = [
         pltpu.make_async_copy(q_cut.at[p], q_home, local.at[0]),
         pltpu.make_async_copy(kv_cut.at[mine], kv_home, local.at[1]),
@@ -1191,13 +1156,13 @@
         def _():
             to_down(z, 1).start()
 
-    keeps[0].wait()
-    q_swap.wait_recv()
-    begin(0)
     keeps[1].wait()
     for copy in pieces:
         copy.wait_recv()
     begin(1)
+    keeps[0].wait()
+    q_swap.wait_recv()
+    begin(0)
     to_other.wait_recv()
     block = tok_out.at[1 - p, y, c]
     far = push(TOK + 3, block, block, side)
@@ -1210,7 +1175,7 @@
     waits.append(push(TOK + 6, block, block, core))
 
     for d in range(1, line):
-        for to_up, to_down in walkers:
+        for to_up, to_down in walkers[::-1]:
 
             @pl.when(z - d >= 0)
             def _():

time: 936 us -> 912 us (0.974)
  Pallas kernels: 768 us -> 744 us
    pallas_call x1, Pallas kernels: 382 us -> 363 us  [feed_forward(): pl.pallas_call(ff_kernel, in_specs=[ANY] * 5, out_specs=[ANY] * 7, out_sh...]
  transfers between devices with their start and end apart: 3 -> 3, of which waited for: 1 -> 1; matrix products, arithmetic and copies ran while one was open for 8% -> 9% of each run, Pallas kernels for 16% -> 16%
where the time goes in v7:
time: 912 us; the launch traced here: 901 us
  Pallas kernels  744 us (82%)
  matrix products  84.3 us (9%)
  local copies, waits for them, and re-layouts  35.2 us (4%)
  other arithmetic  21.9 us (2%)
  between operations  14.9 us (2%)
    pallas_call x1, Pallas kernels, feed_forward(): pl.pallas_call(ff_kernel, in_specs=[ANY] * 5, out_specs=[ANY] * 7, out_sh...  363 us
    pallas_call x1, Pallas kernels, start_all(): pl.pallas_call(partial(start_all_kernel, sizes), in_specs=[VMEM] * 6, out...  123 us
    pallas_call x3, Pallas kernels, cube_reduce(): pl.pallas_call(partial(cube_reduce_kernel, pairs), in_specs=[VMEM], out_s...  88.7 us
    pallas_call x2, Pallas kernels, cube_gather(): pl.pallas_call(partial(cube_gather_kernel, pairs), in_specs=[VMEM], out_s...  58.4 us
    pallas_call x1, Pallas kernels, last_exchange(): pl.pallas_call(partial(last_kernel, sizes), in_specs=[VMEM, VMEM, ANY], o...  50.2 us
    dot_general x9, matrix products, product_tn(): lax.dot_general(left, right, (((0,), (0,)), ((), ())), preferred_element_...  48.3 us
    unnamed x81, local copies, waits for them, and re-layouts  29 us
    pallas_call x1, Pallas kernels, attend_back(): pl.pallas_call(partial(attend_back_kernel, part // HDIM, scale), grid=gri...  25.7 us
  transfers between devices with their start and end apart: 3, of which 1 were waited for; matrix products, arithmetic and copies ran while one was open for 9% of the time, Pallas kernels for 16%

profile of v7, /device:TPU:0, one launch (start us, length us, event | category | flops | bytes accessed | tf_op | source)
XLA Modules:
  0.0 901.3 jit_solution(17528587043095349595)
XLA Ops:
  9.7 1.0 copy-done
  10.8 1.2 copy-done.8
  13.9 122.6 %start_all.1 = (bf16[2,2,2,128,2048]{4,3,2,1,0:T(8,128)(2,1)}, bf16[4,512,1024]{2,1,0:T(8,128)(2,1)}, bf16[4,512,512]{2,1,0:T(8,128)(2,1)S(1)}, bf16[32,10,64]{2,1,0:T(8,128)(2,1)S(1)}, s32[2,16,128]{2,1,0:T(8,128)S(1)}) custom-call(bf16[128,2048]{1,0:T(8,128)(2,1)S(1)} %bitcast.204, bf16[256,2048]{1,0:T(8,128)(2,1)S(1)} %bitcast.214, ...), custom_call_target="tpu_custom_call" | custom-call | tf_op jit(solution)/shard_map/start_all/pallas_call | solution.py:1230
  136.5 1.3 copy-done.14
  140.8 2.2 copy-done.13
  143.0 1.8 copy-done.15
  144.8 5.6 project.1
  150.3 2.0 copy-done.6
  152.5 27.7 %cube_gather.2 = bf16[1,2,2,2048,256]{4,3,2,1,0:T(8,128)(2,1)S(1)} custom-call(bf16[2048,256]{1,0:T(8,128)(2,1)S(1)} %bitcast.213), custom_call_target="tpu_custom_call" | custom-call | bytes 41943040 | tf_op jit(solution)/shard_map/cube_gather/pallas_call | solution.py:371
  180.3 2.0 copy-done.4
  183.3 1.2 multiply_sine_fusion
  184.5 1.3 or_select_fusion.bias_ref
  185.8 10.0 %fusion.85.raw_ref = f32[2,4,2,64,1024]{4,3,2,1,0:T(8,128)} fusion(bf16[2,4,2,64,2048]{4,3,2,1,0:T(8,128)(2,1)} %bitcast.210, bf16[2048,1024,1,1,1]{1,0,4,3,2:T(8,128)(2,1)} %bitcast.220), kind=kOutput, calls=%fused_computation.212 | convolution fusion | flops 4294967296 | bytes 12582912 | tf_op jit(solution)/shard_map/dot_general | solution.py:20
  195.8 20.0 %attend.1 = (bf16[2,4,2,64,1024]{4,3,2,1,0:T(8,128)(2,1)}, bf16[2,4,2,64,1024]{4,3,2,1,0:T(8,128)(2,1)}) custom-call(f32[2,4,2,64,1024]{4,3,2,1,0:T(8,128)} %fusion.85.raw_ref, bf16[4,2,2,4,2,64,256]{6,5,4,3,2,1,0:T(8,128)(2,1)} %bitcast.205, f32[256,64]{1,0:T(8,128)} %get-tuple-element.193.cos_ref, f32[256,64]{1,0:T(8,128)} %get-tuple-element.192.sin_ref, ...), custom_call_target="tpu_custom_call" | custom-call | flops 1073741824 | bytes 12582912 | tf_op jit(solution)/shard_map/attend/pallas_call | solution.py:179
  216.3 1.1 bitcast_convert_fusion.1
  217.8 9.3 %multiply_convert_fusion = (bf16[1024,2048]{1,0:T(8,128)(2,1)S(1)}, bf16[1024,2048]{1,0:T(8,128)(2,1)}) fusion(f32[1024]{0:T(1024)S(1)} %multiply_reduce_fusion.6, bf16[1024,1024]{1,0:T(8,128)(2,1)} %bitcast.271, bf16[1024,2048]{1,0:T(8,128)(2,1)} %all-gather.2.cloned.1.call-done), kind=kOutput, calls=%fused_computation.6 | convolution fusion | flops 4301258752 | bytes 14684160 | tf_op jit(solution)/shard_map/dot_general | solution.py:20
  227.1 30.5 %cube_reduce.3 = bf16[128,2048]{1,0:T(8,128)(2,1)S(1)} custom-call(bf16[2,2,2,128,2048]{4,3,2,1,0:T(8,128)(2,1)S(1)} %bitcast.209), custom_call_target="tpu_custom_call" | custom-call | tf_op jit(solution)/shard_map/cube_reduce/pallas_call | solution.py:307
  260.0 1.1 copy.103
  261.5 1.0 copy.102
  262.5 362.9 %feed_forward.1 = (bf16[4,64,2048]{2,1,0:T(8,128)(2,1)}, bf16[4,64,2048]{2,1,0:T(8,128)(2,1)}, bf16[4,2,256,2048]{3,2,1,0:T(8,128)(2,1)}, bf16[4,2,256,2048]{3,2...) custom-call(bf16[4,64,2048]{2,1,0:T(8,128)(2,1)} %bitcast.233, ...), custom_call_target="tpu_custom_call" | custom-call | flops 35433480192 | bytes 50331648 | tf_op jit(solution)/shard_map/feed_forward/pallas_call | solution.py:819
  625.5 1.7 fusion.15
  627.2 3.9 multiply_reduce_fusion
  632.1 3.2 fusion.82
  635.3 30.7 %cube_gather.3 = bf16[2,2,2,128,2048]{4,3,2,1,0:T(8,128)(2,1)S(1)} custom-call(bf16[128,2048]{1,0:T(8,128)(2,1)S(1)} %get-tuple-element.168.x_ref), custom_call_target="tpu_custom_call" | custom-call | bytes 20971520 | tf_op jit(solution)/shard_map/cube_gather/pallas_call | solution.py:371
  666.0 3.3 fusion.2
  670.9 6.1 convolution_convert_fusion.1
  677.8 9.5 %convolution_convert_fusion.5 = bf16[1024,1024]{1,0:T(8,128)(2,1)} fusion(bf16[1024,2048]{1,0:T(8,128)(2,1)} %get-tuple-element.70, bf16[1024,2048]{1,0:T(8,128)(2,1)} %all-gather.2.cloned.1.call-done), kind=kOutput, calls=%fused_computation.22 | convolution fusion | flops 4296015872 | bytes 10485760 | tf_op jit(solution)/shard_map/dot_general | solution.py:28
  687.3 25.7 %attend_back.1 = (bf16[2,4,2,64,1024]{4,3,2,1,0:T(8,128)(2,1)}, bf16[4,2,2,4,2,64,256]{6,5,4,3,2,1,0:T(8,128)(2,1)}) custom-call(bf16[2,4,2,64,1024]{4,3,2,1,0:T(8,128)(2,1)} %get-tuple-element.68.query_ref, bf16[4,2,2,4,2,64,256]{6,5,4,3,2,1,0:T(8,128)(2,1)} %bitcast.206, bf16[2,4,2,64,1024]{4,3,2,1,0:T(8,128)(2,1)} %bitcast.284, ...), custom_call_target="tpu_custom_call" | custom-call | flops 2684354560 | bytes 14680064 | tf_op jit(solution)/shard_map/attend_back/pallas_call | solution.py:197
  713.0 9.4 %convolution_convert_fusion = bf16[2048,1024]{1,0:T(8,128)(2,1)} fusion(bf16[1024,2048]{1,0:T(8,128)(2,1)} %copy-done.6, bf16[1024,1024]{1,0:T(8,128)(2,1)} %bitcast.225), kind=kOutput, calls=%fused_computation.9 | convolution fusion | flops 4297064448 | bytes 10485760 | tf_op jit(solution)/shard_map/dot_general | solution.py:24
  722.5 2.2 copy-done.5
  724.7 28.6 %cube_reduce.4 = bf16[2048,256]{1,0:T(8,128)(2,1)S(1)} custom-call(bf16[1,2,2,2048,256]{4,3,2,1,0:T(8,128)(2,1)S(1)} %bitcast.207), custom_call_target="tpu_custom_call" | custom-call | tf_op jit(solution)/shard_map/cube_reduce/pallas_call | solution.py:307
  753.6 2.8 fusion.29
  757.1 2.2 copy-done.12
  759.3 1.7 copy-done.16
  761.0 1.8 copy-done.17
  762.8 10.3 %input_gradient.1 = bf16[1024,2048]{1,0:T(8,128)(2,1)S(1)} custom-call(bf16[1024,1024]{1,0:T(8,128)(2,1)S(1)} %bitcast.226, bf16[2048,1024]{1,0:T(8,128)(2,1)S(1)} %bitcast.221, bf16[2,1024,256]{2,1,0:T(8,128)(2,1)S(1)} %bitcast.212, bf16[2048,512]{1,0:T(8,128)(2,1)S(1)} %bitcast.224, f32[1024,4]{1,0:T(8,128)S(1)} %copy.106.dl_ref, ...), custom_call_target="tpu_custom_call" | custom-call | flops 6442450944 | bytes 12582912 | tf_op jit(solution)/shard_map/input_gradient/pallas_call | solution.py:1271
  773.1 29.5 %cube_reduce.5 = bf16[128,2048]{1,0:T(8,128)(2,1)S(1)} custom-call(bf16[2,2,2,128,2048]{4,3,2,1,0:T(8,128)(2,1)S(1)} %bitcast.208), custom_call_target="tpu_custom_call" | custom-call | tf_op jit(solution)/shard_map/cube_reduce/pallas_call | solution.py:307
  803.4 3.7 convolution_convert_fusion.3
  807.1 1.4 convolution_convert_fusion.4
  808.5 1.5 pad_maximum_fusion.g_hbm
  810.0 1.6 bitcast_convert_fusion
  811.6 2.1 fusion.9
  814.2 8.1 convolution_bitcast_fusion.2
  822.3 8.1 convolution_bitcast_fusion.1
  830.5 8.4 convolution_bitcast_fusion
  838.9 1.2 copy-done.9
  840.1 50.2 %last_exchange.1 = (f32[10,64]{1,0:T(8,128)S(1)}, f32[256,2048]{1,0:T(8,128)S(1)}, f32[64,2048]{1,0:T(8,128)S(1)}, f32[64,2048]{1,0:T(8,128)S(1)}) custom-call(f32[32,10,64]{2,1,0:T(8,128)S(1)} %maximum_bitcast_fusion.x_ref, bf16[2,256,1024]{2,1,0:T(8,128)(2,1)S(1)} %bitcast.215, bf16[4,512,512]{2,1,0:T(8,128)(2,1)} %pad_maximum_fusion.g_hbm), custom_call_target="tpu_custom_call" | custom-call | tf_op jit(solution)/shard_map/last_exchange/pallas_call | solution.py:1013
  891.4 1.3 copy.135
  (180 shorter events, 20.3 us)
Async XLA Ops:
  7.2 210.6 %all-gather.2.cloned.1.call-start = ((), (), s32[]{:S(2)}) async-start(), calls=%async_computation.2 | async-start | bytes 5242880 | tf_op jit(solution)/shard_map/all_gather | solution.py:1346
  9.7 1.0 copy-start
  10.8 1.2 copy-start.8
  12.0 0.9 copy-start.10
  13.0 0.9 copy-start.11
  136.5 1.3 copy-start.14
  137.8 615.8 %reduce-scatter.3.cloned.1.call-start = ((), (), s32[]{:S(2)}) async-start(), calls=%async_computation.3 | async-start | bytes 5242880 | tf_op jit(solution)/shard_map/reduce_scatter | solution.py:1350
  140.8 2.2 copy-start.13
  143.0 1.8 copy-start.15
  150.3 2.0 copy-start.6
  180.2 2.0 copy-start.4
  195.8 20.0 %copy-start.27 = (s32[2,1,64,2]{2,3,1,0:T(2,128)S(1)}, s32[2,1,64,2]{2,3,1,0:T(2,128)}, u32[]{:S(2)}) copy-start(s32[2,1,64,2]{2,3,1,0:T(2,128)} %param.30) | copy-start | bytes 3076
  195.8 20.2 %copy-start.29 = (s32[2,1,64]{2,1,0:T(1,128)S(1)}, s32[2,1,64]{2,1,0:T(1,128)}, u32[]{:S(2)}) copy-start(s32[2,1,64]{2,1,0:T(1,128)} %param.31) | copy-start | bytes 1540
  195.8 20.5 %copy-start.20 = (bf16[2,1,64,2048]{3,2,1,0:T(8,128)(2,1)S(1)}, bf16[2,1,64,2048]{3,2,1,0:T(8,128)(2,1)}, u32[]{:S(2)}) copy-start(bf16[2,1,64,2048]{3,2,1,0:T(8,128)(2,1)} %param.33) | copy-start | bytes 1572868
  227.1 30.6 %copy-start.1 = (bf16[2,1,64,2048]{3,2,1,0:T(8,128)(2,1)S(1)}, bf16[2,1,64,2048]{3,2,1,0:T(8,128)(2,1)}, u32[]{:S(2)}) copy-start(bf16[2,1,64,2048]{3,2,1,0:T(8,128)(2,1)} %param.17) | copy-start | bytes 1572868
  257.6 0.8 copy-start.2
  258.7 2.4 copy-start.23
  625.5 5.8 copy-start.3
  625.5 6.6 copy-start.21
  627.1 8.2 copy-start.18
  632.1 33.9 %copy-start.25 = (bf16[1024,2048]{1,0:T(8,128)(2,1)S(1)}, bf16[1024,2048]{1,0:T(8,128)(2,1)}, u32[]{:S(2)}) copy-start(bf16[1024,2048]{1,0:T(8,128)(2,1)} %get-tuple-element.195) | copy-start | bytes 12582916
  669.3 1.6 copy-start.28
  677.0 161.8 %reduce-scatter.5.cloned.1.call-start = ((), (), s32[]{:S(2)}) async-start(), calls=%async_computation.4 | async-start | bytes 5242880 | tf_op jit(solution)/shard_map/reduce_scatter | solution.py:1350
  713.0 40.4 %copy-start.24 = (bf16[128,2048]{1,0:T(8,128)(2,1)S(1)}, bf16[128,2048]{1,0:T(8,128)(2,1)}, u32[]{:S(2)}) copy-start(bf16[128,2048]{1,0:T(8,128)(2,1)} %copy-done.23) | copy-start | bytes 1572868
  722.5 2.2 copy-start.5
  757.1 2.2 copy-start.12
  759.3 1.7 copy-start.16
  761.0 1.8 copy-start.17
  803.4 3.7 copy-start.7
  807.1 6.6 slice-start.2
  808.5 1.6 copy-start.26
  808.5 3.1 copy-start.19
  808.5 3.1 copy-start.22
  808.5 5.2 slice-start.3
  810.0 4.2 copy-start.32
  814.2 8.1 copy-start.31
  814.2 16.3 %slice-start = ((s8[8388608]{0:T(1024)(128)(4,1)}), s8[4194304]{0:T(1024)(128)(4,1)S(1)}, s32[]{:S(2)}) async-start(s8[8388608]{0:T(1024)(128)(4,1)} %bitcast.274), calls=%async_computation.5 | async-start | bytes 8388608
  822.3 8.1 slice-start.1
  822.3 8.1 copy-start.30
  838.9 1.2 copy-start.9
Sparse Core Ops, SparseCore 0:
  137.9 79.7 all-gather.1
  677.2 74.7 reduce-scatter.2
  754.3 77.3 reduce-scatter.4

commit v8 on v7

--- a/solution.py
+++ b/solution.py
@@ -254,7 +254,7 @@
 
 
 def cube_reduce_kernel(pairs, x_ref, o_ref, half, quarter, got_core, got_side, got_pair, send, recv):
-    p = lax.axis_index("pair")
+    p = lax.axis_index("pair") if pairs == 2 else 0
     e = lax.axis_index("expert")
     c, y = lax.rem(e, 2), lax.div(e, 2)
     core = {"expert": e + 1 - 2 * c}
@@ -264,38 +264,66 @@
     rows = x_ref.shape[3]
     shifts = (1, 0) if pairs == 2 else (0,)
     order = [(dx, dy) for dy in (1, 0) for dx in shifts]
-    first, second = [], {}
+    copies = []
+
+    def push(source, place, slot, target):
+        copy = remote(source, place, send.at[slot], recv.at[slot], target)
+        copy.start()
+        copies.append(copy)
+        return copy
+
+    first = []
     for slot, (dx, dy) in enumerate(order):
         px, yy = lax.rem(p + dx, pairs), lax.rem(y + dy, 2)
-        copy = remote(
-            x_ref.at[px, yy, 1 - c], got_core.at[slot], send.at[slot], recv.at[slot], core
-        )
-        copy.start()
-        first.append(copy)
+        first.append(push(x_ref.at[px, yy, 1 - c], got_core.at[slot], slot, core))
     base = len(order)
+    cut = rows // 2 if pairs == 2 else rows
+    upper, lower = pl.ds(0, cut), pl.ds(cut, rows - cut)
+    to_side, to_other = {}, {}
     for slot, (dx, dy) in enumerate(order):
         px, yy = lax.rem(p + dx, pairs), lax.rem(y + dy, 2)
         first[slot].wait_recv()
         add_into(half.at[slot], [x_ref.at[px, yy, c], got_core.at[slot]], rows)
         if dy == 1:
-            copy = remote(
-                half.at[slot], got_side.at[dx], send.at[base + dx], recv.at[base + dx], side
+            to_side[dx] = push(
+                half.at[slot, upper], got_side.at[dx, upper], base + dx, side
             )
-            copy.start()
-            second[dx] = copy
-    last = None
-    for dx in shifts:
-        second[dx].wait_recv()
         if dx == 1:
-            add_into(quarter, [half.at[order.index((1, 0))], got_side.at[1]], rows)
-            last = remote(quarter, got_pair, send.at[base + 2], recv.at[base + 2], other)
-            last.start()
-    if last is not None:
-        last.wait_recv()
-        add_into(o_ref, [half.at[order.index((0, 0))], got_side.at[0], got_pair], rows)
+            to_other[dy] = push(
+                half.at[slot, lower], got_pair.at[dy, lower], base + 2 + dy, other
+            )
+    own = half.at[order.index((0, 0))]
+    if pairs == 2:
+        to_side[1].wait_recv()
+        add_into(
+            quarter.at[upper],
+            [half.at[order.index((1, 0)), upper], got_side.at[1, upper]],
+            cut,
+        )
+        to_pair = push(quarter.at[upper], got_pair.at[0, upper], base + 4, other)
+        to_other[1].wait_recv()
+        add_into(
+            quarter.at[lower],
+            [half.at[order.index((0, 1)), lower], got_pair.at[1, lower]],
+            rows - cut,
+        )
+        to_flank = push(quarter.at[lower], got_side.at[0, lower], base + 5, side)
+        to_side[0].wait_recv()
+        to_pair.wait_recv()
+        add_into(
+            o_ref.at[upper], [own.at[upper], got_side.at[0, upper], got_pair.at[0, upper]], cut
+        )
+        to_other[0].wait_recv()
+        to_flank.wait_recv()
+        add_into(
+            o_ref.at[lower],
+            [own.at[lower], got_side.at[0, lower], got_pair.at[0, lower]],
+            rows - cut,
+        )
     else:
-        add_into(o_ref, [half.at[order.index((0, 0))], got_side.at[0]], rows)
-    for copy in first + list(second.values()) + ([last] if last is not None else []):
+        to_side[0].wait_recv()
+        add_into(o_ref, [own, got_side.at[0]], rows)
+    for copy in copies:
         copy.wait_send()
 
 
@@ -313,10 +341,10 @@
             pltpu.VMEM((slots, rows, cols), value.dtype),
             pltpu.VMEM((rows, cols), value.dtype),
             pltpu.VMEM((slots, rows, cols), value.dtype),
-            pltpu.VMEM((pairs, rows, cols), value.dtype),
-            pltpu.VMEM((rows, cols), value.dtype),
-            DMA((slots + 3,)),
-            DMA((slots + 3,)),
+            pltpu.VMEM((2, rows, cols), value.dtype),
+            pltpu.VMEM((2, rows, cols), value.dtype),
+            DMA((slots + 6,)),
+            DMA((slots + 6,)),
         ],
         compiler_params=params(number, 48 * 2**20),
         cost_estimate=pl.CostEstimate(flops=0, bytes_accessed=0, transcendentals=0),
@@ -344,6 +372,9 @@
         copies.append(copy)
         return copy
 
+    rows = x_ref.shape[0]
+    cut = rows // 2
+    upper, lower = pl.ds(0, cut), pl.ds(cut, rows - cut)
     to_side = push(0, x_ref, own, side)
     to_other = push(1, x_ref, own, other) if pairs == 2 else None
     to_core = push(2, x_ref, own, core)
@@ -351,13 +382,16 @@
     if pairs == 2:
         to_other.wait_recv()
         block = o_ref.at[q, y, c]
-        far = push(3, block, block, side)
+        far = [push(3, block.at[upper], block.at[upper], side)]
         waits.append(push(4, block, block, core))
     to_side.wait_recv()
     block = o_ref.at[p, w, c]
+    if pairs == 2:
+        far.append(push(7, block.at[lower], block.at[lower], other))
     waits.append(push(5, block, block, core))
     if pairs == 2:
-        far.wait_recv()
+        for copy in far:
+            copy.wait_recv()
         block = o_ref.at[q, w, c]
         waits.append(push(6, block, block, core))
     for copy in waits:
@@ -373,7 +407,7 @@
         in_specs=[VMEM],
         out_specs=VMEM,
         out_shape=jax.ShapeDtypeStruct((pairs, 2, 2) + value.shape, value.dtype),
-        scratch_shapes=[DMA((7,)), DMA((7,)), DMA(())],
+        scratch_shapes=[DMA((8,)), DMA((8,)), DMA(())],
         compiler_params=params(number, 48 * 2**20),
         cost_estimate=pl.CostEstimate(
             flops=0, bytes_accessed=80 * value.size, transcendentals=0

time: 912 us -> 892 us (0.978)
  Pallas kernels: 744 us -> 725 us
    pallas_call x3, Pallas kernels: 88.7 us -> 73.9 us  [cube_reduce(): pl.pallas_call(partial(cube_reduce_kernel, pairs), in_specs=[VMEM], out_s...]
  transfers between devices with their start and end apart: 3 -> 3, of which waited for: 1 -> 2; matrix products, arithmetic and copies ran while one was open for 9% -> 9% of each run, Pallas kernels for 16% -> 16%
where the time goes in v8:
time: 892 us; the launch traced here: 882 us
  Pallas kernels  725 us (81%)
  matrix products  84.3 us (9%)
  local copies, waits for them, and re-layouts  35.2 us (4%)
  other arithmetic  21.9 us (2%)
  between operations  14.9 us (2%)
    pallas_call x1, Pallas kernels, feed_forward(): pl.pallas_call(ff_kernel, in_specs=[ANY] * 5, out_specs=[ANY] * 7, out_sh...  362 us
    pallas_call x1, Pallas kernels, start_all(): pl.pallas_call(partial(start_all_kernel, sizes), in_specs=[VMEM] * 6, out...  123 us
    pallas_call x3, Pallas kernels, cube_reduce(): pl.pallas_call(partial(cube_reduce_kernel, pairs), in_specs=[VMEM], out_s...  73.9 us
    pallas_call x2, Pallas kernels, cube_gather(): pl.pallas_call(partial(cube_gather_kernel, pairs), in_specs=[VMEM], out_s...  53.3 us
    pallas_call x1, Pallas kernels, last_exchange(): pl.pallas_call(partial(last_kernel, sizes), in_specs=[VMEM, VMEM, ANY], o...  51.2 us
    dot_general x9, matrix products, product_tn(): lax.dot_general(left, right, (((0,), (0,)), ((), ())), preferred_element_...  48.3 us
    unnamed x81, local copies, waits for them, and re-layouts  29 us
    pallas_call x1, Pallas kernels, attend_back(): pl.pallas_call(partial(attend_back_kernel, part // HDIM, scale), grid=gri...  25.7 us
  transfers between devices with their start and end apart: 3, of which 2 were waited for; matrix products, arithmetic and copies ran while one was open for 9% of the time, Pallas kernels for 16%

profile of v8, /device:TPU:0, one launch (start us, length us, event | category | flops | bytes accessed | tf_op | source)
XLA Modules:
  0.0 882.0 jit_solution(3560470730235234929)
XLA Ops:
  9.7 1.0 copy-done
  10.8 1.2 copy-done.8
  13.9 122.6 %start_all.1 = (bf16[2,2,2,128,2048]{4,3,2,1,0:T(8,128)(2,1)}, bf16[4,512,1024]{2,1,0:T(8,128)(2,1)}, bf16[4,512,512]{2,1,0:T(8,128)(2,1)S(1)}, bf16[32,10,64]{2,1,0:T(8,128)(2,1)S(1)}, s32[2,16,128]{2,1,0:T(8,128)S(1)}) custom-call(bf16[128,2048]{1,0:T(8,128)(2,1)S(1)} %bitcast.204, bf16[256,2048]{1,0:T(8,128)(2,1)S(1)} %bitcast.214, ...), custom_call_target="tpu_custom_call" | custom-call | tf_op jit(solution)/shard_map/start_all/pallas_call | solution.py:1264
  136.5 1.3 copy-done.14
  140.8 2.2 copy-done.13
  143.0 1.8 copy-done.15
  144.8 5.6 project.1
  150.3 2.0 copy-done.6
  152.5 27.7 %cube_gather.2 = bf16[1,2,2,2048,256]{4,3,2,1,0:T(8,128)(2,1)S(1)} custom-call(bf16[2048,256]{1,0:T(8,128)(2,1)S(1)} %bitcast.213), custom_call_target="tpu_custom_call" | custom-call | bytes 41943040 | tf_op jit(solution)/shard_map/cube_gather/pallas_call | solution.py:405
  180.3 2.0 copy-done.4
  183.3 1.2 multiply_sine_fusion
  184.5 1.3 or_select_fusion.bias_ref
  185.9 10.0 %fusion.85.raw_ref = f32[2,4,2,64,1024]{4,3,2,1,0:T(8,128)} fusion(bf16[2,4,2,64,2048]{4,3,2,1,0:T(8,128)(2,1)} %bitcast.210, bf16[2048,1024,1,1,1]{1,0,4,3,2:T(8,128)(2,1)} %bitcast.220), kind=kOutput, calls=%fused_computation.212 | convolution fusion | flops 4294967296 | bytes 12582912 | tf_op jit(solution)/shard_map/dot_general | solution.py:20
  195.9 20.0 %attend.1 = (bf16[2,4,2,64,1024]{4,3,2,1,0:T(8,128)(2,1)}, bf16[2,4,2,64,1024]{4,3,2,1,0:T(8,128)(2,1)}) custom-call(f32[2,4,2,64,1024]{4,3,2,1,0:T(8,128)} %fusion.85.raw_ref, bf16[4,2,2,4,2,64,256]{6,5,4,3,2,1,0:T(8,128)(2,1)} %bitcast.205, f32[256,64]{1,0:T(8,128)} %get-tuple-element.193.cos_ref, f32[256,64]{1,0:T(8,128)} %get-tuple-element.192.sin_ref, ...), custom_call_target="tpu_custom_call" | custom-call | flops 1073741824 | bytes 12582912 | tf_op jit(solution)/shard_map/attend/pallas_call | solution.py:179
  216.3 1.1 bitcast_convert_fusion.1
  217.8 9.3 %multiply_convert_fusion = (bf16[1024,2048]{1,0:T(8,128)(2,1)S(1)}, bf16[1024,2048]{1,0:T(8,128)(2,1)}) fusion(f32[1024]{0:T(1024)S(1)} %multiply_reduce_fusion.6, bf16[1024,1024]{1,0:T(8,128)(2,1)} %bitcast.271, bf16[1024,2048]{1,0:T(8,128)(2,1)} %all-gather.2.cloned.1.call-done), kind=kOutput, calls=%fused_computation.6 | convolution fusion | flops 4301258752 | bytes 14684160 | tf_op jit(solution)/shard_map/dot_general | solution.py:20
  227.1 22.9 %cube_reduce.3 = bf16[128,2048]{1,0:T(8,128)(2,1)S(1)} custom-call(bf16[2,2,2,128,2048]{4,3,2,1,0:T(8,128)(2,1)S(1)} %bitcast.209), custom_call_target="tpu_custom_call" | custom-call | tf_op jit(solution)/shard_map/cube_reduce/pallas_call | solution.py:335
  252.3 1.1 copy.103
  253.8 1.0 copy.102
  254.9 362.5 %feed_forward.1 = (bf16[4,64,2048]{2,1,0:T(8,128)(2,1)}, bf16[4,64,2048]{2,1,0:T(8,128)(2,1)}, bf16[4,2,256,2048]{3,2,1,0:T(8,128)(2,1)}, bf16[4,2,256,2048]{3,2...) custom-call(bf16[4,64,2048]{2,1,0:T(8,128)(2,1)} %bitcast.233, ...), custom_call_target="tpu_custom_call" | custom-call | flops 35433480192 | bytes 50331648 | tf_op jit(solution)/shard_map/feed_forward/pallas_call | solution.py:853
  617.4 1.7 fusion.15
  619.1 3.9 multiply_reduce_fusion
  624.0 3.2 fusion.82
  627.2 25.6 %cube_gather.3 = bf16[2,2,2,128,2048]{4,3,2,1,0:T(8,128)(2,1)S(1)} custom-call(bf16[128,2048]{1,0:T(8,128)(2,1)S(1)} %get-tuple-element.168.x_ref), custom_call_target="tpu_custom_call" | custom-call | bytes 20971520 | tf_op jit(solution)/shard_map/cube_gather/pallas_call | solution.py:405
  652.8 3.3 fusion.2
  657.7 6.1 convolution_convert_fusion.1
  664.7 9.4 %convolution_convert_fusion.5 = bf16[1024,1024]{1,0:T(8,128)(2,1)} fusion(bf16[1024,2048]{1,0:T(8,128)(2,1)} %get-tuple-element.70, bf16[1024,2048]{1,0:T(8,128)(2,1)} %all-gather.2.cloned.1.call-done), kind=kOutput, calls=%fused_computation.22 | convolution fusion | flops 4296015872 | bytes 10485760 | tf_op jit(solution)/shard_map/dot_general | solution.py:28
  674.1 25.7 %attend_back.1 = (bf16[2,4,2,64,1024]{4,3,2,1,0:T(8,128)(2,1)}, bf16[4,2,2,4,2,64,256]{6,5,4,3,2,1,0:T(8,128)(2,1)}) custom-call(bf16[2,4,2,64,1024]{4,3,2,1,0:T(8,128)(2,1)} %get-tuple-element.68.query_ref, bf16[4,2,2,4,2,64,256]{6,5,4,3,2,1,0:T(8,128)(2,1)} %bitcast.206, bf16[2,4,2,64,1024]{4,3,2,1,0:T(8,128)(2,1)} %bitcast.284, ...), custom_call_target="tpu_custom_call" | custom-call | flops 2684354560 | bytes 14680064 | tf_op jit(solution)/shard_map/attend_back/pallas_call | solution.py:197
  699.8 9.4 %convolution_convert_fusion = bf16[2048,1024]{1,0:T(8,128)(2,1)} fusion(bf16[1024,2048]{1,0:T(8,128)(2,1)} %copy-done.6, bf16[1024,1024]{1,0:T(8,128)(2,1)} %bitcast.225), kind=kOutput, calls=%fused_computation.9 | convolution fusion | flops 4297064448 | bytes 10485760 | tf_op jit(solution)/shard_map/dot_general | solution.py:24
  709.2 2.2 copy-done.5
  711.4 28.7 %cube_reduce.4 = bf16[2048,256]{1,0:T(8,128)(2,1)S(1)} custom-call(bf16[1,2,2,2048,256]{4,3,2,1,0:T(8,128)(2,1)S(1)} %bitcast.207), custom_call_target="tpu_custom_call" | custom-call | tf_op jit(solution)/shard_map/cube_reduce/pallas_call | solution.py:335
  740.5 2.8 fusion.29
  744.0 2.2 copy-done.12
  746.2 1.6 copy-done.16
  747.8 1.9 copy-done.17
  749.7 10.3 %input_gradient.1 = bf16[1024,2048]{1,0:T(8,128)(2,1)S(1)} custom-call(bf16[1024,1024]{1,0:T(8,128)(2,1)S(1)} %bitcast.226, bf16[2048,1024]{1,0:T(8,128)(2,1)S(1)} %bitcast.221, bf16[2,1024,256]{2,1,0:T(8,128)(2,1)S(1)} %bitcast.212, bf16[2048,512]{1,0:T(8,128)(2,1)S(1)} %bitcast.224, f32[1024,4]{1,0:T(8,128)S(1)} %copy.106.dl_ref, ...), custom_call_target="tpu_custom_call" | custom-call | flops 6442450944 | bytes 12582912 | tf_op jit(solution)/shard_map/input_gradient/pallas_call | solution.py:1305
  759.9 22.3 %cube_reduce.5 = bf16[128,2048]{1,0:T(8,128)(2,1)S(1)} custom-call(bf16[2,2,2,128,2048]{4,3,2,1,0:T(8,128)(2,1)S(1)} %bitcast.208), custom_call_target="tpu_custom_call" | custom-call | tf_op jit(solution)/shard_map/cube_reduce/pallas_call | solution.py:335
  783.0 3.7 convolution_convert_fusion.3
  786.7 1.4 convolution_convert_fusion.4
  788.2 1.5 pad_maximum_fusion.g_hbm
  789.7 1.6 bitcast_convert_fusion
  791.3 2.1 fusion.9
  793.9 8.1 convolution_bitcast_fusion.2
  802.0 8.1 convolution_bitcast_fusion.1
  810.2 8.4 convolution_bitcast_fusion
  818.6 1.2 copy-done.9
  819.9 51.2 %last_exchange.1 = (f32[10,64]{1,0:T(8,128)S(1)}, f32[256,2048]{1,0:T(8,128)S(1)}, f32[64,2048]{1,0:T(8,128)S(1)}, f32[64,2048]{1,0:T(8,128)S(1)}) custom-call(f32[32,10,64]{2,1,0:T(8,128)S(1)} %maximum_bitcast_fusion.x_ref, bf16[2,256,1024]{2,1,0:T(8,128)(2,1)S(1)} %bitcast.215, bf16[4,512,512]{2,1,0:T(8,128)(2,1)} %pad_maximum_fusion.g_hbm), custom_call_target="tpu_custom_call" | custom-call | tf_op jit(solution)/shard_map/last_exchange/pallas_call | solution.py:1047
  872.1 1.3 copy.135
  (180 shorter events, 20.4 us)
Async XLA Ops:
  7.2 210.6 %all-gather.2.cloned.1.call-start = ((), (), s32[]{:S(2)}) async-start(), calls=%async_computation.2 | async-start | bytes 5242880 | tf_op jit(solution)/shard_map/all_gather | solution.py:1380
  9.7 1.0 copy-start
  10.8 1.2 copy-start.8
  12.0 0.9 copy-start.10
  13.0 0.9 copy-start.11
  136.5 1.3 copy-start.14
  137.8 602.6 %reduce-scatter.3.cloned.1.call-start = ((), (), s32[]{:S(2)}) async-start(), calls=%async_computation.3 | async-start | bytes 5242880 | tf_op jit(solution)/shard_map/reduce_scatter | solution.py:1384
  140.8 2.2 copy-start.13
  143.0 1.8 copy-start.15
  150.3 2.0 copy-start.6
  180.3 2.0 copy-start.4
  195.8 20.0 %copy-start.27 = (s32[2,1,64,2]{2,3,1,0:T(2,128)S(1)}, s32[2,1,64,2]{2,3,1,0:T(2,128)}, u32[]{:S(2)}) copy-start(s32[2,1,64,2]{2,3,1,0:T(2,128)} %param.30) | copy-start | bytes 3076
  195.9 20.2 %copy-start.29 = (s32[2,1,64]{2,1,0:T(1,128)S(1)}, s32[2,1,64]{2,1,0:T(1,128)}, u32[]{:S(2)}) copy-start(s32[2,1,64]{2,1,0:T(1,128)} %param.31) | copy-start | bytes 1540
  195.9 20.5 %copy-start.20 = (bf16[2,1,64,2048]{3,2,1,0:T(8,128)(2,1)S(1)}, bf16[2,1,64,2048]{3,2,1,0:T(8,128)(2,1)}, u32[]{:S(2)}) copy-start(bf16[2,1,64,2048]{3,2,1,0:T(8,128)(2,1)} %param.33) | copy-start | bytes 1572868
  227.1 22.9 %copy-start.1 = (bf16[2,1,64,2048]{3,2,1,0:T(8,128)(2,1)S(1)}, bf16[2,1,64,2048]{3,2,1,0:T(8,128)(2,1)}, u32[]{:S(2)}) copy-start(bf16[2,1,64,2048]{3,2,1,0:T(8,128)(2,1)} %param.17) | copy-start | bytes 1572868
  250.0 0.8 copy-start.2
  251.0 2.4 copy-start.23
  617.4 5.8 copy-start.3
  617.4 6.6 copy-start.21
  619.0 8.2 copy-start.18
  624.0 28.8 %copy-start.25 = (bf16[1024,2048]{1,0:T(8,128)(2,1)S(1)}, bf16[1024,2048]{1,0:T(8,128)(2,1)}, u32[]{:S(2)}) copy-start(bf16[1024,2048]{1,0:T(8,128)(2,1)} %get-tuple-element.195) | copy-start | bytes 12582916
  656.1 1.6 copy-start.28
  663.9 154.7 %reduce-scatter.5.cloned.1.call-start = ((), (), s32[]{:S(2)}) async-start(), calls=%async_computation.4 | async-start | bytes 5242880 | tf_op jit(solution)/shard_map/reduce_scatter | solution.py:1384
  699.8 40.4 %copy-start.24 = (bf16[128,2048]{1,0:T(8,128)(2,1)S(1)}, bf16[128,2048]{1,0:T(8,128)(2,1)}, u32[]{:S(2)}) copy-start(bf16[128,2048]{1,0:T(8,128)(2,1)} %copy-done.23) | copy-start | bytes 1572868
  709.2 2.2 copy-start.5
  744.0 2.2 copy-start.12
  746.1 1.6 copy-start.16
  747.8 1.9 copy-start.17
  783.0 3.7 copy-start.7
  786.7 6.6 slice-start.2
  788.1 1.6 copy-start.26
  788.2 3.1 copy-start.19
  788.2 3.1 copy-start.22
  788.2 5.2 slice-start.3
  789.7 4.2 copy-start.32
  793.9 8.1 copy-start.31
  793.9 16.3 %slice-start = ((s8[8388608]{0:T(1024)(128)(4,1)}), s8[4194304]{0:T(1024)(128)(4,1)S(1)}, s32[]{:S(2)}) async-start(s8[8388608]{0:T(1024)(128)(4,1)} %bitcast.274), calls=%async_computation.5 | async-start | bytes 8388608
  802.0 8.1 slice-start.1
  802.0 8.1 copy-start.30
  818.6 1.2 copy-start.9
Sparse Core Ops, SparseCore 0:
  137.9 79.7 all-gather.1
  664.0 74.8 reduce-scatter.2
  741.3 77.3 reduce-scatter.4

commit v9 on v8

--- a/solution.py
+++ b/solution.py
@@ -534,6 +534,8 @@
     UP, DOWN, SIDE, SUMUP, SUMDOWN, SUMSIDE = (i * line for i in range(6))
     SUMTWIN, SWAP = 6 * line, 6 * line + 1
     BACK = SWAP + experts
+    PART = BACK + experts
+    EARLY = PART + experts
 
     def push(src, dst, kind, use, target):
         return remote(src, dst, send.at[kind, use], recv.at[kind, use], target)
@@ -547,6 +549,10 @@
     def to_other(kind, j):
         return push(bufs[kind].at[j, p], bufs[kind].at[j, p], kind, SIDE + j, other)
 
+    def early(kind, shift):
+        ref = bufs[kind].at[z, p, piece((e + experts - shift) % experts)]
+        return push(ref, ref, kind, EARLY + shift, other)
+
     def sum_up(kind, j):
         return push(bufs[kind].at[j, p], hop.at[kind, j], kind, SUMUP + j, up)
 
@@ -556,11 +562,23 @@
     def sum_other(kind, j):
         return push(bufs[kind].at[j, q], side.at[kind, j], kind, SUMSIDE + j, other)
 
+    def piece(index):
+        return pl.ds(pl.multiple_of(index * size, size), size)
+
+    far_expert = (e + 2) % experts
+    queue = (far_expert, far_expert + 1 - 2 * (far_expert % 2), e + 1 - 2 * (e % 2), e)
+
+    def sum_part(i):
+        return push(
+            b_buf.at[z, q, piece(queue[i])],
+            side.at[1, z, piece(queue[i])],
+            1,
+            PART + i,
+            other,
+        )
+
     def sum_twin():
         return push(bufs[1].at[twin, q], extra, 1, SUMTWIN, across)
-
-    def piece(index):
-        return pl.ds(pl.multiple_of(index * size, size), size)
 
     def save(kind, j, column):
         return pltpu.make_async_copy(
@@ -585,8 +603,10 @@
         for kind in range(2):
             if first:
                 swaps[kind][0].wait()
-                for copy in swaps[kind][1]:
-                    copy.wait_recv()
+                early(kind, 0).start()
+                for shift in range(experts - 1, 0, -1):
+                    swaps[kind][1][shift - 1].wait_recv()
+                    early(kind, shift).start()
             else:
 
                 @pl.when(j < z)
@@ -605,7 +625,8 @@
             def _():
                 to_down(kind, j).start()
 
-            to_other(kind, j).start()
+            if not first:
+                to_other(kind, j).start()
             save(kind, j, p).start()
 
     chunk = 512
@@ -653,7 +674,15 @@
 
     def arrive(j):
         for kind in range(2):
-            to_other(kind, j).wait_recv()
+            @pl.when(j == z)
+            def _():
+                for shift in range(experts):
+                    early(kind, shift).wait_recv()
+
+            @pl.when(j != z)
+            def _():
+                to_other(kind, j).wait_recv()
+
             save(kind, j, q).start()
 
     def emit(t):
@@ -720,8 +749,10 @@
     ):
         copy.start()
     sum_twin().wait_recv()
-    add_into(b_buf.at[z, q], [b_buf.at[z, q], extra], rows)
-    sum_other(1, z).start()
+    for i in range(experts):
+        part = b_buf.at[z, q, piece(queue[i])]
+        add_into(part, [part, extra.at[piece(queue[i])]], size)
+        sum_part(i).start()
 
     def back(kind):
         own = pltpu.make_async_copy(
@@ -738,6 +769,12 @@
             for shift in range(1, experts)
         ]
 
+    def back_part(i):
+        source = b_buf.at[z, p, piece(queue[i])]
+        if i == experts - 1:
+            return pltpu.make_async_copy(source, b_out.at[e], local.at[1])
+        return push(source, b_out.at[e], 1, BACK + 1 + i, {"expert": queue[i]})
+
     def fold(s, carry):
         t = line - 1 - s
         j = order(t)
@@ -752,7 +789,14 @@
             def _():
                 to_down(kind, j).wait_send()
 
-            to_other(kind, j).wait_send()
+            @pl.when(j == z)
+            def _():
+                for shift in range(experts):
+                    early(kind, shift).wait_send()
+
+            @pl.when(j != z)
+            def _():
+                to_other(kind, j).wait_send()
 
         second_half(j, p)
         for kind in range(2):
@@ -762,7 +806,7 @@
                 add_into(mine, [mine, side.at[kind, j]], rows)
             else:
 
-                @pl.when(j != twin)
+                @pl.when((j != twin) & (j != z))
                 def _():
                     sum_other(kind, j).wait_recv()
                     add_into(mine, [mine, side.at[kind, j]], rows)
@@ -784,8 +828,15 @@
 
             @pl.when(j == z)
             def _():
-                for copy in back(kind):
-                    copy.start()
+                if kind == 0:
+                    for copy in back(0):
+                        copy.start()
+                else:
+                    for i in range(experts):
+                        part = b_buf.at[z, p, piece(queue[i])]
+                        sum_part(i).wait_recv()
+                        add_into(part, [part, side.at[1, z, piece(queue[i])]], size)
+                        back_part(i).start()
 
             @pl.when(j > z)
             def _():
@@ -803,9 +854,10 @@
 
     lax.fori_loop(0, line, fold, 0)
 
-    for kind in range(2):
-        for copy in back(kind):
-            copy.wait()
+    for copy in back(0):
+        copy.wait()
+    for i in range(experts):
+        back_part(i).wait()
 
     def drain(j, carry):
         for kind in range(2):
@@ -813,7 +865,7 @@
                 sum_other(kind, j).wait_send()
             else:
 
-                @pl.when(j != twin)
+                @pl.when((j != twin) & (j != z))
                 def _():
                     sum_other(kind, j).wait_send()
 
@@ -829,6 +881,8 @@
 
     lax.fori_loop(0, line, drain, 0)
     sum_twin().wait_send()
+    for i in range(experts):
+        sum_part(i).wait_send()
     for copy in (
         pltpu.make_async_copy(mid.at[:, :, 0], inner_save, local.at[2]),
         pltpu.make_async_copy(mid.at[:, :, 1], dgate_save, local.at[3]),
@@ -848,7 +902,7 @@
     back = jax.ShapeDtypeStruct(first.shape, BF16)
     wide = jax.ShapeDtypeStruct(blocks + (width,), BF16)
     thin = jax.ShapeDtypeStruct(blocks + (hidden,), BF16)
-    uses = 6 * line + 2 + 2 * experts
+    uses = 6 * line + 2 + 4 * experts
     total = line * pairs * rows
     return pl.pallas_call(
         ff_kernel,
@@ -1145,6 +1199,40 @@
     ]
     for copy in keeps:
         copy.start()
+    def walker(block, base):
+        def to_up(j, d):
+            ref = block(j)
+            return remote(ref, ref, send.at[base + d], recv.at[base + d], {"line": z + 1})
+
+        def to_down(j, d):
+            ref, at = block(j), base + line + d
+            return remote(ref, ref, send.at[at], recv.at[at], {"line": z - 1})
+
+        return to_up, to_down
+
+    def q_rows(member):
+        return lambda j: q_out.at[j, pl.ds(pl.multiple_of(member * rows, rows), rows)]
+
+    stride = 2 * line + 2
+    walkers = [
+        walker(q_rows(p), WALK),
+        walker(lambda j: kv_out.at[j], WALK + stride),
+        walker(q_rows(1 - p), WALK + 2 * stride),
+    ]
+
+    def begin(which):
+        to_up, to_down = walkers[which]
+
+        @pl.when(z < line - 1)
+        def _():
+            to_up(z, 1).start()
+
+        @pl.when(z > 0)
+        def _():
+            to_down(z, 1).start()
+
+    keeps[0].wait()
+    begin(0)
     own = tok_out.at[p, y, c]
     to_side = push(TOK, tok_ref, own, side)
     to_other = push(TOK + 1, tok_ref, own, other)
@@ -1165,38 +1253,12 @@
 
     lax.fori_loop(1, count, small_start, 0)
 
-    def walker(ref, base):
-        def to_up(j, d):
-            return remote(
-                ref.at[j], ref.at[j], send.at[base + d], recv.at[base + d], {"line": z + 1}
-            )
-
-        def to_down(j, d):
-            at = base + line + d
-            return remote(ref.at[j], ref.at[j], send.at[at], recv.at[at], {"line": z - 1})
-
-        return to_up, to_down
-
-    walkers = [walker(q_out, WALK), walker(kv_out, WALK + 2 * line + 2)]
-
-    def begin(which):
-        to_up, to_down = walkers[which]
-
-        @pl.when(z < line - 1)
-        def _():
-            to_up(z, 1).start()
-
-        @pl.when(z > 0)
-        def _():
-            to_down(z, 1).start()
-
     keeps[1].wait()
     for copy in pieces:
         copy.wait_recv()
     begin(1)
-    keeps[0].wait()
     q_swap.wait_recv()
-    begin(0)
+    begin(2)
     to_other.wait_recv()
     block = tok_out.at[1 - p, y, c]
     far = push(TOK + 3, block, block, side)
@@ -1209,7 +1271,7 @@
     waits.append(push(TOK + 6, block, block, core))
 
     for d in range(1, line):
-        for to_up, to_down in walkers[::-1]:
+        for to_up, to_down in walkers:
 
             @pl.when(z - d >= 0)
             def _():
@@ -1260,7 +1322,7 @@
     size = w_key.shape[0]
     feats = width // pairs
     thin = 2 * feats // experts
-    uses = 9 + trees + 4 * line + 4
+    uses = 9 + trees + 6 * line + 6
     return pl.pallas_call(
         partial(start_all_kernel, sizes),
         in_specs=[VMEM] * 6,

time: 892 us -> 881 us (0.988)
  Pallas kernels: 725 us -> 711 us
    pallas_call x1, Pallas kernels: 362 us -> 351 us  [feed_forward(): pl.pallas_call(ff_kernel, in_specs=[ANY] * 5, out_specs=[ANY] * 7, out_sh...]
  transfers between devices with their start and end apart: 3 -> 3, of which waited for: 2 -> 3; matrix products, arithmetic and copies ran while one was open for 9% -> 9% of each run, Pallas kernels for 16% -> 16%
where the time goes in v9:
time: 881 us; the launch traced here: 870 us
  Pallas kernels  711 us (81%)
  matrix products  84.3 us (10%)
  local copies, waits for them, and re-layouts  35 us (4%)
  other arithmetic  21.9 us (2%)
  between operations  14.9 us (2%)
    pallas_call x1, Pallas kernels, feed_forward(): pl.pallas_call(ff_kernel, in_specs=[ANY] * 5, out_specs=[ANY] * 7, out_sh...  351 us
    pallas_call x1, Pallas kernels, start_all(): pl.pallas_call(partial(start_all_kernel, sizes), in_specs=[VMEM] * 6, out...  123 us
    pallas_call x3, Pallas kernels, cube_reduce(): pl.pallas_call(partial(cube_reduce_kernel, pairs), in_specs=[VMEM], out_s...  75 us
    pallas_call x1, Pallas kernels, last_exchange(): pl.pallas_call(partial(last_kernel, sizes), in_specs=[VMEM, VMEM, ANY], o...  51.2 us
    pallas_call x2, Pallas kernels, cube_gather(): pl.pallas_call(partial(cube_gather_kernel, pairs), in_specs=[VMEM], out_s...  49.1 us
    dot_general x9, matrix products, product_tn(): lax.dot_general(left, right, (((0,), (0,)), ((), ())), preferred_element_...  48.5 us
    unnamed x81, local copies, waits for them, and re-layouts  28.8 us
    pallas_call x1, Pallas kernels, attend_back(): pl.pallas_call(partial(attend_back_kernel, part // HDIM, scale), grid=gri...  25.7 us
  transfers between devices with their start and end apart: 3, of which 3 were waited for; matrix products, arithmetic and copies ran while one was open for 9% of the time, Pallas kernels for 16%

profile of v9, /device:TPU:0, one launch (start us, length us, event | category | flops | bytes accessed | tf_op | source)
XLA Modules:
  0.0 870.4 jit_solution(6893718861859712239)
XLA Ops:
  10.8 1.2 copy-done.8
  13.9 122.8 %start_all.1 = (bf16[2,2,2,128,2048]{4,3,2,1,0:T(8,128)(2,1)}, bf16[4,512,1024]{2,1,0:T(8,128)(2,1)}, bf16[4,512,512]{2,1,0:T(8,128)(2,1)S(1)}, bf16[32,10,64]{2,1,0:T(8,128)(2,1)S(1)}, s32[2,16,128]{2,1,0:T(8,128)S(1)}) custom-call(bf16[128,2048]{1,0:T(8,128)(2,1)S(1)} %bitcast.204, bf16[256,2048]{1,0:T(8,128)(2,1)S(1)} %bitcast.214, ...), custom_call_target="tpu_custom_call" | custom-call | tf_op jit(solution)/shard_map/start_all/pallas_call | solution.py:1326
  136.7 1.3 copy-done.14
  141.0 2.2 copy-done.13
  143.2 1.8 copy-done.15
  145.0 5.6 project.1
  150.5 2.0 copy-done.6
  152.7 27.7 %cube_gather.2 = bf16[1,2,2,2048,256]{4,3,2,1,0:T(8,128)(2,1)S(1)} custom-call(bf16[2048,256]{1,0:T(8,128)(2,1)S(1)} %bitcast.213), custom_call_target="tpu_custom_call" | custom-call | bytes 41943040 | tf_op jit(solution)/shard_map/cube_gather/pallas_call | solution.py:405
  180.5 2.0 copy-done.4
  183.5 1.2 multiply_sine_fusion
  184.8 1.3 or_select_fusion.bias_ref
  186.1 10.0 %fusion.85.raw_ref = f32[2,4,2,64,1024]{4,3,2,1,0:T(8,128)} fusion(bf16[2,4,2,64,2048]{4,3,2,1,0:T(8,128)(2,1)} %bitcast.210, bf16[2048,1024,1,1,1]{1,0,4,3,2:T(8,128)(2,1)} %bitcast.220), kind=kOutput, calls=%fused_computation.212 | convolution fusion | flops 4294967296 | bytes 12582912 | tf_op jit(solution)/shard_map/dot_general | solution.py:20
  196.1 20.0 %attend.1 = (bf16[2,4,2,64,1024]{4,3,2,1,0:T(8,128)(2,1)}, bf16[2,4,2,64,1024]{4,3,2,1,0:T(8,128)(2,1)}) custom-call(f32[2,4,2,64,1024]{4,3,2,1,0:T(8,128)} %fusion.85.raw_ref, bf16[4,2,2,4,2,64,256]{6,5,4,3,2,1,0:T(8,128)(2,1)} %bitcast.205, f32[256,64]{1,0:T(8,128)} %get-tuple-element.193.cos_ref, f32[256,64]{1,0:T(8,128)} %get-tuple-element.192.sin_ref, ...), custom_call_target="tpu_custom_call" | custom-call | flops 1073741824 | bytes 12582912 | tf_op jit(solution)/shard_map/attend/pallas_call | solution.py:179
  216.6 1.1 bitcast_convert_fusion.1
  218.0 9.3 %multiply_convert_fusion = (bf16[1024,2048]{1,0:T(8,128)(2,1)S(1)}, bf16[1024,2048]{1,0:T(8,128)(2,1)}) fusion(f32[1024]{0:T(1024)S(1)} %multiply_reduce_fusion.6, bf16[1024,1024]{1,0:T(8,128)(2,1)} %bitcast.271, bf16[1024,2048]{1,0:T(8,128)(2,1)} %all-gather.2.cloned.1.call-done), kind=kOutput, calls=%fused_computation.6 | convolution fusion | flops 4301258752 | bytes 14684160 | tf_op jit(solution)/shard_map/dot_general | solution.py:20
  227.3 22.9 %cube_reduce.3 = bf16[128,2048]{1,0:T(8,128)(2,1)S(1)} custom-call(bf16[2,2,2,128,2048]{4,3,2,1,0:T(8,128)(2,1)S(1)} %bitcast.209), custom_call_target="tpu_custom_call" | custom-call | tf_op jit(solution)/shard_map/cube_reduce/pallas_call | solution.py:335
  252.6 1.1 copy.103
  255.1 351.3 %feed_forward.1 = (bf16[4,64,2048]{2,1,0:T(8,128)(2,1)}, bf16[4,64,2048]{2,1,0:T(8,128)(2,1)}, bf16[4,2,256,2048]{3,2,1,0:T(8,128)(2,1)}, bf16[4,2,256,2048]{3,2...) custom-call(bf16[4,64,2048]{2,1,0:T(8,128)(2,1)} %bitcast.233, ...), custom_call_target="tpu_custom_call" | custom-call | flops 35433480192 | bytes 50331648 | tf_op jit(solution)/shard_map/feed_forward/pallas_call | solution.py:907
  606.4 1.7 fusion.15
  608.1 3.9 multiply_reduce_fusion
  613.0 3.2 fusion.82
  616.2 21.3 %cube_gather.3 = bf16[2,2,2,128,2048]{4,3,2,1,0:T(8,128)(2,1)S(1)} custom-call(bf16[128,2048]{1,0:T(8,128)(2,1)S(1)} %get-tuple-element.168.x_ref), custom_call_target="tpu_custom_call" | custom-call | bytes 20971520 | tf_op jit(solution)/shard_map/cube_gather/pallas_call | solution.py:405
  637.6 3.3 fusion.2
  642.5 6.1 convolution_convert_fusion.1
  649.4 9.4 %convolution_convert_fusion.5 = bf16[1024,1024]{1,0:T(8,128)(2,1)} fusion(bf16[1024,2048]{1,0:T(8,128)(2,1)} %get-tuple-element.70, bf16[1024,2048]{1,0:T(8,128)(2,1)} %all-gather.2.cloned.1.call-done), kind=kOutput, calls=%fused_computation.22 | convolution fusion | flops 4296015872 | bytes 10485760 | tf_op jit(solution)/shard_map/dot_general | solution.py:28
  658.8 25.7 %attend_back.1 = (bf16[2,4,2,64,1024]{4,3,2,1,0:T(8,128)(2,1)}, bf16[4,2,2,4,2,64,256]{6,5,4,3,2,1,0:T(8,128)(2,1)}) custom-call(bf16[2,4,2,64,1024]{4,3,2,1,0:T(8,128)(2,1)} %get-tuple-element.68.query_ref, bf16[4,2,2,4,2,64,256]{6,5,4,3,2,1,0:T(8,128)(2,1)} %bitcast.206, bf16[2,4,2,64,1024]{4,3,2,1,0:T(8,128)(2,1)} %bitcast.284, ...), custom_call_target="tpu_custom_call" | custom-call | flops 2684354560 | bytes 14680064 | tf_op jit(solution)/shard_map/attend_back/pallas_call | solution.py:197
  684.5 9.5 %convolution_convert_fusion = bf16[2048,1024]{1,0:T(8,128)(2,1)} fusion(bf16[1024,2048]{1,0:T(8,128)(2,1)} %copy-done.6, bf16[1024,1024]{1,0:T(8,128)(2,1)} %bitcast.225), kind=kOutput, calls=%fused_computation.9 | convolution fusion | flops 4297064448 | bytes 10485760 | tf_op jit(solution)/shard_map/dot_general | solution.py:24
  694.0 2.2 copy-done.5
  696.2 29.2 %cube_reduce.4 = bf16[2048,256]{1,0:T(8,128)(2,1)S(1)} custom-call(bf16[1,2,2,2048,256]{4,3,2,1,0:T(8,128)(2,1)S(1)} %bitcast.207), custom_call_target="tpu_custom_call" | custom-call | tf_op jit(solution)/shard_map/cube_reduce/pallas_call | solution.py:335
  725.7 1.5 reduce-scatter.3.cloned.1.call-done
  727.2 2.8 fusion.29
  730.7 2.2 copy-done.12
  732.9 1.6 copy-done.16
  734.5 1.6 copy-done.17
  736.1 10.3 %input_gradient.1 = bf16[1024,2048]{1,0:T(8,128)(2,1)S(1)} custom-call(bf16[1024,1024]{1,0:T(8,128)(2,1)S(1)} %bitcast.226, bf16[2048,1024]{1,0:T(8,128)(2,1)S(1)} %bitcast.221, bf16[2,1024,256]{2,1,0:T(8,128)(2,1)S(1)} %bitcast.212, bf16[2048,512]{1,0:T(8,128)(2,1)S(1)} %bitcast.224, f32[1024,4]{1,0:T(8,128)S(1)} %copy.106.dl_ref, ...), custom_call_target="tpu_custom_call" | custom-call | flops 6442450944 | bytes 12582912 | tf_op jit(solution)/shard_map/input_gradient/pallas_call | solution.py:1367
  746.4 22.9 %cube_reduce.5 = bf16[128,2048]{1,0:T(8,128)(2,1)S(1)} custom-call(bf16[2,2,2,128,2048]{4,3,2,1,0:T(8,128)(2,1)S(1)} %bitcast.208), custom_call_target="tpu_custom_call" | custom-call | tf_op jit(solution)/shard_map/cube_reduce/pallas_call | solution.py:335
  770.1 3.7 convolution_convert_fusion.3
  773.9 1.4 convolution_convert_fusion.4
  775.3 1.5 pad_maximum_fusion.g_hbm
  776.8 1.6 bitcast_convert_fusion
  778.4 2.1 fusion.9
  781.0 8.1 convolution_bitcast_fusion.2
  789.2 8.1 convolution_bitcast_fusion.1
  797.3 8.4 convolution_bitcast_fusion
  805.7 1.3 reduce-scatter.5.cloned.1.call-done
  807.0 1.2 copy-done.9
  808.2 51.2 %last_exchange.1 = (f32[10,64]{1,0:T(8,128)S(1)}, f32[256,2048]{1,0:T(8,128)S(1)}, f32[64,2048]{1,0:T(8,128)S(1)}, f32[64,2048]{1,0:T(8,128)S(1)}) custom-call(f32[32,10,64]{2,1,0:T(8,128)S(1)} %maximum_bitcast_fusion.x_ref, bf16[2,256,1024]{2,1,0:T(8,128)(2,1)S(1)} %bitcast.215, bf16[4,512,512]{2,1,0:T(8,128)(2,1)} %pad_maximum_fusion.g_hbm), custom_call_target="tpu_custom_call" | custom-call | tf_op jit(solution)/shard_map/last_exchange/pallas_call | solution.py:1101
  860.5 1.3 copy.135
  (180 shorter events, 22.4 us)
Async XLA Ops:
  7.2 210.8 %all-gather.2.cloned.1.call-start = ((), (), s32[]{:S(2)}) async-start(), calls=%async_computation.2 | async-start | bytes 5242880 | tf_op jit(solution)/shard_map/all_gather | solution.py:1442
  9.7 1.0 copy-start
  10.8 1.2 copy-start.8
  12.0 0.9 copy-start.10
  13.0 0.9 copy-start.11
  136.7 1.3 copy-start.14
  138.0 589.2 %reduce-scatter.3.cloned.1.call-start = ((), (), s32[]{:S(2)}) async-start(), calls=%async_computation.3 | async-start | bytes 5242880 | tf_op jit(solution)/shard_map/reduce_scatter | solution.py:1446
  141.0 2.2 copy-start.13
  143.2 1.8 copy-start.15
  150.5 2.0 copy-start.6
  180.5 2.0 copy-start.4
  196.1 20.0 %copy-start.27 = (s32[2,1,64,2]{2,3,1,0:T(2,128)S(1)}, s32[2,1,64,2]{2,3,1,0:T(2,128)}, u32[]{:S(2)}) copy-start(s32[2,1,64,2]{2,3,1,0:T(2,128)} %param.30) | copy-start | bytes 3076
  196.1 20.2 %copy-start.29 = (s32[2,1,64]{2,1,0:T(1,128)S(1)}, s32[2,1,64]{2,1,0:T(1,128)}, u32[]{:S(2)}) copy-start(s32[2,1,64]{2,1,0:T(1,128)} %param.31) | copy-start | bytes 1540
  196.1 20.5 %copy-start.20 = (bf16[2,1,64,2048]{3,2,1,0:T(8,128)(2,1)S(1)}, bf16[2,1,64,2048]{3,2,1,0:T(8,128)(2,1)}, u32[]{:S(2)}) copy-start(bf16[2,1,64,2048]{3,2,1,0:T(8,128)(2,1)} %param.33) | copy-start | bytes 1572868
  227.3 22.9 %copy-start.1 = (bf16[2,1,64,2048]{3,2,1,0:T(8,128)(2,1)S(1)}, bf16[2,1,64,2048]{3,2,1,0:T(8,128)(2,1)}, u32[]{:S(2)}) copy-start(bf16[2,1,64,2048]{3,2,1,0:T(8,128)(2,1)} %param.17) | copy-start | bytes 1572868
  250.2 0.8 copy-start.2
  251.3 2.4 copy-start.23
  606.4 5.8 copy-start.3
  606.4 6.6 copy-start.21
  608.1 8.2 copy-start.18
  613.0 24.6 %copy-start.25 = (bf16[1024,2048]{1,0:T(8,128)(2,1)S(1)}, bf16[1024,2048]{1,0:T(8,128)(2,1)}, u32[]{:S(2)}) copy-start(bf16[1024,2048]{1,0:T(8,128)(2,1)} %get-tuple-element.195) | copy-start | bytes 12582916
  640.9 1.6 copy-start.28
  648.6 158.3 %reduce-scatter.5.cloned.1.call-start = ((), (), s32[]{:S(2)}) async-start(), calls=%async_computation.4 | async-start | bytes 5242880 | tf_op jit(solution)/shard_map/reduce_scatter | solution.py:1446
  684.5 41.0 %copy-start.24 = (bf16[128,2048]{1,0:T(8,128)(2,1)S(1)}, bf16[128,2048]{1,0:T(8,128)(2,1)}, u32[]{:S(2)}) copy-start(bf16[128,2048]{1,0:T(8,128)(2,1)} %copy-done.23) | copy-start | bytes 1572868
  694.0 2.2 copy-start.5
  730.7 2.2 copy-start.12
  732.9 1.6 copy-start.16
  734.5 1.6 copy-start.17
  770.1 3.8 copy-start.7
  773.8 6.6 slice-start.2
  775.2 1.6 copy-start.26
  775.3 3.1 copy-start.19
  775.3 3.1 copy-start.22
  775.3 5.2 slice-start.3
  776.8 4.2 copy-start.32
  781.0 8.1 copy-start.31
  781.0 16.3 %slice-start = ((s8[8388608]{0:T(1024)(128)(4,1)}), s8[4194304]{0:T(1024)(128)(4,1)S(1)}, s32[]{:S(2)}) async-start(s8[8388608]{0:T(1024)(128)(4,1)} %bitcast.274), calls=%async_computation.5 | async-start | bytes 8388608
  789.2 8.1 slice-start.1
  789.2 8.1 copy-start.30
  807.0 1.2 copy-start.9
Sparse Core Ops, SparseCore 0:
  138.2 79.7 all-gather.1
  648.8 78.4 reduce-scatter.2
  729.6 77.3 reduce-scatter.4

commit v10 on v9

--- a/solution.py
+++ b/solution.py
@@ -632,26 +632,43 @@
     chunk = 512
     steps = width // chunk
 
-    def first_half(j, column):
-        for index in range(3):
+    part = 32
+
+    def rows_half(j, column):
+        for index in range(2):
             acc[index] = jnp.zeros(acc.shape[1:], F32)
 
-        def one(k, carry):
-            where = pl.ds(pl.multiple_of(k * chunk, chunk), chunk)
+        def one(n, carry):
+            where = pl.ds(pl.multiple_of(n * chunk, chunk), chunk)
             left = a_buf[j, column, :, where]
             acc[0] += product_nt(left, w_gate[:, where])
             acc[1] += product_nt(left, w_up[:, where])
+            return carry
+
+        lax.fori_loop(0, steps, one, 0)
+
+        def two(i, carry):
+            where = pl.ds(pl.multiple_of(i * part, part), part)
+            gate = acc[0, where]
+            mid[j, column, 0, where] = (gate * jax.nn.sigmoid(gate) * acc[1, where]).astype(BF16)
+            return carry
+
+        lax.fori_loop(0, rows // part, two, 0)
+
+    def grads_half(j, column):
+        acc[2] = jnp.zeros(acc.shape[1:], F32)
+
+        def one(n, carry):
+            where = pl.ds(pl.multiple_of(n * chunk, chunk), chunk)
             acc[2] += product_nt(b_buf[j, column, :, where], w_down[:, where])
             return carry
 
         lax.fori_loop(0, steps, one, 0)
-        part = 32
 
         def two(i, carry):
             where = pl.ds(pl.multiple_of(i * part, part), part)
             gate, lift, grad = acc[0, where], acc[1, where], acc[2, where]
             sigma = jax.nn.sigmoid(gate)
-            mid[j, column, 0, where] = (gate * sigma * lift).astype(BF16)
             mid[j, column, 1, where] = (
                 grad * lift * sigma * (1.0 + gate * (1.0 - sigma))
             ).astype(BF16)
@@ -660,10 +677,17 @@
 
         lax.fori_loop(0, rows // part, two, 0)
 
-    def second_half(j, column):
-        def one(k, carry):
-            where = pl.ds(pl.multiple_of(k * chunk, chunk), chunk)
+    def out_half(j, column):
+        def one(n, carry):
+            where = pl.ds(pl.multiple_of(n * chunk, chunk), chunk)
             a_buf[j, column, :, where] = product(mid[j, column, 0], w_down[:, where]).astype(BF16)
+            return carry
+
+        lax.fori_loop(0, steps, one, 0)
+
+    def back_half(j, column):
+        def one(n, carry):
+            where = pl.ds(pl.multiple_of(n * chunk, chunk), chunk)
             b_buf[j, column, :, where] = (
                 product(mid[j, column, 1], w_gate[:, where])
                 + product(mid[j, column, 2], w_up[:, where])
@@ -672,18 +696,17 @@
 
         lax.fori_loop(0, steps, one, 0)
 
-    def arrive(j):
-        for kind in range(2):
-            @pl.when(j == z)
-            def _():
-                for shift in range(experts):
-                    early(kind, shift).wait_recv()
-
-            @pl.when(j != z)
-            def _():
-                to_other(kind, j).wait_recv()
-
-            save(kind, j, q).start()
+    def arrive(kind, j):
+        @pl.when(j == z)
+        def _():
+            for shift in range(experts):
+                early(kind, shift).wait_recv()
+
+        @pl.when(j != z)
+        def _():
+            to_other(kind, j).wait_recv()
+
+        save(kind, j, q).start()
 
     def emit(t):
         j = order(t)
@@ -723,15 +746,31 @@
 
                 @pl.when(c == 1)
                 def _():
-                    arrive(j)
-
-                first_half(j, column)
+                    arrive(0, j)
+
+                rows_half(j, column)
 
                 @pl.when(c == 1)
                 def _():
-                    for kind in range(2):
-                        save(kind, j, q).wait()
-                    second_half(j, column)
+                    save(0, j, q).wait()
+                    out_half(j, q)
+
+                    @pl.when(t == line - 1)
+                    def _():
+                        sum_other(0, j).start()
+
+                    arrive(1, j)
+
+                grads_half(j, column)
+
+                @pl.when(c == 1)
+                def _():
+                    save(1, j, q).wait()
+                    back_half(j, q)
+
+                    @pl.when(t == line - 1)
+                    def _():
+                        sum_other(1, j).start()
 
             return inner_carry
 
@@ -739,7 +778,7 @@
 
     lax.fori_loop(0, line + 1, step, 0)
 
-    for t in (3, 2, 1, 0):
+    for t in (2, 1, 0):
         emit(t)
 
     for copy in (
@@ -798,8 +837,8 @@
             def _():
                 to_other(kind, j).wait_send()
 
-        second_half(j, p)
         for kind in range(2):
+            (out_half, back_half)[kind](j, p)
             mine = bufs[kind].at[j, p]
             if kind == 0:
                 sum_other(kind, j).wait_recv()

time: 881 us -> 876 us (level)
  no operation moved by 1% of the time
where the time goes in v10:
time: 876 us; the launch traced here: 866 us
  Pallas kernels  706 us (81%)
  matrix products  84.3 us (10%)
  local copies, waits for them, and re-layouts  35 us (4%)
  other arithmetic  21.9 us (2%)
  between operations  14.9 us (2%)
    pallas_call x1, Pallas kernels, feed_forward(): pl.pallas_call(ff_kernel, in_specs=[ANY] * 5, out_specs=[ANY] * 7, out_sh...  346 us
    pallas_call x1, Pallas kernels, start_all(): pl.pallas_call(partial(start_all_kernel, sizes), in_specs=[VMEM] * 6, out...  123 us
    pallas_call x3, Pallas kernels, cube_reduce(): pl.pallas_call(partial(cube_reduce_kernel, pairs), in_specs=[VMEM], out_s...  74.5 us
    pallas_call x1, Pallas kernels, last_exchange(): pl.pallas_call(partial(last_kernel, sizes), in_specs=[VMEM, VMEM, ANY], o...  51.2 us
    pallas_call x2, Pallas kernels, cube_gather(): pl.pallas_call(partial(cube_gather_kernel, pairs), in_specs=[VMEM], out_s...  49.4 us
    dot_general x9, matrix products, product_tn(): lax.dot_general(left, right, (((0,), (0,)), ((), ())), preferred_element_...  48.4 us
    unnamed x81, local copies, waits for them, and re-layouts  28.8 us
    pallas_call x1, Pallas kernels, attend_back(): pl.pallas_call(partial(attend_back_kernel, part // HDIM, scale), grid=gri...  25.7 us
  transfers between devices with their start and end apart: 3, of which 3 were waited for; matrix products, arithmetic and copies ran while one was open for 9% of the time, Pallas kernels for 16%

profile of v10, /device:TPU:0, one launch (start us, length us, event | category | flops | bytes accessed | tf_op | source)
XLA Modules:
  0.0 865.6 jit_solution(1881391872865359266)
XLA Ops:
  10.8 1.2 copy-done.8
  13.9 122.8 %start_all.1 = (bf16[2,2,2,128,2048]{4,3,2,1,0:T(8,128)(2,1)}, bf16[4,512,1024]{2,1,0:T(8,128)(2,1)}, bf16[4,512,512]{2,1,0:T(8,128)(2,1)S(1)}, bf16[32,10,64]{2,1,0:T(8,128)(2,1)S(1)}, s32[2,16,128]{2,1,0:T(8,128)S(1)}) custom-call(bf16[128,2048]{1,0:T(8,128)(2,1)S(1)} %bitcast.204, bf16[256,2048]{1,0:T(8,128)(2,1)S(1)} %bitcast.214, ...), custom_call_target="tpu_custom_call" | custom-call | tf_op jit(solution)/shard_map/start_all/pallas_call | solution.py:1365
  136.7 1.3 copy-done.14
  141.0 2.2 copy-done.13
  143.2 1.8 copy-done.15
  145.0 5.6 project.1
  150.5 2.0 copy-done.6
  152.7 27.7 %cube_gather.2 = bf16[1,2,2,2048,256]{4,3,2,1,0:T(8,128)(2,1)S(1)} custom-call(bf16[2048,256]{1,0:T(8,128)(2,1)S(1)} %bitcast.213), custom_call_target="tpu_custom_call" | custom-call | bytes 41943040 | tf_op jit(solution)/shard_map/cube_gather/pallas_call | solution.py:405
  180.5 2.0 copy-done.4
  183.5 1.2 multiply_sine_fusion
  184.8 1.3 or_select_fusion.bias_ref
  186.1 10.0 %fusion.85.raw_ref = f32[2,4,2,64,1024]{4,3,2,1,0:T(8,128)} fusion(bf16[2,4,2,64,2048]{4,3,2,1,0:T(8,128)(2,1)} %bitcast.210, bf16[2048,1024,1,1,1]{1,0,4,3,2:T(8,128)(2,1)} %bitcast.220), kind=kOutput, calls=%fused_computation.212 | convolution fusion | flops 4294967296 | bytes 12582912 | tf_op jit(solution)/shard_map/dot_general | solution.py:20
  196.1 20.0 %attend.1 = (bf16[2,4,2,64,1024]{4,3,2,1,0:T(8,128)(2,1)}, bf16[2,4,2,64,1024]{4,3,2,1,0:T(8,128)(2,1)}) custom-call(f32[2,4,2,64,1024]{4,3,2,1,0:T(8,128)} %fusion.85.raw_ref, bf16[4,2,2,4,2,64,256]{6,5,4,3,2,1,0:T(8,128)(2,1)} %bitcast.205, f32[256,64]{1,0:T(8,128)} %get-tuple-element.193.cos_ref, f32[256,64]{1,0:T(8,128)} %get-tuple-element.192.sin_ref, ...), custom_call_target="tpu_custom_call" | custom-call | flops 1073741824 | bytes 12582912 | tf_op jit(solution)/shard_map/attend/pallas_call | solution.py:179
  216.6 1.1 bitcast_convert_fusion.1
  218.0 9.3 %multiply_convert_fusion = (bf16[1024,2048]{1,0:T(8,128)(2,1)S(1)}, bf16[1024,2048]{1,0:T(8,128)(2,1)}) fusion(f32[1024]{0:T(1024)S(1)} %multiply_reduce_fusion.6, bf16[1024,1024]{1,0:T(8,128)(2,1)} %bitcast.271, bf16[1024,2048]{1,0:T(8,128)(2,1)} %all-gather.2.cloned.1.call-done), kind=kOutput, calls=%fused_computation.6 | convolution fusion | flops 4301258752 | bytes 14684160 | tf_op jit(solution)/shard_map/dot_general | solution.py:20
  227.3 22.9 %cube_reduce.3 = bf16[128,2048]{1,0:T(8,128)(2,1)S(1)} custom-call(bf16[2,2,2,128,2048]{4,3,2,1,0:T(8,128)(2,1)S(1)} %bitcast.209), custom_call_target="tpu_custom_call" | custom-call | tf_op jit(solution)/shard_map/cube_reduce/pallas_call | solution.py:335
  252.6 1.1 copy.103
  255.1 346.3 %feed_forward.1 = (bf16[4,64,2048]{2,1,0:T(8,128)(2,1)}, bf16[4,64,2048]{2,1,0:T(8,128)(2,1)}, bf16[4,2,256,2048]{3,2,1,0:T(8,128)(2,1)}, bf16[4,2,256,2048]{3,2...) custom-call(bf16[4,64,2048]{2,1,0:T(8,128)(2,1)} %bitcast.233, ...), custom_call_target="tpu_custom_call" | custom-call | flops 35433480192 | bytes 50331648 | tf_op jit(solution)/shard_map/feed_forward/pallas_call | solution.py:946
  601.4 1.7 fusion.15
  603.1 3.9 multiply_reduce_fusion
  608.1 3.2 fusion.82
  611.3 21.7 %cube_gather.3 = bf16[2,2,2,128,2048]{4,3,2,1,0:T(8,128)(2,1)S(1)} custom-call(bf16[128,2048]{1,0:T(8,128)(2,1)S(1)} %get-tuple-element.168.x_ref), custom_call_target="tpu_custom_call" | custom-call | bytes 20971520 | tf_op jit(solution)/shard_map/cube_gather/pallas_call | solution.py:405
  633.0 3.3 fusion.2
  637.9 6.1 convolution_convert_fusion.1
  644.8 9.3 %convolution_convert_fusion.5 = bf16[1024,1024]{1,0:T(8,128)(2,1)} fusion(bf16[1024,2048]{1,0:T(8,128)(2,1)} %get-tuple-element.70, bf16[1024,2048]{1,0:T(8,128)(2,1)} %all-gather.2.cloned.1.call-done), kind=kOutput, calls=%fused_computation.22 | convolution fusion | flops 4296015872 | bytes 10485760 | tf_op jit(solution)/shard_map/dot_general | solution.py:28
  654.2 25.7 %attend_back.1 = (bf16[2,4,2,64,1024]{4,3,2,1,0:T(8,128)(2,1)}, bf16[4,2,2,4,2,64,256]{6,5,4,3,2,1,0:T(8,128)(2,1)}) custom-call(bf16[2,4,2,64,1024]{4,3,2,1,0:T(8,128)(2,1)} %get-tuple-element.68.query_ref, bf16[4,2,2,4,2,64,256]{6,5,4,3,2,1,0:T(8,128)(2,1)} %bitcast.206, bf16[2,4,2,64,1024]{4,3,2,1,0:T(8,128)(2,1)} %bitcast.284, ...), custom_call_target="tpu_custom_call" | custom-call | flops 2684354560 | bytes 14680064 | tf_op jit(solution)/shard_map/attend_back/pallas_call | solution.py:197
  679.9 9.5 %convolution_convert_fusion = bf16[2048,1024]{1,0:T(8,128)(2,1)} fusion(bf16[1024,2048]{1,0:T(8,128)(2,1)} %copy-done.6, bf16[1024,1024]{1,0:T(8,128)(2,1)} %bitcast.225), kind=kOutput, calls=%fused_computation.9 | convolution fusion | flops 4297064448 | bytes 10485760 | tf_op jit(solution)/shard_map/dot_general | solution.py:24
  689.4 2.2 copy-done.5
  691.6 28.7 %cube_reduce.4 = bf16[2048,256]{1,0:T(8,128)(2,1)S(1)} custom-call(bf16[1,2,2,2048,256]{4,3,2,1,0:T(8,128)(2,1)S(1)} %bitcast.207), custom_call_target="tpu_custom_call" | custom-call | tf_op jit(solution)/shard_map/cube_reduce/pallas_call | solution.py:335
  720.6 1.9 reduce-scatter.3.cloned.1.call-done
  722.5 2.8 fusion.29
  726.0 2.2 copy-done.12
  728.2 1.6 copy-done.16
  729.8 1.6 copy-done.17
  731.4 10.3 %input_gradient.1 = bf16[1024,2048]{1,0:T(8,128)(2,1)S(1)} custom-call(bf16[1024,1024]{1,0:T(8,128)(2,1)S(1)} %bitcast.226, bf16[2048,1024]{1,0:T(8,128)(2,1)S(1)} %bitcast.221, bf16[2,1024,256]{2,1,0:T(8,128)(2,1)S(1)} %bitcast.212, bf16[2048,512]{1,0:T(8,128)(2,1)S(1)} %bitcast.224, f32[1024,4]{1,0:T(8,128)S(1)} %copy.106.dl_ref, ...), custom_call_target="tpu_custom_call" | custom-call | flops 6442450944 | bytes 12582912 | tf_op jit(solution)/shard_map/input_gradient/pallas_call | solution.py:1406
  741.7 22.9 %cube_reduce.5 = bf16[128,2048]{1,0:T(8,128)(2,1)S(1)} custom-call(bf16[2,2,2,128,2048]{4,3,2,1,0:T(8,128)(2,1)S(1)} %bitcast.208), custom_call_target="tpu_custom_call" | custom-call | tf_op jit(solution)/shard_map/cube_reduce/pallas_call | solution.py:335
  765.4 3.7 convolution_convert_fusion.3
  769.1 1.4 convolution_convert_fusion.4
  770.6 1.5 pad_maximum_fusion.g_hbm
  772.1 1.6 bitcast_convert_fusion
  773.7 2.1 fusion.9
  776.3 8.1 convolution_bitcast_fusion.2
  784.4 8.1 convolution_bitcast_fusion.1
  792.6 8.4 convolution_bitcast_fusion
  801.0 1.3 reduce-scatter.5.cloned.1.call-done
  802.3 1.2 copy-done.9
  803.5 51.2 %last_exchange.1 = (f32[10,64]{1,0:T(8,128)S(1)}, f32[256,2048]{1,0:T(8,128)S(1)}, f32[64,2048]{1,0:T(8,128)S(1)}, f32[64,2048]{1,0:T(8,128)S(1)}) custom-call(f32[32,10,64]{2,1,0:T(8,128)S(1)} %maximum_bitcast_fusion.x_ref, bf16[2,256,1024]{2,1,0:T(8,128)(2,1)S(1)} %bitcast.215, bf16[4,512,512]{2,1,0:T(8,128)(2,1)} %pad_maximum_fusion.g_hbm), custom_call_target="tpu_custom_call" | custom-call | tf_op jit(solution)/shard_map/last_exchange/pallas_call | solution.py:1140
  855.8 1.3 copy.135
  (180 shorter events, 22.4 us)
Async XLA Ops:
  7.2 210.8 %all-gather.2.cloned.1.call-start = ((), (), s32[]{:S(2)}) async-start(), calls=%async_computation.2 | async-start | bytes 5242880 | tf_op jit(solution)/shard_map/all_gather | solution.py:1481
  9.7 1.0 copy-start
  10.8 1.2 copy-start.8
  12.0 0.9 copy-start.10
  13.0 0.9 copy-start.11
  136.7 1.3 copy-start.14
  138.0 584.5 %reduce-scatter.3.cloned.1.call-start = ((), (), s32[]{:S(2)}) async-start(), calls=%async_computation.3 | async-start | bytes 5242880 | tf_op jit(solution)/shard_map/reduce_scatter | solution.py:1485
  141.0 2.2 copy-start.13
  143.2 1.8 copy-start.15
  150.5 2.0 copy-start.6
  180.5 2.0 copy-start.4
  196.1 20.0 %copy-start.27 = (s32[2,1,64,2]{2,3,1,0:T(2,128)S(1)}, s32[2,1,64,2]{2,3,1,0:T(2,128)}, u32[]{:S(2)}) copy-start(s32[2,1,64,2]{2,3,1,0:T(2,128)} %param.30) | copy-start | bytes 3076
  196.1 20.2 %copy-start.29 = (s32[2,1,64]{2,1,0:T(1,128)S(1)}, s32[2,1,64]{2,1,0:T(1,128)}, u32[]{:S(2)}) copy-start(s32[2,1,64]{2,1,0:T(1,128)} %param.31) | copy-start | bytes 1540
  196.1 20.5 %copy-start.20 = (bf16[2,1,64,2048]{3,2,1,0:T(8,128)(2,1)S(1)}, bf16[2,1,64,2048]{3,2,1,0:T(8,128)(2,1)}, u32[]{:S(2)}) copy-start(bf16[2,1,64,2048]{3,2,1,0:T(8,128)(2,1)} %param.33) | copy-start | bytes 1572868
  227.3 22.9 %copy-start.1 = (bf16[2,1,64,2048]{3,2,1,0:T(8,128)(2,1)S(1)}, bf16[2,1,64,2048]{3,2,1,0:T(8,128)(2,1)}, u32[]{:S(2)}) copy-start(bf16[2,1,64,2048]{3,2,1,0:T(8,128)(2,1)} %param.17) | copy-start | bytes 1572868
  250.2 0.8 copy-start.2
  251.3 2.4 copy-start.23
  601.4 5.8 copy-start.3
  601.4 6.6 copy-start.21
  603.1 8.2 copy-start.18
  608.0 24.9 %copy-start.25 = (bf16[1024,2048]{1,0:T(8,128)(2,1)S(1)}, bf16[1024,2048]{1,0:T(8,128)(2,1)}, u32[]{:S(2)}) copy-start(bf16[1024,2048]{1,0:T(8,128)(2,1)} %get-tuple-element.195) | copy-start | bytes 12582916
  636.3 1.6 copy-start.28
  644.0 158.2 %reduce-scatter.5.cloned.1.call-start = ((), (), s32[]{:S(2)}) async-start(), calls=%async_computation.4 | async-start | bytes 5242880 | tf_op jit(solution)/shard_map/reduce_scatter | solution.py:1485
  679.9 40.5 %copy-start.24 = (bf16[128,2048]{1,0:T(8,128)(2,1)S(1)}, bf16[128,2048]{1,0:T(8,128)(2,1)}, u32[]{:S(2)}) copy-start(bf16[128,2048]{1,0:T(8,128)(2,1)} %copy-done.23) | copy-start | bytes 1572868
  689.4 2.2 copy-start.5
  726.0 2.2 copy-start.12
  728.2 1.6 copy-start.16
  729.8 1.6 copy-start.17
  765.4 3.8 copy-start.7
  769.1 6.6 slice-start.2
  770.5 1.6 copy-start.26
  770.5 3.1 copy-start.19
  770.5 3.1 copy-start.22
  770.5 5.2 slice-start.3
  772.1 4.2 copy-start.32
  776.3 8.1 copy-start.31
  776.3 16.3 %slice-start = ((s8[8388608]{0:T(1024)(128)(4,1)}), s8[4194304]{0:T(1024)(128)(4,1)S(1)}, s32[]{:S(2)}) async-start(s8[8388608]{0:T(1024)(128)(4,1)} %bitcast.274), calls=%async_computation.5 | async-start | bytes 8388608
  784.4 8.1 slice-start.1
  784.4 8.1 copy-start.30
  802.2 1.2 copy-start.9
Sparse Core Ops, SparseCore 0:
  138.2 79.7 all-gather.1
  644.1 78.3 reduce-scatter.2
  724.9 77.2 reduce-scatter.4

commit v11 on v10

--- a/solution.py
+++ b/solution.py
@@ -1005,44 +1005,52 @@
 
     lax.fori_loop(1, count, greet_one, 0)
     pl.semaphore_wait(barrier, count - 1)
-    UP, DOWN, SWAP, PAIR = 0, line, 2 * line, 2 * line + trees
-
-    def sum_up(j):
-        return remote(g_ref.at[j], hop.at[j], send.at[UP + j], recv.at[UP + j], up)
-
-    def sum_down(j, slot):
-        return remote(g_ref.at[j], hop.at[slot], send.at[DOWN + j], recv.at[DOWN + j], down)
-
-    def fold(t):
+    UP, DOWN, SWAP, PAIR = 0, pairs * line, 2 * pairs * line, 2 * pairs * line + trees
+    size = span // pairs
+
+    def sum_up(j, h):
+        where, use = pl.ds(h * size, size), UP + pairs * j + h
+        return remote(g_ref.at[j, where], hop.at[j, where], send.at[use], recv.at[use], up)
+
+    def sum_down(j, slot, h):
+        where, use = pl.ds(h * size, size), DOWN + pairs * j + h
+        return remote(g_ref.at[j, where], hop.at[slot, where], send.at[use], recv.at[use], down)
+
+    def fold(t, done=None):
         j = order(t)
-        own = g_ref.at[j]
-
-        @pl.when((j >= z) & (z > 0))
-        def _():
-            sum_up(j).wait_recv()
-            add_into(own, [own, hop.at[j]], span)
-
-        @pl.when((j < z) & (z < line - 1))
-        def _():
-            sum_down(j, j).wait_recv()
-            add_into(own, [own, hop.at[j]], span)
-
-        @pl.when((j == z) & (z < line - 1))
-        def _():
-            sum_down(j, line).wait_recv()
-            add_into(own, [own, hop.at[line]], span)
-
-        @pl.when(j > z)
-        def _():
-            sum_up(j).start()
-
-        @pl.when((j < z) & (j != z - 1))
-        def _():
-            sum_down(j, j).start()
-
-        @pl.when((j < z) & (j == z - 1))
-        def _():
-            sum_down(j, line).start()
+        for h in range(pairs):
+            where = pl.ds(h * size, size)
+            own = g_ref.at[j, where]
+
+            @pl.when((j >= z) & (z > 0))
+            def _():
+                sum_up(j, h).wait_recv()
+                add_into(own, [own, hop.at[j, where]], size)
+
+            @pl.when((j < z) & (z < line - 1))
+            def _():
+                sum_down(j, j, h).wait_recv()
+                add_into(own, [own, hop.at[j, where]], size)
+
+            @pl.when((j == z) & (z < line - 1))
+            def _():
+                sum_down(j, line, h).wait_recv()
+                add_into(own, [own, hop.at[line, where]], size)
+
+            @pl.when(j > z)
+            def _():
+                sum_up(j, h).start()
+
+            @pl.when((j < z) & (j != z - 1))
+            def _():
+                sum_down(j, j, h).start()
+
+            @pl.when((j < z) & (j == z - 1))
+            def _():
+                sum_down(j, line, h).start()
+
+            if done is not None:
+                done(h)
 
     fetch.wait()
     fold(3)
@@ -1084,28 +1092,36 @@
 
     lax.fori_loop(1, count, finish, 0)
     o_ref[...] = jnp.sum(got[...], axis=0)
-    fold(0)
-
     def share_of(index):
         return g_ref.at[z, pl.ds(pl.multiple_of(index * piece, piece), piece)]
 
     keep = pltpu.make_async_copy(share_of(mine), k_ref.at[mine], local)
-    keep.start()
-    swaps = []
+
+    def deal(index):
+        use = SWAP + (index + trees - mine) % trees
+        return remote(
+            share_of(index),
+            k_ref.at[mine],
+            send.at[use],
+            recv.at[use],
+            {"pair": index // experts, "expert": index % experts},
+        )
+
+    def leave(h):
+        for index in range(h * experts, (h + 1) * experts):
+
+            @pl.when(mine == index)
+            def _():
+                keep.start()
+
+            @pl.when(mine != index)
+            def _():
+                deal(index).start()
+
+    fold(0, leave)
+    keep.wait()
     for shift in range(1, trees):
-        peer = (mine + shift) % trees
-        copy = remote(
-            share_of(peer),
-            k_ref.at[mine],
-            send.at[SWAP + shift],
-            recv.at[SWAP + shift],
-            {"pair": peer // experts, "expert": peer % experts},
-        )
-        copy.start()
-        swaps.append(copy)
-    keep.wait()
-    for copy in swaps:
-        copy.wait()
+        deal((mine + shift) % trees).wait()
     share = k_ref.shape[2] // 2
     for source in range(trees):
         column = ((source % experts) * pairs + source // experts) * share
@@ -1116,13 +1132,15 @@
     swap.wait_send()
 
     def drain(j, carry):
-        @pl.when(j > z)
-        def _():
-            sum_up(j).wait_send()
-
-        @pl.when(j < z)
-        def _():
-            sum_down(j, j).wait_send()
+        for h in range(pairs):
+
+            @pl.when(j > z)
+            def _():
+                sum_up(j, h).wait_send()
+
+            @pl.when(j < z)
+            def _():
+                sum_down(j, j, h).wait_send()
 
         return carry
 
@@ -1135,7 +1153,7 @@
     count, block = sums.shape[0], sums.shape[1:]
     _, rows, cols = query.shape
     span, thin = grads.shape[0] // line, grads.shape[1]
-    uses = 2 * line + trees + 1
+    uses = 2 * pairs * line + trees + 1
     wide = jax.ShapeDtypeStruct((span // trees, trees * thin // 2), F32)
     return pl.pallas_call(
         partial(last_kernel, sizes),

time: 876 us -> 875 us (level)
  no operation moved by 1% of the time
where the time goes in v11:
time: 875 us; the launch traced here: 865 us
  Pallas kernels  705 us (81%)
  matrix products  84.3 us (10%)
  local copies, waits for them, and re-layouts  35 us (4%)
  other arithmetic  21.9 us (3%)
  between operations  14.9 us (2%)
    pallas_call x1, Pallas kernels, feed_forward(): pl.pallas_call(ff_kernel, in_specs=[ANY] * 5, out_specs=[ANY] * 7, out_sh...  346 us
    pallas_call x1, Pallas kernels, start_all(): pl.pallas_call(partial(start_all_kernel, sizes), in_specs=[VMEM] * 6, out...  123 us
    pallas_call x3, Pallas kernels, cube_reduce(): pl.pallas_call(partial(cube_reduce_kernel, pairs), in_specs=[VMEM], out_s...  74.5 us
    pallas_call x1, Pallas kernels, last_exchange(): pl.pallas_call(partial(last_kernel, sizes), in_specs=[VMEM, VMEM, ANY], o...  50.7 us
    pallas_call x2, Pallas kernels, cube_gather(): pl.pallas_call(partial(cube_gather_kernel, pairs), in_specs=[VMEM], out_s...  49.4 us
    dot_general x9, matrix products, product_tn(): lax.dot_general(left, right, (((0,), (0,)), ((), ())), preferred_element_...  48.4 us
    unnamed x81, local copies, waits for them, and re-layouts  28.8 us
    pallas_call x1, Pallas kernels, attend_back(): pl.pallas_call(partial(attend_back_kernel, part // HDIM, scale), grid=gri...  25.7 us
  transfers between devices with their start and end apart: 3, of which 3 were waited for; matrix products, arithmetic and copies ran while one was open for 9% of the time, Pallas kernels for 16%

profile of v11, /device:TPU:0, one launch (start us, length us, event | category | flops | bytes accessed | tf_op | source)
XLA Modules:
  0.0 865.1 jit_solution(5098955551754130145)
XLA Ops:
  10.8 1.2 copy-done.8
  13.9 122.8 %start_all.1 = (bf16[2,2,2,128,2048]{4,3,2,1,0:T(8,128)(2,1)}, bf16[4,512,1024]{2,1,0:T(8,128)(2,1)}, bf16[4,512,512]{2,1,0:T(8,128)(2,1)S(1)}, bf16[32,10,64]{2,1,0:T(8,128)(2,1)S(1)}, s32[2,16,128]{2,1,0:T(8,128)S(1)}) custom-call(bf16[128,2048]{1,0:T(8,128)(2,1)S(1)} %bitcast.204, bf16[256,2048]{1,0:T(8,128)(2,1)S(1)} %bitcast.214, ...), custom_call_target="tpu_custom_call" | custom-call | tf_op jit(solution)/shard_map/start_all/pallas_call | solution.py:1383
  136.7 1.3 copy-done.14
  141.0 2.2 copy-done.13
  143.2 1.8 copy-done.15
  145.0 5.6 project.1
  150.5 2.0 copy-done.6
  152.7 27.7 %cube_gather.2 = bf16[1,2,2,2048,256]{4,3,2,1,0:T(8,128)(2,1)S(1)} custom-call(bf16[2048,256]{1,0:T(8,128)(2,1)S(1)} %bitcast.213), custom_call_target="tpu_custom_call" | custom-call | bytes 41943040 | tf_op jit(solution)/shard_map/cube_gather/pallas_call | solution.py:405
  180.5 2.0 copy-done.4
  183.5 1.2 multiply_sine_fusion
  184.8 1.3 or_select_fusion.bias_ref
  186.1 10.0 %fusion.85.raw_ref = f32[2,4,2,64,1024]{4,3,2,1,0:T(8,128)} fusion(bf16[2,4,2,64,2048]{4,3,2,1,0:T(8,128)(2,1)} %bitcast.210, bf16[2048,1024,1,1,1]{1,0,4,3,2:T(8,128)(2,1)} %bitcast.220), kind=kOutput, calls=%fused_computation.212 | convolution fusion | flops 4294967296 | bytes 12582912 | tf_op jit(solution)/shard_map/dot_general | solution.py:20
  196.1 20.0 %attend.1 = (bf16[2,4,2,64,1024]{4,3,2,1,0:T(8,128)(2,1)}, bf16[2,4,2,64,1024]{4,3,2,1,0:T(8,128)(2,1)}) custom-call(f32[2,4,2,64,1024]{4,3,2,1,0:T(8,128)} %fusion.85.raw_ref, bf16[4,2,2,4,2,64,256]{6,5,4,3,2,1,0:T(8,128)(2,1)} %bitcast.205, f32[256,64]{1,0:T(8,128)} %get-tuple-element.193.cos_ref, f32[256,64]{1,0:T(8,128)} %get-tuple-element.192.sin_ref, ...), custom_call_target="tpu_custom_call" | custom-call | flops 1073741824 | bytes 12582912 | tf_op jit(solution)/shard_map/attend/pallas_call | solution.py:179
  216.6 1.1 bitcast_convert_fusion.1
  218.0 9.3 %multiply_convert_fusion = (bf16[1024,2048]{1,0:T(8,128)(2,1)S(1)}, bf16[1024,2048]{1,0:T(8,128)(2,1)}) fusion(f32[1024]{0:T(1024)S(1)} %multiply_reduce_fusion.6, bf16[1024,1024]{1,0:T(8,128)(2,1)} %bitcast.271, bf16[1024,2048]{1,0:T(8,128)(2,1)} %all-gather.2.cloned.1.call-done), kind=kOutput, calls=%fused_computation.6 | convolution fusion | flops 4301258752 | bytes 14684160 | tf_op jit(solution)/shard_map/dot_general | solution.py:20
  227.3 22.9 %cube_reduce.3 = bf16[128,2048]{1,0:T(8,128)(2,1)S(1)} custom-call(bf16[2,2,2,128,2048]{4,3,2,1,0:T(8,128)(2,1)S(1)} %bitcast.209), custom_call_target="tpu_custom_call" | custom-call | tf_op jit(solution)/shard_map/cube_reduce/pallas_call | solution.py:335
  252.6 1.1 copy.103
  255.1 346.3 %feed_forward.1 = (bf16[4,64,2048]{2,1,0:T(8,128)(2,1)}, bf16[4,64,2048]{2,1,0:T(8,128)(2,1)}, bf16[4,2,256,2048]{3,2,1,0:T(8,128)(2,1)}, bf16[4,2,256,2048]{3,2...) custom-call(bf16[4,64,2048]{2,1,0:T(8,128)(2,1)} %bitcast.233, ...), custom_call_target="tpu_custom_call" | custom-call | flops 35433480192 | bytes 50331648 | tf_op jit(solution)/shard_map/feed_forward/pallas_call | solution.py:946
  601.4 1.7 fusion.15
  603.1 3.9 multiply_reduce_fusion
  608.1 3.2 fusion.82
  611.3 21.7 %cube_gather.3 = bf16[2,2,2,128,2048]{4,3,2,1,0:T(8,128)(2,1)S(1)} custom-call(bf16[128,2048]{1,0:T(8,128)(2,1)S(1)} %get-tuple-element.168.x_ref), custom_call_target="tpu_custom_call" | custom-call | bytes 20971520 | tf_op jit(solution)/shard_map/cube_gather/pallas_call | solution.py:405
  633.0 3.3 fusion.2
  637.9 6.1 convolution_convert_fusion.1
  644.8 9.3 %convolution_convert_fusion.5 = bf16[1024,1024]{1,0:T(8,128)(2,1)} fusion(bf16[1024,2048]{1,0:T(8,128)(2,1)} %get-tuple-element.70, bf16[1024,2048]{1,0:T(8,128)(2,1)} %all-gather.2.cloned.1.call-done), kind=kOutput, calls=%fused_computation.22 | convolution fusion | flops 4296015872 | bytes 10485760 | tf_op jit(solution)/shard_map/dot_general | solution.py:28
  654.2 25.7 %attend_back.1 = (bf16[2,4,2,64,1024]{4,3,2,1,0:T(8,128)(2,1)}, bf16[4,2,2,4,2,64,256]{6,5,4,3,2,1,0:T(8,128)(2,1)}) custom-call(bf16[2,4,2,64,1024]{4,3,2,1,0:T(8,128)(2,1)} %get-tuple-element.68.query_ref, bf16[4,2,2,4,2,64,256]{6,5,4,3,2,1,0:T(8,128)(2,1)} %bitcast.206, bf16[2,4,2,64,1024]{4,3,2,1,0:T(8,128)(2,1)} %bitcast.284, ...), custom_call_target="tpu_custom_call" | custom-call | flops 2684354560 | bytes 14680064 | tf_op jit(solution)/shard_map/attend_back/pallas_call | solution.py:197
  679.9 9.5 %convolution_convert_fusion = bf16[2048,1024]{1,0:T(8,128)(2,1)} fusion(bf16[1024,2048]{1,0:T(8,128)(2,1)} %copy-done.6, bf16[1024,1024]{1,0:T(8,128)(2,1)} %bitcast.225), kind=kOutput, calls=%fused_computation.9 | convolution fusion | flops 4297064448 | bytes 10485760 | tf_op jit(solution)/shard_map/dot_general | solution.py:24
  689.4 2.2 copy-done.5
  691.6 28.7 %cube_reduce.4 = bf16[2048,256]{1,0:T(8,128)(2,1)S(1)} custom-call(bf16[1,2,2,2048,256]{4,3,2,1,0:T(8,128)(2,1)S(1)} %bitcast.207), custom_call_target="tpu_custom_call" | custom-call | tf_op jit(solution)/shard_map/cube_reduce/pallas_call | solution.py:335
  720.6 1.9 reduce-scatter.3.cloned.1.call-done
  722.5 2.8 fusion.29
  726.0 2.2 copy-done.12
  728.2 1.6 copy-done.16
  729.8 1.6 copy-done.17
  731.4 10.3 %input_gradient.1 = bf16[1024,2048]{1,0:T(8,128)(2,1)S(1)} custom-call(bf16[1024,1024]{1,0:T(8,128)(2,1)S(1)} %bitcast.226, bf16[2048,1024]{1,0:T(8,128)(2,1)S(1)} %bitcast.221, bf16[2,1024,256]{2,1,0:T(8,128)(2,1)S(1)} %bitcast.212, bf16[2048,512]{1,0:T(8,128)(2,1)S(1)} %bitcast.224, f32[1024,4]{1,0:T(8,128)S(1)} %copy.106.dl_ref, ...), custom_call_target="tpu_custom_call" | custom-call | flops 6442450944 | bytes 12582912 | tf_op jit(solution)/shard_map/input_gradient/pallas_call | solution.py:1424
  741.7 22.9 %cube_reduce.5 = bf16[128,2048]{1,0:T(8,128)(2,1)S(1)} custom-call(bf16[2,2,2,128,2048]{4,3,2,1,0:T(8,128)(2,1)S(1)} %bitcast.208), custom_call_target="tpu_custom_call" | custom-call | tf_op jit(solution)/shard_map/cube_reduce/pallas_call | solution.py:335
  765.4 3.7 convolution_convert_fusion.3
  769.1 1.4 convolution_convert_fusion.4
  770.6 1.5 pad_maximum_fusion.g_hbm
  772.1 1.6 bitcast_convert_fusion
  773.7 2.1 fusion.9
  776.3 8.1 convolution_bitcast_fusion.2
  784.4 8.1 convolution_bitcast_fusion.1
  792.6 8.4 convolution_bitcast_fusion
  801.0 1.3 reduce-scatter.5.cloned.1.call-done
  802.3 1.2 copy-done.9
  803.5 50.7 %last_exchange.1 = (f32[10,64]{1,0:T(8,128)S(1)}, f32[256,2048]{1,0:T(8,128)S(1)}, f32[64,2048]{1,0:T(8,128)S(1)}, f32[64,2048]{1,0:T(8,128)S(1)}) custom-call(f32[32,10,64]{2,1,0:T(8,128)S(1)} %maximum_bitcast_fusion.x_ref, bf16[2,256,1024]{2,1,0:T(8,128)(2,1)S(1)} %bitcast.215, bf16[4,512,512]{2,1,0:T(8,128)(2,1)} %pad_maximum_fusion.g_hbm), custom_call_target="tpu_custom_call" | custom-call | tf_op jit(solution)/shard_map/last_exchange/pallas_call | solution.py:1158
  855.3 1.3 copy.135
  (180 shorter events, 22.4 us)
Async XLA Ops:
  7.2 210.8 %all-gather.2.cloned.1.call-start = ((), (), s32[]{:S(2)}) async-start(), calls=%async_computation.2 | async-start | bytes 5242880 | tf_op jit(solution)/shard_map/all_gather | solution.py:1499
  9.7 1.0 copy-start
  10.8 1.2 copy-start.8
  12.0 0.9 copy-start.10
  13.0 0.9 copy-start.11
  136.7 1.3 copy-start.14
  138.0 584.5 %reduce-scatter.3.cloned.1.call-start = ((), (), s32[]{:S(2)}) async-start(), calls=%async_computation.3 | async-start | bytes 5242880 | tf_op jit(solution)/shard_map/reduce_scatter | solution.py:1503
  141.0 2.2 copy-start.13
  143.2 1.8 copy-start.15
  150.5 2.0 copy-start.6
  180.5 2.0 copy-start.4
  196.1 20.0 %copy-start.27 = (s32[2,1,64,2]{2,3,1,0:T(2,128)S(1)}, s32[2,1,64,2]{2,3,1,0:T(2,128)}, u32[]{:S(2)}) copy-start(s32[2,1,64,2]{2,3,1,0:T(2,128)} %param.30) | copy-start | bytes 3076
  196.1 20.2 %copy-start.29 = (s32[2,1,64]{2,1,0:T(1,128)S(1)}, s32[2,1,64]{2,1,0:T(1,128)}, u32[]{:S(2)}) copy-start(s32[2,1,64]{2,1,0:T(1,128)} %param.31) | copy-start | bytes 1540
  196.1 20.5 %copy-start.20 = (bf16[2,1,64,2048]{3,2,1,0:T(8,128)(2,1)S(1)}, bf16[2,1,64,2048]{3,2,1,0:T(8,128)(2,1)}, u32[]{:S(2)}) copy-start(bf16[2,1,64,2048]{3,2,1,0:T(8,128)(2,1)} %param.33) | copy-start | bytes 1572868
  227.3 22.9 %copy-start.1 = (bf16[2,1,64,2048]{3,2,1,0:T(8,128)(2,1)S(1)}, bf16[2,1,64,2048]{3,2,1,0:T(8,128)(2,1)}, u32[]{:S(2)}) copy-start(bf16[2,1,64,2048]{3,2,1,0:T(8,128)(2,1)} %param.17) | copy-start | bytes 1572868
  250.2 0.8 copy-start.2
  251.3 2.4 copy-start.23
  601.4 5.8 copy-start.3
  601.4 6.6 copy-start.21
  603.1 8.2 copy-start.18
  608.0 24.9 %copy-start.25 = (bf16[1024,2048]{1,0:T(8,128)(2,1)S(1)}, bf16[1024,2048]{1,0:T(8,128)(2,1)}, u32[]{:S(2)}) copy-start(bf16[1024,2048]{1,0:T(8,128)(2,1)} %get-tuple-element.195) | copy-start | bytes 12582916
  636.3 1.6 copy-start.28
  644.0 158.2 %reduce-scatter.5.cloned.1.call-start = ((), (), s32[]{:S(2)}) async-start(), calls=%async_computation.4 | async-start | bytes 5242880 | tf_op jit(solution)/shard_map/reduce_scatter | solution.py:1503
  679.9 40.5 %copy-start.24 = (bf16[128,2048]{1,0:T(8,128)(2,1)S(1)}, bf16[128,2048]{1,0:T(8,128)(2,1)}, u32[]{:S(2)}) copy-start(bf16[128,2048]{1,0:T(8,128)(2,1)} %copy-done.23) | copy-start | bytes 1572868
  689.4 2.2 copy-start.5
  726.0 2.2 copy-start.12
  728.2 1.6 copy-start.16
  729.8 1.6 copy-start.17
  765.4 3.8 copy-start.7
  769.1 6.6 slice-start.2
  770.5 1.6 copy-start.26
  770.5 3.1 copy-start.19
  770.5 3.1 copy-start.22
  770.5 5.2 slice-start.3
  772.1 4.2 copy-start.32
  776.3 8.1 copy-start.31
  776.3 16.3 %slice-start = ((s8[8388608]{0:T(1024)(128)(4,1)}), s8[4194304]{0:T(1024)(128)(4,1)S(1)}, s32[]{:S(2)}) async-start(s8[8388608]{0:T(1024)(128)(4,1)} %bitcast.274), calls=%async_computation.5 | async-start | bytes 8388608
  784.4 8.1 slice-start.1
  784.4 8.1 copy-start.30
  802.2 1.2 copy-start.9
Sparse Core Ops, SparseCore 0:
  138.2 79.7 all-gather.1
  644.1 78.3 reduce-scatter.2
  724.9 77.2 reduce-scatter.4
